TPU v7x, 32 devices: a whole 2x2x4 slice. The times are simulated.
32 devices in a mesh: dp: 8 (over y, x, core), expert: 4 (over z).
Axes of the slice: x: 2, y: 2, z: 4, core: 2. Of those that a mesh axis runs over, the one named last changes fastest.
Arguments:
- hidden: bfloat16 [16384, 1024], P(('dp', 'expert')), may hold values from -6 to 6
- cotangent: bfloat16 [16384, 1024], P(('dp', 'expert')), may hold values from -6 to 6
- lengths: int32 [32], replicated, may hold values from 128 to 512, as said below
- adapter_ids: int32 [32], replicated, may hold values from 0 to 7
- routes: int32 [16384, 8], P('dp'), may hold values from 0 to 15, all different within a row; in each aligned block of 512 rows (0 to 511, 512 to 1023, ...) at most 384 rows name the same one
- attn_gain: bfloat16 [1024], replicated, may hold values from 0.25 to 1.75
- ffn_gain: bfloat16 [1024], replicated, may hold values from 0.25 to 1.75
- query_key_value_weight: bfloat16 [1024, 2048], P('dp'), may hold values from -0.1875 to 0.1875
- w_out: bfloat16 [1024, 1024], P('dp'), may hold values from -0.75 to 0.75
- w_router: bfloat16 [1024, 16], replicated, may hold values from -0.09375 to 0.09375
- w_gate_up: bfloat16 [16, 1024, 1024], P('expert'), may hold values from -0.1875 to 0.1875
- w_down: bfloat16 [16, 512, 1024], P('expert'), may hold values from -0.75 to 0.75
- attention_lowmap: bfloat16 [4, 8, 1024, 16], P(None, None, 'dp'), may hold values from -0.1875 to 0.1875
- attention_query_key_value_upmap: bfloat16 [8, 16, 2048], P(None, None, 'dp'), may hold values from -1.5 to 1.5
- attention_output_upmap: bfloat16 [8, 16, 1024], P(None, None, 'dp'), may hold values from -6 to 6
- expert_gate_up_lowmap: bfloat16 [16, 8, 1024, 32], P('expert'), may hold values from -0.1875 to 0.1875
- expert_gate_up_upmap: bfloat16 [16, 8, 2, 16, 512], P('expert'), may hold values from -1.5 to 1.5
- expert_down_lowmap: bfloat16 [16, 8, 512, 16], P('expert'), may hold values from -0.25 to 0.25
- expert_down_upmap: bfloat16 [16, 8, 16, 1024], P('expert'), may hold values from -4 to 4
Outputs:
- out: bfloat16 [16384, 1024], P(('dp', 'expert'))
- grad_hidden: bfloat16 [16384, 1024], P(('dp', 'expert'))
- grad_mixer_a: float32 [4, 8, 1024, 16], P(None, None, ('dp', 'expert'))
- grad_mixer_b_qkv: float32 [8, 16, 2048], P(None, None, ('dp', 'expert'))
- grad_mixer_b_out: float32 [8, 16, 1024], P(None, None, ('dp', 'expert'))
- grad_exp_a_in: float32 [16, 8, 1024, 32], P('expert', None, 'dp')
- grad_exp_b_in: float32 [16, 8, 2, 16, 512], P('expert', None, None, None, 'dp')
- grad_exp_a_down: float32 [16, 8, 512, 16], P('expert', None, 'dp')
- grad_exp_b_down: float32 [16, 8, 16, 1024], P('expert', None, None, 'dp')
Inputs may be any that keep to these rules, and one draw needn't show every extreme that they name: `routes`: each row names 8 different experts. Among the 512 rows of one sequence no expert is named more than 384 times, and in every draw some sequence names some expert exactly 384 times. `lengths`: some sequence is 512 long in every draw.
All inputs are finite; a program needn't handle non-finite values.
Results may differ from a plain program's by a relative error of at most 0.022.
The roundings to bfloat16 on the way count: a program that leaves them out, or rounds other values in their place, can miss the bound.
Values may be sent and summed in bfloat16 or wider, within the bound.
No kernel may reach another device: no remote copies, remote signals or barrier semaphores. Data moves between devices by JAX's collectives and lax.ppermute only.
A program may use at most 320 MiB of HBM per device.

v0:
```python
import numpy as np
import jax
import jax.numpy as jnp
from jax import lax
from jax.experimental import pallas as pl
from jax.experimental.pallas import tpu as pltpu
from jax.sharding import PartitionSpec as P

MODEL_WIDTH = 1024
HQ = 16
KVH = 8
HS = 64
H = 512
TOP = 8
R = 16
NA = 8
QD = HQ * HS
KD = KVH * HS
QKV = QD + 2 * KD

epsilon = 1e-06
f32 = jnp.float32
bf16 = jnp.bfloat16


def nn(left, right):
    return lax.dot_general(left, right, (((1,), (0,)), ((), ())), preferred_element_type=f32)


def nt(left, right):
    return lax.dot_general(left, right, (((1,), (1,)), ((), ())), preferred_element_type=f32)


def tn(left, right):
    return lax.dot_general(left, right, (((0,), (0,)), ((), ())), preferred_element_type=f32)


def lanes_of(shape):
    return lax.broadcasted_iota(jnp.int32, shape, len(shape) - 1)


def row_scale(rows):
    return lax.rsqrt(jnp.mean(rows * rows, -1, keepdims=True) + epsilon)


def norm_back(rows, gain, grad):
    scale = row_scale(rows)
    scaled = grad * gain
    return scale * scaled - rows * (scale * scale * scale) * jnp.mean(
        rows * scaled, -1, keepdims=True
    )


def rope_swap(rows):
    width = rows.shape[-1]
    lane = lanes_of(rows.shape)
    return jnp.where(
        lane % HS < HS // 2,
        pltpu.roll(rows, width - HS // 2, 1),
        pltpu.roll(rows, HS // 2, 1),
    )


def both_halves(pair, half):
    rows = pair.astype(f32)
    lane = lanes_of(rows.shape)
    rolled = pltpu.roll(rows, HS, 1)
    keep = (lane < HS) == (half == 0)
    return jnp.where(keep, rows, rolled).astype(bf16)


def stacked_heads(pair):
    lane = lanes_of(pair.shape)
    zero = jnp.zeros_like(pair)
    return jnp.concatenate(
        [jnp.where(lane < HS, pair, zero), jnp.where(lane < HS, zero, pair)], 0
    )


def params_of(count):
    return pltpu.CompilerParams(
        dimension_semantics=("arbitrary",) * count, vmem_limit_bytes=56 * 1024 * 1024
    )


BLOCK = 128
BLOCKS = MODEL_WIDTH // BLOCK
HALF = MODEL_WIDTH // 2


def column(order, at):
    return pl.ds(pl.multiple_of(order[at] * BLOCK, BLOCK), BLOCK)


def project_kernel(
    order, hid, gain, weight_a, weight_b, low_map, up_map, cos, sin, qkv, low, normed, turned_rows
):
    step = pl.program_id(0)
    blocks = pl.num_programs(0)

    @pl.when(step == 0)
    def _():
        rows = hid[...].astype(f32)
        value = (rows * row_scale(rows) * gain[...].astype(f32)).astype(bf16)
        normed[...] = value
        low[...] = nt(value, low_map[...]).astype(bf16)
        for at in range(BLOCKS):
            turned_rows[:, at * BLOCK : (at + 1) * BLOCK] = normed[:, column(order, at)]

    value = (
        nn(turned_rows[:, :HALF], weight_a[...])
        + nn(turned_rows[:, HALF:], weight_b[...])
        + nn(low[...], up_map[...])
    )

    @pl.when(step < blocks * 3 // 4)
    def _():
        for part in range(value.shape[1] // 128):
            piece = value[:, part * 128 : part * 128 + 128]
            turned = piece * cos[...] + rope_swap(piece) * sin[...]
            qkv[:, part * 128 : part * 128 + 128] = turned.astype(bf16)

    @pl.when(step >= blocks * 3 // 4)
    def _():
        qkv[...] = value.astype(bf16)


def project(order, hidden, gain, weights, low_map, up_map, cos, sin):
    rows = hidden.shape[0]
    block = 256
    ranks = low_map.shape[0]
    full = lambda shape: pl.BlockSpec(shape, lambda n, s: (0, 0))
    return pl.pallas_call(
        project_kernel,
        grid_spec=pltpu.PrefetchScalarGridSpec(
            num_scalar_prefetch=1,
            grid=(QKV // block,),
            in_specs=[
                full((rows, MODEL_WIDTH)),
                full((1, MODEL_WIDTH)),
                pl.BlockSpec((HALF, block), lambda n, s: (0, n)),
                pl.BlockSpec((HALF, block), lambda n, s: (0, n)),
                full((ranks, MODEL_WIDTH)),
                pl.BlockSpec((ranks, block), lambda n, s: (0, n)),
                full((rows, 128)),
                full((rows, 128)),
            ],
            out_specs=[
                pl.BlockSpec((rows, block), lambda n, s: (0, n)),
                full((rows, ranks)),
                full((rows, MODEL_WIDTH)),
            ],
            scratch_shapes=[pltpu.VMEM((rows, MODEL_WIDTH), bf16)],
        ),
        out_shape=[
            jax.ShapeDtypeStruct((rows, QKV), bf16),
            jax.ShapeDtypeStruct((rows, ranks), bf16),
            jax.ShapeDtypeStruct((rows, MODEL_WIDTH), bf16),
        ],
        compiler_params=params_of(1),
        name="project",
        cost_estimate=pl.CostEstimate(
            flops=2 * rows * QKV * MODEL_WIDTH, transcendentals=0, bytes_accessed=8 << 20
        ),
    )(order, hidden, gain, *weights, low_map, up_map, cos, sin)


ROWB = 128


def masked_scores(length, queries, keys, start, count):
    scores = 0.125 * nt(queries, keys)
    row = lax.broadcasted_iota(jnp.int32, scores.shape, 0)
    col = lanes_of(scores.shape)
    allowed = (col <= start + row % ROWB) & (col < length)
    return scores, allowed


def attend_kernel(scalars, query, key, value, result, lse):
    half = pl.program_id(0) % 2
    length = scalars[0]
    keys = both_halves(key[...], half)
    values = both_halves(value[...], half)
    rows = query.shape[0]
    for start in range(0, rows, ROWB):
        count = start + ROWB
        stacked = stacked_heads(query[start:count, :])
        scores, allowed = masked_scores(length, stacked, keys[:count], start, count)
        scores = jnp.where(allowed, scores, -1e30)
        top = jnp.max(scores, -1, keepdims=True)
        shifted = jnp.exp(scores - top)
        total = jnp.sum(shifted, -1, keepdims=True)
        prob = (shifted * (1.0 / total)).astype(bf16)
        mixed = nn(prob, values[:count])
        lane = lanes_of((ROWB, 128))
        result[start:count, :] = jnp.where(lane < HS, mixed[:ROWB], mixed[ROWB:]).astype(bf16)
        logs = top + jnp.log(total)
        lse[0, start:count, :] = jnp.concatenate([logs[:ROWB], logs[ROWB:]], 1)


def attend(length, qkv):
    rows = qkv.shape[0]
    pairs = KVH
    return pl.pallas_call(
        attend_kernel,
        grid_spec=pltpu.PrefetchScalarGridSpec(
            num_scalar_prefetch=1,
            grid=(pairs,),
            in_specs=[
                pl.BlockSpec((rows, 128), lambda g, s: (0, g)),
                pl.BlockSpec((rows, 128), lambda g, s: (0, QD // 128 + g // 2)),
                pl.BlockSpec((rows, 128), lambda g, s: (0, (QD + KD) // 128 + g // 2)),
            ],
            out_specs=[
                pl.BlockSpec((rows, 128), lambda g, s: (0, g)),
                pl.BlockSpec((1, rows, 2), lambda g, s: (g, 0, 0)),
            ],
        ),
        out_shape=[
            jax.ShapeDtypeStruct((rows, QD), bf16),
            jax.ShapeDtypeStruct((pairs, rows, 2), f32),
        ],
        compiler_params=params_of(1),
        name="attend",
        cost_estimate=pl.CostEstimate(
            flops=8 * rows * rows * QD, transcendentals=rows * rows * HQ, bytes_accessed=4 << 20
        ),
    )(length, qkv, qkv, qkv)


def attend_back_kernel(
    scalars, query, key, value, grad, lse, cos, sin, grad_query, grad_key, grad_value, key_acc, value_acc
):
    half = pl.program_id(0) % 2
    length = scalars[0]
    keys = both_halves(key[...], half)
    values = both_halves(value[...], half)
    rows = query.shape[0]
    key_acc[...] = jnp.zeros_like(key_acc)
    value_acc[...] = jnp.zeros_like(value_acc)
    for start in range(0, rows, ROWB):
        count = start + ROWB
        stacked = stacked_heads(query[start:count, :])
        grads = stacked_heads(grad[start:count, :])
        scores, allowed = masked_scores(length, stacked, keys[:count], start, count)
        logs = lse[0, start:count, :]
        logs = jnp.concatenate([logs[:, 0:1], logs[:, 1:2]], 0)
        prob = jnp.where(allowed, jnp.exp(scores - logs), 0.0)
        grad_prob = nt(grads, values[:count])
        delta = jnp.sum(prob * grad_prob, -1, keepdims=True)
        grad_score = (prob * (grad_prob - delta)).astype(bf16)
        mixed = nn(grad_score, keys[:count])
        lane = lanes_of((ROWB, 128))
        turned = 0.125 * jnp.where(lane < HS, mixed[:ROWB], mixed[ROWB:])
        turned = turned * cos[start:count, :] - rope_swap(turned) * sin[start:count, :]
        grad_query[start:count, :] = turned.astype(bf16)
        key_acc[:count, :] += tn(grad_score, stacked)
        value_acc[:count, :] += tn(prob.astype(bf16), grads)
    total = key_acc[...]
    total = 0.125 * (total + pltpu.roll(total, HS, 1))
    total = (total * cos[...] - rope_swap(total) * sin[...]).astype(bf16)
    other = value_acc[...]
    other = (other + pltpu.roll(other, HS, 1)).astype(bf16)

    @pl.when(half == 0)
    def _():
        grad_key[...] = total
        grad_value[...] = other

    @pl.when(half == 1)
    def _():
        low_half = lanes_of(total.shape) < HS
        grad_key[...] = jnp.where(low_half, grad_key[...], total)
        grad_value[...] = jnp.where(low_half, grad_value[...], other)


def attend_back(length, qkv, grad, lse, cos, sin):
    rows = qkv.shape[0]
    pairs = KVH
    return pl.pallas_call(
        attend_back_kernel,
        grid_spec=pltpu.PrefetchScalarGridSpec(
            num_scalar_prefetch=1,
            grid=(pairs,),
            in_specs=[
                pl.BlockSpec((rows, 128), lambda g, s: (0, g)),
                pl.BlockSpec((rows, 128), lambda g, s: (0, QD // 128 + g // 2)),
                pl.BlockSpec((rows, 128), lambda g, s: (0, (QD + KD) // 128 + g // 2)),
                pl.BlockSpec((rows, 128), lambda g, s: (0, g)),
                pl.BlockSpec((1, rows, 2), lambda g, s: (g, 0, 0)),
                pl.BlockSpec((rows, 128), lambda g, s: (0, 0)),
                pl.BlockSpec((rows, 128), lambda g, s: (0, 0)),
            ],
            out_specs=[
                pl.BlockSpec((rows, 128), lambda g, s: (0, g)),
                pl.BlockSpec((rows, 128), lambda g, s: (0, g // 2)),
                pl.BlockSpec((rows, 128), lambda g, s: (0, g // 2)),
            ],
            scratch_shapes=[pltpu.VMEM((rows, 128), f32), pltpu.VMEM((rows, 128), f32)],
        ),
        out_shape=[
            jax.ShapeDtypeStruct((rows, QD), bf16),
            jax.ShapeDtypeStruct((rows, KD), bf16),
            jax.ShapeDtypeStruct((rows, KD), bf16),
        ],
        compiler_params=params_of(1),
        name="attend_back",
        cost_estimate=pl.CostEstimate(
            flops=20 * rows * rows * QD, transcendentals=rows * rows * HQ, bytes_accessed=8 << 20
        ),
    )(length, qkv, qkv, qkv, grad, lse, cos, sin)


def close_kernel(order, att, hid, gain, weight_a, weight_b, low_map, up_map, mid, normed, low):
    low_value = nt(att[...], low_map[...]).astype(bf16)
    low[...] = low_value
    turned = jnp.concatenate([att[:, column(order, at)] for at in range(BLOCKS)], 1)
    stream = hid[...].astype(f32) + (
        nn(turned[:, :HALF], weight_a[...])
        + nn(turned[:, HALF:], weight_b[...])
        + nn(low_value, up_map[...])
    )
    mid[...] = stream
    normed[...] = (stream * row_scale(stream) * gain[...].astype(f32)).astype(bf16)


def close_mixer(order, att, hidden, gain, weights, low_map, up_map):
    rows = hidden.shape[0]
    block = 256
    ranks = low_map.shape[0]
    full = lambda shape: pl.BlockSpec(shape, lambda n, s: (0, 0))
    part = lambda width: pl.BlockSpec((block, width), lambda n, s: (n, 0))
    return pl.pallas_call(
        close_kernel,
        grid_spec=pltpu.PrefetchScalarGridSpec(
            num_scalar_prefetch=1,
            grid=(rows // block,),
            in_specs=[
                part(QD),
                part(MODEL_WIDTH),
                full((1, MODEL_WIDTH)),
                full((HALF, MODEL_WIDTH)),
                full((HALF, MODEL_WIDTH)),
                full((ranks, QD)),
                full((ranks, MODEL_WIDTH)),
            ],
            out_specs=[part(MODEL_WIDTH), part(MODEL_WIDTH), part(ranks)],
        ),
        out_shape=[
            jax.ShapeDtypeStruct((rows, MODEL_WIDTH), f32),
            jax.ShapeDtypeStruct((rows, MODEL_WIDTH), bf16),
            jax.ShapeDtypeStruct((rows, ranks), bf16),
        ],
        compiler_params=params_of(1),
        name="close_mixer",
        cost_estimate=pl.CostEstimate(
            flops=2 * rows * QD * MODEL_WIDTH, transcendentals=0, bytes_accessed=8 << 20
        ),
    )(order, att, hidden, gain, *weights, low_map, up_map)


def side_by_side(left, right):
    values = []
    for at in range(BLOCKS):
        tile = slice(at // 2 * BLOCK, (at // 2 + 1) * BLOCK)
        low_half = lanes_of((R, BLOCK)) < BLOCK // 2
        if at % 2 == 0:
            value = jnp.where(low_half, left[:, tile], pltpu.roll(right[:, tile], BLOCK // 2, 1))
        else:
            value = jnp.where(low_half, pltpu.roll(left[:, tile], BLOCK // 2, 1), right[:, tile])
        values.append(value.astype(bf16))
    return values


def expert_kernel(
    scalars,
    x,
    cot,
    routes,
    router,
    w_in,
    w_down,
    a_in,
    b_in,
    a_down,
    b_down,
    *rest,
):
    (
        out,
        grad_normed,
        gates_out,
        packed,
        gates,
        gate_sums,
        low_in,
        low_in_turned,
        b_in_all,
        back_low,
        gated_low,
        back_in,
        acts,
        grads,
        low_grads,
        down_acc,
        out_acc,
        grad_acc,
    ) = rest[-18:]
    expert = pl.program_id(0)
    last = pl.num_programs(0) - 1
    rows = x.shape[0]
    block = 256
    local = a_in.shape[0]
    a_in_all = a_in[...].reshape(local * 2 * R, MODEL_WIDTH)
    a_down_all = a_down[...].reshape(local * R, H)
    b_down_all = b_down[...].reshape(local * R, MODEL_WIDTH)

    @pl.when(expert == 0)
    def _():
        logits = nt(x[...], router[...])
        lane = lanes_of(logits.shape)
        chosen = lane == routes[:, 0:1]
        for k in range(1, TOP):
            chosen = chosen | (lane == routes[:, k : k + 1])
        top = jnp.max(jnp.where(chosen, logits, -1e30), -1, keepdims=True)
        shifted = jnp.where(chosen, jnp.exp(jnp.where(chosen, logits - top, 0.0)), 0.0)
        weights = shifted / jnp.sum(shifted, -1, keepdims=True)
        gates[...] = weights
        gates_out[...] = weights.T[: gates_out.shape[0], :]
        low = nt(x[...], a_in_all)
        low_in[...] = low.astype(bf16)
        low_in_turned[...] = low.T.astype(bf16)
        back_low[...] = nt(cot[...], b_down_all)
        b_in_all[...] = jnp.zeros_like(b_in_all)
        for e in range(local):
            b_in_all[e * 2 * R : e * 2 * R + R, :H] = b_in[e, 0, 0]
            b_in_all[e * 2 * R + R : (e + 1) * 2 * R, H:] = b_in[e, 0, 1]
        gate_sums[...] = jnp.zeros_like(gate_sums)
        gated_low[...] = jnp.zeros_like(gated_low)
        back_in[...] = jnp.zeros_like(back_in)
        out_acc[...] = jnp.zeros_like(out_acc)
        grad_acc[...] = jnp.zeros_like(grad_acc)
        down_acc[...] = jnp.zeros_like(down_acc)

    def row_step(index, carry):
        at = pl.ds(pl.multiple_of(index * block, block), block)
        lane_in = lanes_of((block, local * 2 * R))
        lane_down = lanes_of((block, local * R))
        in_mine = (lane_in >= expert * 2 * R) & (lane_in < (expert + 1) * 2 * R)
        down_mine = (lane_down >= expert * R) & (lane_down < (expert + 1) * R)
        gate_all = gates[at, :]
        gate_lane = lanes_of(gate_all.shape) == expert
        weight = jnp.sum(jnp.where(gate_lane, gate_all, 0.0), -1, keepdims=True)
        mine = low_in[at, :]
        mine = jnp.where(in_mine, mine, jnp.zeros_like(mine))
        both = nn(x[at, :], w_in[0]) + nn(mine, b_in_all[...])
        gate = both[:, :H]
        upper = both[:, H:]
        sigmoid = jax.nn.sigmoid(gate)
        silu = gate * sigmoid
        act = (silu * upper).astype(bf16)
        acts[at, :] = act
        act_wide = act.astype(f32)
        low = jnp.where(down_mine, nt(act, a_down_all), 0.0).astype(bf16).astype(f32)
        plain = nt(cot[at, :], w_down[0])
        low_plain = back_low[at, :]
        dots = jnp.sum(act_wide * plain, -1, keepdims=True) + jnp.sum(
            low * low_plain, -1, keepdims=True
        )
        sum_lane = lanes_of(gate_all.shape) == expert + scalars[2]
        gate_sums[at, :] += jnp.where(sum_lane, dots, 0.0)
        low_grad = jnp.where(down_mine, weight * low_plain, 0.0).astype(bf16)
        low_grads[at, :] = low_grad
        grad_act = weight * plain + nn(low_grad, a_down_all)
        grad_first = grad_act * upper * sigmoid * (1.0 + gate * (1.0 - sigmoid))
        grad_second = grad_act * silu
        grad_both = jnp.concatenate(
            [grad_first.astype(bf16), grad_second.astype(bf16)], 1
        )
        grads[at, :] = grad_both
        gated_low[at, :] += (weight * low).astype(bf16)
        out_acc[at, :] += nn((weight * act_wide).astype(bf16), w_down[0])
        grad_acc[at, :] += nt(grad_both, w_in[0])
        low_back = jnp.where(in_mine, nt(grad_both, b_in_all[...]), 0.0)
        back_in[at, :] += low_back.astype(bf16)
        return carry

    lax.fori_loop(0, rows // block, row_step, 0)

    turned = low_in_turned[pl.ds(pl.multiple_of(expert * 2 * R, 2 * R), 2 * R), :]
    product = nn(turned, grads[...])
    first_b_in = local * 3 * R
    here = pl.ds(pl.multiple_of(first_b_in + expert * R, R), R)
    for at, value in enumerate(side_by_side(product[:R, :H], product[R:, H:])):
        packed[at, 0, here, :] = value
    down_acc[...] += tn(low_grads[...], acts[...])

    @pl.when(expert == last)
    def _():
        out[...] = (out_acc[...] + nn(gated_low[...], b_down_all)).astype(bf16)
        grad_normed[:rows, :] = (grad_acc[...] + nn(back_in[...], a_in_all)).astype(bf16)
        experts = gates_out.shape[0]
        sums = gate_sums[...].T[:experts, :]
        sums = jnp.concatenate([sums[: experts // 2], sums[experts // 2 :]], 1)
        high = sums.astype(bf16).astype(f32)
        grad_normed[rows:, :] = jnp.concatenate([high, sums - high], 0).astype(bf16)
        wide = tn(back_in[...], x[...]).astype(bf16)
        tall = tn(gated_low[...], cot[...]).astype(bf16)
        for at in range(BLOCKS):
            columns = slice(at * BLOCK, (at + 1) * BLOCK)
            packed[at, 0, : local * 2 * R, :] = wide[:, columns]
            packed[at, 0, local * 2 * R : first_b_in, :] = tall[:, columns]
        for pair in range(local // 2):
            lower = down_acc[pair * 2 * R : pair * 2 * R + R, :]
            upper = down_acc[pair * 2 * R + R : (pair + 1) * 2 * R, :]
            row = local * 4 * R + pair * R
            for at, value in enumerate(side_by_side(lower, upper)):
                packed[at, 0, row : row + R, :] = value


def run_experts(
    scalars, x, cot, routes, router, w_in, w_down, a_in, b_in, a_down, b_down, experts, slots, packed
):
    rows = x.shape[0]
    local = w_in.shape[0]
    ranks_in = local * 2 * R
    ranks_down = local * R
    height = local * 9 * R // 2
    kept = [] if packed is None else [packed]
    full = lambda shape: pl.BlockSpec(shape, lambda e, s: (0,) * len(shape))
    return pl.pallas_call(
        expert_kernel,
        grid_spec=pltpu.PrefetchScalarGridSpec(
            num_scalar_prefetch=1,
            grid=(local,),
            in_specs=[
                full((rows, MODEL_WIDTH)),
                pl.BlockSpec((rows, MODEL_WIDTH), lambda e, s: (s[4], 0)),
                pl.BlockSpec((rows, TOP), lambda e, s: (s[0], 0)),
                full((128, MODEL_WIDTH)),
                pl.BlockSpec((1, MODEL_WIDTH, 2 * H), lambda e, s: (e, 0, 0)),
                pl.BlockSpec((1, H, MODEL_WIDTH), lambda e, s: (e, 0, 0)),
                pl.BlockSpec((local, 1, 2 * R, MODEL_WIDTH), lambda e, s: (0, s[1], 0, 0)),
                pl.BlockSpec((local, 1, 2, R, H), lambda e, s: (0, s[1], 0, 0, 0)),
                pl.BlockSpec((local, 1, R, H), lambda e, s: (0, s[1], 0, 0)),
                pl.BlockSpec((local, 1, R, MODEL_WIDTH), lambda e, s: (0, s[1], 0, 0)),
            ]
            + [pl.BlockSpec(memory_space=pl.ANY)] * len(kept),
            out_specs=[
                full((rows, MODEL_WIDTH)),
                full((rows + experts, MODEL_WIDTH)),
                full((experts, rows)),
                pl.BlockSpec((BLOCKS, 1, height, BLOCK), lambda e, s: (0, s[3], 0, 0)),
            ],
            scratch_shapes=[
                pltpu.VMEM((rows, 128), f32),
                pltpu.VMEM((rows, 128), f32),
                pltpu.VMEM((rows, ranks_in), bf16),
                pltpu.VMEM((ranks_in, rows), bf16),
                pltpu.VMEM((ranks_in, 2 * H), bf16),
                pltpu.VMEM((rows, ranks_down), f32),
                pltpu.VMEM((rows, ranks_down), bf16),
                pltpu.VMEM((rows, ranks_in), bf16),
                pltpu.VMEM((rows, H), bf16),
                pltpu.VMEM((rows, 2 * H), bf16),
                pltpu.VMEM((rows, ranks_down), bf16),
                pltpu.VMEM((ranks_down, H), f32),
                pltpu.VMEM((rows, MODEL_WIDTH), f32),
                pltpu.VMEM((rows, MODEL_WIDTH), f32),
            ],
        ),
        out_shape=[
            jax.ShapeDtypeStruct((rows, MODEL_WIDTH), bf16),
            jax.ShapeDtypeStruct((rows + experts, MODEL_WIDTH), bf16),
            jax.ShapeDtypeStruct((experts, rows), f32),
            jax.ShapeDtypeStruct((BLOCKS, slots, height, BLOCK), bf16),
        ],
        input_output_aliases={11: 3} if kept else {},
        compiler_params=params_of(1),
        name="experts",
        cost_estimate=pl.CostEstimate(
            flops=local * rows * 9 * (1 << 20),
            transcendentals=local * rows * H,
            bytes_accessed=20 << 20,
        ),
    )(scalars, x, cot, routes, router, w_in, w_down, a_in, b_in, a_down, b_down, *kept)


def open_back_kernel(count, order, cot, mid, gain, gates, router, weight_a, weight_b, low_map, up_map, low, att, *rest):
    parts = rest[:count]
    sums = rest[count : 3 * count]
    grad_mid, grad_att, grad_up, grad_low, columns = rest[3 * count :]
    gate_value = gates[...]
    half = gate_value.shape[0] // 2
    sides = []
    for side in range(2):
        value = None
        for at in range(count):
            pair = sums[2 * at + side][...].astype(f32)
            pair = pair[:half] + pair[half:]
            value = pair if value is None else value + pair
        sides.append(value)
    gate_grad = jnp.concatenate(sides, 0)
    logit = gate_value * (gate_grad - jnp.sum(gate_value * gate_grad, 0, keepdims=True))
    first = logit.astype(bf16)
    left = logit - first.astype(f32)
    second = left.astype(bf16)
    third = (left - second.astype(f32)).astype(bf16)
    grad = tn(first, router[...]) + (tn(second, router[...]) + tn(third, router[...]))
    for piece in parts:
        grad = grad + piece[...].astype(f32)
    total = cot[...].astype(f32) + norm_back(mid[...], gain[...].astype(f32), grad)
    grad_mid[...] = total
    branch = total.astype(bf16)
    low_grad = nt(branch, up_map[...]).astype(bf16)
    columns[...] = nn(low_grad, low_map[...])
    for side, weight in enumerate((weight_a, weight_b)):
        value = nt(branch, weight[...])
        for at in range(BLOCKS // 2):
            columns[:, column(order, side * BLOCKS // 2 + at)] += value[:, at * BLOCK : (at + 1) * BLOCK]
    grad_att[...] = columns[...].astype(bf16)
    up_part = tn(low[...], branch)
    low_part = tn(low_grad, att[...])

    @pl.when(pl.program_id(0) == 0)
    def _():
        grad_up[...] = up_part
        grad_low[...] = low_part

    @pl.when(pl.program_id(0) > 0)
    def _():
        grad_up[...] += up_part
        grad_low[...] += low_part


def open_back(order, cot, mid, gain, gates, router, weights, low_map, up_map, low, att, parts):
    rows = cot.shape[0]
    block = 256
    ranks = low_map.shape[0]
    experts = gates.shape[0]
    full = lambda shape: pl.BlockSpec(shape, lambda n, s: (0, 0))
    part = lambda width: pl.BlockSpec((block, width), lambda n, s: (n, 0))
    count = len(parts)
    below = rows // experts
    sums = [
        pl.BlockSpec((experts, block), lambda n, s: (below, n)),
        pl.BlockSpec((experts, block), lambda n, s: (below, rows // block + n)),
    ]

    def body(*refs):
        open_back_kernel(count, *refs)

    return pl.pallas_call(
        body,
        grid_spec=pltpu.PrefetchScalarGridSpec(
            num_scalar_prefetch=1,
            grid=(rows // block,),
            in_specs=[
                part(MODEL_WIDTH),
                part(MODEL_WIDTH),
                full((1, MODEL_WIDTH)),
                pl.BlockSpec((experts, block), lambda n, s: (0, n)),
                full((experts, MODEL_WIDTH)),
                full((HALF, MODEL_WIDTH)),
                full((HALF, MODEL_WIDTH)),
                full((ranks, QD)),
                full((ranks, MODEL_WIDTH)),
                part(ranks),
                part(QD),
            ]
            + [part(MODEL_WIDTH)] * count
            + sums * count,
            out_specs=[
                part(MODEL_WIDTH),
                part(QD),
                full((ranks, MODEL_WIDTH)),
                full((ranks, QD)),
            ],
            scratch_shapes=[pltpu.VMEM((block, QD), f32)],
        ),
        out_shape=[
            jax.ShapeDtypeStruct((rows, MODEL_WIDTH), f32),
            jax.ShapeDtypeStruct((rows, QD), bf16),
            jax.ShapeDtypeStruct((ranks, MODEL_WIDTH), f32),
            jax.ShapeDtypeStruct((ranks, QD), f32),
        ],
        compiler_params=params_of(1),
        name="open_back",
        cost_estimate=pl.CostEstimate(
            flops=2 * rows * QD * MODEL_WIDTH, transcendentals=0, bytes_accessed=14 << 20
        ),
    )(
        order, cot, mid, gain, gates, router, *weights, low_map, up_map, low, att, *parts,
        *[piece for piece in parts for _ in range(2)],
    )


def adapters_back_kernel(
    grad_query, grad_key, grad_value, low, normed, up_map, grad_up, grad_low, low_out
):
    pieces = (grad_query, grad_key, grad_value)
    bounds = (0, QD, QD + KD, QKV)
    back = None
    for at in range(3):
        block = pieces[at][...]
        product = tn(low[...], block)
        grad_up[:, bounds[at] : bounds[at + 1]] = product[at * R : (at + 1) * R]
        part = nt(block, up_map[:, bounds[at] : bounds[at + 1]])
        back = part if back is None else back + part
    value = back.astype(bf16)
    low_out[...] = value
    grad_low[...] = tn(value, normed[...])


def adapters_back(grad_query, grad_key, grad_value, low, normed, up_map):
    rows = normed.shape[0]
    ranks = up_map.shape[0]
    return pl.pallas_call(
        adapters_back_kernel,
        out_shape=[
            jax.ShapeDtypeStruct((R, QKV), f32),
            jax.ShapeDtypeStruct((ranks, MODEL_WIDTH), f32),
            jax.ShapeDtypeStruct((rows, ranks), bf16),
        ],
        compiler_params=pltpu.CompilerParams(vmem_limit_bytes=56 * 1024 * 1024),
        name="adapters_back",
        cost_estimate=pl.CostEstimate(
            flops=6 * rows * 256 * QKV, transcendentals=0, bytes_accessed=4 << 20
        ),
    )(grad_query, grad_key, grad_value, low, normed, up_map)


def input_back_kernel(
    order, grad_query, grad_key, grad_value, low, weight_a, weight_b, low_map, hid, gain, mid, grad, columns
):
    columns[...] = nn(low[...], low_map[...])
    for side, weight in enumerate((weight_a, weight_b)):
        value = nt(grad_query[...], weight[:, :QD])
        value = value + nt(grad_key[...], weight[:, QD : QD + KD])
        value = value + nt(grad_value[...], weight[:, QD + KD :])
        for at in range(BLOCKS // 2):
            columns[:, column(order, side * BLOCKS // 2 + at)] += value[:, at * BLOCK : (at + 1) * BLOCK]
    rows = hid[...].astype(f32)
    grad[...] = (mid[...] + norm_back(rows, gain[...].astype(f32), columns[...])).astype(bf16)


def input_back(order, grad_query, grad_key, grad_value, low, weights, low_map, hidden, gain, mid):
    rows = hidden.shape[0]
    block = 256
    ranks = low_map.shape[0]
    full = lambda shape: pl.BlockSpec(shape, lambda n, s: (0, 0))
    part = lambda width: pl.BlockSpec((block, width), lambda n, s: (n, 0))
    return pl.pallas_call(
        input_back_kernel,
        grid_spec=pltpu.PrefetchScalarGridSpec(
            num_scalar_prefetch=1,
            grid=(rows // block,),
            in_specs=[
                part(QD),
                part(KD),
                part(KD),
                part(ranks),
                full((HALF, QKV)),
                full((HALF, QKV)),
                full((ranks, MODEL_WIDTH)),
                part(MODEL_WIDTH),
                full((1, MODEL_WIDTH)),
                part(MODEL_WIDTH),
            ],
            out_specs=part(MODEL_WIDTH),
            scratch_shapes=[pltpu.VMEM((block, MODEL_WIDTH), f32)],
        ),
        out_shape=jax.ShapeDtypeStruct((rows, MODEL_WIDTH), bf16),
        compiler_params=params_of(1),
        name="input_back",
        cost_estimate=pl.CostEstimate(
            flops=2 * rows * QKV * MODEL_WIDTH, transcendentals=0, bytes_accessed=12 << 20
        ),
    )(order, grad_query, grad_key, grad_value, low, *weights, low_map, hidden, gain, mid)


def sum_experts_kernel(ids, pieces, a_in, b_in, a_down, b_down, acc):
    local = a_in.shape[0]
    small = a_down.shape[-1]
    acc[...] = jnp.zeros_like(acc)

    def step(index, carry):
        acc[ids[index]] += pieces[index].astype(f32)
        return carry

    lax.fori_loop(0, pieces.shape[0], step, 0)
    for e in range(local):
        a_in[e] = acc[:, e * 2 * R : (e + 1) * 2 * R, :]
        at = local * 2 * R + e * R
        b_down[e] = acc[:, at : at + R, :]
        at = local * 3 * R + e * R
        both = acc[:, at : at + R, :]
        b_in[e, :, 0] = both[:, :, :small]
        b_in[e, :, 1] = both[:, :, small:]
        at = local * 4 * R + e // 2 * R
        a_down[e] = acc[:, at : at + R, e % 2 * small : (e % 2 + 1) * small]


def sum_experts(ids, pieces, local):
    height = pieces.shape[1]
    lanes = pieces.shape[2]
    small = lanes // 2
    vmem = pl.BlockSpec(memory_space=pltpu.VMEM)
    return pl.pallas_call(
        sum_experts_kernel,
        in_specs=[pl.BlockSpec(memory_space=pltpu.SMEM), vmem],
        out_specs=[vmem, vmem, vmem, vmem],
        out_shape=[
            jax.ShapeDtypeStruct((local, NA, 2 * R, lanes), f32),
            jax.ShapeDtypeStruct((local, NA, 2, R, small), f32),
            jax.ShapeDtypeStruct((local, NA, R, small), f32),
            jax.ShapeDtypeStruct((local, NA, R, lanes), f32),
        ],
        scratch_shapes=[pltpu.VMEM((NA, height, lanes), f32)],
        compiler_params=pltpu.CompilerParams(vmem_limit_bytes=56 * 1024 * 1024),
        name="sum_experts",
    )(ids, pieces)


def sum_mixer_kernel(ids, pieces, grad_low, grad_up, grad_out, acc):
    width = grad_low.shape[-1]
    acc[...] = jnp.zeros_like(acc)

    def step(index, carry):
        acc[ids[index]] += pieces[index]
        return carry

    lax.fori_loop(0, pieces.shape[0], step, 0)
    total = acc[...]
    for at in range(4):
        grad_low[at] = total[:, :, at * width : (at + 1) * width]
    grad_up[...] = total[:, :, 4 * width : 6 * width]
    grad_out[...] = total[:, :, 6 * width : 7 * width]


def sum_mixer(ids, pieces):
    width = pieces.shape[2] // 8
    vmem = pl.BlockSpec(memory_space=pltpu.VMEM)
    return pl.pallas_call(
        sum_mixer_kernel,
        in_specs=[pl.BlockSpec(memory_space=pltpu.SMEM), vmem],
        out_specs=[vmem, vmem, vmem],
        out_shape=[
            jax.ShapeDtypeStruct((4, NA, R, width), f32),
            jax.ShapeDtypeStruct((NA, R, 2 * width), f32),
            jax.ShapeDtypeStruct((NA, R, width), f32),
        ],
        scratch_shapes=[pltpu.VMEM((NA, R, 8 * width), f32)],
        compiler_params=pltpu.CompilerParams(vmem_limit_bytes=56 * 1024 * 1024),
        name="sum_mixer",
    )(ids, pieces)


def rope_tables(rows):
    half = HS // 2
    frequency = (10000.0 ** (-2.0 * np.arange(half, dtype=np.float32) / HS)).astype(np.float32)
    angles = np.arange(rows, dtype=np.float32)[:, None] * frequency[None, :]
    cos = np.cos(angles.astype(np.float64)).astype(np.float32)
    sin = np.sin(angles.astype(np.float64)).astype(np.float32)
    return (
        jnp.asarray(np.concatenate([cos, cos, cos, cos], 1)),
        jnp.asarray(np.concatenate([-sin, sin, -sin, sin], 1)),
    )


def swap(value, bit):
    return lax.ppermute(value, "dp", [(at, at ^ bit) for at in range(BLOCKS)])


def gather_rows(weight):
    if lax.axis_size("dp") != BLOCKS:
        whole = lax.all_gather(weight, "dp", axis=0, tiled=True)
        return whole[:HALF], whole[HALF:]
    middle = weight.shape[0] // 2
    one = swap(weight, 2)
    two = swap(weight, 4)
    both = [swap(two[:middle], 2), swap(one[middle:], 4)]
    near = jnp.concatenate([weight, one, two] + both, 0)
    return near, swap(near, 1)


def order_of(row):
    if lax.axis_size("dp") != BLOCKS:
        return jnp.arange(BLOCKS, dtype=jnp.int32)
    return row.astype(jnp.int32) ^ jnp.array([0, 2, 4, 6, 1, 3, 5, 7], jnp.int32)


def to_owners(packed, owners, local):
    split = owners // BLOCKS
    if split == 1:
        return packed
    slots = packed.shape[1]
    edge = local * 3 * R
    wide = packed[:, :, :edge].reshape(BLOCKS, slots, edge, split, BLOCK // split)
    wide = wide.transpose(0, 3, 1, 2, 4).reshape(owners, slots, edge, BLOCK // split)
    rest = packed.shape[2] - edge
    narrow = packed[:, :, edge:].reshape(BLOCKS, slots, rest, 2, split, BLOCK // 2 // split)
    narrow = narrow.transpose(0, 4, 1, 2, 3, 5).reshape(owners, slots, rest, BLOCK // split)
    return jnp.concatenate([wide, narrow], 2)


def joined(left, right):
    return (left.astype(f32) + right.astype(f32)).astype(bf16)


def on_device(
    hidden,
    cotangent,
    lengths,
    adapter_ids,
    routes,
    attn_gain,
    ffn_gain,
    query_key_value_weight,
    w_out,
    w_router,
    w_gate_up,
    w_down,
    attention_lowmap,
    attention_query_key_value_upmap,
    attention_output_upmap,
    expert_gate_up_lowmap,
    expert_gate_up_upmap,
    expert_down_lowmap,
    expert_down_upmap,
):
    groups = lax.axis_size("expert")
    owners = lax.axis_size("dp")
    place = lax.axis_index("expert")
    row = lax.axis_index("dp")
    devices = groups * owners
    sequence = row * groups + place
    rows = hidden.shape[0]
    experts = w_router.shape[1]
    local = w_gate_up.shape[0]
    width = MODEL_WIDTH // owners
    attn_gain = attn_gain.reshape(1, MODEL_WIDTH)
    ffn_gain = ffn_gain.reshape(1, MODEL_WIDTH)
    length = lax.dynamic_slice(lengths, (sequence,), (1,))
    forward = [(at, (at + 1) % groups) for at in range(groups)]

    mine = lax.dynamic_slice(adapter_ids.reshape(owners, groups), (0, place), (owners, 1))[:, 0]
    low_turned = attention_lowmap.transpose(1, 0, 3, 2).reshape(NA, 4 * R, width)
    up_turned = (
        attention_query_key_value_upmap.reshape(NA, R, 2, width)
        .transpose(0, 2, 1, 3)
        .reshape(NA, 2 * R, width)
    )
    adapters = jnp.concatenate([low_turned, up_turned, attention_output_upmap], 1)[mine]
    adapters = lax.all_to_all(adapters, "dp", 0, 0, tiled=True)
    order = order_of(row)
    weight_in = gather_rows(query_key_value_weight)
    late, weight_in = lax.optimization_barrier((w_out, weight_in))
    weight_out = gather_rows(late)

    low_map = adapters[:, : 4 * R].transpose(1, 0, 2).reshape(4 * R, MODEL_WIDTH)
    up = (
        adapters[:, 4 * R : 6 * R]
        .reshape(owners, 2, R, width)
        .transpose(2, 0, 1, 3)
        .reshape(R, QKV)
    )
    up_out = adapters[:, 6 * R :].transpose(1, 0, 2).reshape(R, MODEL_WIDTH)
    column = jnp.arange(QKV, dtype=jnp.int32)
    part = jnp.where(column < QD, 0, jnp.where(column < QD + KD, 1, 2))
    up_map = jnp.where(
        part[None, None, :] == jnp.arange(4, dtype=jnp.int32)[:, None, None], up[None], 0
    ).reshape(4 * R, QKV)
    up_out_map = jnp.concatenate([jnp.zeros((3 * R, MODEL_WIDTH), bf16), up_out], 0)

    cos, sin = rope_tables(rows)

    cots = lax.all_gather(cotangent, "expert", axis=0, tiled=True)

    qkv, low, normed_in = project(order, hidden, attn_gain, weight_in, low_map, up_map, cos, sin)
    attended, lse = attend(length, qkv)
    mid, normed_mid, low_out = close_mixer(
        order, attended, hidden, ffn_gain, weight_out, low_map, up_out_map
    )

    first = place * local
    routes_here = (routes - first + experts) % experts
    router = jnp.roll(w_router.T, -first, axis=0)
    router_wide = jnp.concatenate(
        [router, jnp.zeros((128 - experts, MODEL_WIDTH), router.dtype)], 0
    )
    a_in = expert_gate_up_lowmap.transpose(0, 1, 3, 2)
    a_down = expert_down_lowmap.transpose(0, 1, 3, 2)

    source = (place - jnp.arange(groups, dtype=jnp.int32) + groups) % groups
    tags = adapter_ids.reshape(owners, groups)[:, source]
    at = jnp.arange(groups, dtype=jnp.int32)
    table = jnp.stack(
        [source, lax.dynamic_slice(tags, (row, 0), (1, groups))[0], at * local, at, jnp.where(at == 0, 0, source)], 1
    )

    x = normed_mid
    packed = None
    for at in range(groups):
        out_part, grad_part, gate_part, packed = run_experts(
            table[at],
            x,
            cotangent if at == 0 else cots,
            routes_here,
            router_wide,
            w_gate_up,
            w_down,
            a_in,
            expert_gate_up_upmap,
            a_down,
            expert_down_upmap,
            experts,
            groups,
            packed,
        )
        if at < groups - 1:
            x = lax.ppermute(x, "expert", forward)
        if at == 0:
            gates, out_here, grad_here = gate_part, out_part, grad_part
            continue
        if at > 1:
            grad_part = joined(grad_part, grad_far)
            out_part = joined(out_part, out_far)
        grad_far = lax.ppermute(grad_part, "expert", forward)
        out_far = lax.ppermute(out_part, "expert", forward)

    pieces = lax.all_to_all(to_owners(packed, owners, local), "dp", 0, 0, tiled=True)
    pieces = pieces.reshape(devices, pieces.shape[2], width)
    g_a_in, g_b_in, g_a_down, g_b_down = sum_experts(tags.reshape(devices), pieces, local)

    grad_mid, grad_attended, grad_up_out, grad_low_out = open_back(
        order,
        cotangent,
        mid,
        ffn_gain,
        gates,
        router,
        weight_out,
        low_map,
        up_out_map,
        low_out,
        attended,
        [grad_here, grad_far],
    )
    grad_query, grad_key, grad_value = attend_back(length, qkv, grad_attended, lse, cos, sin)
    grad_up, grad_low, back_low = adapters_back(
        grad_query, grad_key, grad_value, low, normed_in, up_map
    )

    grad_low = grad_low + grad_low_out
    small = MODEL_WIDTH // devices
    packed = jnp.concatenate(
        [
            grad_low.reshape(4, R, devices, small).transpose(2, 1, 0, 3).reshape(devices, R, 4 * small),
            grad_up.reshape(R, devices, 2 * small).transpose(1, 0, 2),
            grad_up_out[3 * R :].reshape(R, devices, small).transpose(1, 0, 2),
            jnp.zeros((devices, R, small), f32),
        ],
        -1,
    )
    packed = lax.all_to_all(packed, ("dp", "expert"), 0, 0, tiled=True)
    m_a, m_b, m_o = sum_mixer(adapter_ids, packed)

    grad_hidden = input_back(
        order, grad_query, grad_key, grad_value, back_low, weight_in, low_map, hidden, attn_gain, grad_mid
    )
    out = (mid + out_here.astype(f32) + out_far.astype(f32)).astype(bf16)
    return (
        out,
        grad_hidden,
        m_a.transpose(0, 1, 3, 2),
        m_b,
        m_o,
        g_a_in.transpose(0, 1, 3, 2),
        g_b_in,
        g_a_down.transpose(0, 1, 3, 2),
        g_b_down,
    )


def solution(mesh):
    in_specs = (
        P(("dp", "expert"), None),
        P(("dp", "expert"), None),
        P(),
        P(),
        P("dp", None),
        P(),
        P(),
        P("dp", None),
        P("dp", None),
        P(),
        P("expert", None, None),
        P("expert", None, None),
        P(None, None, "dp", None),
        P(None, None, "dp"),
        P(None, None, "dp"),
        P("expert", None, None, None),
        P("expert", None, None, None, None),
        P("expert", None, None, None),
        P("expert", None, None, None),
    )
    out_specs = (
        P(("dp", "expert"), None),
        P(("dp", "expert"), None),
        P(None, None, ("dp", "expert"), None),
        P(None, None, ("dp", "expert")),
        P(None, None, ("dp", "expert")),
        P("expert", None, "dp", None),
        P("expert", None, None, None, "dp"),
        P("expert", None, "dp", None),
        P("expert", None, None, "dp"),
    )
    return jax.shard_map(
        on_device, mesh=mesh, in_specs=in_specs, out_specs=out_specs, check_vma=False
    )
```

profile of v0, /device:TPU:0, one launch (start us, length us, event | category | flops | bytes accessed | tf_op | source)
XLA Modules:
  0.0 384.6 jit_solution(1513933672089226752)
XLA Ops:
  7.2 3.0 collective-permute-start
  10.3 1.5 collective-permute-start.1
  15.3 1.3 gather_fusion
  16.6 3.4 all-to-all-start
  20.0 1.1 constant_dynamic-update-slice_fusion.4
  21.2 1.2 collective-permute-done
  22.4 1.8 collective-permute-start.3
  25.2 1.2 collective-permute-start.2
  26.5 5.2 %collective-permute-done.2 = bf16[64,2048]{1,0:T(8,128)(2,1)S(1)} collective-permute-done((bf16[64,2048]{1,0:T(8,128)(2,1)S(1)}, bf16[64,2048]{1,0:T(8,128)(2,1)S(1)}, u32[]{:S(2)}, u32[]{:S(2)}) %collective-permute-start.2) | collective-permute-done | bytes 262176 | tf_op jit(solution)/shard_map/ppermute | solution.py:872
  36.8 1.4 add_select_fusion.routes
  38.9 2.3 collective-permute-start.6
  42.9 5.4 %collective-permute-done.6 = bf16[128,1024]{1,0:T(8,128)(2,1)S(1)} collective-permute-done((bf16[128,1024]{1,0:T(8,128)(2,1)}, bf16[128,1024]{1,0:T(8,128)(2,1)S(1)}, u32[]{:S(2)}, u32[]{:S(2)}) %collective-permute-start.6) | collective-permute-done | bytes 262176 | tf_op jit(solution)/shard_map/ppermute | solution.py:872
  50.3 3.4 collective-permute-done.7
  53.6 1.2 collective-permute-done.8
  56.4 12.3 %project.1 = (bf16[512,2048]{1,0:T(8,128)(2,1)}, bf16[512,64]{1,0:T(8,128)(2,1)}, bf16[512,1024]{1,0:T(8,128)(2,1)}) custom-call(s32[8]{0:T(128)} %broadcast_xor_fusion.order.refs_0_, bf16[512,1024]{1,0:T(8,128)(2,1)} %hid.5, bf16[1,1024]{1,0:T(2,128)(2,1)} %reshape.171.gain, bf16[512,2048]{1,0:T(8,128)(2,1)} %copy-done.4, ...), custom_call_target="tpu_custom_call" | custom-call | flops 2147483648 | bytes 8388608 | tf_op jit(solution)/shard_map/project/pallas_call | solution.py:133
  68.7 17.2 %attend.1 = (bf16[512,1024]{1,0:T(8,128)(2,1)}, f32[8,512,2]{2,1,0:T(8,128)}) custom-call(s32[1]{0:T(128)} %dynamic_slice.13.scalars, bf16[512,2048]{1,0:T(8,128)(2,1)} %get-tuple-element.52.query.key.value, bf16[512,2048]{1,0:T(8,128)(2,1)} %get-tuple-element.52.query.key.value, bf16[512,2048]{1,0:T(8,128)(2,1)} %get-tuple-element.52.query.key.value), custom_call_target="tpu_custom_call" | custom-call | flops 2147483648 | bytes 4194304 | tf_op jit(solution)/shard_map/attend/pallas_call | solution.py:204
  86.9 6.0 %close_mixer.1 = (f32[512,1024]{1,0:T(8,128)}, bf16[512,1024]{1,0:T(8,128)(2,1)}, bf16[512,64]{1,0:T(8,128)(2,1)}) custom-call(s32[8]{0:T(128)} %broadcast_xor_fusion.order.refs_0_, bf16[512,1024]{1,0:T(8,128)(2,1)} %get-tuple-element.53.att.refs_11_, bf16[512,1024]{1,0:T(8,128)(2,1)} %hid.5, bf16[1,1024]{1,0:T(2,128)(2,1)} %reshape.178.gain.refs_3_, ...), custom_call_target="tpu_custom_call" | custom-call | flops 1073741824 | bytes 8388608 | tf_op jit(solution)/shard_map/close_mixer/pallas_call | solution.py:333
  92.8 1.8 collective-permute-start.10
  94.6 30.2 %experts.4 = (bf16[512,1024]{1,0:T(8,128)(2,1)}, bf16[528,1024]{1,0:T(8,128)(2,1)}, f32[16,512]{1,0:T(8,128)}, bf16[8,4,288,128]{3,2,1,0:T(8,128)(2,1)}) custom-call(s32[5]{0:T(128)} %get-tuple-element.94.scalars, bf16[512,1024]{1,0:T(8,128)(2,1)} %get-tuple-element.56.x, bf16[512,1024]{1,0:T(8,128)(2,1)} %refs_1_.1, s32[2048,8]{1,0:T(8,128)} %add_select_fusion.routes, ...), custom_call_target="tpu_custom_call" | custom-call | flops 19327352832 | bytes 20971520 | tf_op jit(solution)/shard_map/experts/pallas_call | solution.py:531
  124.8 1.6 collective-permute-start.11
  126.4 30.1 %experts.5 = (bf16[512,1024]{1,0:T(8,128)(2,1)}, bf16[528,1024]{1,0:T(8,128)(2,1)}, f32[16,512]{1,0:T(8,128)}, bf16[8,4,288,128]{3,2,1,0:T(8,128)(2,1)}) custom-call(s32[5]{0:T(128)} %get-tuple-element.92.scalars, bf16[512,1024]{1,0:T(8,128)(2,1)} %copy-done.15, ...), custom_call_target="tpu_custom_call", output_to_operand_aliasing={{3}: (11, {})} | custom-call | flops 19327352832 | bytes 20971520 | tf_op jit(solution)/shard_map/experts/pallas_call | solution.py:531
  156.5 1.6 collective-permute-start.13
  160.1 30.1 %experts.6 = (bf16[512,1024]{1,0:T(8,128)(2,1)}, bf16[528,1024]{1,0:T(8,128)(2,1)}, f32[16,512]{1,0:T(8,128)}, bf16[8,4,288,128]{3,2,1,0:T(8,128)(2,1)}) custom-call(s32[5]{0:T(128)} %get-tuple-element.93.scalars, bf16[512,1024]{1,0:T(8,128)(2,1)} %copy-done.13, ...), custom_call_target="tpu_custom_call", output_to_operand_aliasing={{3}: (11, {})} | custom-call | flops 19327352832 | bytes 20971520 | tf_op jit(solution)/shard_map/experts/pallas_call | solution.py:531
  190.2 2.8 add_convert_fusion.4
  193.0 1.6 collective-permute-start.14
  194.6 13.2 %collective-permute-done.16 = bf16[528,1024]{1,0:T(8,128)(2,1)S(1)} collective-permute-done((bf16[528,1024]{1,0:T(8,128)(2,1)}, bf16[528,1024]{1,0:T(8,128)(2,1)S(1)}, u32[]{:S(2)}, u32[]{:S(2)}) %collective-permute-start.16) | collective-permute-done | bytes 1081376 | tf_op jit(solution)/shard_map/ppermute | solution.py:1029
  208.2 22.0 %collective-permute-done.12.x = bf16[512,1024]{1,0:T(8,128)(2,1)S(1)} collective-permute-done((bf16[512,1024]{1,0:T(8,128)(2,1)S(1)}, bf16[512,1024]{1,0:T(8,128)(2,1)S(1)}, u32[]{:S(2)}, u32[]{:S(2)}) %collective-permute-start.12) | collective-permute-done | bytes 1048608 | tf_op jit(solution)/shard_map/ppermute | solution.py:1022
  231.2 30.2 %experts.7 = (bf16[512,1024]{1,0:T(8,128)(2,1)}, bf16[528,1024]{1,0:T(8,128)(2,1)}, f32[16,512]{1,0:T(8,128)}, bf16[8,4,288,128]{3,2,1,0:T(8,128)(2,1)}) custom-call(s32[5]{0:T(128)} %get-tuple-element.91.scalars, bf16[512,1024]{1,0:T(8,128)(2,1)} %copy-done.14, ...), custom_call_target="tpu_custom_call", output_to_operand_aliasing={{3}: (11, {})} | custom-call | flops 19327352832 | bytes 20971520 | tf_op jit(solution)/shard_map/experts/pallas_call | solution.py:531
  261.3 13.4 %collective-permute-done.17 = bf16[528,1024]{1,0:T(8,128)(2,1)S(1)} collective-permute-done((bf16[528,1024]{1,0:T(8,128)(2,1)S(1)}, bf16[528,1024]{1,0:T(8,128)(2,1)S(1)}, u32[]{:S(2)}, u32[]{:S(2)}) %collective-permute-start.17) | collective-permute-done | bytes 1081376 | tf_op jit(solution)/shard_map/ppermute | solution.py:1029
  274.7 2.6 add_convert_fusion
  277.4 3.6 all-to-all-start.2
  281.1 2.9 add_convert_fusion.3
  284.0 1.3 collective-permute-start.15
  285.3 20.8 %collective-permute-done.18.refs_13_.refs_16_.refs_17_ = bf16[528,1024]{1,0:T(8,128)(2,1)S(1)} collective-permute-done((bf16[528,1024]{1,0:T(8,128)(2,1)}, bf16[528,1024]{1,0:T(8,128)(2,1)S(1)}, u32[]{:S(2)}, u32[]{:S(2)}) %collective-permute-start.18) | collective-permute-done | bytes 1081376 | tf_op jit(solution)/shard_map/ppermute | solution.py:1029
  307.1 9.5 %open_back.1 = (f32[512,1024]{1,0:T(8,128)}, bf16[512,1024]{1,0:T(8,128)(2,1)}, f32[64,1024]{1,0:T(8,128)}, f32[64,1024]{1,0:T(8,128)}) custom-call(s32[8]{0:T(128)} %broadcast_xor_fusion.order.refs_0_, bf16[512,1024]{1,0:T(8,128)(2,1)} %refs_1_.1, f32[512,1024]{1,0:T(8,128)} %get-tuple-element.55.refs_2_, bf16[1,1024]{1,0:T(2,128)(2,1)} %reshape.178.gain.refs_3_, ...), custom_call_target="tpu_custom_call" | custom-call | flops 1073741824 | bytes 14680064 | tf_op jit(solution)/shard_map/open_back/pallas_call | solution.py:653
  316.5 22.5 %attend_back.1 = (bf16[512,1024]{1,0:T(8,128)(2,1)}, bf16[512,512]{1,0:T(8,128)(2,1)}, bf16[512,512]{1,0:T(8,128)(2,1)}) custom-call(s32[1]{0:T(128)} %dynamic_slice.13.scalars, bf16[512,2048]{1,0:T(8,128)(2,1)} %get-tuple-element.52.query.key.value, bf16[512,2048]{1,0:T(8,128)(2,1)} %get-tuple-element.52.query.key.value, ...), custom_call_target="tpu_custom_call" | custom-call | flops 5368709120 | bytes 8388608 | tf_op jit(solution)/shard_map/attend_back/pallas_call | solution.py:280
  340.9 4.3 %adapters_back.1 = (f32[16,2048]{1,0:T(8,128)}, f32[64,1024]{1,0:T(8,128)}, bf16[512,64]{1,0:T(8,128)(2,1)}) custom-call(bf16[512,1024]{1,0:T(8,128)(2,1)} %get-tuple-element.72.grad_query, bf16[512,512]{1,0:T(8,128)(2,1)} %get-tuple-element.73.grad_key, bf16[512,512]{1,0:T(8,128)(2,1)} %get-tuple-element.74.grad_value, ...), custom_call_target="tpu_custom_call" | custom-call | flops 1610612736 | bytes 4194304 | tf_op jit(solution)/shard_map/adapters_back/pallas_call | solution.py:718
  345.1 1.0 reshape.182
  347.0 1.7 add.131
  348.7 1.3 reshape.180
  350.0 1.7 copy.81
  351.6 1.7 reshape.181
  353.3 2.0 maximum_maximum_fusion
  355.4 2.6 all-to-all-start.1
  358.7 3.7 add_convert_fusion.2
  362.4 3.5 sum_experts.1
  365.9 8.5 %input_back.1 = bf16[512,1024]{1,0:T(8,128)(2,1)} custom-call(s32[8]{0:T(128)} %broadcast_xor_fusion.order.refs_0_, bf16[512,1024]{1,0:T(8,128)(2,1)} %get-tuple-element.72.grad_query, bf16[512,512]{1,0:T(8,128)(2,1)} %get-tuple-element.73.grad_key, bf16[512,512]{1,0:T(8,128)(2,1)} %get-tuple-element.74.grad_value, bf16[512,64]{1,0:T(8,128)(2,1)} %get-tuple-element.77.low, ...), custom_call_target="tpu_custom_call" | custom-call | flops 2147483648 | bytes 12582912 | tf_op jit(solution)/shard_map/input_back/pallas_call | solution.py:753
  375.2 2.1 sum_mixer.1
  (116 shorter events, 25.2 us)
Async XLA Ops:
  7.2 119.2 %all-gather.2.cloned.1.call-start = ((), (), s32[]{:S(2)}) async-start(), calls=%async_computation.3 | async-start | bytes 5242880 | tf_op jit(solution)/shard_map/all_gather | solution.py:978
  7.2 15.2 %collective-permute-start = (bf16[128,2048]{1,0:T(8,128)(2,1)}, bf16[128,2048]{1,0:T(8,128)(2,1)S(1)}, u32[]{:S(2)}, u32[]{:S(2)}) collective-permute-start(bf16[128,2048]{1,0:T(8,128)(2,1)} %param.29), channel_id=1, source_target_pairs={{0,8},{4,12},{8,0},{12,4},{16,24},{20,28},{24,16},{28,20},{1,9},{5... | collective-permute-start | bytes 1572872 | tf_op jit(solution)/shard_map/ppermute | solution.py:872
  10.3 14.9 %collective-permute-start.1 = (bf16[128,2048]{1,0:T(8,128)(2,1)}, bf16[128,2048]{1,0:T(8,128)(2,1)S(1)}, u32[]{:S(2)}, u32[]{:S(2)}) collective-permute-start(bf16[128,2048]{1,0:T(8,128)(2,1)} %param.29), channel_id=1, source_target_pairs={{0,16},{4,20},{8,24},{12,28},{16,0},{20,4},{24,8},{28,12},{1,17},{... | collective-permute-start | bytes 1572872 | tf_op jit(solution)/shard_map/ppermute | solution.py:872
  16.6 22.2 %all-to-all-start = ((bf16[8,112,128]{2,1,0:T(8,128)(2,1)}), bf16[8,112,128]{2,1,0:T(8,128)(2,1)S(1)}, u32[]{:S(2)}, u32[]{:S(2)}) async-start(bf16[8,112,128]{2,1,0:T(8,128)(2,1)} %gather_fusion), calls=%async_computation | async-start | bytes 458752 | tf_op jit(solution)/shard_map/all_to_all | solution.py:955
  21.1 10.9 %copy-start.9 = (s32[2048,8]{0,1:T(8,128)S(1)}, s32[2048,8]{0,1:T(8,128)}, u32[]{:S(2)}) copy-start(s32[2048,8]{0,1:T(8,128)} %param.26) | copy-start | bytes 196612
  21.1 11.0 %copy-start.11 = (bf16[1024]{0:T(1024)(128)(2,1)S(1)}, bf16[1024]{0:T(1024)(128)(2,1)}, u32[]{:S(2)}) copy-start(bf16[1024]{0:T(1024)(128)(2,1)} %param.27) | copy-start | bytes 6148
  21.2 11.8 %copy-start.12 = (bf16[1024]{0:T(1024)(128)(2,1)S(1)}, bf16[1024]{0:T(1024)(128)(2,1)}, u32[]{:S(2)}) copy-start(bf16[1024]{0:T(1024)(128)(2,1)} %param.28) | copy-start | bytes 6148
  22.4 9.5 %collective-permute-start.3 = (bf16[64,2048]{1,0:T(8,128)(2,1)S(1)}, bf16[64,2048]{1,0:T(8,128)(2,1)S(1)}, u32[]{:S(2)}, u32[]{:S(2)}) collective-permute-start(bf16[64,2048]{1,0:T(8,128)(2,1)S(1)} %slice.53), channel_id=1, source_target_pairs={{0,16},{4,20},{8,24},{12,28},{16,0},{20,4},{24,8},{28,12},{1,17},{... | collective-permute-start | bytes 786440 | tf_op jit(solution)/shard_map/ppermute | solution.py:872
  25.1 8.7 %copy-start.16 = (s32[32]{0:T(128)S(1)}, s32[32]{0:T(128)}, u32[]{:S(2)}) copy-start(s32[32]{0:T(128)} %param.24) | copy-start | bytes 388
  25.2 10.1 %copy-start.10 = (bf16[1024,16]{0,1:T(8,128)(2,1)S(1)}, bf16[1024,16]{0,1:T(8,128)(2,1)}, u32[]{:S(2)}) copy-start(bf16[1024,16]{0,1:T(8,128)(2,1)} %param.31) | copy-start | bytes 98308
  25.2 6.4 %collective-permute-start.2 = (bf16[64,2048]{1,0:T(8,128)(2,1)S(1)}, bf16[64,2048]{1,0:T(8,128)(2,1)S(1)}, u32[]{:S(2)}, u32[]{:S(2)}) collective-permute-start(bf16[64,2048]{1,0:T(8,128)(2,1)S(1)} %slice.52), channel_id=1, source_target_pairs={{0,8},{4,12},{8,0},{12,4},{16,24},{20,28},{24,16},{28,20},{1,9},{5... | collective-permute-start | bytes 786440 | tf_op jit(solution)/shard_map/ppermute | solution.py:872
  31.6 6.6 %copy-start.17 = (s32[8]{0:T(128)S(1)}, s32[8]{0:T(128)}, u32[]{:S(2)}) copy-start(s32[8]{0:T(128)} %constant.84.clone) | copy-start | bytes 100
  31.9 7.0 %copy-start.4 = (bf16[512,2048]{1,0:T(8,128)(2,1)}, bf16[512,2048]{1,0:T(8,128)(2,1)S(1)}, u32[]{:S(2)}) copy-start(bf16[512,2048]{1,0:T(8,128)(2,1)S(1)} %constant_dynamic-update-slice_fusion.weight_a) | copy-start | bytes 6291460
  32.0 7.0 %collective-permute-start.4 = (bf16[512,2048]{1,0:T(8,128)(2,1)S(1)}, bf16[512,2048]{1,0:T(8,128)(2,1)}, u32[]{:S(2)}, u32[]{:S(2)}) collective-permute-start(bf16[512,2048]{1,0:T(8,128)(2,1)S(1)} %constant_dynamic-update-slice_fusion.weight_a), channel_id=1, source_target_pairs={{0,4},{4,0},{8,12},{12,8},{16,20},{20,16},{24,28},{28,24},{1,5},{5... | collective-permute-start | bytes 6291464 | tf_op jit(solution)/shard_map/ppermute | solution.py:872
  35.3 15.0 %copy-start.7 = (bf16[16,1024]{1,0:T(8,128)(2,1)}, bf16[16,1024]{1,0:T(8,128)(2,1)S(1)}, u32[]{:S(2)}) copy-start(bf16[16,1024]{1,0:T(8,128)(2,1)S(1)} %fusion.1.refs_5_) | copy-start | bytes 98308
  38.9 9.3 %collective-permute-start.6 = (bf16[128,1024]{1,0:T(8,128)(2,1)}, bf16[128,1024]{1,0:T(8,128)(2,1)S(1)}, u32[]{:S(2)}, u32[]{:S(2)}) collective-permute-start(bf16[128,1024]{1,0:T(8,128)(2,1)} %param.30), channel_id=1, source_target_pairs={{0,16},{4,20},{8,24},{12,28},{16,0},{20,4},{24,8},{28,12},{1,17},{... | collective-permute-start | bytes 786440 | tf_op jit(solution)/shard_map/ppermute | solution.py:872
  41.3 8.5 %collective-permute-start.5 = (bf16[128,1024]{1,0:T(8,128)(2,1)}, bf16[128,1024]{1,0:T(8,128)(2,1)S(1)}, u32[]{:S(2)}, u32[]{:S(2)}) collective-permute-start(bf16[128,1024]{1,0:T(8,128)(2,1)} %param.30), channel_id=1, source_target_pairs={{0,8},{4,12},{8,0},{12,4},{16,24},{20,28},{24,16},{28,20},{1,9},{5... | collective-permute-start | bytes 786440 | tf_op jit(solution)/shard_map/ppermute | solution.py:872
  48.3 5.3 %collective-permute-start.7 = (bf16[64,1024]{1,0:T(8,128)(2,1)S(1)}, bf16[64,1024]{1,0:T(8,128)(2,1)S(1)}, u32[]{:S(2)}, u32[]{:S(2)}) collective-permute-start(bf16[64,1024]{1,0:T(8,128)(2,1)S(1)} %slice.56), channel_id=1, source_target_pairs={{0,8},{4,12},{8,0},{12,4},{16,24},{20,28},{24,16},{28,20},{1,9},{5... | collective-permute-start | bytes 393224 | tf_op jit(solution)/shard_map/ppermute | solution.py:872
  49.8 5.0 %collective-permute-start.8 = (bf16[64,1024]{1,0:T(8,128)(2,1)S(1)}, bf16[64,1024]{1,0:T(8,128)(2,1)S(1)}, u32[]{:S(2)}, u32[]{:S(2)}) collective-permute-start(bf16[64,1024]{1,0:T(8,128)(2,1)S(1)} %slice.57), channel_id=1, source_target_pairs={{0,16},{4,20},{8,24},{12,28},{16,0},{20,4},{24,8},{28,12},{1,17},{... | collective-permute-start | bytes 393224 | tf_op jit(solution)/shard_map/ppermute | solution.py:872
  54.8 13.9 %copy-start.2 = (bf16[512,1024]{1,0:T(8,128)(2,1)}, bf16[512,1024]{1,0:T(8,128)(2,1)S(1)}, u32[]{:S(2)}) copy-start(bf16[512,1024]{1,0:T(8,128)(2,1)S(1)} %constant_dynamic-update-slice_fusion.5.weight_a.refs_6_) | copy-start | bytes 3145732
  54.8 31.1 %collective-permute-start.9 = (bf16[512,1024]{1,0:T(8,128)(2,1)S(1)}, bf16[512,1024]{1,0:T(8,128)(2,1)S(1)}, u32[]{:S(2)}, u32[]{:S(2)}) collective-permute-start(bf16[512,1024]{1,0:T(8,128)(2,1)S(1)} %constant_dynamic-update-slice_fusion.5.weight_a.refs_6_), channel_id=1, source_target_pairs={{0,4},{4,0},{8,12},{12,8},{16,20},{20,16},{24,28},{28,24},{1,5},{5... | collective-permute-start | bytes 3145736 | tf_op jit(solution)/shard_map/ppermute | solution.py:872
  85.9 1.0 copy-start.3
  92.8 31.9 %collective-permute-start.10 = (bf16[512,1024]{1,0:T(8,128)(2,1)}, bf16[512,1024]{1,0:T(8,128)(2,1)S(1)}, u32[]{:S(2)}, u32[]{:S(2)}) collective-permute-start(bf16[512,1024]{1,0:T(8,128)(2,1)} %get-tuple-element.56.x), channel_id=1, source_target_pairs={{0,1},{1,2},{2,3},{3,0},{4,5},{5,6},{6,7},{7,4},{8,9},{9,10},{10,1... | collective-permute-start | bytes 3145736 | tf_op jit(solution)/shard_map/ppermute | solution.py:1022
  124.7 1.6 copy-start.15
  124.8 34.3 %collective-permute-start.11 = (bf16[512,1024]{1,0:T(8,128)(2,1)S(1)}, bf16[512,1024]{1,0:T(8,128)(2,1)S(1)}, u32[]{:S(2)}, u32[]{:S(2)}) collective-permute-start(bf16[512,1024]{1,0:T(8,128)(2,1)S(1)} %collective-permute-done.10.x), channel_id=1, source_target_pairs={{0,1},{1,2},{2,3},{3,0},{4,5},{5,6},{6,7},{7,4},{8,9},{9,10},{10,1... | collective-permute-start | bytes 3145736 | tf_op jit(solution)/shard_map/ppermute | solution.py:1022
  156.5 33.7 %collective-permute-start.13 = (bf16[512,1024]{1,0:T(8,128)(2,1)}, bf16[512,1024]{1,0:T(8,128)(2,1)S(1)}, u32[]{:S(2)}, u32[]{:S(2)}) collective-permute-start(bf16[512,1024]{1,0:T(8,128)(2,1)} %get-tuple-element.63), channel_id=1, source_target_pairs={{0,1},{1,2},{2,3},{3,0},{4,5},{5,6},{6,7},{7,4},{8,9},{9,10},{10,1... | collective-permute-start | bytes 3145736 | tf_op jit(solution)/shard_map/ppermute | solution.py:1030
  158.1 49.6 %collective-permute-start.16 = (bf16[528,1024]{1,0:T(8,128)(2,1)}, bf16[528,1024]{1,0:T(8,128)(2,1)S(1)}, u32[]{:S(2)}, u32[]{:S(2)}) collective-permute-start(bf16[528,1024]{1,0:T(8,128)(2,1)} %get-tuple-element.69), channel_id=1, source_target_pairs={{0,1},{1,2},{2,3},{3,0},{4,5},{5,6},{6,7},{7,4},{8,9},{9,10},{10,1... | collective-permute-start | bytes 3244040 | tf_op jit(solution)/shard_map/ppermute | solution.py:1029
  159.1 1.0 copy-start.13
  159.1 71.1 %collective-permute-start.12 = (bf16[512,1024]{1,0:T(8,128)(2,1)S(1)}, bf16[512,1024]{1,0:T(8,128)(2,1)S(1)}, u32[]{:S(2)}, u32[]{:S(2)}) collective-permute-start(bf16[512,1024]{1,0:T(8,128)(2,1)S(1)} %collective-permute-done.11.x), channel_id=1, source_target_pairs={{0,1},{1,2},{2,3},{3,0},{4,5},{5,6},{6,7},{7,4},{8,9},{9,10},{10,1... | collective-permute-start | bytes 3145736 | tf_op jit(solution)/shard_map/ppermute | solution.py:1022
  190.2 17.5 %copy-start.6 = (bf16[528,1024]{1,0:T(8,128)(2,1)S(1)}, bf16[528,1024]{1,0:T(8,128)(2,1)}, u32[]{:S(2)}) copy-start(bf16[528,1024]{1,0:T(8,128)(2,1)} %get-tuple-element.68) | copy-start | bytes 3244036
  193.0 88.1 %collective-permute-start.14 = (bf16[512,1024]{1,0:T(8,128)(2,1)}, bf16[512,1024]{1,0:T(8,128)(2,1)}, u32[]{:S(2)}, u32[]{:S(2)}) collective-permute-start(bf16[512,1024]{1,0:T(8,128)(2,1)} %add_convert_fusion.4), channel_id=1, source_target_pairs={{0,1},{1,2},{2,3},{3,0},{4,5},{5,6},{6,7},{7,4},{8,9},{9,10},{10,1... | collective-permute-start | bytes 3145736 | tf_op jit(solution)/shard_map/ppermute | solution.py:1030
  208.1 66.6 %collective-permute-start.17 = (bf16[528,1024]{1,0:T(8,128)(2,1)S(1)}, bf16[528,1024]{1,0:T(8,128)(2,1)S(1)}, u32[]{:S(2)}, u32[]{:S(2)}) collective-permute-start(bf16[528,1024]{1,0:T(8,128)(2,1)S(1)} %add_convert_fusion.1), channel_id=1, source_target_pairs={{0,1},{1,2},{2,3},{3,0},{4,5},{5,6},{6,7},{7,4},{8,9},{9,10},{10,1... | collective-permute-start | bytes 3244040 | tf_op jit(solution)/shard_map/ppermute | solution.py:1029
  230.2 1.0 copy-start.14
  277.3 28.7 %collective-permute-start.18 = (bf16[528,1024]{1,0:T(8,128)(2,1)}, bf16[528,1024]{1,0:T(8,128)(2,1)S(1)}, u32[]{:S(2)}, u32[]{:S(2)}) collective-permute-start(bf16[528,1024]{1,0:T(8,128)(2,1)} %add_convert_fusion), channel_id=1, source_target_pairs={{0,1},{1,2},{2,3},{3,0},{4,5},{5,6},{6,7},{7,4},{8,9},{9,10},{10,1... | collective-permute-start | bytes 3244040 | tf_op jit(solution)/shard_map/ppermute | solution.py:1029
  277.4 78.0 %all-to-all-start.2 = ((bf16[8,4,288,128]{3,2,1,0:T(8,128)(2,1)}), bf16[8,4,288,128]{3,2,1,0:T(8,128)(2,1)S(1)}, u32[]{:S(2)}, u32[]{:S(2)}) async-start(bf16[8,4,288,128]{3,2,1,0:T(8,128)(2,1)} %get-tuple-element.86), calls=%async_computation.2 | async-start | bytes 4718592 | tf_op jit(solution)/shard_map/all_to_all | solution.py:1032
  284.0 74.7 %collective-permute-start.15 = (bf16[512,1024]{1,0:T(8,128)(2,1)}, bf16[512,1024]{1,0:T(8,128)(2,1)}, u32[]{:S(2)}, u32[]{:S(2)}) collective-permute-start(bf16[512,1024]{1,0:T(8,128)(2,1)} %add_convert_fusion.3), channel_id=1, source_target_pairs={{0,1},{1,2},{2,3},{3,0},{4,5},{5,6},{6,7},{7,4},{8,9},{9,10},{10,1... | collective-permute-start | bytes 3145736 | tf_op jit(solution)/shard_map/ppermute | solution.py:1030
  306.1 1.0 copy-start
  340.8 6.2 %copy-start.8 = (f32[64,1024]{1,0:T(8,128)S(1)}, f32[64,1024]{1,0:T(8,128)}, u32[]{:S(2)}) copy-start(f32[64,1024]{1,0:T(8,128)} %get-tuple-element.80) | copy-start | bytes 786436
  355.4 7.0 %copy-start.1 = (bf16[8,4,288,128]{3,2,1,0:T(8,128)(2,1)}, bf16[8,4,288,128]{3,2,1,0:T(8,128)(2,1)S(1)}, u32[]{:S(2)}) copy-start(bf16[8,4,288,128]{3,2,1,0:T(8,128)(2,1)S(1)} %all-to-all-done.2) | copy-start | bytes 7077892
  355.4 19.0 %all-to-all-start.1 = ((f32[32,16,256]{2,1,0:T(8,128)}), f32[32,16,256]{2,1,0:T(8,128)S(1)}, u32[]{:S(2)}, u32[]{:S(2)}) async-start(f32[32,16,256]{2,1,0:T(8,128)} %maximum_maximum_fusion), calls=%async_computation.1 | async-start | bytes 1048576 | tf_op jit(solution)/shard_map/all_to_all | solution.py:1066
  374.4 0.8 copy-start.5
Sparse Core Ops, SparseCore 0:
  11.9 81.0 all-gather.1
where the time goes:
time: 391 us; the launch traced here: 385 us
  Pallas kernels  206 us (53%)
  waiting for transfers between devices  87.7 us (22%)
  starting transfers between devices  30.5 us (8%)
  local copies, waits for them, and re-layouts  24.9 us (6%)
  other arithmetic  20.1 us (5%)
  between operations  14.9 us (4%)
    pallas_call x4, Pallas kernels, run_experts(): pl.pallas_call(expert_kernel, grid_spec=pltpu.PrefetchScalarGridSpec(num_...  121 us
    ppermute x3, waiting for transfers between devices, on_device(): grad_far = lax.ppermute(grad_part, 'expert', forward)  47.4 us
    pallas_call x1, Pallas kernels, attend_back(): pl.pallas_call(attend_back_kernel, grid_spec=pltpu.PrefetchScalarGridSpec...  22.5 us
    ppermute x3, waiting for transfers between devices, on_device(): x = lax.ppermute(x, 'expert', forward)  22 us
    ppermute x10, waiting for transfers between devices, swap(): return lax.ppermute(value, 'dp', [(at, at ^ bit) for at in range(BLOCKS)])  18.4 us
    pallas_call x1, Pallas kernels, attend(): pl.pallas_call(attend_kernel, grid_spec=pltpu.PrefetchScalarGridSpec(num_...  17.2 us
    pallas_call x1, Pallas kernels, project(): pl.pallas_call(project_kernel, grid_spec=pltpu.PrefetchScalarGridSpec(num...  12.3 us
    ppermute x10, starting transfers between devices, swap(): return lax.ppermute(value, 'dp', [(at, at ^ bit) for at in range(BLOCKS)])  11 us
  transfers between devices with their start and end apart: 23, of which 12 were waited for; matrix products, arithmetic and copies ran while one was open for 11% of the time, Pallas kernels for 53%

commit v1 on v0

--- a/solution.py
+++ b/solution.py
@@ -387,8 +387,7 @@
     *rest,
 ):
     (
-        out,
-        grad_normed,
+        sums_out,
         gates_out,
         packed,
         gates,
@@ -405,11 +404,11 @@
         down_acc,
         out_acc,
         grad_acc,
-    ) = rest[-18:]
+    ) = rest[-17:]
     expert = pl.program_id(0)
     last = pl.num_programs(0) - 1
     rows = x.shape[0]
-    block = 256
+    block = rows
     local = a_in.shape[0]
     a_in_all = a_in[...].reshape(local * 2 * R, MODEL_WIDTH)
     a_down_all = a_down[...].reshape(local * R, H)
@@ -497,13 +496,14 @@
 
     @pl.when(expert == last)
     def _():
-        out[...] = (out_acc[...] + nn(gated_low[...], b_down_all)).astype(bf16)
-        grad_normed[:rows, :] = (grad_acc[...] + nn(back_in[...], a_in_all)).astype(bf16)
+        sums_out[:rows, :] = (grad_acc[...] + nn(back_in[...], a_in_all)).astype(bf16)
         experts = gates_out.shape[0]
         sums = gate_sums[...].T[:experts, :]
         sums = jnp.concatenate([sums[: experts // 2], sums[experts // 2 :]], 1)
         high = sums.astype(bf16).astype(f32)
-        grad_normed[rows:, :] = jnp.concatenate([high, sums - high], 0).astype(bf16)
+        edge = rows + experts
+        sums_out[rows:edge, :] = jnp.concatenate([high, sums - high], 0).astype(bf16)
+        sums_out[edge:, :] = (out_acc[...] + nn(gated_low[...], b_down_all)).astype(bf16)
         wide = tn(back_in[...], x[...]).astype(bf16)
         tall = tn(gated_low[...], cot[...]).astype(bf16)
         for at in range(BLOCKS):
@@ -547,8 +547,7 @@
             ]
             + [pl.BlockSpec(memory_space=pl.ANY)] * len(kept),
             out_specs=[
-                full((rows, MODEL_WIDTH)),
-                full((rows + experts, MODEL_WIDTH)),
+                full((2 * rows + experts, MODEL_WIDTH)),
                 full((experts, rows)),
                 pl.BlockSpec((BLOCKS, 1, height, BLOCK), lambda e, s: (0, s[3], 0, 0)),
             ],
@@ -570,12 +569,11 @@
             ],
         ),
         out_shape=[
-            jax.ShapeDtypeStruct((rows, MODEL_WIDTH), bf16),
-            jax.ShapeDtypeStruct((rows + experts, MODEL_WIDTH), bf16),
+            jax.ShapeDtypeStruct((2 * rows + experts, MODEL_WIDTH), bf16),
             jax.ShapeDtypeStruct((experts, rows), f32),
             jax.ShapeDtypeStruct((BLOCKS, slots, height, BLOCK), bf16),
         ],
-        input_output_aliases={11: 3} if kept else {},
+        input_output_aliases={11: 2} if kept else {},
         compiler_params=params_of(1),
         name="experts",
         cost_estimate=pl.CostEstimate(
@@ -696,38 +694,84 @@
 
 
 def adapters_back_kernel(
-    grad_query, grad_key, grad_value, low, normed, up_map, grad_up, grad_low, low_out
+    grad_query, grad_key, grad_value, low, normed, up_map, low_there, up_there, low_out, *results
 ):
     pieces = (grad_query, grad_key, grad_value)
     bounds = (0, QD, QD + KD, QKV)
     back = None
+    ups = []
     for at in range(3):
         block = pieces[at][...]
-        product = tn(low[...], block)
-        grad_up[:, bounds[at] : bounds[at + 1]] = product[at * R : (at + 1) * R]
+        ups.append(tn(low[...], block)[at * R : (at + 1) * R])
         part = nt(block, up_map[:, bounds[at] : bounds[at + 1]])
         back = part if back is None else back + part
     value = back.astype(bf16)
     low_out[...] = value
-    grad_low[...] = tn(value, normed[...])
-
-
-def adapters_back(grad_query, grad_key, grad_value, low, normed, up_map):
+    lows = tn(value, normed[...]) + low_there[...]
+    if len(results) == 2:
+        grad_up, grad_low = results
+        grad_low[...] = lows
+        for at in range(3):
+            grad_up[:, bounds[at] : bounds[at + 1]] = ups[at]
+        return
+    (packed,) = results
+    grad_up = jnp.concatenate(ups, 1)
+    grad_out = up_there[3 * R :, :]
+    small = BLOCK // 4
+    lane = lanes_of((R, BLOCK))
+    for owner in range(packed.shape[0]):
+        tile = slice(owner // 4 * BLOCK, (owner // 4 + 1) * BLOCK)
+        offset = owner % 4 * small
+        first = jnp.zeros((R, BLOCK), f32)
+        for at in range(4):
+            piece = lows[at * R : (at + 1) * R, tile]
+            shift = (at * small - offset) % BLOCK
+            piece = pltpu.roll(piece, shift, 1) if shift else piece
+            first = jnp.where((lane >= at * small) & (lane < (at + 1) * small), piece, first)
+        piece = grad_up[:, owner // 2 * BLOCK : (owner // 2 + 1) * BLOCK]
+        piece = pltpu.roll(piece, BLOCK // 2, 1) if owner % 2 else piece
+        other = grad_out[:, tile]
+        shift = (2 * small - offset) % BLOCK
+        other = pltpu.roll(other, shift, 1) if shift else other
+        packed[owner, :, :BLOCK] = first
+        packed[owner, :, BLOCK:] = jnp.where(
+            lane < 2 * small, piece, jnp.where(lane < 3 * small, other, 0.0)
+        )
+
+
+def adapters_back(grad_query, grad_key, grad_value, low, normed, up_map, low_there, up_there, devices):
     rows = normed.shape[0]
     ranks = up_map.shape[0]
-    return pl.pallas_call(
-        adapters_back_kernel,
-        out_shape=[
+    if devices * BLOCK // 4 == MODEL_WIDTH:
+        results = [jax.ShapeDtypeStruct((devices, R, 2 * BLOCK), f32)]
+    else:
+        results = [
             jax.ShapeDtypeStruct((R, QKV), f32),
             jax.ShapeDtypeStruct((ranks, MODEL_WIDTH), f32),
-            jax.ShapeDtypeStruct((rows, ranks), bf16),
-        ],
+        ]
+    back_low, *results = pl.pallas_call(
+        adapters_back_kernel,
+        out_shape=[jax.ShapeDtypeStruct((rows, ranks), bf16)] + results,
         compiler_params=pltpu.CompilerParams(vmem_limit_bytes=56 * 1024 * 1024),
         name="adapters_back",
         cost_estimate=pl.CostEstimate(
             flops=6 * rows * 256 * QKV, transcendentals=0, bytes_accessed=4 << 20
         ),
-    )(grad_query, grad_key, grad_value, low, normed, up_map)
+    )(grad_query, grad_key, grad_value, low, normed, up_map, low_there, up_there)
+    if len(results) == 1:
+        return results[0], back_low
+    grad_up, grad_low = results
+    small = MODEL_WIDTH // devices
+    packed = jnp.concatenate(
+        [
+            grad_low.reshape(4, R, devices, small).transpose(2, 1, 0, 3).reshape(devices, R, 4 * small),
+            grad_up.reshape(R, devices, 2 * small).transpose(1, 0, 2),
+            up_there[3 * R :].reshape(R, devices, small).transpose(1, 0, 2),
+            jnp.zeros((devices, R, small), f32),
+        ],
+        -1,
+    )
+    return packed, back_low
 
 
 def input_back_kernel(
@@ -872,16 +916,18 @@
     return lax.ppermute(value, "dp", [(at, at ^ bit) for at in range(BLOCKS)])
 
 
-def gather_rows(weight):
-    if lax.axis_size("dp") != BLOCKS:
-        whole = lax.all_gather(weight, "dp", axis=0, tiled=True)
-        return whole[:HALF], whole[HALF:]
-    middle = weight.shape[0] // 2
-    one = swap(weight, 2)
-    two = swap(weight, 4)
-    both = [swap(two[:middle], 2), swap(one[middle:], 4)]
-    near = jnp.concatenate([weight, one, two] + both, 0)
-    return near, swap(near, 1)
+def both_neighbours(weight):
+    return swap(weight, 2), swap(weight, 4)
+
+
+def across(pair):
+    one, two = pair
+    middle = one.shape[0] // 2
+    return swap(two[:middle], 2), swap(one[middle:], 4)
+
+
+def tied(value, *others):
+    return lax.optimization_barrier((value, *others))[0]
 
 
 def order_of(row):
@@ -943,6 +989,7 @@
     ffn_gain = ffn_gain.reshape(1, MODEL_WIDTH)
     length = lax.dynamic_slice(lengths, (sequence,), (1,))
     forward = [(at, (at + 1) % groups) for at in range(groups)]
+    backward = [(at, (at - 1) % groups) for at in range(groups)]
 
     mine = lax.dynamic_slice(adapter_ids.reshape(owners, groups), (0, place), (owners, 1))[:, 0]
     low_turned = attention_lowmap.transpose(1, 0, 3, 2).reshape(NA, 4 * R, width)
@@ -954,9 +1001,18 @@
     adapters = jnp.concatenate([low_turned, up_turned, attention_output_upmap], 1)[mine]
     adapters = lax.all_to_all(adapters, "dp", 0, 0, tiled=True)
     order = order_of(row)
-    weight_in = gather_rows(query_key_value_weight)
-    late, weight_in = lax.optimization_barrier((w_out, weight_in))
-    weight_out = gather_rows(late)
+    short = owners == BLOCKS
+    if short:
+        pair_in = both_neighbours(query_key_value_weight)
+        pair_out = both_neighbours(tied(w_out, *pair_in))
+        near_in = jnp.concatenate([query_key_value_weight, *pair_in, *across(pair_in)], 0)
+        weight_in = near_in, swap(near_in, 1)
+        across_out = across(tied(pair_out, weight_in[1]))
+    else:
+        whole = lax.all_gather(query_key_value_weight, "dp", axis=0, tiled=True)
+        weight_in = whole[:HALF], whole[HALF:]
+        whole = lax.all_gather(w_out, "dp", axis=0, tiled=True)
+        weight_out = whole[:HALF], whole[HALF:]
 
     low_map = adapters[:, : 4 * R].transpose(1, 0, 2).reshape(4 * R, MODEL_WIDTH)
     up = (
@@ -978,6 +1034,9 @@
     cots = lax.all_gather(cotangent, "expert", axis=0, tiled=True)
 
     qkv, low, normed_in = project(order, hidden, attn_gain, weight_in, low_map, up_map, cos, sin)
+    if short:
+        near_out = jnp.concatenate([w_out, *pair_out, *tied(across_out, low)], 0)
+        weight_out = near_out, swap(near_out, 1)
     attended, lse = attend(length, qkv)
     mid, normed_mid, low_out = close_mixer(
         order, attended, hidden, ffn_gain, weight_out, low_map, up_out_map
@@ -992,19 +1051,31 @@
     a_in = expert_gate_up_lowmap.transpose(0, 1, 3, 2)
     a_down = expert_down_lowmap.transpose(0, 1, 3, 2)
 
-    source = (place - jnp.arange(groups, dtype=jnp.int32) + groups) % groups
+    offsets = [0, 1] + [groups - 1] * (groups > 2) + list(range(2, groups - 1))
+    offset = jnp.array(offsets, jnp.int32)
+    source = (place - offset + groups) % groups
     tags = adapter_ids.reshape(owners, groups)[:, source]
-    at = jnp.arange(groups, dtype=jnp.int32)
+    slot = jnp.arange(groups, dtype=jnp.int32)
     table = jnp.stack(
-        [source, lax.dynamic_slice(tags, (row, 0), (1, groups))[0], at * local, at, jnp.where(at == 0, 0, source)], 1
-    )
-
-    x = normed_mid
+        [
+            source,
+            lax.dynamic_slice(tags, (row, 0), (1, groups))[0],
+            offset * local,
+            slot,
+            jnp.where(slot == 0, 0, source),
+        ],
+        1,
+    )
+
+    xs = {0: normed_mid, 1: lax.ppermute(normed_mid, "expert", forward)}
+    if groups > 2:
+        xs[groups - 1] = lax.ppermute(normed_mid, "expert", backward)
     packed = None
-    for at in range(groups):
-        out_part, grad_part, gate_part, packed = run_experts(
+    ran = {}
+    for at, offset in enumerate(offsets):
+        ran[offset], gate_part, packed = run_experts(
             table[at],
-            x,
+            xs[offset],
             cotangent if at == 0 else cots,
             routes_here,
             router_wide,
@@ -1018,20 +1089,27 @@
             groups,
             packed,
         )
-        if at < groups - 1:
-            x = lax.ppermute(x, "expert", forward)
-        if at == 0:
-            gates, out_here, grad_here = gate_part, out_part, grad_part
-            continue
-        if at > 1:
-            grad_part = joined(grad_part, grad_far)
-            out_part = joined(out_part, out_far)
-        grad_far = lax.ppermute(grad_part, "expert", forward)
-        out_far = lax.ppermute(out_part, "expert", forward)
+        if offset == 0:
+            gates = gate_part
+            xs[1] = tied(xs[1], gates)
+        if 2 <= offset + 2 < groups - 1:
+            xs[offset + 2] = lax.ppermute(xs[offset + 1], "expert", forward)
 
     pieces = lax.all_to_all(to_owners(packed, owners, local), "dp", 0, 0, tiled=True)
     pieces = pieces.reshape(devices, pieces.shape[2], width)
     g_a_in, g_b_in, g_a_down, g_b_down = sum_experts(tags.reshape(devices), pieces, local)
+
+    edge = rows + experts
+    both_far = lax.ppermute(ran[1], "expert", forward)
+    grad_far, out_far = both_far, both_far[edge:]
+    for offset in range(2, groups):
+        grad_part = joined(ran[offset][:edge], grad_far[:edge])
+        if offset == groups - 1:
+            grad_part = tied(grad_part, g_a_down)
+        grad_far = lax.ppermute(grad_part, "expert", forward)
+    for offset in range(2, groups):
+        out_part = joined(ran[offset][edge:], out_far)
+        out_far = lax.ppermute(tied(out_part, grad_far), "expert", forward)
 
     grad_mid, grad_attended, grad_up_out, grad_low_out = open_back(
         order,
@@ -1045,23 +1123,11 @@
         up_out_map,
         low_out,
         attended,
-        [grad_here, grad_far],
+        [ran[0], grad_far],
     )
     grad_query, grad_key, grad_value = attend_back(length, qkv, grad_attended, lse, cos, sin)
-    grad_up, grad_low, back_low = adapters_back(
-        grad_query, grad_key, grad_value, low, normed_in, up_map
-    )
-
-    grad_low = grad_low + grad_low_out
-    small = MODEL_WIDTH // devices
-    packed = jnp.concatenate(
-        [
-            grad_low.reshape(4, R, devices, small).transpose(2, 1, 0, 3).reshape(devices, R, 4 * small),
-            grad_up.reshape(R, devices, 2 * small).transpose(1, 0, 2),
-            grad_up_out[3 * R :].reshape(R, devices, small).transpose(1, 0, 2),
-            jnp.zeros((devices, R, small), f32),
-        ],
-        -1,
+    packed, back_low = adapters_back(
+        grad_query, grad_key, grad_value, low, normed_in, up_map, grad_low_out, grad_up_out, devices
     )
     packed = lax.all_to_all(packed, ("dp", "expert"), 0, 0, tiled=True)
     m_a, m_b, m_o = sum_mixer(adapter_ids, packed)
@@ -1069,7 +1135,7 @@
     grad_hidden = input_back(
         order, grad_query, grad_key, grad_value, back_low, weight_in, low_map, hidden, attn_gain, grad_mid
     )
-    out = (mid + out_here.astype(f32) + out_far.astype(f32)).astype(bf16)
+    out = (mid + ran[0][edge:].astype(f32) + out_far.astype(f32)).astype(bf16)
     return (
         out,
         grad_hidden,

time: 391 us -> 380 us (0.972)
  starting transfers between devices: 30.5 us -> 60.6 us
  waiting for transfers between devices: 87.7 us -> 69.2 us
  Pallas kernels: 206 us -> 194 us
  other arithmetic: 20.1 us -> 14.2 us
  local copies, waits for them, and re-layouts: 24.9 us -> 20.4 us
    ppermute x3 -> x2, starting transfers between devices: 1.05 us -> 27.3 us  [on_device(): grad_far = lax.ppermute(grad_part, 'expert', forward)]
    ppermute x6, waiting for transfers between devices: 22 us -> 0.02 us  [the longest x2 0.01 us: on_device(): out_far = lax.ppermute(tied(out_part, grad_far), 'expert', forward)]
    all_to_all x1, waiting for transfers between devices: 0.01 us -> 18.7 us  [on_device(): packed = lax.all_to_all(packed, ('dp', 'expert'), 0, 0, tiled=True)]
    ppermute x3 -> x2, waiting for transfers between devices: 47.4 us -> 32.8 us  [on_device(): grad_far = lax.ppermute(grad_part, 'expert', forward)]
    pallas_call x4, Pallas kernels: 121 us -> 107 us  [run_experts(): pl.pallas_call(expert_kernel, grid_spec=pltpu.PrefetchScalarGridSpec(num_...]
    reshape x7 -> x0, local copies, waits for them, and re-layouts: 7.47 us -> none  [the longest x3 4.62 us: on_device(): grad_low.reshape(4, R, devices, small).transpose(2, 1, 0, 3)]
    ppermute x10, waiting for transfers between devices: 18.4 us -> 12.3 us  [swap(): return lax.ppermute(value, 'dp', [(at, at ^ bit) for at in range(BLOCKS)])]
    all_to_all x1, waiting for transfers between devices: 0.01 us -> 5.47 us  [on_device(): lax.all_to_all(to_owners(packed, owners, local), 'dp', 0, 0, tiled=True)]
  transfers between devices with their start and end apart: 23 -> 22, of which waited for: 12 -> 8; matrix products, arithmetic and copies ran while one was open for 11% -> 6% of each run, Pallas kernels for 53% -> 52%
where the time goes in v1:
time: 380 us; the launch traced here: 373 us
  Pallas kernels  194 us (51%)
  waiting for transfers between devices  69.2 us (18%)
  starting transfers between devices  60.6 us (16%)
  local copies, waits for them, and re-layouts  20.4 us (5%)
  between operations  15 us (4%)
  other arithmetic  14.2 us (4%)
    pallas_call x4, Pallas kernels, run_experts(): pl.pallas_call(expert_kernel, grid_spec=pltpu.PrefetchScalarGridSpec(num_...  107 us
    ppermute x2, waiting for transfers between devices, on_device(): grad_far = lax.ppermute(grad_part, 'expert', forward)  32.8 us
    ppermute x2, starting transfers between devices, on_device(): grad_far = lax.ppermute(grad_part, 'expert', forward)  27.3 us
    pallas_call x1, Pallas kernels, attend_back(): pl.pallas_call(attend_back_kernel, grid_spec=pltpu.PrefetchScalarGridSpec...  22.5 us
    all_to_all x1, waiting for transfers between devices, on_device(): packed = lax.all_to_all(packed, ('dp', 'expert'), 0, 0, tiled=True)  18.7 us
    pallas_call x1, Pallas kernels, attend(): pl.pallas_call(attend_kernel, grid_spec=pltpu.PrefetchScalarGridSpec(num_...  17.2 us
    ppermute x10, starting transfers between devices, swap(): return lax.ppermute(value, 'dp', [(at, at ^ bit) for at in range(BLOCKS)])  12.4 us
    pallas_call x1, Pallas kernels, project(): pl.pallas_call(project_kernel, grid_spec=pltpu.PrefetchScalarGridSpec(num...  12.3 us
  transfers between devices with their start and end apart: 22, of which 8 were waited for; matrix products, arithmetic and copies ran while one was open for 6% of the time, Pallas kernels for 52%

profile of v1, /device:TPU:0, one launch (start us, length us, event | category | flops | bytes accessed | tf_op | source)
XLA Modules:
  0.0 373.4 jit_solution(1451279214375490011)
XLA Ops:
  7.2 3.0 collective-permute-start
  10.3 1.5 collective-permute-start.1
  13.2 0.9 reshape.90
  14.1 0.9 copy.62
  16.0 1.3 gather_fusion
  17.3 3.4 all-to-all-start
  21.5 0.9 collective-permute-done
  22.4 1.8 collective-permute-start.3
  24.3 1.6 collective-permute-start.2
  27.6 4.3 %collective-permute-done.2 = bf16[64,2048]{1,0:T(8,128)(2,1)S(1)} collective-permute-done((bf16[64,2048]{1,0:T(8,128)(2,1)S(1)}, bf16[64,2048]{1,0:T(8,128)(2,1)S(1)}, u32[]{:S(2)}, u32[]{:S(2)}) %collective-permute-start.2) | collective-permute-done | bytes 262176 | tf_op jit(solution)/shard_map/ppermute | solution.py:916
  38.1 1.4 collective-permute-start.5
  41.6 5.3 %collective-permute-done.5 = bf16[128,1024]{1,0:T(8,128)(2,1)S(1)} collective-permute-done((bf16[128,1024]{1,0:T(8,128)(2,1)S(1)}, bf16[128,1024]{1,0:T(8,128)(2,1)S(1)}, u32[]{:S(2)}, u32[]{:S(2)}) %collective-permute-start.5) | collective-permute-done | bytes 262176 | tf_op jit(solution)/shard_map/ppermute | solution.py:916
  46.9 1.8 collective-permute-done.6
  49.5 1.5 collective-permute-start.7
  51.0 12.3 %project.1 = (bf16[512,2048]{1,0:T(8,128)(2,1)}, bf16[512,64]{1,0:T(8,128)(2,1)}, bf16[512,1024]{1,0:T(8,128)(2,1)}) custom-call(s32[8]{0:T(128)} %broadcast_xor_fusion.order.refs_0_, bf16[512,1024]{1,0:T(8,128)(2,1)} %hid.5, bf16[1,1024]{1,0:T(2,128)(2,1)} %reshape.88.gain, bf16[512,2048]{1,0:T(8,128)(2,1)} %constant_dynamic-update-slice_fusion.weight_a, ...), custom_call_target="tpu_custom_call" | custom-call | flops 2147483648 | bytes 8388608 | tf_op jit(solution)/shard_map/project/pallas_call | solution.py:133
  64.0 1.4 add_select_fusion.routes
  66.1 17.2 %attend.1 = (bf16[512,1024]{1,0:T(8,128)(2,1)}, f32[8,512,2]{2,1,0:T(8,128)}) custom-call(s32[1]{0:T(128)} %dynamic_slice.13.scalars, bf16[512,2048]{1,0:T(8,128)(2,1)} %get-tuple-element.51.query.key.value, bf16[512,2048]{1,0:T(8,128)(2,1)} %get-tuple-element.51.query.key.value, bf16[512,2048]{1,0:T(8,128)(2,1)} %get-tuple-element.51.query.key.value), custom_call_target="tpu_custom_call" | custom-call | flops 2147483648 | bytes 4194304 | tf_op jit(solution)/shard_map/attend/pallas_call | solution.py:204
  83.4 1.0 copy-done.4
  84.4 5.9 %close_mixer.1 = (f32[512,1024]{1,0:T(8,128)}, bf16[512,1024]{1,0:T(8,128)(2,1)}, bf16[512,64]{1,0:T(8,128)(2,1)}) custom-call(s32[8]{0:T(128)} %broadcast_xor_fusion.order.refs_0_, bf16[512,1024]{1,0:T(8,128)(2,1)} %get-tuple-element.52.att.refs_11_, bf16[512,1024]{1,0:T(8,128)(2,1)} %hid.5, bf16[1,1024]{1,0:T(2,128)(2,1)} %reshape.95.gain.refs_3_, ...), custom_call_target="tpu_custom_call" | custom-call | flops 1073741824 | bytes 8388608 | tf_op jit(solution)/shard_map/close_mixer/pallas_call | solution.py:333
  90.3 1.6 collective-permute-start.11
  91.9 2.7 collective-permute-start.10
  94.6 26.8 %experts.4 = (bf16[1040,1024]{1,0:T(8,128)(2,1)}, f32[16,512]{1,0:T(8,128)}, bf16[8,4,288,128]{3,2,1,0:T(8,128)(2,1)}) custom-call(s32[5]{0:T(128)} %get-tuple-element.98.scalars, bf16[512,1024]{1,0:T(8,128)(2,1)} %get-tuple-element.60.x, bf16[512,1024]{1,0:T(8,128)(2,1)} %refs_1_.1, s32[2048,8]{1,0:T(8,128)} %add_select_fusion.routes, ...), custom_call_target="tpu_custom_call" | custom-call | flops 19327352832 | bytes 20971520 | tf_op jit(solution)/shard_map/experts/pallas_call | solution.py:531
  122.4 26.8 %experts.5 = (bf16[1040,1024]{1,0:T(8,128)(2,1)}, f32[16,512]{1,0:T(8,128)}, bf16[8,4,288,128]{3,2,1,0:T(8,128)(2,1)}) custom-call(s32[5]{0:T(128)} %get-tuple-element.97.scalars, bf16[512,1024]{1,0:T(8,128)(2,1)} %copy-done.15, bf16[2048,1024]{1,0:T(8,128)(2,1)} %all-gather.2.cloned.1.call-done.cot, ...), custom_call_target="tpu_custom_call", output_to_operand_aliasing={{2}: (11, {})} | custom-call | flops 19327352832 | bytes 20971520 | tf_op jit(solution)/shard_map/experts/pallas_call | solution.py:531
  150.0 1.0 copy-done.17
  151.0 26.8 %experts.6 = (bf16[1040,1024]{1,0:T(8,128)(2,1)}, f32[16,512]{1,0:T(8,128)}, bf16[8,4,288,128]{3,2,1,0:T(8,128)(2,1)}) custom-call(s32[5]{0:T(128)} %get-tuple-element.95.scalars, bf16[512,1024]{1,0:T(8,128)(2,1)} %copy-done.17, bf16[2048,1024]{1,0:T(8,128)(2,1)} %all-gather.2.cloned.1.call-done.cot, ...), custom_call_target="tpu_custom_call", output_to_operand_aliasing={{2}: (11, {})} | custom-call | flops 19327352832 | bytes 20971520 | tf_op jit(solution)/shard_map/experts/pallas_call | solution.py:531
  177.8 1.0 copy-done.16
  178.8 27.0 %experts.7 = (bf16[1040,1024]{1,0:T(8,128)(2,1)}, f32[16,512]{1,0:T(8,128)}, bf16[8,4,288,128]{3,2,1,0:T(8,128)(2,1)}) custom-call(s32[5]{0:T(128)} %get-tuple-element.96.scalars, bf16[512,1024]{1,0:T(8,128)(2,1)} %copy-done.16, bf16[2048,1024]{1,0:T(8,128)(2,1)} %all-gather.2.cloned.1.call-done.cot, ...), custom_call_target="tpu_custom_call", output_to_operand_aliasing={{2}: (11, {})} | custom-call | flops 19327352832 | bytes 20971520 | tf_op jit(solution)/shard_map/experts/pallas_call | solution.py:531
  205.8 3.6 all-to-all-start.1
  209.4 3.0 add_convert_fusion.1
  212.4 20.2 %collective-permute-start.14 = (bf16[528,1024]{1,0:T(8,128)(2,1)}, bf16[528,1024]{1,0:T(8,128)(2,1)S(1)}, u32[]{:S(2)}, u32[]{:S(2)}) collective-permute-start(bf16[528,1024]{1,0:T(8,128)(2,1)} %add_convert_fusion.1), channel_id=1, source_target_pairs={{0,1},{1,2},{2,3},{3,0},{4,5},{5,6},{6,7},{7,4},{8,9},{9,10},{10,1... | collective-permute-start | bytes 3244040 | tf_op jit(solution)/shard_map/ppermute | solution.py:1109
  233.3 5.5 %all-to-all-done.1 = bf16[8,4,288,128]{3,2,1,0:T(8,128)(2,1)S(1)} async-done(((bf16[8,4,288,128]{3,2,1,0:T(8,128)(2,1)}), bf16[8,4,288,128]{3,2,1,0:T(8,128)(2,1)S(1)}, u32[]{:S(2)}, u32[]{:S(2)}) %all-to-all-start.1) | async-done | bytes 2359328 | tf_op jit(solution)/shard_map/all_to_all | solution.py:1098
  238.8 1.4 copy-done.1
  240.2 3.6 sum_experts.1
  243.8 13.2 %collective-permute-done.14 = bf16[528,1024]{1,0:T(8,128)(2,1)S(1)} collective-permute-done((bf16[528,1024]{1,0:T(8,128)(2,1)}, bf16[528,1024]{1,0:T(8,128)(2,1)S(1)}, u32[]{:S(2)}, u32[]{:S(2)}) %collective-permute-start.14) | collective-permute-done | bytes 1081376 | tf_op jit(solution)/shard_map/ppermute | solution.py:1109
  257.4 7.1 %collective-permute-start.15 = (bf16[528,1024]{1,0:T(8,128)(2,1)S(1)}, bf16[528,1024]{1,0:T(8,128)(2,1)S(1)}, u32[]{:S(2)}, u32[]{:S(2)}) collective-permute-start(bf16[528,1024]{1,0:T(8,128)(2,1)S(1)} %add_convert_fusion), channel_id=1, source_target_pairs={{0,1},{1,2},{2,3},{3,0},{4,5},{5,6},{6,7},{7,4},{8,9},{9,10},{10,1... | collective-permute-start | bytes 3244040 | tf_op jit(solution)/shard_map/ppermute | solution.py:1109
  264.5 1.9 add_convert_fusion.4
  266.4 19.6 %collective-permute-done.15.refs_13_.refs_16_.refs_17_ = bf16[528,1024]{1,0:T(8,128)(2,1)S(1)} collective-permute-done((bf16[528,1024]{1,0:T(8,128)(2,1)S(1)}, bf16[528,1024]{1,0:T(8,128)(2,1)S(1)}, u32[]{:S(2)}, u32[]{:S(2)}) %collective-permute-start.15) | collective-permute-done | bytes 1081376 | tf_op jit(solution)/shard_map/ppermute | solution.py:1109
  286.0 2.5 collective-permute-start.16
  288.5 9.8 %open_back.1 = (f32[512,1024]{1,0:T(8,128)}, bf16[512,1024]{1,0:T(8,128)(2,1)}, f32[64,1024]{1,0:T(8,128)}, f32[64,1024]{1,0:T(8,128)}) custom-call(s32[8]{0:T(128)} %broadcast_xor_fusion.order.refs_0_, bf16[512,1024]{1,0:T(8,128)(2,1)} %refs_1_.1, f32[512,1024]{1,0:T(8,128)} %get-tuple-element.59.refs_2_, bf16[1,1024]{1,0:T(2,128)(2,1)} %reshape.95.gain.refs_3_, ...), custom_call_target="tpu_custom_call" | custom-call | flops 1073741824 | bytes 14680064 | tf_op jit(solution)/shard_map/open_back/pallas_call | solution.py:651
  298.3 22.5 %attend_back.1 = (bf16[512,1024]{1,0:T(8,128)(2,1)}, bf16[512,512]{1,0:T(8,128)(2,1)}, bf16[512,512]{1,0:T(8,128)(2,1)}) custom-call(s32[1]{0:T(128)} %dynamic_slice.13.scalars, bf16[512,2048]{1,0:T(8,128)(2,1)} %get-tuple-element.51.query.key.value, bf16[512,2048]{1,0:T(8,128)(2,1)} %get-tuple-element.51.query.key.value, ...), custom_call_target="tpu_custom_call" | custom-call | flops 5368709120 | bytes 8388608 | tf_op jit(solution)/shard_map/attend_back/pallas_call | solution.py:280
  320.8 1.4 add_convert_fusion.3
  322.2 1.0 collective-permute-start.17
  323.2 4.6 %adapters_back.1 = (bf16[512,64]{1,0:T(8,128)(2,1)}, f32[32,16,256]{2,1,0:T(8,128)}) custom-call(bf16[512,1024]{1,0:T(8,128)(2,1)} %get-tuple-element.78.grad_query, bf16[512,512]{1,0:T(8,128)(2,1)} %get-tuple-element.79.grad_key, bf16[512,512]{1,0:T(8,128)(2,1)} %get-tuple-element.80.grad_value, bf16[512,64]{1,0:T(8,128)(2,1)} %get-tuple-element.56.low, ...), custom_call_target="tpu_custom_call" | custom-call | flops 1610612736 | bytes 4194304 | tf_op jit(solution)/shard_map/adapters_back/pallas_call | solution.py:752
  327.7 5.0 %all-to-all-start.2 = ((f32[32,16,256]{2,1,0:T(8,128)}), f32[32,16,256]{2,1,0:T(8,128)S(1)}, u32[]{:S(2)}, u32[]{:S(2)}) async-start(f32[32,16,256]{2,1,0:T(8,128)} %get-tuple-element.86), calls=%async_computation.2 | async-start | bytes 1048576 | tf_op jit(solution)/shard_map/all_to_all | solution.py:1132
  332.7 8.6 %input_back.1 = bf16[512,1024]{1,0:T(8,128)(2,1)} custom-call(s32[8]{0:T(128)} %broadcast_xor_fusion.order.refs_0_, bf16[512,1024]{1,0:T(8,128)(2,1)} %get-tuple-element.78.grad_query, bf16[512,512]{1,0:T(8,128)(2,1)} %get-tuple-element.79.grad_key, bf16[512,512]{1,0:T(8,128)(2,1)} %get-tuple-element.80.grad_value, bf16[512,64]{1,0:T(8,128)(2,1)} %get-tuple-element.84.low, ...), custom_call_target="tpu_custom_call" | custom-call | flops 2147483648 | bytes 12582912 | tf_op jit(solution)/shard_map/input_back/pallas_call | solution.py:797
  341.3 18.7 %all-to-all-done.2.pieces = f32[32,16,256]{2,1,0:T(8,128)S(1)} async-done(((f32[32,16,256]{2,1,0:T(8,128)}), f32[32,16,256]{2,1,0:T(8,128)S(1)}, u32[]{:S(2)}, u32[]{:S(2)}) %all-to-all-start.2) | async-done | bytes 524320 | tf_op jit(solution)/shard_map/all_to_all | solution.py:1132
  360.8 2.1 sum_mixer.1
  363.0 3.0 add_convert_fusion.2
  (107 shorter events, 19.2 us)
Async XLA Ops:
  7.2 13.5 %copy-start.7 = (bf16[128,2048]{1,0:T(8,128)(2,1)S(1)}, bf16[128,2048]{1,0:T(8,128)(2,1)}, u32[]{:S(2)}) copy-start(bf16[128,2048]{1,0:T(8,128)(2,1)} %param.30) | copy-start | bytes 1572868
  7.2 114.5 %all-gather.2.cloned.1.call-start = ((), (), s32[]{:S(2)}) async-start(), calls=%async_computation.3 | async-start | bytes 5242880 | tf_op jit(solution)/shard_map/all_gather | solution.py:1034
  7.2 15.2 %collective-permute-start = (bf16[128,2048]{1,0:T(8,128)(2,1)}, bf16[128,2048]{1,0:T(8,128)(2,1)S(1)}, u32[]{:S(2)}, u32[]{:S(2)}) collective-permute-start(bf16[128,2048]{1,0:T(8,128)(2,1)} %param.30), channel_id=1, source_target_pairs={{0,8},{4,12},{8,0},{12,4},{16,24},{20,28},{24,16},{28,20},{1,9},{5... | collective-permute-start | bytes 1572872 | tf_op jit(solution)/shard_map/ppermute | solution.py:916
  10.3 14.0 %collective-permute-start.1 = (bf16[128,2048]{1,0:T(8,128)(2,1)}, bf16[128,2048]{1,0:T(8,128)(2,1)S(1)}, u32[]{:S(2)}, u32[]{:S(2)}) collective-permute-start(bf16[128,2048]{1,0:T(8,128)(2,1)} %param.30), channel_id=1, source_target_pairs={{0,16},{4,20},{8,24},{12,28},{16,0},{20,4},{24,8},{28,12},{1,17},{... | collective-permute-start | bytes 1572872 | tf_op jit(solution)/shard_map/ppermute | solution.py:916
  17.3 20.7 %all-to-all-start = ((bf16[8,112,128]{2,1,0:T(8,128)(2,1)}), bf16[8,112,128]{2,1,0:T(8,128)(2,1)S(1)}, u32[]{:S(2)}, u32[]{:S(2)}) async-start(bf16[8,112,128]{2,1,0:T(8,128)(2,1)} %gather_fusion), calls=%async_computation | async-start | bytes 458752 | tf_op jit(solution)/shard_map/all_to_all | solution.py:1002
  21.5 11.8 %copy-start.10 = (s32[2048,8]{0,1:T(8,128)S(1)}, s32[2048,8]{0,1:T(8,128)}, u32[]{:S(2)}) copy-start(s32[2048,8]{0,1:T(8,128)} %param.27) | copy-start | bytes 196612
  21.5 12.1 %copy-start.12 = (bf16[1024]{0:T(1024)(128)(2,1)S(1)}, bf16[1024]{0:T(1024)(128)(2,1)}, u32[]{:S(2)}) copy-start(bf16[1024]{0:T(1024)(128)(2,1)} %param.28) | copy-start | bytes 6148
  21.5 12.7 %copy-start.13 = (bf16[1024]{0:T(1024)(128)(2,1)S(1)}, bf16[1024]{0:T(1024)(128)(2,1)}, u32[]{:S(2)}) copy-start(bf16[1024]{0:T(1024)(128)(2,1)} %param.29) | copy-start | bytes 6148
  22.4 10.2 %collective-permute-start.3 = (bf16[64,2048]{1,0:T(8,128)(2,1)S(1)}, bf16[64,2048]{1,0:T(8,128)(2,1)S(1)}, u32[]{:S(2)}, u32[]{:S(2)}) collective-permute-start(bf16[64,2048]{1,0:T(8,128)(2,1)S(1)} %slice.77), channel_id=1, source_target_pairs={{0,16},{4,20},{8,24},{12,28},{16,0},{20,4},{24,8},{28,12},{1,17},{... | collective-permute-start | bytes 786440 | tf_op jit(solution)/shard_map/ppermute | solution.py:916
  24.3 10.9 %copy-start.18 = (s32[32]{0:T(128)S(1)}, s32[32]{0:T(128)}, u32[]{:S(2)}) copy-start(s32[32]{0:T(128)} %param.25) | copy-start | bytes 388
  24.3 12.1 %copy-start.11 = (bf16[1024,16]{0,1:T(8,128)(2,1)S(1)}, bf16[1024,16]{0,1:T(8,128)(2,1)}, u32[]{:S(2)}) copy-start(bf16[1024,16]{0,1:T(8,128)(2,1)} %param.32) | copy-start | bytes 98308
  24.3 7.6 %collective-permute-start.2 = (bf16[64,2048]{1,0:T(8,128)(2,1)S(1)}, bf16[64,2048]{1,0:T(8,128)(2,1)S(1)}, u32[]{:S(2)}, u32[]{:S(2)}) collective-permute-start(bf16[64,2048]{1,0:T(8,128)(2,1)S(1)} %slice.76), channel_id=1, source_target_pairs={{0,8},{4,12},{8,0},{12,4},{16,24},{20,28},{24,16},{28,20},{1,9},{5... | collective-permute-start | bytes 786440 | tf_op jit(solution)/shard_map/ppermute | solution.py:916
  26.7 10.5 %copy-start.14 = (s32[4,1]{1,0:T(4,128)S(1)}, s32[4,1]{1,0:T(4,128)}, u32[]{:S(2)}) copy-start(s32[4,1]{1,0:T(4,128)} %constant.94) | copy-start | bytes 52
  26.7 10.6 %copy-start.9 = (bf16[128,1024]{1,0:T(8,128)(2,1)S(1)}, bf16[128,1024]{1,0:T(8,128)(2,1)}, u32[]{:S(2)}) copy-start(bf16[128,1024]{1,0:T(8,128)(2,1)} %param.31) | copy-start | bytes 786436
  26.7 10.7 %copy-start.19 = (s32[8]{0:T(128)S(1)}, s32[8]{0:T(128)}, u32[]{:S(2)}) copy-start(s32[8]{0:T(128)} %constant.84.clone) | copy-start | bytes 100
  33.3 15.4 %collective-permute-start.4 = (bf16[512,2048]{1,0:T(8,128)(2,1)}, bf16[512,2048]{1,0:T(8,128)(2,1)}, u32[]{:S(2)}, u32[]{:S(2)}) collective-permute-start(bf16[512,2048]{1,0:T(8,128)(2,1)} %constant_dynamic-update-slice_fusion.weight_a), channel_id=1, source_target_pairs={{0,4},{4,0},{8,12},{12,8},{16,20},{20,16},{24,28},{28,24},{1,5},{5... | collective-permute-start | bytes 6291464 | tf_op jit(solution)/shard_map/ppermute | solution.py:916
  36.4 26.8 %copy-start.8 = (bf16[16,1024]{1,0:T(8,128)(2,1)}, bf16[16,1024]{1,0:T(8,128)(2,1)S(1)}, u32[]{:S(2)}) copy-start(bf16[16,1024]{1,0:T(8,128)(2,1)S(1)} %fusion.1.refs_5_) | copy-start | bytes 98308
  38.1 8.8 %collective-permute-start.5 = (bf16[128,1024]{1,0:T(8,128)(2,1)S(1)}, bf16[128,1024]{1,0:T(8,128)(2,1)S(1)}, u32[]{:S(2)}, u32[]{:S(2)}) collective-permute-start(bf16[128,1024]{1,0:T(8,128)(2,1)S(1)} %copy-done.9), channel_id=1, source_target_pairs={{0,8},{4,12},{8,0},{12,4},{16,24},{20,28},{24,16},{28,20},{1,9},{5... | collective-permute-start | bytes 786440 | tf_op jit(solution)/shard_map/ppermute | solution.py:916
  40.2 8.4 %collective-permute-start.6 = (bf16[128,1024]{1,0:T(8,128)(2,1)S(1)}, bf16[128,1024]{1,0:T(8,128)(2,1)S(1)}, u32[]{:S(2)}, u32[]{:S(2)}) collective-permute-start(bf16[128,1024]{1,0:T(8,128)(2,1)S(1)} %copy-done.9), channel_id=1, source_target_pairs={{0,16},{4,20},{8,24},{12,28},{16,0},{20,4},{24,8},{28,12},{1,17},{... | collective-permute-start | bytes 786440 | tf_op jit(solution)/shard_map/ppermute | solution.py:916
  48.7 14.5 %collective-permute-start.8 = (bf16[64,1024]{1,0:T(8,128)(2,1)S(1)}, bf16[64,1024]{1,0:T(8,128)(2,1)S(1)}, u32[]{:S(2)}, u32[]{:S(2)}) collective-permute-start(bf16[64,1024]{1,0:T(8,128)(2,1)S(1)} %slice.59), channel_id=1, source_target_pairs={{0,16},{4,20},{8,24},{12,28},{16,0},{20,4},{24,8},{28,12},{1,17},{... | collective-permute-start | bytes 393224 | tf_op jit(solution)/shard_map/ppermute | solution.py:916
  49.5 13.8 %collective-permute-start.7 = (bf16[64,1024]{1,0:T(8,128)(2,1)S(1)}, bf16[64,1024]{1,0:T(8,128)(2,1)S(1)}, u32[]{:S(2)}, u32[]{:S(2)}) collective-permute-start(bf16[64,1024]{1,0:T(8,128)(2,1)S(1)} %slice.58), channel_id=1, source_target_pairs={{0,8},{4,12},{8,0},{12,4},{16,24},{20,28},{24,16},{28,20},{1,9},{5... | collective-permute-start | bytes 393224 | tf_op jit(solution)/shard_map/ppermute | solution.py:916
  63.3 20.0 %copy-start.3 = (bf16[512,1024]{1,0:T(8,128)(2,1)}, bf16[512,1024]{1,0:T(8,128)(2,1)S(1)}, u32[]{:S(2)}) copy-start(bf16[512,1024]{1,0:T(8,128)(2,1)S(1)} %constant_dynamic-update-slice_fusion.5.weight_a.refs_6_) | copy-start | bytes 3145732
  63.3 20.0 %collective-permute-start.9 = (bf16[512,1024]{1,0:T(8,128)(2,1)S(1)}, bf16[512,1024]{1,0:T(8,128)(2,1)S(1)}, u32[]{:S(2)}, u32[]{:S(2)}) collective-permute-start(bf16[512,1024]{1,0:T(8,128)(2,1)S(1)} %constant_dynamic-update-slice_fusion.5.weight_a.refs_6_), channel_id=1, source_target_pairs={{0,4},{4,0},{8,12},{12,8},{16,20},{20,16},{24,28},{28,24},{1,5},{5... | collective-permute-start | bytes 3145736 | tf_op jit(solution)/shard_map/ppermute | solution.py:916
  83.4 1.0 copy-start.4
  90.3 31.1 %collective-permute-start.11 = (bf16[512,1024]{1,0:T(8,128)(2,1)}, bf16[512,1024]{1,0:T(8,128)(2,1)S(1)}, u32[]{:S(2)}, u32[]{:S(2)}) collective-permute-start(bf16[512,1024]{1,0:T(8,128)(2,1)} %get-tuple-element.60.x), channel_id=1, source_target_pairs={{0,1},{1,2},{2,3},{3,0},{4,5},{5,6},{6,7},{7,4},{8,9},{9,10},{10,1... | collective-permute-start | bytes 3145736 | tf_op jit(solution)/shard_map/ppermute | solution.py:1070
  91.9 58.1 %collective-permute-start.10 = (bf16[512,1024]{1,0:T(8,128)(2,1)}, bf16[512,1024]{1,0:T(8,128)(2,1)S(1)}, u32[]{:S(2)}, u32[]{:S(2)}) collective-permute-start(bf16[512,1024]{1,0:T(8,128)(2,1)} %get-tuple-element.60.x), channel_id=1, source_target_pairs={{0,3},{1,0},{2,1},{3,2},{4,7},{5,4},{6,5},{7,6},{8,11},{9,8},{10,9... | collective-permute-start | bytes 3145736 | tf_op jit(solution)/shard_map/ppermute | solution.py:1072
  121.4 1.0 copy-start.15
  121.4 56.3 %collective-permute-start.12 = (bf16[512,1024]{1,0:T(8,128)(2,1)S(1)}, bf16[512,1024]{1,0:T(8,128)(2,1)S(1)}, u32[]{:S(2)}, u32[]{:S(2)}) collective-permute-start(bf16[512,1024]{1,0:T(8,128)(2,1)S(1)} %collective-permute-done.11.x), channel_id=1, source_target_pairs={{0,1},{1,2},{2,3},{3,0},{4,5},{5,6},{6,7},{7,4},{8,9},{9,10},{10,1... | collective-permute-start | bytes 3145736 | tf_op jit(solution)/shard_map/ppermute | solution.py:1096
  149.2 60.2 %collective-permute-start.13 = (bf16[1040,1024]{1,0:T(8,128)(2,1)}, bf16[1040,1024]{1,0:T(8,128)(2,1)}, u32[]{:S(2)}, u32[]{:S(2)}) collective-permute-start(bf16[1040,1024]{1,0:T(8,128)(2,1)} %get-tuple-element.69), channel_id=1, source_target_pairs={{0,1},{1,2},{2,3},{3,0},{4,5},{5,6},{6,7},{7,4},{8,9},{9,10},{10,1... | collective-permute-start | bytes 6389768 | tf_op jit(solution)/shard_map/ppermute | solution.py:1103
  150.0 1.0 copy-start.17
  177.8 1.0 copy-start.16
  205.8 33.0 %all-to-all-start.1 = ((bf16[8,4,288,128]{3,2,1,0:T(8,128)(2,1)}), bf16[8,4,288,128]{3,2,1,0:T(8,128)(2,1)S(1)}, u32[]{:S(2)}, u32[]{:S(2)}) async-start(bf16[8,4,288,128]{3,2,1,0:T(8,128)(2,1)} %get-tuple-element.70), calls=%async_computation.1 | async-start | bytes 4718592 | tf_op jit(solution)/shard_map/all_to_all | solution.py:1098
  212.4 44.6 %collective-permute-start.14 = (bf16[528,1024]{1,0:T(8,128)(2,1)}, bf16[528,1024]{1,0:T(8,128)(2,1)S(1)}, u32[]{:S(2)}, u32[]{:S(2)}) collective-permute-start(bf16[528,1024]{1,0:T(8,128)(2,1)} %add_convert_fusion.1), channel_id=1, source_target_pairs={{0,1},{1,2},{2,3},{3,0},{4,5},{5,6},{6,7},{7,4},{8,9},{9,10},{10,1... | collective-permute-start | bytes 3244040 | tf_op jit(solution)/shard_map/ppermute | solution.py:1109
  238.8 1.4 copy-start.1
  238.8 18.2 %copy-start.5 = (bf16[1040,1024]{1,0:T(8,128)(2,1)S(1)}, bf16[1040,1024]{1,0:T(8,128)(2,1)}, u32[]{:S(2)}) copy-start(bf16[1040,1024]{1,0:T(8,128)(2,1)} %get-tuple-element.66) | copy-start | bytes 6389764
  257.4 28.6 %collective-permute-start.15 = (bf16[528,1024]{1,0:T(8,128)(2,1)S(1)}, bf16[528,1024]{1,0:T(8,128)(2,1)S(1)}, u32[]{:S(2)}, u32[]{:S(2)}) collective-permute-start(bf16[528,1024]{1,0:T(8,128)(2,1)S(1)} %add_convert_fusion), channel_id=1, source_target_pairs={{0,1},{1,2},{2,3},{3,0},{4,5},{5,6},{6,7},{7,4},{8,9},{9,10},{10,1... | collective-permute-start | bytes 3244040 | tf_op jit(solution)/shard_map/ppermute | solution.py:1109
  286.0 2.5 copy-start
  286.0 34.7 %collective-permute-start.16 = (bf16[512,1024]{1,0:T(8,128)(2,1)S(1)}, bf16[512,1024]{1,0:T(8,128)(2,1)S(1)}, u32[]{:S(2)}, u32[]{:S(2)}) collective-permute-start(bf16[512,1024]{1,0:T(8,128)(2,1)S(1)} %add_convert_fusion.4), channel_id=1, source_target_pairs={{0,1},{1,2},{2,3},{3,0},{4,5},{5,6},{6,7},{7,4},{8,9},{9,10},{10,1... | collective-permute-start | bytes 3145736 | tf_op jit(solution)/shard_map/ppermute | solution.py:1112
  322.2 40.8 %collective-permute-start.17 = (bf16[512,1024]{1,0:T(8,128)(2,1)}, bf16[512,1024]{1,0:T(8,128)(2,1)}, u32[]{:S(2)}, u32[]{:S(2)}) collective-permute-start(bf16[512,1024]{1,0:T(8,128)(2,1)} %add_convert_fusion.3), channel_id=1, source_target_pairs={{0,1},{1,2},{2,3},{3,0},{4,5},{5,6},{6,7},{7,4},{8,9},{9,10},{10,1... | collective-permute-start | bytes 3145736 | tf_op jit(solution)/shard_map/ppermute | solution.py:1112
  327.7 32.3 %all-to-all-start.2 = ((f32[32,16,256]{2,1,0:T(8,128)}), f32[32,16,256]{2,1,0:T(8,128)S(1)}, u32[]{:S(2)}, u32[]{:S(2)}) async-start(f32[32,16,256]{2,1,0:T(8,128)} %get-tuple-element.86), calls=%async_computation.2 | async-start | bytes 1048576 | tf_op jit(solution)/shard_map/all_to_all | solution.py:1132
  332.7 30.3 %copy-start.2 = (f32[512,1024]{1,0:T(8,128)S(1)}, f32[512,1024]{1,0:T(8,128)}, u32[]{:S(2)}) copy-start(f32[512,1024]{1,0:T(8,128)} %get-tuple-element.59.refs_2_) | copy-start | bytes 6291460
  360.0 0.8 copy-start.6
Sparse Core Ops, SparseCore 0:
  11.9 81.0 all-gather.1

commit v2 on v1

--- a/solution.py
+++ b/solution.py
@@ -926,8 +926,8 @@
     return swap(two[:middle], 2), swap(one[middle:], 4)
 
 
-def tied(value, *others):
-    return lax.optimization_barrier((value, *others))[0]
+def tied(*values):
+    return lax.optimization_barrier(values)
 
 
 def order_of(row):
@@ -1004,10 +1004,13 @@
     short = owners == BLOCKS
     if short:
         pair_in = both_neighbours(query_key_value_weight)
-        pair_out = both_neighbours(tied(w_out, *pair_in))
-        near_in = jnp.concatenate([query_key_value_weight, *pair_in, *across(pair_in)], 0)
+        pair_out = both_neighbours(w_out)
+        pair_in, pair_out = tied(pair_in, pair_out)
+        across_in = across(pair_in)
+        pair_out, across_in = tied(pair_out, across_in)
+        near_in = jnp.concatenate([query_key_value_weight, *pair_in, *across_in], 0)
         weight_in = near_in, swap(near_in, 1)
-        across_out = across(tied(pair_out, weight_in[1]))
+        across_out = across(pair_out)
     else:
         whole = lax.all_gather(query_key_value_weight, "dp", axis=0, tiled=True)
         weight_in = whole[:HALF], whole[HALF:]
@@ -1035,7 +1038,8 @@
 
     qkv, low, normed_in = project(order, hidden, attn_gain, weight_in, low_map, up_map, cos, sin)
     if short:
-        near_out = jnp.concatenate([w_out, *pair_out, *tied(across_out, low)], 0)
+        across_out, low = tied(across_out, low)
+        near_out = jnp.concatenate([w_out, *pair_out, *across_out], 0)
         weight_out = near_out, swap(near_out, 1)
     attended, lse = attend(length, qkv)
     mid, normed_mid, low_out = close_mixer(
@@ -1068,8 +1072,6 @@
     )
 
     xs = {0: normed_mid, 1: lax.ppermute(normed_mid, "expert", forward)}
-    if groups > 2:
-        xs[groups - 1] = lax.ppermute(normed_mid, "expert", backward)
     packed = None
     ran = {}
     for at, offset in enumerate(offsets):
@@ -1089,27 +1091,34 @@
             groups,
             packed,
         )
-        if offset == 0:
+        if at == 0:
             gates = gate_part
-            xs[1] = tied(xs[1], gates)
-        if 2 <= offset + 2 < groups - 1:
-            xs[offset + 2] = lax.ppermute(xs[offset + 1], "expert", forward)
+            if groups > 2:
+                normed_mid, packed = tied(normed_mid, packed)
+                xs[groups - 1] = lax.ppermute(normed_mid, "expert", backward)
+        elif at < groups - 2:
+            value, packed = tied(xs[at], packed)
+            xs[at + 1] = lax.ppermute(value, "expert", forward)
+        if at == 2:
+            first_sums, packed = tied(ran[1], packed)
 
     pieces = lax.all_to_all(to_owners(packed, owners, local), "dp", 0, 0, tiled=True)
     pieces = pieces.reshape(devices, pieces.shape[2], width)
     g_a_in, g_b_in, g_a_down, g_b_down = sum_experts(tags.reshape(devices), pieces, local)
 
     edge = rows + experts
-    both_far = lax.ppermute(ran[1], "expert", forward)
+    both_far = lax.ppermute(first_sums if groups > 2 else ran[1], "expert", forward)
     grad_far, out_far = both_far, both_far[edge:]
     for offset in range(2, groups):
         grad_part = joined(ran[offset][:edge], grad_far[:edge])
         if offset == groups - 1:
-            grad_part = tied(grad_part, g_a_down)
+            grad_part, g_a_down = tied(grad_part, g_a_down)
         grad_far = lax.ppermute(grad_part, "expert", forward)
     for offset in range(2, groups):
         out_part = joined(ran[offset][edge:], out_far)
-        out_far = lax.ppermute(tied(out_part, grad_far), "expert", forward)
+        if offset == 2:
+            out_part, grad_far = tied(out_part, grad_far)
+        out_far = lax.ppermute(out_part, "expert", forward)
 
     grad_mid, grad_attended, grad_up_out, grad_low_out = open_back(
         order,

time: 380 us -> 371 us (0.976)
  starting transfers between devices: 60.6 us -> 30.2 us
  waiting for transfers between devices: 69.2 us -> 90.9 us
    ppermute x2, starting transfers between devices: 27.3 us -> 0.06 us  [on_device(): grad_far = lax.ppermute(grad_part, 'expert', forward)]
    ppermute x4, waiting for transfers between devices: 0.01 us -> 17.6 us  [the longest x1 17.5 us: on_device(): lax.ppermute(first_sums if groups > 2 else ran[1], 'expert', forward)]
    ppermute x2, waiting for transfers between devices: 32.8 us -> 36.8 us  [on_device(): grad_far = lax.ppermute(grad_part, 'expert', forward)]
  transfers between devices with their start and end apart: 22 -> 22, of which waited for: 8 -> 9; matrix products, arithmetic and copies ran while one was open for 6% -> 7% of each run, Pallas kernels for 52% -> 53%
where the time goes in v2:
time: 371 us; the launch traced here: 365 us
  Pallas kernels  194 us (52%)
  waiting for transfers between devices  90.9 us (25%)
  starting transfers between devices  30.2 us (8%)
  local copies, waits for them, and re-layouts  20.4 us (5%)
  between operations  15 us (4%)
  other arithmetic  14.2 us (4%)
    pallas_call x4, Pallas kernels, run_experts(): pl.pallas_call(expert_kernel, grid_spec=pltpu.PrefetchScalarGridSpec(num_...  108 us
    ppermute x2, waiting for transfers between devices, on_device(): grad_far = lax.ppermute(grad_part, 'expert', forward)  36.8 us
    pallas_call x1, Pallas kernels, attend_back(): pl.pallas_call(attend_back_kernel, grid_spec=pltpu.PrefetchScalarGridSpec...  22.5 us
    all_to_all x1, waiting for transfers between devices, on_device(): packed = lax.all_to_all(packed, ('dp', 'expert'), 0, 0, tiled=True)  17.9 us
    ppermute x1, waiting for transfers between devices, on_device(): lax.ppermute(first_sums if groups > 2 else ran[1], 'expert', forward)  17.5 us
    pallas_call x1, Pallas kernels, attend(): pl.pallas_call(attend_kernel, grid_spec=pltpu.PrefetchScalarGridSpec(num_...  17.2 us
    pallas_call x1, Pallas kernels, project(): pl.pallas_call(project_kernel, grid_spec=pltpu.PrefetchScalarGridSpec(num...  12.3 us
    ppermute x10, starting transfers between devices, swap(): return lax.ppermute(value, 'dp', [(at, at ^ bit) for at in range(BLOCKS)])  11.5 us
  transfers between devices with their start and end apart: 22, of which 9 were waited for; matrix products, arithmetic and copies ran while one was open for 7% of the time, Pallas kernels for 53%

profile of v2, /device:TPU:0, one launch (start us, length us, event | category | flops | bytes accessed | tf_op | source)
XLA Modules:
  0.0 364.5 jit_solution(8986110190354611207)
XLA Ops:
  7.2 3.0 collective-permute-start.2
  10.3 1.5 collective-permute-start.3
  13.8 0.9 reshape.90
  14.7 0.9 copy.62
  16.6 1.3 gather_fusion
  17.9 4.2 %all-to-all-start = ((bf16[8,112,128]{2,1,0:T(8,128)(2,1)}), bf16[8,112,128]{2,1,0:T(8,128)(2,1)S(1)}, u32[]{:S(2)}, u32[]{:S(2)}) async-start(bf16[8,112,128]{2,1,0:T(8,128)(2,1)} %gather_fusion), calls=%async_computation | async-start | bytes 458752 | tf_op jit(solution)/shard_map/all_to_all | solution.py:1002
  22.0 0.8 constant_dynamic-update-slice_fusion.4
  22.9 6.0 %collective-permute-done = bf16[128,2048]{1,0:T(8,128)(2,1)S(1)} collective-permute-done((bf16[128,2048]{1,0:T(8,128)(2,1)}, bf16[128,2048]{1,0:T(8,128)(2,1)S(1)}, u32[]{:S(2)}, u32[]{:S(2)}) %collective-permute-start) | collective-permute-done | bytes 524320 | tf_op jit(solution)/shard_map/ppermute | solution.py:916
  28.9 1.8 collective-permute-done.1
  31.0 2.2 collective-permute-start.5
  33.2 0.9 constant_dynamic-update-slice_fusion.3
  34.1 0.8 constant_dynamic-update-slice_fusion.2
  34.9 2.3 collective-permute-done.4
  45.2 1.9 collective-permute-start.7
  47.1 2.0 collective-permute-start.8
  49.1 12.3 %project.1 = (bf16[512,2048]{1,0:T(8,128)(2,1)}, bf16[512,64]{1,0:T(8,128)(2,1)}, bf16[512,1024]{1,0:T(8,128)(2,1)}) custom-call(s32[8]{0:T(128)} %broadcast_xor_fusion.order.refs_0_, bf16[512,1024]{1,0:T(8,128)(2,1)} %hid.5, bf16[1,1024]{1,0:T(2,128)(2,1)} %reshape.88.gain, bf16[512,2048]{1,0:T(8,128)(2,1)} %constant_dynamic-update-slice_fusion.weight_a, ...), custom_call_target="tpu_custom_call" | custom-call | flops 2147483648 | bytes 8388608 | tf_op jit(solution)/shard_map/project/pallas_call | solution.py:133
  62.2 1.4 add_select_fusion.routes
  64.3 17.2 %attend.1 = (bf16[512,1024]{1,0:T(8,128)(2,1)}, f32[8,512,2]{2,1,0:T(8,128)}) custom-call(s32[1]{0:T(128)} %dynamic_slice.13.scalars, bf16[512,2048]{1,0:T(8,128)(2,1)} %get-tuple-element.69.query.key.value, bf16[512,2048]{1,0:T(8,128)(2,1)} %get-tuple-element.69.query.key.value, bf16[512,2048]{1,0:T(8,128)(2,1)} %get-tuple-element.69.query.key.value), custom_call_target="tpu_custom_call" | custom-call | flops 2147483648 | bytes 4194304 | tf_op jit(solution)/shard_map/attend/pallas_call | solution.py:204
  81.5 1.0 copy-done.4
  82.5 6.0 %close_mixer.1 = (f32[512,1024]{1,0:T(8,128)}, bf16[512,1024]{1,0:T(8,128)(2,1)}, bf16[512,64]{1,0:T(8,128)(2,1)}) custom-call(s32[8]{0:T(128)} %broadcast_xor_fusion.order.refs_0_, bf16[512,1024]{1,0:T(8,128)(2,1)} %get-tuple-element.70.att.refs_11_, bf16[512,1024]{1,0:T(8,128)(2,1)} %hid.5, bf16[1,1024]{1,0:T(2,128)(2,1)} %reshape.95.gain.refs_3_, ...), custom_call_target="tpu_custom_call" | custom-call | flops 1073741824 | bytes 8388608 | tf_op jit(solution)/shard_map/close_mixer/pallas_call | solution.py:333
  88.5 2.1 collective-permute-start.11
  90.6 27.2 %experts.4 = (bf16[1040,1024]{1,0:T(8,128)(2,1)}, f32[16,512]{1,0:T(8,128)}, bf16[8,4,288,128]{3,2,1,0:T(8,128)(2,1)}) custom-call(s32[5]{0:T(128)} %get-tuple-element.122.scalars, bf16[512,1024]{1,0:T(8,128)(2,1)} %get-tuple-element.80.x, bf16[512,1024]{1,0:T(8,128)(2,1)} %refs_1_.1, s32[2048,8]{1,0:T(8,128)} %add_select_fusion.routes, ...), custom_call_target="tpu_custom_call" | custom-call | flops 19327352832 | bytes 20971520 | tf_op jit(solution)/shard_map/experts/pallas_call | solution.py:531
  117.8 2.5 collective-permute-start.10
  120.2 1.0 copy-done.15
  121.2 26.8 %experts.5 = (bf16[1040,1024]{1,0:T(8,128)(2,1)}, f32[16,512]{1,0:T(8,128)}, bf16[8,4,288,128]{3,2,1,0:T(8,128)(2,1)}) custom-call(s32[5]{0:T(128)} %get-tuple-element.120.scalars, bf16[512,1024]{1,0:T(8,128)(2,1)} %copy-done.15, bf16[2048,1024]{1,0:T(8,128)(2,1)} %all-gather.2.cloned.1.call-done.cot, ...), custom_call_target="tpu_custom_call", output_to_operand_aliasing={{2}: (11, {})} | custom-call | flops 19327352832 | bytes 20971520 | tf_op jit(solution)/shard_map/experts/pallas_call | solution.py:531
  148.2 26.8 %experts.6 = (bf16[1040,1024]{1,0:T(8,128)(2,1)}, f32[16,512]{1,0:T(8,128)}, bf16[8,4,288,128]{3,2,1,0:T(8,128)(2,1)}) custom-call(s32[5]{0:T(128)} %get-tuple-element.121.scalars, bf16[512,1024]{1,0:T(8,128)(2,1)} %collective-permute-done.10.x, bf16[2048,1024]{1,0:T(8,128)(2,1)} %all-gather.2.cloned.1.call-done.cot, ...), custom_call_target="tpu_custom_call", output_to_operand_aliasing={{2}: (11, {})} | custom-call | flops 19327352832 | bytes 20971520 | tf_op jit(solution)/shard_map/experts/pallas_call | solution.py:531
  175.0 1.6 collective-permute-start.13
  176.6 1.0 copy-done.17
  177.6 26.8 %experts.7 = (bf16[1040,1024]{1,0:T(8,128)(2,1)}, f32[16,512]{1,0:T(8,128)}, bf16[8,4,288,128]{3,2,1,0:T(8,128)(2,1)}) custom-call(s32[5]{0:T(128)} %get-tuple-element.119.scalars, bf16[512,1024]{1,0:T(8,128)(2,1)} %copy-done.17, bf16[2048,1024]{1,0:T(8,128)(2,1)} %all-gather.2.cloned.1.call-done.cot, ...), custom_call_target="tpu_custom_call", output_to_operand_aliasing={{2}: (11, {})} | custom-call | flops 19327352832 | bytes 20971520 | tf_op jit(solution)/shard_map/experts/pallas_call | solution.py:531
  204.3 3.6 all-to-all-start.1
  208.0 17.5 %collective-permute-done.13 = bf16[1040,1024]{1,0:T(8,128)(2,1)} collective-permute-done((bf16[1040,1024]{1,0:T(8,128)(2,1)}, bf16[1040,1024]{1,0:T(8,128)(2,1)}, u32[]{:S(2)}, u32[]{:S(2)}) %collective-permute-start.13) | collective-permute-done | bytes 2129952 | tf_op jit(solution)/shard_map/ppermute | solution.py:1110
  225.5 3.0 add_convert_fusion.1
  229.2 8.2 %all-to-all-done.1 = bf16[8,4,288,128]{3,2,1,0:T(8,128)(2,1)S(1)} async-done(((bf16[8,4,288,128]{3,2,1,0:T(8,128)(2,1)}), bf16[8,4,288,128]{3,2,1,0:T(8,128)(2,1)S(1)}, u32[]{:S(2)}, u32[]{:S(2)}) %all-to-all-start.1) | async-done | bytes 2359328 | tf_op jit(solution)/shard_map/all_to_all | solution.py:1105
  237.3 1.4 copy-done.1
  238.7 3.6 sum_experts.1
  242.3 13.0 %collective-permute-done.14 = bf16[528,1024]{1,0:T(8,128)(2,1)S(1)} collective-permute-done((bf16[528,1024]{1,0:T(8,128)(2,1)}, bf16[528,1024]{1,0:T(8,128)(2,1)S(1)}, u32[]{:S(2)}, u32[]{:S(2)}) %collective-permute-start.14) | collective-permute-done | bytes 1081376 | tf_op jit(solution)/shard_map/ppermute | solution.py:1116
  255.8 1.9 add_convert_fusion.4
  257.8 23.8 %collective-permute-done.15.refs_13_.refs_16_.refs_17_ = bf16[528,1024]{1,0:T(8,128)(2,1)S(1)} collective-permute-done((bf16[528,1024]{1,0:T(8,128)(2,1)S(1)}, bf16[528,1024]{1,0:T(8,128)(2,1)S(1)}, u32[]{:S(2)}, u32[]{:S(2)}) %collective-permute-start.15) | collective-permute-done | bytes 1081376 | tf_op jit(solution)/shard_map/ppermute | solution.py:1116
  282.6 9.5 %open_back.1 = (f32[512,1024]{1,0:T(8,128)}, bf16[512,1024]{1,0:T(8,128)(2,1)}, f32[64,1024]{1,0:T(8,128)}, f32[64,1024]{1,0:T(8,128)}) custom-call(s32[8]{0:T(128)} %broadcast_xor_fusion.order.refs_0_, bf16[512,1024]{1,0:T(8,128)(2,1)} %refs_1_.1, f32[512,1024]{1,0:T(8,128)} %get-tuple-element.76.refs_2_, bf16[1,1024]{1,0:T(2,128)(2,1)} %reshape.95.gain.refs_3_, ...), custom_call_target="tpu_custom_call" | custom-call | flops 1073741824 | bytes 14680064 | tf_op jit(solution)/shard_map/open_back/pallas_call | solution.py:651
  292.1 22.5 %attend_back.1 = (bf16[512,1024]{1,0:T(8,128)(2,1)}, bf16[512,512]{1,0:T(8,128)(2,1)}, bf16[512,512]{1,0:T(8,128)(2,1)}) custom-call(s32[1]{0:T(128)} %dynamic_slice.13.scalars, bf16[512,2048]{1,0:T(8,128)(2,1)} %get-tuple-element.69.query.key.value, bf16[512,2048]{1,0:T(8,128)(2,1)} %get-tuple-element.69.query.key.value, ...), custom_call_target="tpu_custom_call" | custom-call | flops 5368709120 | bytes 8388608 | tf_op jit(solution)/shard_map/attend_back/pallas_call | solution.py:280
  314.5 1.4 add_convert_fusion.3
  315.9 4.6 %adapters_back.1 = (bf16[512,64]{1,0:T(8,128)(2,1)}, f32[32,16,256]{2,1,0:T(8,128)}) custom-call(bf16[512,1024]{1,0:T(8,128)(2,1)} %get-tuple-element.100.grad_query, bf16[512,512]{1,0:T(8,128)(2,1)} %get-tuple-element.101.grad_key, bf16[512,512]{1,0:T(8,128)(2,1)} %get-tuple-element.102.grad_value, bf16[512,64]{1,0:T(8,128)(2,1)} %get-tuple-element.103.low, ...), custom_call_target="tpu_custom_call" | custom-call | flops 1610612736 | bytes 4194304 | tf_op jit(solution)/shard_map/adapters_back/pallas_call | solution.py:752
  320.5 4.2 %all-to-all-start.2 = ((f32[32,16,256]{2,1,0:T(8,128)}), f32[32,16,256]{2,1,0:T(8,128)S(1)}, u32[]{:S(2)}, u32[]{:S(2)}) async-start(f32[32,16,256]{2,1,0:T(8,128)} %get-tuple-element.109), calls=%async_computation.2 | async-start | bytes 1048576 | tf_op jit(solution)/shard_map/all_to_all | solution.py:1141
  324.7 8.6 %input_back.1 = bf16[512,1024]{1,0:T(8,128)(2,1)} custom-call(s32[8]{0:T(128)} %broadcast_xor_fusion.order.refs_0_, bf16[512,1024]{1,0:T(8,128)(2,1)} %get-tuple-element.100.grad_query, bf16[512,512]{1,0:T(8,128)(2,1)} %get-tuple-element.101.grad_key, bf16[512,512]{1,0:T(8,128)(2,1)} %get-tuple-element.102.grad_value, ...), custom_call_target="tpu_custom_call" | custom-call | flops 2147483648 | bytes 12582912 | tf_op jit(solution)/shard_map/input_back/pallas_call | solution.py:797
  333.3 17.9 %all-to-all-done.2.pieces = f32[32,16,256]{2,1,0:T(8,128)S(1)} async-done(((f32[32,16,256]{2,1,0:T(8,128)}), f32[32,16,256]{2,1,0:T(8,128)S(1)}, u32[]{:S(2)}, u32[]{:S(2)}) %all-to-all-start.2) | async-done | bytes 524320 | tf_op jit(solution)/shard_map/all_to_all | solution.py:1141
  351.2 0.8 copy-done.6
  352.0 2.1 sum_mixer.1
  354.1 3.0 add_convert_fusion.2
  (107 shorter events, 15.0 us)
Async XLA Ops:
  7.2 14.9 %copy-start.7 = (bf16[128,2048]{1,0:T(8,128)(2,1)S(1)}, bf16[128,2048]{1,0:T(8,128)(2,1)}, u32[]{:S(2)}) copy-start(bf16[128,2048]{1,0:T(8,128)(2,1)} %param.30) | copy-start | bytes 1572868
  7.2 113.1 %all-gather.2.cloned.1.call-start = ((), (), s32[]{:S(2)}) async-start(), calls=%async_computation.3 | async-start | bytes 5242880 | tf_op jit(solution)/shard_map/all_gather | solution.py:1037
  7.2 15.7 %collective-permute-start.2 = (bf16[128,1024]{1,0:T(8,128)(2,1)}, bf16[128,1024]{1,0:T(8,128)(2,1)S(1)}, u32[]{:S(2)}, u32[]{:S(2)}) collective-permute-start(bf16[128,1024]{1,0:T(8,128)(2,1)} %param.31), channel_id=1, source_target_pairs={{0,8},{4,12},{8,0},{12,4},{16,24},{20,28},{24,16},{28,20},{1,9},{5... | collective-permute-start | bytes 786440 | tf_op jit(solution)/shard_map/ppermute | solution.py:916
  10.3 12.6 %collective-permute-start.3 = (bf16[128,1024]{1,0:T(8,128)(2,1)}, bf16[128,1024]{1,0:T(8,128)(2,1)S(1)}, u32[]{:S(2)}, u32[]{:S(2)}) collective-permute-start(bf16[128,1024]{1,0:T(8,128)(2,1)} %param.31), channel_id=1, source_target_pairs={{0,16},{4,20},{8,24},{12,28},{16,0},{20,4},{24,8},{28,12},{1,17},{... | collective-permute-start | bytes 786440 | tf_op jit(solution)/shard_map/ppermute | solution.py:916
  11.8 17.1 %collective-permute-start = (bf16[128,2048]{1,0:T(8,128)(2,1)}, bf16[128,2048]{1,0:T(8,128)(2,1)S(1)}, u32[]{:S(2)}, u32[]{:S(2)}) collective-permute-start(bf16[128,2048]{1,0:T(8,128)(2,1)} %param.30), channel_id=1, source_target_pairs={{0,8},{4,12},{8,0},{12,4},{16,24},{20,28},{24,16},{28,20},{1,9},{5... | collective-permute-start | bytes 1572872 | tf_op jit(solution)/shard_map/ppermute | solution.py:916
  12.3 18.4 %collective-permute-start.1 = (bf16[128,2048]{1,0:T(8,128)(2,1)}, bf16[128,2048]{1,0:T(8,128)(2,1)S(1)}, u32[]{:S(2)}, u32[]{:S(2)}) collective-permute-start(bf16[128,2048]{1,0:T(8,128)(2,1)} %param.30), channel_id=1, source_target_pairs={{0,16},{4,20},{8,24},{12,28},{16,0},{20,4},{24,8},{28,12},{1,17},{... | collective-permute-start | bytes 1572872 | tf_op jit(solution)/shard_map/ppermute | solution.py:916
  17.9 25.8 %all-to-all-start = ((bf16[8,112,128]{2,1,0:T(8,128)(2,1)}), bf16[8,112,128]{2,1,0:T(8,128)(2,1)S(1)}, u32[]{:S(2)}, u32[]{:S(2)}) async-start(bf16[8,112,128]{2,1,0:T(8,128)(2,1)} %gather_fusion), calls=%async_computation | async-start | bytes 458752 | tf_op jit(solution)/shard_map/all_to_all | solution.py:1002
  22.9 16.1 %copy-start.10 = (s32[2048,8]{0,1:T(8,128)S(1)}, s32[2048,8]{0,1:T(8,128)}, u32[]{:S(2)}) copy-start(s32[2048,8]{0,1:T(8,128)} %param.27) | copy-start | bytes 196612
  22.9 16.4 %copy-start.12 = (bf16[1024]{0:T(1024)(128)(2,1)S(1)}, bf16[1024]{0:T(1024)(128)(2,1)}, u32[]{:S(2)}) copy-start(bf16[1024]{0:T(1024)(128)(2,1)} %param.28) | copy-start | bytes 6148
  22.9 17.0 %copy-start.13 = (bf16[1024]{0:T(1024)(128)(2,1)S(1)}, bf16[1024]{0:T(1024)(128)(2,1)}, u32[]{:S(2)}) copy-start(bf16[1024]{0:T(1024)(128)(2,1)} %param.29) | copy-start | bytes 6148
  30.8 10.1 %copy-start.18 = (s32[32]{0:T(128)S(1)}, s32[32]{0:T(128)}, u32[]{:S(2)}) copy-start(s32[32]{0:T(128)} %param.25) | copy-start | bytes 388
  30.8 11.3 %copy-start.11 = (bf16[1024,16]{0,1:T(8,128)(2,1)S(1)}, bf16[1024,16]{0,1:T(8,128)(2,1)}, u32[]{:S(2)}) copy-start(bf16[1024,16]{0,1:T(8,128)(2,1)} %param.32) | copy-start | bytes 98308
  30.8 6.4 %collective-permute-start.4 = (bf16[64,2048]{1,0:T(8,128)(2,1)S(1)}, bf16[64,2048]{1,0:T(8,128)(2,1)S(1)}, u32[]{:S(2)}, u32[]{:S(2)}) collective-permute-start(bf16[64,2048]{1,0:T(8,128)(2,1)S(1)} %slice.54), channel_id=1, source_target_pairs={{0,8},{4,12},{8,0},{12,4},{16,24},{20,28},{24,16},{28,20},{1,9},{5... | collective-permute-start | bytes 786440 | tf_op jit(solution)/shard_map/ppermute | solution.py:916
  31.0 6.5 %collective-permute-start.5 = (bf16[64,2048]{1,0:T(8,128)(2,1)S(1)}, bf16[64,2048]{1,0:T(8,128)(2,1)S(1)}, u32[]{:S(2)}, u32[]{:S(2)}) collective-permute-start(bf16[64,2048]{1,0:T(8,128)(2,1)S(1)} %slice.55), channel_id=1, source_target_pairs={{0,16},{4,20},{8,24},{12,28},{16,0},{20,4},{24,8},{28,12},{1,17},{... | collective-permute-start | bytes 786440 | tf_op jit(solution)/shard_map/ppermute | solution.py:916
  34.1 8.9 %copy-start.14 = (s32[4,1]{1,0:T(4,128)S(1)}, s32[4,1]{1,0:T(4,128)}, u32[]{:S(2)}) copy-start(s32[4,1]{1,0:T(4,128)} %constant.94) | copy-start | bytes 52
  34.1 9.0 %copy-start.9 = (bf16[128,1024]{1,0:T(8,128)(2,1)S(1)}, bf16[128,1024]{1,0:T(8,128)(2,1)}, u32[]{:S(2)}) copy-start(bf16[128,1024]{1,0:T(8,128)(2,1)} %param.31) | copy-start | bytes 786436
  34.1 9.0 %copy-start.19 = (s32[8]{0:T(128)S(1)}, s32[8]{0:T(128)}, u32[]{:S(2)}) copy-start(s32[8]{0:T(128)} %constant.84.clone) | copy-start | bytes 100
  39.0 10.2 %collective-permute-start.6 = (bf16[512,2048]{1,0:T(8,128)(2,1)}, bf16[512,2048]{1,0:T(8,128)(2,1)}, u32[]{:S(2)}, u32[]{:S(2)}) collective-permute-start(bf16[512,2048]{1,0:T(8,128)(2,1)} %constant_dynamic-update-slice_fusion.weight_a), channel_id=1, source_target_pairs={{0,4},{4,0},{8,12},{12,8},{16,20},{20,16},{24,28},{28,24},{1,5},{5... | collective-permute-start | bytes 6291464 | tf_op jit(solution)/shard_map/ppermute | solution.py:916
  42.1 19.3 %copy-start.8 = (bf16[16,1024]{1,0:T(8,128)(2,1)}, bf16[16,1024]{1,0:T(8,128)(2,1)S(1)}, u32[]{:S(2)}) copy-start(bf16[16,1024]{1,0:T(8,128)(2,1)S(1)} %fusion.1.refs_5_) | copy-start | bytes 98308
  45.2 16.2 %collective-permute-start.7 = (bf16[64,1024]{1,0:T(8,128)(2,1)S(1)}, bf16[64,1024]{1,0:T(8,128)(2,1)S(1)}, u32[]{:S(2)}, u32[]{:S(2)}) collective-permute-start(bf16[64,1024]{1,0:T(8,128)(2,1)S(1)} %slice.58), channel_id=1, source_target_pairs={{0,8},{4,12},{8,0},{12,4},{16,24},{20,28},{24,16},{28,20},{1,9},{5... | collective-permute-start | bytes 393224 | tf_op jit(solution)/shard_map/ppermute | solution.py:916
  47.1 14.4 %collective-permute-start.8 = (bf16[64,1024]{1,0:T(8,128)(2,1)S(1)}, bf16[64,1024]{1,0:T(8,128)(2,1)S(1)}, u32[]{:S(2)}, u32[]{:S(2)}) collective-permute-start(bf16[64,1024]{1,0:T(8,128)(2,1)S(1)} %slice.59), channel_id=1, source_target_pairs={{0,16},{4,20},{8,24},{12,28},{16,0},{20,4},{24,8},{28,12},{1,17},{... | collective-permute-start | bytes 393224 | tf_op jit(solution)/shard_map/ppermute | solution.py:916
  61.5 20.0 %copy-start.3 = (bf16[512,1024]{1,0:T(8,128)(2,1)}, bf16[512,1024]{1,0:T(8,128)(2,1)S(1)}, u32[]{:S(2)}) copy-start(bf16[512,1024]{1,0:T(8,128)(2,1)S(1)} %constant_dynamic-update-slice_fusion.5.weight_a.refs_6_) | copy-start | bytes 3145732
  61.5 20.0 %collective-permute-start.9 = (bf16[512,1024]{1,0:T(8,128)(2,1)S(1)}, bf16[512,1024]{1,0:T(8,128)(2,1)S(1)}, u32[]{:S(2)}, u32[]{:S(2)}) collective-permute-start(bf16[512,1024]{1,0:T(8,128)(2,1)S(1)} %constant_dynamic-update-slice_fusion.5.weight_a.refs_6_), channel_id=1, source_target_pairs={{0,4},{4,0},{8,12},{12,8},{16,20},{20,16},{24,28},{28,24},{1,5},{5... | collective-permute-start | bytes 3145736 | tf_op jit(solution)/shard_map/ppermute | solution.py:916
  81.5 1.0 copy-start.4
  88.5 31.7 %collective-permute-start.11 = (bf16[512,1024]{1,0:T(8,128)(2,1)}, bf16[512,1024]{1,0:T(8,128)(2,1)S(1)}, u32[]{:S(2)}, u32[]{:S(2)}) collective-permute-start(bf16[512,1024]{1,0:T(8,128)(2,1)} %get-tuple-element.80.x), channel_id=1, source_target_pairs={{0,1},{1,2},{2,3},{3,0},{4,5},{5,6},{6,7},{7,4},{8,9},{9,10},{10,1... | collective-permute-start | bytes 3145736 | tf_op jit(solution)/shard_map/ppermute | solution.py:1074
  90.6 27.2 %copy-start.16 = (bf16[512,1024]{1,0:T(8,128)(2,1)S(1)}, bf16[512,1024]{1,0:T(8,128)(2,1)}, u32[]{:S(2)}) copy-start(bf16[512,1024]{1,0:T(8,128)(2,1)} %get-tuple-element.80.x) | copy-start | bytes 3145732
  117.8 30.4 %collective-permute-start.10 = (bf16[512,1024]{1,0:T(8,128)(2,1)S(1)}, bf16[512,1024]{1,0:T(8,128)(2,1)}, u32[]{:S(2)}, u32[]{:S(2)}) collective-permute-start(bf16[512,1024]{1,0:T(8,128)(2,1)S(1)} %copy-done.16), channel_id=1, source_target_pairs={{0,3},{1,0},{2,1},{3,2},{4,7},{5,4},{6,5},{7,6},{8,11},{9,8},{10,9... | collective-permute-start | bytes 3145736 | tf_op jit(solution)/shard_map/ppermute | solution.py:1098
  120.2 1.0 copy-start.15
  148.0 28.6 %collective-permute-start.12 = (bf16[512,1024]{1,0:T(8,128)(2,1)}, bf16[512,1024]{1,0:T(8,128)(2,1)S(1)}, u32[]{:S(2)}, u32[]{:S(2)}) collective-permute-start(bf16[512,1024]{1,0:T(8,128)(2,1)} %copy-done.15), channel_id=1, source_target_pairs={{0,1},{1,2},{2,3},{3,0},{4,5},{5,6},{6,7},{7,4},{8,9},{9,10},{10,1... | collective-permute-start | bytes 3145736 | tf_op jit(solution)/shard_map/ppermute | solution.py:1101
  175.0 50.5 %collective-permute-start.13 = (bf16[1040,1024]{1,0:T(8,128)(2,1)}, bf16[1040,1024]{1,0:T(8,128)(2,1)}, u32[]{:S(2)}, u32[]{:S(2)}) collective-permute-start(bf16[1040,1024]{1,0:T(8,128)(2,1)} %get-tuple-element.90), channel_id=1, source_target_pairs={{0,1},{1,2},{2,3},{3,0},{4,5},{5,6},{6,7},{7,4},{8,9},{9,10},{10,1... | collective-permute-start | bytes 6389768 | tf_op jit(solution)/shard_map/ppermute | solution.py:1110
  176.6 1.0 copy-start.17
  204.3 33.0 %all-to-all-start.1 = ((bf16[8,4,288,128]{3,2,1,0:T(8,128)(2,1)}), bf16[8,4,288,128]{3,2,1,0:T(8,128)(2,1)S(1)}, u32[]{:S(2)}, u32[]{:S(2)}) async-start(bf16[8,4,288,128]{3,2,1,0:T(8,128)(2,1)} %get-tuple-element.91), calls=%async_computation.1 | async-start | bytes 4718592 | tf_op jit(solution)/shard_map/all_to_all | solution.py:1105
  228.5 26.8 %collective-permute-start.14 = (bf16[528,1024]{1,0:T(8,128)(2,1)}, bf16[528,1024]{1,0:T(8,128)(2,1)S(1)}, u32[]{:S(2)}, u32[]{:S(2)}) collective-permute-start(bf16[528,1024]{1,0:T(8,128)(2,1)} %add_convert_fusion.1), channel_id=1, source_target_pairs={{0,1},{1,2},{2,3},{3,0},{4,5},{5,6},{6,7},{7,4},{8,9},{9,10},{10,1... | collective-permute-start | bytes 3244040 | tf_op jit(solution)/shard_map/ppermute | solution.py:1116
  237.3 1.4 copy-start.1
  237.3 18.0 %copy-start.5 = (bf16[1040,1024]{1,0:T(8,128)(2,1)S(1)}, bf16[1040,1024]{1,0:T(8,128)(2,1)}, u32[]{:S(2)}) copy-start(bf16[1040,1024]{1,0:T(8,128)(2,1)} %get-tuple-element.84) | copy-start | bytes 6389764
  255.8 25.8 %collective-permute-start.15 = (bf16[528,1024]{1,0:T(8,128)(2,1)S(1)}, bf16[528,1024]{1,0:T(8,128)(2,1)S(1)}, u32[]{:S(2)}, u32[]{:S(2)}) collective-permute-start(bf16[528,1024]{1,0:T(8,128)(2,1)S(1)} %add_convert_fusion), channel_id=1, source_target_pairs={{0,1},{1,2},{2,3},{3,0},{4,5},{5,6},{6,7},{7,4},{8,9},{9,10},{10,1... | collective-permute-start | bytes 3244040 | tf_op jit(solution)/shard_map/ppermute | solution.py:1116
  281.6 1.0 copy-start
  281.6 33.0 %collective-permute-start.16 = (bf16[512,1024]{1,0:T(8,128)(2,1)S(1)}, bf16[512,1024]{1,0:T(8,128)(2,1)S(1)}, u32[]{:S(2)}, u32[]{:S(2)}) collective-permute-start(bf16[512,1024]{1,0:T(8,128)(2,1)S(1)} %add_convert_fusion.4), channel_id=1, source_target_pairs={{0,1},{1,2},{2,3},{3,0},{4,5},{5,6},{6,7},{7,4},{8,9},{9,10},{10,1... | collective-permute-start | bytes 3145736 | tf_op jit(solution)/shard_map/ppermute | solution.py:1121
  315.9 38.2 %collective-permute-start.17 = (bf16[512,1024]{1,0:T(8,128)(2,1)}, bf16[512,1024]{1,0:T(8,128)(2,1)}, u32[]{:S(2)}, u32[]{:S(2)}) collective-permute-start(bf16[512,1024]{1,0:T(8,128)(2,1)} %add_convert_fusion.3), channel_id=1, source_target_pairs={{0,1},{1,2},{2,3},{3,0},{4,5},{5,6},{6,7},{7,4},{8,9},{9,10},{10,1... | collective-permute-start | bytes 3145736 | tf_op jit(solution)/shard_map/ppermute | solution.py:1121
  320.5 30.7 %all-to-all-start.2 = ((f32[32,16,256]{2,1,0:T(8,128)}), f32[32,16,256]{2,1,0:T(8,128)S(1)}, u32[]{:S(2)}, u32[]{:S(2)}) async-start(f32[32,16,256]{2,1,0:T(8,128)} %get-tuple-element.109), calls=%async_computation.2 | async-start | bytes 1048576 | tf_op jit(solution)/shard_map/all_to_all | solution.py:1141
  324.7 29.4 %copy-start.2 = (f32[512,1024]{1,0:T(8,128)S(1)}, f32[512,1024]{1,0:T(8,128)}, u32[]{:S(2)}) copy-start(f32[512,1024]{1,0:T(8,128)} %get-tuple-element.76.refs_2_) | copy-start | bytes 6291460
  351.2 0.8 copy-start.6
Sparse Core Ops, SparseCore 0:
  12.5 82.7 all-gather.1

commit v3 on v2

--- a/solution.py
+++ b/solution.py
@@ -90,6 +90,14 @@
 
 def column(order, at):
     return pl.ds(pl.multiple_of(order[at] * BLOCK, BLOCK), BLOCK)
+
+
+def halves(weights, width, index):
+    there = 1 if weights[0] is weights[1] else 0
+    return [
+        pl.BlockSpec((HALF, width), lambda n, s: (0, index(n))),
+        pl.BlockSpec((HALF, width), lambda n, s: (there, index(n))),
+    ]
 
 
 def project_kernel(
@@ -138,8 +146,7 @@
             in_specs=[
                 full((rows, MODEL_WIDTH)),
                 full((1, MODEL_WIDTH)),
-                pl.BlockSpec((HALF, block), lambda n, s: (0, n)),
-                pl.BlockSpec((HALF, block), lambda n, s: (0, n)),
+                *halves(weights, block, lambda n: n),
                 full((ranks, MODEL_WIDTH)),
                 pl.BlockSpec((ranks, block), lambda n, s: (0, n)),
                 full((rows, 128)),
@@ -168,30 +175,40 @@
 ROWB = 128
 
 
-def masked_scores(length, queries, keys, start, count):
-    scores = 0.125 * nt(queries, keys)
-    row = lax.broadcasted_iota(jnp.int32, scores.shape, 0)
-    col = lanes_of(scores.shape)
-    allowed = (col <= start + row % ROWB) & (col < length)
-    return scores, allowed
+def length_row(length, count):
+    col = lax.broadcasted_iota(jnp.int32, (1, count), 1)
+    return jnp.where(col < length, 0.0, -1e30)
+
+
+def causal_block():
+    row = lax.broadcasted_iota(jnp.int32, (2 * ROWB, ROWB), 0) % ROWB
+    return jnp.where(lanes_of((2 * ROWB, ROWB)) <= row, 0.0, -1e30)
+
+
+def masked_scores(queries, keys, start, bias, causal):
+    scores = nt((queries.astype(f32) * 0.125).astype(bf16), keys)
+    count = start + ROWB
+    near = scores[:, start:] + (bias[:, start:count] + causal)
+    if start == 0:
+        return near
+    return jnp.concatenate([scores[:, :start] + bias[:, :start], near], 1)
 
 
 def attend_kernel(scalars, query, key, value, result, lse):
     half = pl.program_id(0) % 2
-    length = scalars[0]
     keys = both_halves(key[...], half)
     values = both_halves(value[...], half)
     rows = query.shape[0]
+    bias = length_row(scalars[0], rows)
+    causal = causal_block()
     for start in range(0, rows, ROWB):
         count = start + ROWB
         stacked = stacked_heads(query[start:count, :])
-        scores, allowed = masked_scores(length, stacked, keys[:count], start, count)
-        scores = jnp.where(allowed, scores, -1e30)
+        scores = masked_scores(stacked, keys[:count], start, bias, causal)
         top = jnp.max(scores, -1, keepdims=True)
         shifted = jnp.exp(scores - top)
         total = jnp.sum(shifted, -1, keepdims=True)
-        prob = (shifted * (1.0 / total)).astype(bf16)
-        mixed = nn(prob, values[:count])
+        mixed = nn(shifted.astype(bf16), values[:count]) * (1.0 / total)
         lane = lanes_of((ROWB, 128))
         result[start:count, :] = jnp.where(lane < HS, mixed[:ROWB], mixed[ROWB:]).astype(bf16)
         logs = top + jnp.log(total)
@@ -232,7 +249,8 @@
     scalars, query, key, value, grad, lse, cos, sin, grad_query, grad_key, grad_value, key_acc, value_acc
 ):
     half = pl.program_id(0) % 2
-    length = scalars[0]
+    bias = length_row(scalars[0], query.shape[0])
+    causal = causal_block()
     keys = both_halves(key[...], half)
     values = both_halves(value[...], half)
     rows = query.shape[0]
@@ -242,10 +260,10 @@
         count = start + ROWB
         stacked = stacked_heads(query[start:count, :])
         grads = stacked_heads(grad[start:count, :])
-        scores, allowed = masked_scores(length, stacked, keys[:count], start, count)
+        scores = masked_scores(stacked, keys[:count], start, bias, causal)
         logs = lse[0, start:count, :]
         logs = jnp.concatenate([logs[:, 0:1], logs[:, 1:2]], 0)
-        prob = jnp.where(allowed, jnp.exp(scores - logs), 0.0)
+        prob = jnp.exp(scores - logs)
         grad_prob = nt(grads, values[:count])
         delta = jnp.sum(prob * grad_prob, -1, keepdims=True)
         grad_score = (prob * (grad_prob - delta)).astype(bf16)
@@ -339,8 +357,7 @@
                 part(QD),
                 part(MODEL_WIDTH),
                 full((1, MODEL_WIDTH)),
-                full((HALF, MODEL_WIDTH)),
-                full((HALF, MODEL_WIDTH)),
+                *halves(weights, MODEL_WIDTH, lambda n: 0),
                 full((ranks, QD)),
                 full((ranks, MODEL_WIDTH)),
             ],
@@ -387,7 +404,8 @@
     *rest,
 ):
     (
-        sums_out,
+        out,
+        grad_normed,
         gates_out,
         packed,
         gates,
@@ -404,7 +422,7 @@
         down_acc,
         out_acc,
         grad_acc,
-    ) = rest[-17:]
+    ) = rest[-18:]
     expert = pl.program_id(0)
     last = pl.num_programs(0) - 1
     rows = x.shape[0]
@@ -496,14 +514,13 @@
 
     @pl.when(expert == last)
     def _():
-        sums_out[:rows, :] = (grad_acc[...] + nn(back_in[...], a_in_all)).astype(bf16)
+        out[...] = (out_acc[...] + nn(gated_low[...], b_down_all)).astype(bf16)
+        grad_normed[:rows, :] = (grad_acc[...] + nn(back_in[...], a_in_all)).astype(bf16)
         experts = gates_out.shape[0]
         sums = gate_sums[...].T[:experts, :]
         sums = jnp.concatenate([sums[: experts // 2], sums[experts // 2 :]], 1)
         high = sums.astype(bf16).astype(f32)
-        edge = rows + experts
-        sums_out[rows:edge, :] = jnp.concatenate([high, sums - high], 0).astype(bf16)
-        sums_out[edge:, :] = (out_acc[...] + nn(gated_low[...], b_down_all)).astype(bf16)
+        grad_normed[rows:, :] = jnp.concatenate([high, sums - high], 0).astype(bf16)
         wide = tn(back_in[...], x[...]).astype(bf16)
         tall = tn(gated_low[...], cot[...]).astype(bf16)
         for at in range(BLOCKS):
@@ -519,14 +536,13 @@
 
 
 def run_experts(
-    scalars, x, cot, routes, router, w_in, w_down, a_in, b_in, a_down, b_down, experts, slots, packed
+    scalars, x, cot, routes, router, w_in, w_down, a_in, b_in, a_down, b_down, experts, packed
 ):
     rows = x.shape[0]
     local = w_in.shape[0]
     ranks_in = local * 2 * R
     ranks_down = local * R
-    height = local * 9 * R // 2
-    kept = [] if packed is None else [packed]
+    height = packed.shape[2]
     full = lambda shape: pl.BlockSpec(shape, lambda e, s: (0,) * len(shape))
     return pl.pallas_call(
         expert_kernel,
@@ -535,7 +551,7 @@
             grid=(local,),
             in_specs=[
                 full((rows, MODEL_WIDTH)),
-                pl.BlockSpec((rows, MODEL_WIDTH), lambda e, s: (s[4], 0)),
+                full((rows, MODEL_WIDTH)),
                 pl.BlockSpec((rows, TOP), lambda e, s: (s[0], 0)),
                 full((128, MODEL_WIDTH)),
                 pl.BlockSpec((1, MODEL_WIDTH, 2 * H), lambda e, s: (e, 0, 0)),
@@ -545,9 +561,10 @@
                 pl.BlockSpec((local, 1, R, H), lambda e, s: (0, s[1], 0, 0)),
                 pl.BlockSpec((local, 1, R, MODEL_WIDTH), lambda e, s: (0, s[1], 0, 0)),
             ]
-            + [pl.BlockSpec(memory_space=pl.ANY)] * len(kept),
+            + [pl.BlockSpec(memory_space=pl.ANY)],
             out_specs=[
-                full((2 * rows + experts, MODEL_WIDTH)),
+                full((rows, MODEL_WIDTH)),
+                full((rows + experts, MODEL_WIDTH)),
                 full((experts, rows)),
                 pl.BlockSpec((BLOCKS, 1, height, BLOCK), lambda e, s: (0, s[3], 0, 0)),
             ],
@@ -569,11 +586,12 @@
             ],
         ),
         out_shape=[
-            jax.ShapeDtypeStruct((2 * rows + experts, MODEL_WIDTH), bf16),
+            jax.ShapeDtypeStruct((rows, MODEL_WIDTH), bf16),
+            jax.ShapeDtypeStruct((rows + experts, MODEL_WIDTH), bf16),
             jax.ShapeDtypeStruct((experts, rows), f32),
-            jax.ShapeDtypeStruct((BLOCKS, slots, height, BLOCK), bf16),
+            jax.ShapeDtypeStruct(packed.shape, bf16),
         ],
-        input_output_aliases={11: 2} if kept else {},
+        input_output_aliases={11: 3},
         compiler_params=params_of(1),
         name="experts",
         cost_estimate=pl.CostEstimate(
@@ -581,7 +599,53 @@
             transcendentals=local * rows * H,
             bytes_accessed=20 << 20,
         ),
-    )(scalars, x, cot, routes, router, w_in, w_down, a_in, b_in, a_down, b_down, *kept)
+    )(scalars, x, cot, routes, router, w_in, w_down, a_in, b_in, a_down, b_down, packed)
+
+
+def room_for(shape):
+    return pl.pallas_call(
+        lambda ref: None,
+        out_specs=pl.BlockSpec(memory_space=pl.ANY),
+        out_shape=jax.ShapeDtypeStruct(shape, bf16),
+        name="room",
+    )()
+
+
+def join_kernel(left, right, result):
+    result[...] = (left[...].astype(f32) + right[...].astype(f32)).astype(bf16)
+
+
+def joined(left, right):
+    rows = left.shape[0]
+    steps = max(count for count in range(1, 5) if rows % (16 * count) == 0)
+    block = pl.BlockSpec((rows // steps, MODEL_WIDTH), lambda n: (n, 0))
+    return pl.pallas_call(
+        join_kernel,
+        grid=(steps,),
+        in_specs=[block, block],
+        out_specs=block,
+        out_shape=jax.ShapeDtypeStruct(left.shape, bf16),
+        compiler_params=params_of(1),
+        name="joined",
+    )(left, right)
+
+
+def finish_kernel(mid, here, far, result):
+    result[...] = (mid[...] + here[...].astype(f32) + far[...].astype(f32)).astype(bf16)
+
+
+def finish(mid, here, far):
+    rows = mid.shape[0]
+    block = pl.BlockSpec((rows // 4, MODEL_WIDTH), lambda n: (n, 0))
+    return pl.pallas_call(
+        finish_kernel,
+        grid=(4,),
+        in_specs=[block] * 3,
+        out_specs=block,
+        out_shape=jax.ShapeDtypeStruct(mid.shape, bf16),
+        compiler_params=params_of(1),
+        name="finish",
+    )(mid, here, far)
 
 
 def open_back_kernel(count, order, cot, mid, gain, gates, router, weight_a, weight_b, low_map, up_map, low, att, *rest):
@@ -659,8 +723,7 @@
                 full((1, MODEL_WIDTH)),
                 pl.BlockSpec((experts, block), lambda n, s: (0, n)),
                 full((experts, MODEL_WIDTH)),
-                full((HALF, MODEL_WIDTH)),
-                full((HALF, MODEL_WIDTH)),
+                *halves(weights, MODEL_WIDTH, lambda n: 0),
                 full((ranks, QD)),
                 full((ranks, MODEL_WIDTH)),
                 part(ranks),
@@ -804,8 +867,7 @@
                 part(KD),
                 part(KD),
                 part(ranks),
-                full((HALF, QKV)),
-                full((HALF, QKV)),
+                *halves(weights, QKV, lambda n: 0),
                 full((ranks, MODEL_WIDTH)),
                 part(MODEL_WIDTH),
                 full((1, MODEL_WIDTH)),
@@ -948,10 +1010,6 @@
     narrow = packed[:, :, edge:].reshape(BLOCKS, slots, rest, 2, split, BLOCK // 2 // split)
     narrow = narrow.transpose(0, 4, 1, 2, 3, 5).reshape(owners, slots, rest, BLOCK // split)
     return jnp.concatenate([wide, narrow], 2)
-
-
-def joined(left, right):
-    return (left.astype(f32) + right.astype(f32)).astype(bf16)
 
 
 def on_device(
@@ -1001,21 +1059,23 @@
     adapters = jnp.concatenate([low_turned, up_turned, attention_output_upmap], 1)[mine]
     adapters = lax.all_to_all(adapters, "dp", 0, 0, tiled=True)
     order = order_of(row)
-    short = owners == BLOCKS
-    if short:
+    plain = jnp.arange(BLOCKS, dtype=jnp.int32)
+    cots = {0: cotangent, 1: lax.ppermute(cotangent, "expert", forward)}
+    if owners == BLOCKS:
         pair_in = both_neighbours(query_key_value_weight)
-        pair_out = both_neighbours(w_out)
-        pair_in, pair_out = tied(pair_in, pair_out)
         across_in = across(pair_in)
-        pair_out, across_in = tied(pair_out, across_in)
+        w_out, across_in = tied(w_out, across_in)
         near_in = jnp.concatenate([query_key_value_weight, *pair_in, *across_in], 0)
+        if groups > 2:
+            near_in, cotangent, cots[1] = tied(near_in, cotangent, cots[1])
         weight_in = near_in, swap(near_in, 1)
-        across_out = across(pair_out)
     else:
         whole = lax.all_gather(query_key_value_weight, "dp", axis=0, tiled=True)
-        weight_in = whole[:HALF], whole[HALF:]
-        whole = lax.all_gather(w_out, "dp", axis=0, tiled=True)
-        weight_out = whole[:HALF], whole[HALF:]
+        weight_in = whole, whole
+    if groups > 2:
+        cots[groups - 1] = lax.ppermute(cotangent, "expert", backward)
+    weight_out = lax.all_gather(w_out, "dp", axis=0, tiled=True)
+    weight_out = weight_out, weight_out
 
     low_map = adapters[:, : 4 * R].transpose(1, 0, 2).reshape(4 * R, MODEL_WIDTH)
     up = (
@@ -1034,16 +1094,14 @@
 
     cos, sin = rope_tables(rows)
 
-    cots = lax.all_gather(cotangent, "expert", axis=0, tiled=True)
-
     qkv, low, normed_in = project(order, hidden, attn_gain, weight_in, low_map, up_map, cos, sin)
-    if short:
-        across_out, low = tied(across_out, low)
-        near_out = jnp.concatenate([w_out, *pair_out, *across_out], 0)
-        weight_out = near_out, swap(near_out, 1)
+    if groups > 3:
+        cots[1], low = tied(cots[1], low)
+    for at in range(2, groups - 1):
+        cots[at] = lax.ppermute(cots[at - 1], "expert", forward)
     attended, lse = attend(length, qkv)
     mid, normed_mid, low_out = close_mixer(
-        order, attended, hidden, ffn_gain, weight_out, low_map, up_out_map
+        plain, attended, hidden, ffn_gain, weight_out, low_map, up_out_map
     )
 
     first = place * local
@@ -1066,19 +1124,18 @@
             lax.dynamic_slice(tags, (row, 0), (1, groups))[0],
             offset * local,
             slot,
-            jnp.where(slot == 0, 0, source),
         ],
         1,
     )
 
     xs = {0: normed_mid, 1: lax.ppermute(normed_mid, "expert", forward)}
-    packed = None
+    packed = room_for((BLOCKS, groups, local * 9 * R // 2, BLOCK))
     ran = {}
     for at, offset in enumerate(offsets):
-        ran[offset], gate_part, packed = run_experts(
+        *ran[offset], gate_part, packed = run_experts(
             table[at],
             xs[offset],
-            cotangent if at == 0 else cots,
+            cots[offset],
             routes_here,
             router_wide,
             w_gate_up,
@@ -1088,7 +1145,6 @@
             a_down,
             expert_down_upmap,
             experts,
-            groups,
             packed,
         )
         if at == 0:
@@ -1100,28 +1156,22 @@
             value, packed = tied(xs[at], packed)
             xs[at + 1] = lax.ppermute(value, "expert", forward)
         if at == 2:
-            first_sums, packed = tied(ran[1], packed)
+            ran[1][1], packed = tied(ran[1][1], packed)
 
     pieces = lax.all_to_all(to_owners(packed, owners, local), "dp", 0, 0, tiled=True)
     pieces = pieces.reshape(devices, pieces.shape[2], width)
     g_a_in, g_b_in, g_a_down, g_b_down = sum_experts(tags.reshape(devices), pieces, local)
 
-    edge = rows + experts
-    both_far = lax.ppermute(first_sums if groups > 2 else ran[1], "expert", forward)
-    grad_far, out_far = both_far, both_far[edge:]
+    grad_far = lax.ppermute(ran[1][1], "expert", forward)
     for offset in range(2, groups):
-        grad_part = joined(ran[offset][:edge], grad_far[:edge])
+        grad_part = joined(ran[offset][1], grad_far)
         if offset == groups - 1:
             grad_part, g_a_down = tied(grad_part, g_a_down)
         grad_far = lax.ppermute(grad_part, "expert", forward)
-    for offset in range(2, groups):
-        out_part = joined(ran[offset][edge:], out_far)
-        if offset == 2:
-            out_part, grad_far = tied(out_part, grad_far)
-        out_far = lax.ppermute(out_part, "expert", forward)
-
+    out_part, grad_far = tied(ran[1][0], grad_far)
+    out_far = lax.ppermute(out_part, "expert", forward)
     grad_mid, grad_attended, grad_up_out, grad_low_out = open_back(
-        order,
+        plain,
         cotangent,
         mid,
         ffn_gain,
@@ -1132,19 +1182,26 @@
         up_out_map,
         low_out,
         attended,
-        [ran[0], grad_far],
+        [ran[0][1], grad_far],
     )
     grad_query, grad_key, grad_value = attend_back(length, qkv, grad_attended, lse, cos, sin)
+    if groups > 2:
+        out_far, grad_query = tied(out_far, grad_query)
+        out_far = lax.ppermute(joined(ran[2][0], out_far), "expert", forward)
     packed, back_low = adapters_back(
         grad_query, grad_key, grad_value, low, normed_in, up_map, grad_low_out, grad_up_out, devices
     )
     packed = lax.all_to_all(packed, ("dp", "expert"), 0, 0, tiled=True)
-    m_a, m_b, m_o = sum_mixer(adapter_ids, packed)
 
     grad_hidden = input_back(
         order, grad_query, grad_key, grad_value, back_low, weight_in, low_map, hidden, attn_gain, grad_mid
     )
-    out = (mid + ran[0][edge:].astype(f32) + out_far.astype(f32)).astype(bf16)
+    if groups > 3:
+        out_far, grad_hidden, packed = tied(out_far, grad_hidden, packed)
+    for offset in range(3, groups):
+        out_far = lax.ppermute(joined(ran[offset][0], out_far), "expert", forward)
+    m_a, m_b, m_o = sum_mixer(adapter_ids, packed)
+    out = finish(mid, ran[0][0], out_far)
     return (
         out,
         grad_hidden,

time: 371 us -> 412 us (1.11)
  waiting for transfers between devices: 90.9 us -> 115 us
  Pallas kernels: 194 us -> 210 us
  other arithmetic: 14.2 us -> 5.36 us
  starting transfers between devices: 30.2 us -> 36.6 us
  local copies, waits for them, and re-layouts: 20.4 us -> 24.7 us
    pallas_call x0 -> x6, Pallas kernels: none -> 18.1 us  [the longest x4 14.1 us: joined(): pl.pallas_call(join_kernel, grid=(steps,), in_specs=[block, block], out_s...]
    ppermute x1 -> x6, waiting for transfers between devices: 17.5 us -> 34.7 us  [the longest x1 23 us: on_device(): out_far = lax.ppermute(joined(ran[offset][0], out_far), 'expert', forward)]
    ppermute x2, waiting for transfers between devices: 36.8 us -> 53.4 us  [on_device(): grad_far = lax.ppermute(grad_part, 'expert', forward)]
    convert_element_type x5 -> x0, other arithmetic: 9.73 us -> none  [the longest x4 6.71 us: joined(): return (left.astype(f32) + right.astype(f32)).astype(bf16)]
    all_to_all x1, waiting for transfers between devices: 8.15 us -> 0.01 us  [on_device(): lax.all_to_all(to_owners(packed, owners, local), 'dp', 0, 0, tiled=True)]
    ppermute x1 -> x6, starting transfers between devices: 1.58 us -> 7.72 us  [the longest x1 2.12 us: on_device(): out_far = lax.ppermute(joined(ran[offset][0], out_far), 'expert', forward)]
    ppermute x10 -> x5, waiting for transfers between devices: 10.5 us -> 5.25 us  [swap(): return lax.ppermute(value, 'dp', [(at, at ^ bit) for at in range(BLOCKS)])]
    ppermute x10 -> x5, starting transfers between devices: 11.5 us -> 8 us  [swap(): return lax.ppermute(value, 'dp', [(at, at ^ bit) for at in range(BLOCKS)])]
  transfers between devices with their start and end apart: 22 -> 21, of which waited for: 9 -> 8; matrix products, arithmetic and copies ran while one was open for 7% -> 5% of each run, Pallas kernels for 53% -> 48%
where the time goes in v3:
time: 412 us; the launch traced here: 406 us
  Pallas kernels  210 us (51%)
  waiting for transfers between devices  115 us (28%)
  starting transfers between devices  36.6 us (9%)
  local copies, waits for them, and re-layouts  24.7 us (6%)
  between operations  14.7 us (4%)
  other arithmetic  5.36 us (1%)
    pallas_call x4, Pallas kernels, run_experts(): pl.pallas_call(expert_kernel, grid_spec=pltpu.PrefetchScalarGridSpec(num_...  108 us
    ppermute x2, waiting for transfers between devices, on_device(): grad_far = lax.ppermute(grad_part, 'expert', forward)  53.4 us
    ppermute x1, waiting for transfers between devices, on_device(): out_far = lax.ppermute(joined(ran[offset][0], out_far), 'expert', forward)  23 us
    pallas_call x1, Pallas kernels, attend_back(): pl.pallas_call(attend_back_kernel, grid_spec=pltpu.PrefetchScalarGridSpec...  22.5 us
    all_to_all x1, waiting for transfers between devices, on_device(): packed = lax.all_to_all(packed, ('dp', 'expert'), 0, 0, tiled=True)  17.7 us
    pallas_call x1, Pallas kernels, attend(): pl.pallas_call(attend_kernel, grid_spec=pltpu.PrefetchScalarGridSpec(num_...  14.5 us
    pallas_call x4, Pallas kernels, joined(): pl.pallas_call(join_kernel, grid=(steps,), in_specs=[block, block], out_s...  14.1 us
    unnamed x51, local copies, waits for them, and re-layouts  13.4 us
  transfers between devices with their start and end apart: 21, of which 8 were waited for; matrix products, arithmetic and copies ran while one was open for 5% of the time, Pallas kernels for 48%

profile of v3, /device:TPU:0, one launch (start us, length us, event | category | flops | bytes accessed | tf_op | source)
XLA Modules:
  0.0 406.1 jit_solution(17880929848033233978)
XLA Ops:
  7.2 3.0 collective-permute-start
  10.2 1.5 collective-permute-start.1
  15.9 1.3 gather_fusion
  17.2 3.4 all-to-all-start
  20.7 1.6 collective-permute-start.4
  24.0 1.9 collective-permute-start.3
  25.9 1.5 collective-permute-start.2
  27.5 1.1 constant_dynamic-update-slice_fusion.4
  28.6 4.1 %collective-permute-done.3 = bf16[64,2048]{1,0:T(8,128)(2,1)} collective-permute-done((bf16[64,2048]{1,0:T(8,128)(2,1)S(1)}, bf16[64,2048]{1,0:T(8,128)(2,1)}, u32[]{:S(2)}, u32[]{:S(2)}) %collective-permute-start.3) | collective-permute-done | bytes 262176 | tf_op jit(solution)/shard_map/ppermute | solution.py:978
  32.7 1.2 collective-permute-done.2
  36.6 11.6 %collective-permute-done.4.cot = bf16[512,1024]{1,0:T(8,128)(2,1)} collective-permute-done((bf16[512,1024]{1,0:T(8,128)(2,1)}, bf16[512,1024]{1,0:T(8,128)(2,1)}, u32[]{:S(2)}, u32[]{:S(2)}) %collective-permute-start.4) | collective-permute-done | bytes 1048608 | tf_op jit(solution)/shard_map/ppermute | solution.py:1063
  51.2 1.4 add_select_fusion.routes
  55.4 1.7 collective-permute-start.7
  57.2 12.3 %project.1 = (bf16[512,2048]{1,0:T(8,128)(2,1)}, bf16[512,64]{1,0:T(8,128)(2,1)}, bf16[512,1024]{1,0:T(8,128)(2,1)}) custom-call(s32[8]{0:T(128)} %broadcast_xor_fusion.order, bf16[512,1024]{1,0:T(8,128)(2,1)} %hid.5, bf16[1,1024]{1,0:T(2,128)(2,1)} %reshape.88.gain, bf16[512,2048]{1,0:T(8,128)(2,1)} %copy-done.2, ...), custom_call_target="tpu_custom_call" | custom-call | flops 2147483648 | bytes 8388608 | tf_op jit(solution)/shard_map/project/pallas_call | solution.py:141
  69.7 14.5 %attend.1 = (bf16[512,1024]{1,0:T(8,128)(2,1)}, f32[8,512,2]{2,1,0:T(8,128)}) custom-call(s32[1]{0:T(128)} %dynamic_slice.13.scalars, bf16[512,2048]{1,0:T(8,128)(2,1)} %get-tuple-element.72.query.key.value, bf16[512,2048]{1,0:T(8,128)(2,1)} %get-tuple-element.72.query.key.value, bf16[512,2048]{1,0:T(8,128)(2,1)} %get-tuple-element.72.query.key.value), custom_call_target="tpu_custom_call" | custom-call | flops 2147483648 | bytes 4194304 | tf_op jit(solution)/shard_map/attend/pallas_call | solution.py:221
  84.8 5.9 %close_mixer.1 = (f32[512,1024]{1,0:T(8,128)}, bf16[512,1024]{1,0:T(8,128)(2,1)}, bf16[512,64]{1,0:T(8,128)(2,1)}) custom-call(s32[8]{0:T(128)} %iota.22.order, bf16[512,1024]{1,0:T(8,128)(2,1)} %get-tuple-element.73.att.refs_11_, bf16[512,1024]{1,0:T(8,128)(2,1)} %hid.5, bf16[1,1024]{1,0:T(2,128)(2,1)} %reshape.95.gain.refs_3_, ...), custom_call_target="tpu_custom_call" | custom-call | flops 1073741824 | bytes 8388608 | tf_op jit(solution)/shard_map/close_mixer/pallas_call | solution.py:351
  91.3 27.7 %experts.4 = (bf16[512,1024]{1,0:T(8,128)(2,1)}, bf16[528,1024]{1,0:T(8,128)(2,1)}, f32[16,512]{1,0:T(8,128)}, bf16[8,4,288,128]{3,2,1,0:T(8,128)(2,1)}) custom-call(s32[4]{0:T(128)} %get-tuple-element.134.scalars, bf16[512,1024]{1,0:T(8,128)(2,1)} %get-tuple-element.79.x, bf16[512,1024]{1,0:T(8,128)(2,1)} %refs_1_, ...), custom_call_target="tpu_custom_call", output_to_operand_aliasing={{3}: (11, {})} | custom-call | flops 19327352832 | bytes 20971520 | tf_op jit(solution)/shard_map/experts/pallas_call | solution.py:547
  119.0 4.0 collective-permute-start.6
  123.0 3.8 collective-permute-done.8.x
  126.9 1.0 copy-done.17
  127.9 26.8 %experts.5 = (bf16[512,1024]{1,0:T(8,128)(2,1)}, bf16[528,1024]{1,0:T(8,128)(2,1)}, f32[16,512]{1,0:T(8,128)}, bf16[8,4,288,128]{3,2,1,0:T(8,128)(2,1)}) custom-call(s32[4]{0:T(128)} %get-tuple-element.132.scalars, bf16[512,1024]{1,0:T(8,128)(2,1)} %copy-done.17, bf16[512,1024]{1,0:T(8,128)(2,1)} %collective-permute-done.4.cot, ...), custom_call_target="tpu_custom_call", output_to_operand_aliasing={{3}: (11, {})} | custom-call | flops 19327352832 | bytes 20971520 | tf_op jit(solution)/shard_map/experts/pallas_call | solution.py:547
  154.7 1.7 collective-permute-start.9
  157.4 26.8 %experts.6 = (bf16[512,1024]{1,0:T(8,128)(2,1)}, bf16[528,1024]{1,0:T(8,128)(2,1)}, f32[16,512]{1,0:T(8,128)}, bf16[8,4,288,128]{3,2,1,0:T(8,128)(2,1)}) custom-call(s32[4]{0:T(128)} %get-tuple-element.133.scalars, bf16[512,1024]{1,0:T(8,128)(2,1)} %copy-done.20, bf16[512,1024]{1,0:T(8,128)(2,1)} %collective-permute-done.7.cot, ...), custom_call_target="tpu_custom_call", output_to_operand_aliasing={{3}: (11, {})} | custom-call | flops 19327352832 | bytes 20971520 | tf_op jit(solution)/shard_map/experts/pallas_call | solution.py:547
  184.2 1.6 collective-permute-start.11
  187.2 26.8 %experts.7 = (bf16[512,1024]{1,0:T(8,128)(2,1)}, bf16[528,1024]{1,0:T(8,128)(2,1)}, f32[16,512]{1,0:T(8,128)}, bf16[8,4,288,128]{3,2,1,0:T(8,128)(2,1)}) custom-call(s32[4]{0:T(128)} %get-tuple-element.131.scalars, bf16[512,1024]{1,0:T(8,128)(2,1)} %copy-done.18, bf16[512,1024]{1,0:T(8,128)(2,1)} %copy-done.16, ...), custom_call_target="tpu_custom_call", output_to_operand_aliasing={{3}: (11, {})} | custom-call | flops 19327352832 | bytes 20971520 | tf_op jit(solution)/shard_map/experts/pallas_call | solution.py:547
  214.0 3.9 all-to-all-start.1
  218.0 1.0 copy-done.4
  219.0 3.4 joined.4
  222.4 1.4 collective-permute-start.12
  224.5 26.2 %collective-permute-done.12.right = bf16[528,1024]{1,0:T(8,128)(2,1)S(1)} collective-permute-done((bf16[528,1024]{1,0:T(8,128)(2,1)}, bf16[528,1024]{1,0:T(8,128)(2,1)S(1)}, u32[]{:S(2)}, u32[]{:S(2)}) %collective-permute-start.12) | collective-permute-done | bytes 1081376 | tf_op jit(solution)/shard_map/ppermute | solution.py:1170
  251.6 3.4 joined.5
  255.1 1.4 copy-done.1
  256.5 3.6 sum_experts.1
  260.1 27.2 %collective-permute-done.13.refs_13_.refs_16_.refs_17_ = bf16[528,1024]{1,0:T(8,128)(2,1)S(1)} collective-permute-done((bf16[528,1024]{1,0:T(8,128)(2,1)S(1)}, bf16[528,1024]{1,0:T(8,128)(2,1)S(1)}, u32[]{:S(2)}, u32[]{:S(2)}) %collective-permute-start.13) | collective-permute-done | bytes 1081376 | tf_op jit(solution)/shard_map/ppermute | solution.py:1170
  288.3 9.5 %open_back.1 = (f32[512,1024]{1,0:T(8,128)}, bf16[512,1024]{1,0:T(8,128)(2,1)}, f32[64,1024]{1,0:T(8,128)}, f32[64,1024]{1,0:T(8,128)}) custom-call(s32[8]{0:T(128)} %iota.25.refs_0_, bf16[512,1024]{1,0:T(8,128)(2,1)} %refs_1_, f32[512,1024]{1,0:T(8,128)} %get-tuple-element.75.refs_2_.mid, bf16[1,1024]{1,0:T(2,128)(2,1)} %reshape.95.gain.refs_3_, ...), custom_call_target="tpu_custom_call" | custom-call | flops 1073741824 | bytes 14680064 | tf_op jit(solution)/shard_map/open_back/pallas_call | solution.py:715
  297.8 22.5 %attend_back.1 = (bf16[512,1024]{1,0:T(8,128)(2,1)}, bf16[512,512]{1,0:T(8,128)(2,1)}, bf16[512,512]{1,0:T(8,128)(2,1)}) custom-call(s32[1]{0:T(128)} %dynamic_slice.13.scalars, bf16[512,2048]{1,0:T(8,128)(2,1)} %get-tuple-element.72.query.key.value, bf16[512,2048]{1,0:T(8,128)(2,1)} %get-tuple-element.72.query.key.value, ...), custom_call_target="tpu_custom_call" | custom-call | flops 5368709120 | bytes 8388608 | tf_op jit(solution)/shard_map/attend_back/pallas_call | solution.py:298
  321.3 3.6 joined.6
  325.2 4.6 %adapters_back.1 = (bf16[512,64]{1,0:T(8,128)(2,1)}, f32[32,16,256]{2,1,0:T(8,128)}) custom-call(bf16[512,1024]{1,0:T(8,128)(2,1)} %get-tuple-element.109.grad_query, bf16[512,512]{1,0:T(8,128)(2,1)} %get-tuple-element.110.grad_key, bf16[512,512]{1,0:T(8,128)(2,1)} %get-tuple-element.111.grad_value, bf16[512,64]{1,0:T(8,128)(2,1)} %get-tuple-element.112.low, ...), custom_call_target="tpu_custom_call" | custom-call | flops 1610612736 | bytes 4194304 | tf_op jit(solution)/shard_map/adapters_back/pallas_call | solution.py:815
  329.8 5.8 %all-to-all-start.2 = ((f32[32,16,256]{2,1,0:T(8,128)}), f32[32,16,256]{2,1,0:T(8,128)S(1)}, u32[]{:S(2)}, u32[]{:S(2)}) async-start(f32[32,16,256]{2,1,0:T(8,128)} %get-tuple-element.118), calls=%async_computation.2 | async-start | bytes 1048576 | tf_op jit(solution)/shard_map/all_to_all | solution.py:1194
  335.7 8.5 %input_back.1 = bf16[512,1024]{1,0:T(8,128)(2,1)} custom-call(s32[8]{0:T(128)} %broadcast_xor_fusion.order, bf16[512,1024]{1,0:T(8,128)(2,1)} %get-tuple-element.109.grad_query, bf16[512,512]{1,0:T(8,128)(2,1)} %get-tuple-element.110.grad_key, bf16[512,512]{1,0:T(8,128)(2,1)} %get-tuple-element.111.grad_value, bf16[512,64]{1,0:T(8,128)(2,1)} %get-tuple-element.116.low, ...), custom_call_target="tpu_custom_call" | custom-call | flops 2147483648 | bytes 12582912 | tf_op jit(solution)/shard_map/input_back/pallas_call | solution.py:860
  344.2 17.7 %all-to-all-done.2.pieces = f32[32,16,256]{2,1,0:T(8,128)S(1)} async-done(((f32[32,16,256]{2,1,0:T(8,128)}), f32[32,16,256]{2,1,0:T(8,128)S(1)}, u32[]{:S(2)}, u32[]{:S(2)}) %all-to-all-start.2) | async-done | bytes 524320 | tf_op jit(solution)/shard_map/all_to_all | solution.py:1194
  361.9 1.0 copy-done.7
  362.9 3.6 joined.7
  366.6 2.1 collective-permute-start.16
  368.7 2.1 sum_mixer.1
  370.8 23.0 %collective-permute-done.16.far = bf16[512,1024]{1,0:T(8,128)(2,1)S(1)} collective-permute-done((bf16[512,1024]{1,0:T(8,128)(2,1)}, bf16[512,1024]{1,0:T(8,128)(2,1)S(1)}, u32[]{:S(2)}, u32[]{:S(2)}) %collective-permute-start.16) | collective-permute-done | bytes 1048608 | tf_op jit(solution)/shard_map/ppermute | solution.py:1202
  393.9 1.0 copy-done.9
  394.9 4.0 finish.1
  (105 shorter events, 22.2 us)
Async XLA Ops:
  7.2 20.3 %copy-start.14 = (s32[4,1]{1,0:T(4,128)S(1)}, s32[4,1]{1,0:T(4,128)}, u32[]{:S(2)}) copy-start(s32[4,1]{1,0:T(4,128)} %constant.94) | copy-start | bytes 52
  7.2 16.8 %collective-permute-start = (bf16[128,2048]{1,0:T(8,128)(2,1)}, bf16[128,2048]{1,0:T(8,128)(2,1)S(1)}, u32[]{:S(2)}, u32[]{:S(2)}) collective-permute-start(bf16[128,2048]{1,0:T(8,128)(2,1)} %param.30), channel_id=1, source_target_pairs={{0,8},{4,12},{8,0},{12,4},{16,24},{20,28},{24,16},{28,20},{1,9},{5... | collective-permute-start | bytes 1572872 | tf_op jit(solution)/shard_map/ppermute | solution.py:978
  10.2 15.7 %collective-permute-start.1 = (bf16[128,2048]{1,0:T(8,128)(2,1)}, bf16[128,2048]{1,0:T(8,128)(2,1)S(1)}, u32[]{:S(2)}, u32[]{:S(2)}) collective-permute-start(bf16[128,2048]{1,0:T(8,128)(2,1)} %param.30), channel_id=1, source_target_pairs={{0,16},{4,20},{8,24},{12,28},{16,0},{20,4},{24,8},{28,12},{1,17},{... | collective-permute-start | bytes 1572872 | tf_op jit(solution)/shard_map/ppermute | solution.py:978
  14.0 20.5 %copy-start.11 = (bf16[1024,16]{0,1:T(8,128)(2,1)S(1)}, bf16[1024,16]{0,1:T(8,128)(2,1)}, u32[]{:S(2)}) copy-start(bf16[1024,16]{0,1:T(8,128)(2,1)} %param.32) | copy-start | bytes 98308
  17.2 36.0 %all-to-all-start = ((bf16[8,112,128]{2,1,0:T(8,128)(2,1)}), bf16[8,112,128]{2,1,0:T(8,128)(2,1)S(1)}, u32[]{:S(2)}, u32[]{:S(2)}) async-start(bf16[8,112,128]{2,1,0:T(8,128)(2,1)} %gather_fusion), calls=%async_computation | async-start | bytes 458752 | tf_op jit(solution)/shard_map/all_to_all | solution.py:1060
  20.6 63.7 %all-gather.2.cloned.1.call-start = ((), (), s32[]{:S(2)}) async-start(), calls=%async_computation.3 | async-start | bytes 2359296 | tf_op jit(solution)/shard_map/all_gather | solution.py:1077
  20.7 27.6 %collective-permute-start.4 = (bf16[512,1024]{1,0:T(8,128)(2,1)}, bf16[512,1024]{1,0:T(8,128)(2,1)}, u32[]{:S(2)}, u32[]{:S(2)}) collective-permute-start(bf16[512,1024]{1,0:T(8,128)(2,1)} %refs_1_), channel_id=1, source_target_pairs={{0,1},{1,2},{2,3},{3,0},{4,5},{5,6},{6,7},{7,4},{8,9},{9,10},{10,1... | collective-permute-start | bytes 3145736 | tf_op jit(solution)/shard_map/ppermute | solution.py:1063
  24.0 8.7 %collective-permute-start.3 = (bf16[64,2048]{1,0:T(8,128)(2,1)S(1)}, bf16[64,2048]{1,0:T(8,128)(2,1)}, u32[]{:S(2)}, u32[]{:S(2)}) collective-permute-start(bf16[64,2048]{1,0:T(8,128)(2,1)S(1)} %slice.41), channel_id=1, source_target_pairs={{0,16},{4,20},{8,24},{12,28},{16,0},{20,4},{24,8},{28,12},{1,17},{... | collective-permute-start | bytes 786440 | tf_op jit(solution)/shard_map/ppermute | solution.py:978
  25.9 7.9 %collective-permute-start.2 = (bf16[64,2048]{1,0:T(8,128)(2,1)S(1)}, bf16[64,2048]{1,0:T(8,128)(2,1)}, u32[]{:S(2)}, u32[]{:S(2)}) collective-permute-start(bf16[64,2048]{1,0:T(8,128)(2,1)S(1)} %slice.40), channel_id=1, source_target_pairs={{0,8},{4,12},{8,0},{12,4},{16,24},{20,28},{24,16},{28,20},{1,9},{5... | collective-permute-start | bytes 786440 | tf_op jit(solution)/shard_map/ppermute | solution.py:978
  34.5 16.0 %copy-start.10 = (bf16[16,1024]{1,0:T(8,128)(2,1)}, bf16[16,1024]{1,0:T(8,128)(2,1)S(1)}, u32[]{:S(2)}) copy-start(bf16[16,1024]{1,0:T(8,128)(2,1)S(1)} %fusion.1.refs_5_) | copy-start | bytes 98308
  34.6 13.7 %copy-start.12 = (bf16[1024]{0:T(1024)(128)(2,1)S(1)}, bf16[1024]{0:T(1024)(128)(2,1)}, u32[]{:S(2)}) copy-start(bf16[1024]{0:T(1024)(128)(2,1)} %param.28) | copy-start | bytes 6148
  34.6 14.3 %copy-start.13 = (bf16[1024]{0:T(1024)(128)(2,1)S(1)}, bf16[1024]{0:T(1024)(128)(2,1)}, u32[]{:S(2)}) copy-start(bf16[1024]{0:T(1024)(128)(2,1)} %param.29) | copy-start | bytes 6148
  35.6 14.2 %copy-start.21 = (s32[32]{0:T(128)S(1)}, s32[32]{0:T(128)}, u32[]{:S(2)}) copy-start(s32[32]{0:T(128)} %param.25) | copy-start | bytes 388
  36.6 16.0 %copy-start.2 = (bf16[512,2048]{1,0:T(8,128)(2,1)}, bf16[512,2048]{1,0:T(8,128)(2,1)S(1)}, u32[]{:S(2)}) copy-start(bf16[512,2048]{1,0:T(8,128)(2,1)S(1)} %constant_dynamic-update-slice_fusion.weight_a) | copy-start | bytes 6291460
  48.3 8.9 %collective-permute-start.5 = (bf16[512,2048]{1,0:T(8,128)(2,1)S(1)}, bf16[512,2048]{1,0:T(8,128)(2,1)}, u32[]{:S(2)}, u32[]{:S(2)}) collective-permute-start(bf16[512,2048]{1,0:T(8,128)(2,1)S(1)} %constant_dynamic-update-slice_fusion.weight_a), channel_id=1, source_target_pairs={{0,4},{4,0},{8,12},{12,8},{16,20},{20,16},{24,28},{28,24},{1,5},{5... | collective-permute-start | bytes 6291464 | tf_op jit(solution)/shard_map/ppermute | solution.py:978
  48.3 4.4 %copy-start.22 = (s32[8]{0:T(128)S(1)}, s32[8]{0:T(128)}, u32[]{:S(2)}) copy-start(s32[8]{0:T(128)} %constant.84.clone) | copy-start | bytes 100
  55.4 101.0 %collective-permute-start.7 = (bf16[512,1024]{1,0:T(8,128)(2,1)}, bf16[512,1024]{1,0:T(8,128)(2,1)}, u32[]{:S(2)}, u32[]{:S(2)}) collective-permute-start(bf16[512,1024]{1,0:T(8,128)(2,1)} %refs_1_), channel_id=1, source_target_pairs={{0,3},{1,0},{2,1},{3,2},{4,7},{5,4},{6,5},{7,6},{8,11},{9,8},{10,9... | collective-permute-start | bytes 3145736 | tf_op jit(solution)/shard_map/ppermute | solution.py:1076
  69.4 116.4 %collective-permute-start.10 = (bf16[512,1024]{1,0:T(8,128)(2,1)}, bf16[512,1024]{1,0:T(8,128)(2,1)S(1)}, u32[]{:S(2)}, u32[]{:S(2)}) collective-permute-start(bf16[512,1024]{1,0:T(8,128)(2,1)} %collective-permute-done.4.cot), channel_id=1, source_target_pairs={{0,1},{1,2},{2,3},{3,0},{4,5},{5,6},{6,7},{7,4},{8,9},{9,10},{10,1... | collective-permute-start | bytes 3145736 | tf_op jit(solution)/shard_map/ppermute | solution.py:1101
  90.7 36.2 %collective-permute-start.8 = (bf16[512,1024]{1,0:T(8,128)(2,1)}, bf16[512,1024]{1,0:T(8,128)(2,1)S(1)}, u32[]{:S(2)}, u32[]{:S(2)}) collective-permute-start(bf16[512,1024]{1,0:T(8,128)(2,1)} %get-tuple-element.79.x), channel_id=1, source_target_pairs={{0,1},{1,2},{2,3},{3,0},{4,5},{5,6},{6,7},{7,4},{8,9},{9,10},{10,1... | collective-permute-start | bytes 3145736 | tf_op jit(solution)/shard_map/ppermute | solution.py:1131
  91.3 27.8 %copy-start.19 = (bf16[512,1024]{1,0:T(8,128)(2,1)S(1)}, bf16[512,1024]{1,0:T(8,128)(2,1)}, u32[]{:S(2)}) copy-start(bf16[512,1024]{1,0:T(8,128)(2,1)} %get-tuple-element.79.x) | copy-start | bytes 3145732
  119.0 37.4 %collective-permute-start.6 = (bf16[512,1024]{1,0:T(8,128)(2,1)S(1)}, bf16[512,1024]{1,0:T(8,128)(2,1)S(1)}, u32[]{:S(2)}, u32[]{:S(2)}) collective-permute-start(bf16[512,1024]{1,0:T(8,128)(2,1)S(1)} %copy-done.19), channel_id=1, source_target_pairs={{0,3},{1,0},{2,1},{3,2},{4,7},{5,4},{6,5},{7,6},{8,11},{9,8},{10,9... | collective-permute-start | bytes 3145736 | tf_op jit(solution)/shard_map/ppermute | solution.py:1154
  126.9 1.1 copy-start.17
  154.7 31.1 %collective-permute-start.9 = (bf16[512,1024]{1,0:T(8,128)(2,1)}, bf16[512,1024]{1,0:T(8,128)(2,1)S(1)}, u32[]{:S(2)}, u32[]{:S(2)}) collective-permute-start(bf16[512,1024]{1,0:T(8,128)(2,1)} %copy-done.17), channel_id=1, source_target_pairs={{0,1},{1,2},{2,3},{3,0},{4,5},{5,6},{6,7},{7,4},{8,9},{9,10},{10,1... | collective-permute-start | bytes 3145736 | tf_op jit(solution)/shard_map/ppermute | solution.py:1157
  156.4 1.0 copy-start.20
  184.2 33.8 %collective-permute-start.11 = (bf16[528,1024]{1,0:T(8,128)(2,1)}, bf16[528,1024]{1,0:T(8,128)(2,1)S(1)}, u32[]{:S(2)}, u32[]{:S(2)}) collective-permute-start(bf16[528,1024]{1,0:T(8,128)(2,1)} %get-tuple-element.96), channel_id=1, source_target_pairs={{0,1},{1,2},{2,3},{3,0},{4,5},{5,6},{6,7},{7,4},{8,9},{9,10},{10,1... | collective-permute-start | bytes 3244040 | tf_op jit(solution)/shard_map/ppermute | solution.py:1165
  185.8 1.0 copy-start.16
  185.8 1.4 copy-start.18
  214.0 41.0 %all-to-all-start.1 = ((bf16[8,4,288,128]{3,2,1,0:T(8,128)(2,1)}), bf16[8,4,288,128]{3,2,1,0:T(8,128)(2,1)S(1)}, u32[]{:S(2)}, u32[]{:S(2)}) async-start(bf16[8,4,288,128]{3,2,1,0:T(8,128)(2,1)} %get-tuple-element.97), calls=%async_computation.1 | async-start | bytes 4718592 | tf_op jit(solution)/shard_map/all_to_all | solution.py:1161
  217.9 1.0 copy-start.4
  222.4 28.3 %collective-permute-start.12 = (bf16[528,1024]{1,0:T(8,128)(2,1)}, bf16[528,1024]{1,0:T(8,128)(2,1)S(1)}, u32[]{:S(2)}, u32[]{:S(2)}) collective-permute-start(bf16[528,1024]{1,0:T(8,128)(2,1)} %joined.4), channel_id=1, source_target_pairs={{0,1},{1,2},{2,3},{3,0},{4,5},{5,6},{6,7},{7,4},{8,9},{9,10},{10,1... | collective-permute-start | bytes 3244040 | tf_op jit(solution)/shard_map/ppermute | solution.py:1170
  250.6 1.0 copy-start.6
  255.1 5.0 %copy-start.5 = (bf16[528,1024]{1,0:T(8,128)(2,1)S(1)}, bf16[528,1024]{1,0:T(8,128)(2,1)}, u32[]{:S(2)}) copy-start(bf16[528,1024]{1,0:T(8,128)(2,1)} %joined.5) | copy-start | bytes 3244036
  255.1 1.4 copy-start.1
  255.1 32.2 %copy-start.15 = (bf16[512,1024]{1,0:T(8,128)(2,1)S(1)}, bf16[512,1024]{1,0:T(8,128)(2,1)}, u32[]{:S(2)}) copy-start(bf16[512,1024]{1,0:T(8,128)(2,1)} %get-tuple-element.100) | copy-start | bytes 3145732
  260.1 27.2 %collective-permute-start.13 = (bf16[528,1024]{1,0:T(8,128)(2,1)S(1)}, bf16[528,1024]{1,0:T(8,128)(2,1)S(1)}, u32[]{:S(2)}, u32[]{:S(2)}) collective-permute-start(bf16[528,1024]{1,0:T(8,128)(2,1)S(1)} %copy-done.5), channel_id=1, source_target_pairs={{0,1},{1,2},{2,3},{3,0},{4,5},{5,6},{6,7},{7,4},{8,9},{9,10},{10,1... | collective-permute-start | bytes 3244040 | tf_op jit(solution)/shard_map/ppermute | solution.py:1170
  287.3 1.0 copy-start
  287.3 33.0 %collective-permute-start.14 = (bf16[512,1024]{1,0:T(8,128)(2,1)S(1)}, bf16[512,1024]{1,0:T(8,128)(2,1)S(1)}, u32[]{:S(2)}, u32[]{:S(2)}) collective-permute-start(bf16[512,1024]{1,0:T(8,128)(2,1)S(1)} %copy-done.15), channel_id=1, source_target_pairs={{0,1},{1,2},{2,3},{3,0},{4,5},{5,6},{6,7},{7,4},{8,9},{9,10},{10,1... | collective-permute-start | bytes 3145736 | tf_op jit(solution)/shard_map/ppermute | solution.py:1172
  320.3 1.0 copy-start.8
  324.9 37.0 %collective-permute-start.15 = (bf16[512,1024]{1,0:T(8,128)(2,1)}, bf16[512,1024]{1,0:T(8,128)(2,1)S(1)}, u32[]{:S(2)}, u32[]{:S(2)}) collective-permute-start(bf16[512,1024]{1,0:T(8,128)(2,1)} %joined.6), channel_id=1, source_target_pairs={{0,1},{1,2},{2,3},{3,0},{4,5},{5,6},{6,7},{7,4},{8,9},{9,10},{10,1... | collective-permute-start | bytes 3145736 | tf_op jit(solution)/shard_map/ppermute | solution.py:1190
  329.8 32.1 %all-to-all-start.2 = ((f32[32,16,256]{2,1,0:T(8,128)}), f32[32,16,256]{2,1,0:T(8,128)S(1)}, u32[]{:S(2)}, u32[]{:S(2)}) async-start(f32[32,16,256]{2,1,0:T(8,128)} %get-tuple-element.118), calls=%async_computation.2 | async-start | bytes 1048576 | tf_op jit(solution)/shard_map/all_to_all | solution.py:1194
  361.9 6.8 %copy-start.3 = (f32[32,16,256]{2,1,0:T(8,128)}, f32[32,16,256]{2,1,0:T(8,128)S(1)}, u32[]{:S(2)}) copy-start(f32[32,16,256]{2,1,0:T(8,128)S(1)} %all-to-all-done.2.pieces) | copy-start | bytes 1572868
  361.9 1.0 copy-start.7
  366.6 27.3 %collective-permute-start.16 = (bf16[512,1024]{1,0:T(8,128)(2,1)}, bf16[512,1024]{1,0:T(8,128)(2,1)S(1)}, u32[]{:S(2)}, u32[]{:S(2)}) collective-permute-start(bf16[512,1024]{1,0:T(8,128)(2,1)} %joined.7), channel_id=1, source_target_pairs={{0,1},{1,2},{2,3},{3,0},{4,5},{5,6},{6,7},{7,4},{8,9},{9,10},{10,1... | collective-permute-start | bytes 3145736 | tf_op jit(solution)/shard_map/ppermute | solution.py:1202
  393.9 1.0 copy-start.9
Sparse Core Ops, SparseCore 0:
  34.0 27.0 all-gather.1

commit v4 on v2

--- a/solution.py
+++ b/solution.py
@@ -92,6 +92,14 @@
     return pl.ds(pl.multiple_of(order[at] * BLOCK, BLOCK), BLOCK)
 
 
+def halves(weights, width, index):
+    there = 1 if weights[0] is weights[1] else 0
+    return [
+        pl.BlockSpec((HALF, width), lambda n, s: (0, index(n))),
+        pl.BlockSpec((HALF, width), lambda n, s: (there, index(n))),
+    ]
+
+
 def project_kernel(
     order, hid, gain, weight_a, weight_b, low_map, up_map, cos, sin, qkv, low, normed, turned_rows
 ):
@@ -127,7 +135,7 @@
 
 def project(order, hidden, gain, weights, low_map, up_map, cos, sin):
     rows = hidden.shape[0]
-    block = 256
+    block = 512
     ranks = low_map.shape[0]
     full = lambda shape: pl.BlockSpec(shape, lambda n, s: (0, 0))
     return pl.pallas_call(
@@ -138,8 +146,7 @@
             in_specs=[
                 full((rows, MODEL_WIDTH)),
                 full((1, MODEL_WIDTH)),
-                pl.BlockSpec((HALF, block), lambda n, s: (0, n)),
-                pl.BlockSpec((HALF, block), lambda n, s: (0, n)),
+                *halves(weights, block, lambda n: n),
                 full((ranks, MODEL_WIDTH)),
                 pl.BlockSpec((ranks, block), lambda n, s: (0, n)),
                 full((rows, 128)),
@@ -168,34 +175,46 @@
 ROWB = 128
 
 
-def masked_scores(length, queries, keys, start, count):
-    scores = 0.125 * nt(queries, keys)
-    row = lax.broadcasted_iota(jnp.int32, scores.shape, 0)
-    col = lanes_of(scores.shape)
-    allowed = (col <= start + row % ROWB) & (col < length)
-    return scores, allowed
+def length_column(length, count):
+    key = lax.broadcasted_iota(jnp.int32, (count, 1), 0)
+    return jnp.where(key < length, 0.0, -1e30)
+
+
+def causal_block():
+    key = lax.broadcasted_iota(jnp.int32, (ROWB, 2 * ROWB), 0)
+    return jnp.where(key <= lanes_of((ROWB, 2 * ROWB)) % ROWB, 0.0, -1e30)
+
+
+def masked_scores(queries, keys, start, bias, causal):
+    count = start + ROWB
+    scores = nt(keys[:count], (queries.astype(f32) * 0.125).astype(bf16))
+    near = scores[start:] + (bias[start:count] + causal)
+    if start == 0:
+        return near
+    return jnp.concatenate([scores[:start] + bias[:start], near], 0)
 
 
 def attend_kernel(scalars, query, key, value, result, lse):
     half = pl.program_id(0) % 2
-    length = scalars[0]
     keys = both_halves(key[...], half)
     values = both_halves(value[...], half)
     rows = query.shape[0]
+    bias = length_column(scalars[0], rows)
+    causal = causal_block()
     for start in range(0, rows, ROWB):
         count = start + ROWB
         stacked = stacked_heads(query[start:count, :])
-        scores, allowed = masked_scores(length, stacked, keys[:count], start, count)
-        scores = jnp.where(allowed, scores, -1e30)
-        top = jnp.max(scores, -1, keepdims=True)
+        scores = masked_scores(stacked, keys, start, bias, causal)
+        top = jnp.max(scores, 0, keepdims=True)
         shifted = jnp.exp(scores - top)
-        total = jnp.sum(shifted, -1, keepdims=True)
+        total = jnp.sum(shifted, 0, keepdims=True)
         prob = (shifted * (1.0 / total)).astype(bf16)
-        mixed = nn(prob, values[:count])
+        mixed = tn(prob, values[:count])
         lane = lanes_of((ROWB, 128))
         result[start:count, :] = jnp.where(lane < HS, mixed[:ROWB], mixed[ROWB:]).astype(bf16)
         logs = top + jnp.log(total)
-        lse[0, start:count, :] = jnp.concatenate([logs[:ROWB], logs[ROWB:]], 1)
+        lse[0, 0:1, start:count] = logs[:, :ROWB]
+        lse[0, 1:2, start:count] = logs[:, ROWB:]
 
 
 def attend(length, qkv):
@@ -213,12 +232,12 @@
             ],
             out_specs=[
                 pl.BlockSpec((rows, 128), lambda g, s: (0, g)),
-                pl.BlockSpec((1, rows, 2), lambda g, s: (g, 0, 0)),
+                pl.BlockSpec((1, 2, rows), lambda g, s: (g, 0, 0)),
             ],
         ),
         out_shape=[
             jax.ShapeDtypeStruct((rows, QD), bf16),
-            jax.ShapeDtypeStruct((pairs, rows, 2), f32),
+            jax.ShapeDtypeStruct((pairs, 2, rows), f32),
         ],
         compiler_params=params_of(1),
         name="attend",
@@ -232,30 +251,34 @@
     scalars, query, key, value, grad, lse, cos, sin, grad_query, grad_key, grad_value, key_acc, value_acc
 ):
     half = pl.program_id(0) % 2
-    length = scalars[0]
     keys = both_halves(key[...], half)
     values = both_halves(value[...], half)
     rows = query.shape[0]
-    key_acc[...] = jnp.zeros_like(key_acc)
-    value_acc[...] = jnp.zeros_like(value_acc)
-    for start in range(0, rows, ROWB):
+    bias = length_column(scalars[0], rows)
+    causal = causal_block()
+    for start in reversed(range(0, rows, ROWB)):
         count = start + ROWB
         stacked = stacked_heads(query[start:count, :])
         grads = stacked_heads(grad[start:count, :])
-        scores, allowed = masked_scores(length, stacked, keys[:count], start, count)
-        logs = lse[0, start:count, :]
-        logs = jnp.concatenate([logs[:, 0:1], logs[:, 1:2]], 0)
-        prob = jnp.where(allowed, jnp.exp(scores - logs), 0.0)
-        grad_prob = nt(grads, values[:count])
-        delta = jnp.sum(prob * grad_prob, -1, keepdims=True)
+        scores = masked_scores(stacked, keys, start, bias, causal)
+        logs = jnp.concatenate([lse[0, 0:1, start:count], lse[0, 1:2, start:count]], 1)
+        prob = jnp.exp(scores - logs)
+        grad_prob = nt(values[:count], grads)
+        delta = jnp.sum(prob * grad_prob, 0, keepdims=True)
         grad_score = (prob * (grad_prob - delta)).astype(bf16)
-        mixed = nn(grad_score, keys[:count])
+        mixed = tn(grad_score, keys[:count])
         lane = lanes_of((ROWB, 128))
         turned = 0.125 * jnp.where(lane < HS, mixed[:ROWB], mixed[ROWB:])
         turned = turned * cos[start:count, :] - rope_swap(turned) * sin[start:count, :]
         grad_query[start:count, :] = turned.astype(bf16)
-        key_acc[:count, :] += tn(grad_score, stacked)
-        value_acc[:count, :] += tn(prob.astype(bf16), grads)
+        key_part = nn(grad_score, stacked)
+        value_part = nn(prob.astype(bf16), grads)
+        if count == rows:
+            key_acc[...] = key_part
+            value_acc[...] = value_part
+        else:
+            key_acc[:count, :] += key_part
+            value_acc[:count, :] += value_part
     total = key_acc[...]
     total = 0.125 * (total + pltpu.roll(total, HS, 1))
     total = (total * cos[...] - rope_swap(total) * sin[...]).astype(bf16)
@@ -287,7 +310,7 @@
                 pl.BlockSpec((rows, 128), lambda g, s: (0, QD // 128 + g // 2)),
                 pl.BlockSpec((rows, 128), lambda g, s: (0, (QD + KD) // 128 + g // 2)),
                 pl.BlockSpec((rows, 128), lambda g, s: (0, g)),
-                pl.BlockSpec((1, rows, 2), lambda g, s: (g, 0, 0)),
+                pl.BlockSpec((1, 2, rows), lambda g, s: (g, 0, 0)),
                 pl.BlockSpec((rows, 128), lambda g, s: (0, 0)),
                 pl.BlockSpec((rows, 128), lambda g, s: (0, 0)),
             ],
@@ -339,8 +362,7 @@
                 part(QD),
                 part(MODEL_WIDTH),
                 full((1, MODEL_WIDTH)),
-                full((HALF, MODEL_WIDTH)),
-                full((HALF, MODEL_WIDTH)),
+                *halves(weights, MODEL_WIDTH, lambda n: QKV // MODEL_WIDTH),
                 full((ranks, QD)),
                 full((ranks, MODEL_WIDTH)),
             ],
@@ -659,8 +681,7 @@
                 full((1, MODEL_WIDTH)),
                 pl.BlockSpec((experts, block), lambda n, s: (0, n)),
                 full((experts, MODEL_WIDTH)),
-                full((HALF, MODEL_WIDTH)),
-                full((HALF, MODEL_WIDTH)),
+                *halves(weights, MODEL_WIDTH, lambda n: QKV // MODEL_WIDTH),
                 full((ranks, QD)),
                 full((ranks, MODEL_WIDTH)),
                 part(ranks),
@@ -733,17 +754,17 @@
         other = grad_out[:, tile]
         shift = (2 * small - offset) % BLOCK
         other = pltpu.roll(other, shift, 1) if shift else other
-        packed[owner, :, :BLOCK] = first
+        packed[owner, :, :BLOCK] = first.astype(bf16)
         packed[owner, :, BLOCK:] = jnp.where(
             lane < 2 * small, piece, jnp.where(lane < 3 * small, other, 0.0)
-        )
+        ).astype(bf16)
 
 
 def adapters_back(grad_query, grad_key, grad_value, low, normed, up_map, low_there, up_there, devices):
     rows = normed.shape[0]
     ranks = up_map.shape[0]
     if devices * BLOCK // 4 == MODEL_WIDTH:
-        results = [jax.ShapeDtypeStruct((devices, R, 2 * BLOCK), f32)]
+        results = [jax.ShapeDtypeStruct((devices, R, 2 * BLOCK), bf16)]
     else:
         results = [
             jax.ShapeDtypeStruct((R, QKV), f32),
@@ -771,7 +792,7 @@
         ],
         -1,
     )
-    return packed, back_low
+    return packed.astype(bf16), back_low
 
 
 def input_back_kernel(
@@ -804,8 +825,7 @@
                 part(KD),
                 part(KD),
                 part(ranks),
-                full((HALF, QKV)),
-                full((HALF, QKV)),
+                *halves(weights, QKV, lambda n: 0),
                 full((ranks, MODEL_WIDTH)),
                 part(MODEL_WIDTH),
                 full((1, MODEL_WIDTH)),
@@ -871,7 +891,7 @@
     acc[...] = jnp.zeros_like(acc)
 
     def step(index, carry):
-        acc[ids[index]] += pieces[index]
+        acc[ids[index]] += pieces[index].astype(f32)
         return carry
 
     lax.fori_loop(0, pieces.shape[0], step, 0)
@@ -1001,21 +1021,15 @@
     adapters = jnp.concatenate([low_turned, up_turned, attention_output_upmap], 1)[mine]
     adapters = lax.all_to_all(adapters, "dp", 0, 0, tiled=True)
     order = order_of(row)
-    short = owners == BLOCKS
-    if short:
-        pair_in = both_neighbours(query_key_value_weight)
-        pair_out = both_neighbours(w_out)
-        pair_in, pair_out = tied(pair_in, pair_out)
-        across_in = across(pair_in)
-        pair_out, across_in = tied(pair_out, across_in)
-        near_in = jnp.concatenate([query_key_value_weight, *pair_in, *across_in], 0)
-        weight_in = near_in, swap(near_in, 1)
-        across_out = across(pair_out)
+    both = jnp.concatenate([query_key_value_weight, w_out], 1)
+    if owners == BLOCKS:
+        pair = both_neighbours(both)
+        near = jnp.concatenate([both, *pair, *across(pair)], 0)
+        near, adapters = tied(near, adapters)
+        weights = near, swap(near, 1)
     else:
-        whole = lax.all_gather(query_key_value_weight, "dp", axis=0, tiled=True)
-        weight_in = whole[:HALF], whole[HALF:]
-        whole = lax.all_gather(w_out, "dp", axis=0, tiled=True)
-        weight_out = whole[:HALF], whole[HALF:]
+        whole = lax.all_gather(both, "dp", axis=0, tiled=True)
+        weights = whole, whole
 
     low_map = adapters[:, : 4 * R].transpose(1, 0, 2).reshape(4 * R, MODEL_WIDTH)
     up = (
@@ -1036,14 +1050,10 @@
 
     cots = lax.all_gather(cotangent, "expert", axis=0, tiled=True)
 
-    qkv, low, normed_in = project(order, hidden, attn_gain, weight_in, low_map, up_map, cos, sin)
-    if short:
-        across_out, low = tied(across_out, low)
-        near_out = jnp.concatenate([w_out, *pair_out, *across_out], 0)
-        weight_out = near_out, swap(near_out, 1)
+    qkv, low, normed_in = project(order, hidden, attn_gain, weights, low_map, up_map, cos, sin)
     attended, lse = attend(length, qkv)
     mid, normed_mid, low_out = close_mixer(
-        order, attended, hidden, ffn_gain, weight_out, low_map, up_out_map
+        order, attended, hidden, ffn_gain, weights, low_map, up_out_map
     )
 
     first = place * local
@@ -1114,10 +1124,9 @@
         if offset == groups - 1:
             grad_part, g_a_down = tied(grad_part, g_a_down)
         grad_far = lax.ppermute(grad_part, "expert", forward)
-    for offset in range(2, groups):
-        out_part = joined(ran[offset][edge:], out_far)
-        if offset == 2:
-            out_part, grad_far = tied(out_part, grad_far)
+    if groups > 2:
+        out_part = joined(ran[2][edge:], out_far)
+        out_part, grad_far = tied(out_part, grad_far)
         out_far = lax.ppermute(out_part, "expert", forward)
 
     grad_mid, grad_attended, grad_up_out, grad_low_out = open_back(
@@ -1127,7 +1136,7 @@
         ffn_gain,
         gates,
         router,
-        weight_out,
+        weights,
         low_map,
         up_out_map,
         low_out,
@@ -1135,6 +1144,9 @@
         [ran[0], grad_far],
     )
     grad_query, grad_key, grad_value = attend_back(length, qkv, grad_attended, lse, cos, sin)
+    out_far, grad_query = tied(out_far, grad_query)
+    for offset in range(3, groups):
+        out_far = lax.ppermute(joined(ran[offset][edge:], out_far), "expert", forward)
     packed, back_low = adapters_back(
         grad_query, grad_key, grad_value, low, normed_in, up_map, grad_low_out, grad_up_out, devices
     )
@@ -1142,7 +1154,7 @@
     m_a, m_b, m_o = sum_mixer(adapter_ids, packed)
 
     grad_hidden = input_back(
-        order, grad_query, grad_key, grad_value, back_low, weight_in, low_map, hidden, attn_gain, grad_mid
+        order, grad_query, grad_key, grad_value, back_low, weights, low_map, hidden, attn_gain, grad_mid
     )
     out = (mid + ran[0][edge:].astype(f32) + out_far.astype(f32)).astype(bf16)
     return (

time: 371 us -> 363 us (0.978)
  Pallas kernels: 194 us -> 185 us
    all_to_all x1, waiting for transfers between devices: 17.9 us -> 11.4 us  [on_device(): packed = lax.all_to_all(packed, ('dp', 'expert'), 0, 0, tiled=True)]
    pallas_call x1, Pallas kernels: 17.2 us -> 12.6 us  [attend(): pl.pallas_call(attend_kernel, grid_spec=pltpu.PrefetchScalarGridSpec(num_...]
    ppermute x10 -> x5, waiting for transfers between devices: 10.5 us -> 14.7 us  [swap(): return lax.ppermute(value, 'dp', [(at, at ^ bit) for at in range(BLOCKS)])]
    ppermute x10 -> x5, starting transfers between devices: 11.5 us -> 8.23 us  [swap(): return lax.ppermute(value, 'dp', [(at, at ^ bit) for at in range(BLOCKS)])]
    unnamed x49 -> x51, local copies, waits for them, and re-layouts: 10.2 us -> 10.4 us
  transfers between devices with their start and end apart: 22 -> 17, of which waited for: 9 -> 8; matrix products, arithmetic and copies ran while one was open for 7% -> 7% of each run, Pallas kernels for 53% -> 52%
where the time goes in v4:
time: 363 us; the launch traced here: 357 us
  Pallas kernels  185 us (51%)
  waiting for transfers between devices  88.5 us (24%)
  starting transfers between devices  27.9 us (8%)
  local copies, waits for them, and re-layouts  24 us (7%)
  other arithmetic  17 us (5%)
  between operations  14.9 us (4%)
    pallas_call x4, Pallas kernels, run_experts(): pl.pallas_call(expert_kernel, grid_spec=pltpu.PrefetchScalarGridSpec(num_...  108 us
    ppermute x2, waiting for transfers between devices, on_device(): grad_far = lax.ppermute(grad_part, 'expert', forward)  36.8 us
    pallas_call x1, Pallas kernels, attend_back(): pl.pallas_call(attend_back_kernel, grid_spec=pltpu.PrefetchScalarGridSpec...  19.6 us
    ppermute x1, waiting for transfers between devices, on_device(): lax.ppermute(first_sums if groups > 2 else ran[1], 'expert', forward)  17.5 us
    ppermute x5, waiting for transfers between devices, swap(): return lax.ppermute(value, 'dp', [(at, at ^ bit) for at in range(BLOCKS)])  14.7 us
    pallas_call x1, Pallas kernels, attend(): pl.pallas_call(attend_kernel, grid_spec=pltpu.PrefetchScalarGridSpec(num_...  12.6 us
    all_to_all x1, waiting for transfers between devices, on_device(): packed = lax.all_to_all(packed, ('dp', 'expert'), 0, 0, tiled=True)  11.4 us
    pallas_call x1, Pallas kernels, project(): pl.pallas_call(project_kernel, grid_spec=pltpu.PrefetchScalarGridSpec(num...  10.4 us
  transfers between devices with their start and end apart: 17, of which 8 were waited for; matrix products, arithmetic and copies ran while one was open for 7% of the time, Pallas kernels for 52%

profile of v4, /device:TPU:0, one launch (start us, length us, event | category | flops | bytes accessed | tf_op | source)
XLA Modules:
  0.0 356.8 jit_solution(118649448543260245)
XLA Ops:
  7.3 2.0 constant_dynamic-update-slice_fusion.1
  9.3 1.7 constant_dynamic-update-slice_fusion
  11.0 3.0 collective-permute-start.1
  14.0 1.5 collective-permute-start
  17.9 1.3 gather_fusion
  19.1 3.4 all-to-all-start
  22.6 9.9 %collective-permute-done.1 = bf16[128,3072]{1,0:T(8,128)(2,1)} collective-permute-done((bf16[128,3072]{1,0:T(8,128)(2,1)}, bf16[128,3072]{1,0:T(8,128)(2,1)}, u32[]{:S(2)}, u32[]{:S(2)}) %collective-permute-start.1) | collective-permute-done | bytes 786464 | tf_op jit(solution)/shard_map/ppermute | solution.py:936
  32.4 1.0 slice.68
  33.5 2.1 collective-permute-start.2
  35.6 1.0 slice.69
  36.6 1.6 collective-permute-start.3
  38.2 1.2 constant_dynamic-update-slice_fusion.5
  39.5 1.2 constant_dynamic-update-slice_fusion.4
  40.7 3.4 collective-permute-done.2
  44.1 1.4 collective-permute-done.3
  47.4 1.3 copy.70
  52.7 2.6 add_select_fusion.routes
  57.5 10.4 %project.1 = (bf16[512,2048]{1,0:T(8,128)(2,1)}, bf16[512,64]{1,0:T(8,128)(2,1)}, bf16[512,1024]{1,0:T(8,128)(2,1)}) custom-call(s32[8]{0:T(128)} %broadcast_xor_fusion.order.refs_0_, bf16[512,1024]{1,0:T(8,128)(2,1)} %hid.5, bf16[1,1024]{1,0:T(2,128)(2,1)} %reshape.88.gain, bf16[512,3072]{1,0:T(8,128)(2,1)} %copy-done, ...), custom_call_target="tpu_custom_call" | custom-call | flops 2147483648 | bytes 8388608 | tf_op jit(solution)/shard_map/project/pallas_call | solution.py:141
  68.0 12.6 %attend.1 = (bf16[512,1024]{1,0:T(8,128)(2,1)}, f32[8,2,512]{2,1,0:T(2,128)}) custom-call(s32[1]{0:T(128)} %dynamic_slice.13.scalars, bf16[512,2048]{1,0:T(8,128)(2,1)} %get-tuple-element.58.query.key.value, bf16[512,2048]{1,0:T(8,128)(2,1)} %get-tuple-element.58.query.key.value, bf16[512,2048]{1,0:T(8,128)(2,1)} %get-tuple-element.58.query.key.value), custom_call_target="tpu_custom_call" | custom-call | flops 2147483648 | bytes 4194304 | tf_op jit(solution)/shard_map/attend/pallas_call | solution.py:223
  80.6 6.0 %close_mixer.1 = (f32[512,1024]{1,0:T(8,128)}, bf16[512,1024]{1,0:T(8,128)(2,1)}, bf16[512,64]{1,0:T(8,128)(2,1)}) custom-call(s32[8]{0:T(128)} %broadcast_xor_fusion.order.refs_0_, bf16[512,1024]{1,0:T(8,128)(2,1)} %get-tuple-element.59.att.refs_11_, bf16[512,1024]{1,0:T(8,128)(2,1)} %hid.5, bf16[1,1024]{1,0:T(2,128)(2,1)} %reshape.95.gain.refs_3_, ...), custom_call_target="tpu_custom_call" | custom-call | flops 1073741824 | bytes 8388608 | tf_op jit(solution)/shard_map/close_mixer/pallas_call | solution.py:356
  86.6 2.1 collective-permute-start.6
  88.6 27.1 %experts.4 = (bf16[1040,1024]{1,0:T(8,128)(2,1)}, f32[16,512]{1,0:T(8,128)}, bf16[8,4,288,128]{3,2,1,0:T(8,128)(2,1)}) custom-call(s32[5]{0:T(128)} %get-tuple-element.112.scalars, bf16[512,1024]{1,0:T(8,128)(2,1)} %get-tuple-element.64.x, bf16[512,1024]{1,0:T(8,128)(2,1)} %refs_1_.1, s32[2048,8]{1,0:T(8,128)} %add_select_fusion.routes, ...), custom_call_target="tpu_custom_call" | custom-call | flops 19327352832 | bytes 20971520 | tf_op jit(solution)/shard_map/experts/pallas_call | solution.py:553
  115.8 2.5 collective-permute-start.5
  118.3 1.0 copy-done.17
  119.3 26.8 %experts.5 = (bf16[1040,1024]{1,0:T(8,128)(2,1)}, f32[16,512]{1,0:T(8,128)}, bf16[8,4,288,128]{3,2,1,0:T(8,128)(2,1)}) custom-call(s32[5]{0:T(128)} %get-tuple-element.110.scalars, bf16[512,1024]{1,0:T(8,128)(2,1)} %copy-done.17, bf16[2048,1024]{1,0:T(8,128)(2,1)} %all-gather.2.cloned.1.call-done.cot, ...), custom_call_target="tpu_custom_call", output_to_operand_aliasing={{2}: (11, {})} | custom-call | flops 19327352832 | bytes 20971520 | tf_op jit(solution)/shard_map/experts/pallas_call | solution.py:553
  147.3 26.8 %experts.6 = (bf16[1040,1024]{1,0:T(8,128)(2,1)}, f32[16,512]{1,0:T(8,128)}, bf16[8,4,288,128]{3,2,1,0:T(8,128)(2,1)}) custom-call(s32[5]{0:T(128)} %get-tuple-element.111.scalars, bf16[512,1024]{1,0:T(8,128)(2,1)} %copy-done.20, bf16[2048,1024]{1,0:T(8,128)(2,1)} %all-gather.2.cloned.1.call-done.cot, ...), custom_call_target="tpu_custom_call", output_to_operand_aliasing={{2}: (11, {})} | custom-call | flops 19327352832 | bytes 20971520 | tf_op jit(solution)/shard_map/experts/pallas_call | solution.py:553
  174.1 1.6 collective-permute-start.8
  175.7 1.0 copy-done.19
  176.7 26.7 %experts.7 = (bf16[1040,1024]{1,0:T(8,128)(2,1)}, f32[16,512]{1,0:T(8,128)}, bf16[8,4,288,128]{3,2,1,0:T(8,128)(2,1)}) custom-call(s32[5]{0:T(128)} %get-tuple-element.109.scalars, bf16[512,1024]{1,0:T(8,128)(2,1)} %copy-done.19, bf16[2048,1024]{1,0:T(8,128)(2,1)} %all-gather.2.cloned.1.call-done.cot, ...), custom_call_target="tpu_custom_call", output_to_operand_aliasing={{2}: (11, {})} | custom-call | flops 19327352832 | bytes 20971520 | tf_op jit(solution)/shard_map/experts/pallas_call | solution.py:553
  203.5 3.6 %all-to-all-start.1 = ((bf16[8,4,288,128]{3,2,1,0:T(8,128)(2,1)}), bf16[8,4,288,128]{3,2,1,0:T(8,128)(2,1)S(1)}, u32[]{:S(2)}, u32[]{:S(2)}) async-start(bf16[8,4,288,128]{3,2,1,0:T(8,128)(2,1)} %get-tuple-element.75), calls=%async_computation.1 | async-start | bytes 4718592 | tf_op jit(solution)/shard_map/all_to_all | solution.py:1115
  207.1 17.5 %collective-permute-done.8 = bf16[1040,1024]{1,0:T(8,128)(2,1)} collective-permute-done((bf16[1040,1024]{1,0:T(8,128)(2,1)}, bf16[1040,1024]{1,0:T(8,128)(2,1)}, u32[]{:S(2)}, u32[]{:S(2)}) %collective-permute-start.8) | collective-permute-done | bytes 2129952 | tf_op jit(solution)/shard_map/ppermute | solution.py:1120
  224.6 3.0 add_convert_fusion.1
  228.3 8.2 %all-to-all-done.1 = bf16[8,4,288,128]{3,2,1,0:T(8,128)(2,1)S(1)} async-done(((bf16[8,4,288,128]{3,2,1,0:T(8,128)(2,1)}), bf16[8,4,288,128]{3,2,1,0:T(8,128)(2,1)S(1)}, u32[]{:S(2)}, u32[]{:S(2)}) %all-to-all-start.1) | async-done | bytes 2359328 | tf_op jit(solution)/shard_map/all_to_all | solution.py:1115
  236.4 1.4 copy-done.2
  237.8 3.6 %sum_experts.1 = (f32[4,8,32,128]{3,2,1,0:T(8,128)}, f32[4,8,2,16,64]{4,3,2,1,0:T(8,128)}, f32[4,8,16,64]{3,2,1,0:T(8,128)}, f32[4,8,16,128]{3,2,1,0:T(8,128)}) custom-call(s32[32]{0:T(128)} %reshape.97.ids, bf16[32,288,128]{2,1,0:T(8,128)(2,1)} %bitcast.41), custom_call_target="tpu_custom_call" | custom-call | tf_op jit(solution)/shard_map/sum_experts/pallas_call | solution.py:873
  241.5 13.0 %collective-permute-done.9 = bf16[528,1024]{1,0:T(8,128)(2,1)} collective-permute-done((bf16[528,1024]{1,0:T(8,128)(2,1)}, bf16[528,1024]{1,0:T(8,128)(2,1)}, u32[]{:S(2)}, u32[]{:S(2)}) %collective-permute-start.9) | collective-permute-done | bytes 1081376 | tf_op jit(solution)/shard_map/ppermute | solution.py:1126
  254.5 1.6 add_convert_fusion
  256.2 1.9 add_convert_fusion.4
  258.1 23.8 %collective-permute-done.10.refs_13_.refs_16_.refs_17_ = bf16[528,1024]{1,0:T(8,128)(2,1)S(1)} collective-permute-done((bf16[528,1024]{1,0:T(8,128)(2,1)S(1)}, bf16[528,1024]{1,0:T(8,128)(2,1)S(1)}, u32[]{:S(2)}, u32[]{:S(2)}) %collective-permute-start.10) | collective-permute-done | bytes 1081376 | tf_op jit(solution)/shard_map/ppermute | solution.py:1126
  283.0 9.6 %open_back.1 = (f32[512,1024]{1,0:T(8,128)}, bf16[512,1024]{1,0:T(8,128)(2,1)}, f32[64,1024]{1,0:T(8,128)}, f32[64,1024]{1,0:T(8,128)}) custom-call(s32[8]{0:T(128)} %broadcast_xor_fusion.order.refs_0_, bf16[512,1024]{1,0:T(8,128)(2,1)} %refs_1_.1, f32[512,1024]{1,0:T(8,128)} %get-tuple-element.60.refs_2_, bf16[1,1024]{1,0:T(2,128)(2,1)} %reshape.95.gain.refs_3_, ...), custom_call_target="tpu_custom_call" | custom-call | flops 1073741824 | bytes 14680064 | tf_op jit(solution)/shard_map/open_back/pallas_call | solution.py:673
  292.5 19.6 %attend_back.1 = (bf16[512,1024]{1,0:T(8,128)(2,1)}, bf16[512,512]{1,0:T(8,128)(2,1)}, bf16[512,512]{1,0:T(8,128)(2,1)}) custom-call(s32[1]{0:T(128)} %dynamic_slice.13.scalars, bf16[512,2048]{1,0:T(8,128)(2,1)} %get-tuple-element.58.query.key.value, bf16[512,2048]{1,0:T(8,128)(2,1)} %get-tuple-element.58.query.key.value, ...), custom_call_target="tpu_custom_call" | custom-call | flops 5368709120 | bytes 8388608 | tf_op jit(solution)/shard_map/attend_back/pallas_call | solution.py:303
  312.2 1.4 add_convert_fusion.3
  313.6 4.5 %adapters_back.1 = (bf16[512,64]{1,0:T(8,128)(2,1)}, bf16[32,16,256]{2,1,0:T(8,128)(2,1)}) custom-call(bf16[512,1024]{1,0:T(8,128)(2,1)} %get-tuple-element.86.grad_query, bf16[512,512]{1,0:T(8,128)(2,1)} %get-tuple-element.87.grad_key, bf16[512,512]{1,0:T(8,128)(2,1)} %get-tuple-element.88.grad_value, bf16[512,64]{1,0:T(8,128)(2,1)} %get-tuple-element.89.low, ...), custom_call_target="tpu_custom_call" | custom-call | flops 1610612736 | bytes 4194304 | tf_op jit(solution)/shard_map/adapters_back/pallas_call | solution.py:773
  318.0 5.9 %all-to-all-start.2 = ((bf16[32,16,256]{2,1,0:T(8,128)(2,1)}), bf16[32,16,256]{2,1,0:T(8,128)(2,1)S(1)}, u32[]{:S(2)}, u32[]{:S(2)}) async-start(bf16[32,16,256]{2,1,0:T(8,128)(2,1)} %get-tuple-element.95), calls=%async_computation.2 | async-start | bytes 524288 | tf_op jit(solution)/shard_map/all_to_all | solution.py:1153
  324.0 8.6 %input_back.1 = bf16[512,1024]{1,0:T(8,128)(2,1)} custom-call(s32[8]{0:T(128)} %broadcast_xor_fusion.order.refs_0_, bf16[512,1024]{1,0:T(8,128)(2,1)} %get-tuple-element.86.grad_query, bf16[512,512]{1,0:T(8,128)(2,1)} %get-tuple-element.87.grad_key, bf16[512,512]{1,0:T(8,128)(2,1)} %get-tuple-element.88.grad_value, bf16[512,64]{1,0:T(8,128)(2,1)} %get-tuple-element.93.low, ...), custom_call_target="tpu_custom_call" | custom-call | flops 2147483648 | bytes 12582912 | tf_op jit(solution)/shard_map/input_back/pallas_call | solution.py:818
  332.6 11.4 %all-to-all-done.2.pieces = bf16[32,16,256]{2,1,0:T(8,128)(2,1)S(1)} async-done(((bf16[32,16,256]{2,1,0:T(8,128)(2,1)}), bf16[32,16,256]{2,1,0:T(8,128)(2,1)S(1)}, u32[]{:S(2)}, u32[]{:S(2)}) %all-to-all-start.2) | async-done | bytes 262176 | tf_op jit(solution)/shard_map/all_to_all | solution.py:1153
  344.7 2.0 sum_mixer.1
  346.7 2.7 add_convert_fusion.2
  (97 shorter events, 14.2 us)
Async XLA Ops:
  7.2 9.3 %copy-start.16 = (s32[4]{0:T(128)S(1)}, s32[4]{0:T(128)}, u32[]{:S(2)}) copy-start(s32[4]{0:T(128)} %constant.92) | copy-start | bytes 52
  7.2 8.3 %copy-start.11 = (s32[32]{0:T(128)S(1)}, s32[32]{0:T(128)}, u32[]{:S(2)}) copy-start(s32[32]{0:T(128)} %ids.1) | copy-start | bytes 388
  7.2 8.4 %copy-start.8 = (bf16[8,16,256]{2,1,0:T(8,128)(2,1)S(1)}, bf16[8,16,256]{2,1,0:T(8,128)(2,1)}, u32[]{:S(2)}) copy-start(bf16[8,16,256]{2,1,0:T(8,128)(2,1)} %param.36) | copy-start | bytes 196612
  7.2 9.1 %copy-start.7 = (bf16[4,8,128,16]{2,3,1,0:T(8,128)(2,1)S(1)}, bf16[4,8,128,16]{2,3,1,0:T(8,128)(2,1)}, u32[]{:S(2)}) copy-start(bf16[4,8,128,16]{2,3,1,0:T(8,128)(2,1)} %param.35) | copy-start | bytes 393220
  7.2 9.8 %copy-start.10 = (bf16[8,16,128]{2,1,0:T(8,128)(2,1)S(1)}, bf16[8,16,128]{2,1,0:T(8,128)(2,1)}, u32[]{:S(2)}) copy-start(bf16[8,16,128]{2,1,0:T(8,128)(2,1)} %param.37) | copy-start | bytes 98308
  7.2 111.0 %all-gather.2.cloned.1.call-start = ((), (), s32[]{:S(2)}) async-start(), calls=%async_computation.3 | async-start | bytes 5242880 | tf_op jit(solution)/shard_map/all_gather | solution.py:1051
  11.0 21.5 %collective-permute-start.1 = (bf16[128,3072]{1,0:T(8,128)(2,1)}, bf16[128,3072]{1,0:T(8,128)(2,1)}, u32[]{:S(2)}, u32[]{:S(2)}) collective-permute-start(bf16[128,3072]{1,0:T(8,128)(2,1)} %get-tuple-element.107), channel_id=1, source_target_pairs={{0,16},{4,20},{8,24},{12,28},{16,0},{20,4},{24,8},{28,12},{1,17},{... | collective-permute-start | bytes 2359304 | tf_op jit(solution)/shard_map/ppermute | solution.py:936
  14.0 21.6 %collective-permute-start = (bf16[128,3072]{1,0:T(8,128)(2,1)}, bf16[128,3072]{1,0:T(8,128)(2,1)}, u32[]{:S(2)}, u32[]{:S(2)}) collective-permute-start(bf16[128,3072]{1,0:T(8,128)(2,1)} %get-tuple-element.107), channel_id=1, source_target_pairs={{0,8},{4,12},{8,0},{12,4},{16,24},{20,28},{24,16},{28,20},{1,9},{5... | collective-permute-start | bytes 2359304 | tf_op jit(solution)/shard_map/ppermute | solution.py:936
  19.1 26.4 %all-to-all-start = ((bf16[8,112,128]{2,1,0:T(8,128)(2,1)}), bf16[8,112,128]{2,1,0:T(8,128)(2,1)S(1)}, u32[]{:S(2)}, u32[]{:S(2)}) async-start(bf16[8,112,128]{2,1,0:T(8,128)(2,1)} %gather_fusion), calls=%async_computation | async-start | bytes 458752 | tf_op jit(solution)/shard_map/all_to_all | solution.py:1022
  33.5 10.6 %collective-permute-start.2 = (bf16[64,3072]{1,0:T(8,128)(2,1)S(1)}, bf16[64,3072]{1,0:T(8,128)(2,1)S(1)}, u32[]{:S(2)}, u32[]{:S(2)}) collective-permute-start(bf16[64,3072]{1,0:T(8,128)(2,1)S(1)} %slice.68), channel_id=1, source_target_pairs={{0,8},{4,12},{8,0},{12,4},{16,24},{20,28},{24,16},{28,20},{1,9},{5... | collective-permute-start | bytes 1179656 | tf_op jit(solution)/shard_map/ppermute | solution.py:936
  36.6 8.9 %collective-permute-start.3 = (bf16[64,3072]{1,0:T(8,128)(2,1)S(1)}, bf16[64,3072]{1,0:T(8,128)(2,1)S(1)}, u32[]{:S(2)}, u32[]{:S(2)}) collective-permute-start(bf16[64,3072]{1,0:T(8,128)(2,1)S(1)} %slice.69), channel_id=1, source_target_pairs={{0,16},{4,20},{8,24},{12,28},{16,0},{20,4},{24,8},{28,12},{1,17},{... | collective-permute-start | bytes 1179656 | tf_op jit(solution)/shard_map/ppermute | solution.py:936
  38.2 7.5 %copy-start.14 = (s32[4,1]{0,1:T(1,128)S(1)}, s32[4,1]{0,1:T(1,128)}, u32[]{:S(2)}) copy-start(s32[4,1]{0,1:T(1,128)} %get-tuple-element.103) | copy-start | bytes 52
  38.2 7.7 %copy-start.12 = (bf16[1024]{0:T(1024)(128)(2,1)S(1)}, bf16[1024]{0:T(1024)(128)(2,1)}, u32[]{:S(2)}) copy-start(bf16[1024]{0:T(1024)(128)(2,1)} %param.28) | copy-start | bytes 6148
  38.2 8.6 %copy-start.13 = (bf16[1024]{0:T(1024)(128)(2,1)S(1)}, bf16[1024]{0:T(1024)(128)(2,1)}, u32[]{:S(2)}) copy-start(bf16[1024]{0:T(1024)(128)(2,1)} %param.29) | copy-start | bytes 6148
  38.2 9.2 %copy-start.9 = (s32[2048,8]{0,1:T(8,128)S(1)}, s32[2048,8]{0,1:T(8,128)}, u32[]{:S(2)}) copy-start(s32[2048,8]{0,1:T(8,128)} %param.27) | copy-start | bytes 196612
  39.4 9.3 %copy-start.21 = (s32[32]{0:T(128)S(1)}, s32[32]{0:T(128)}, u32[]{:S(2)}) copy-start(s32[32]{0:T(128)} %param.25) | copy-start | bytes 388
  39.4 12.1 %copy-start.15 = (s32[4,1]{1,0:T(4,128)S(1)}, s32[4,1]{1,0:T(4,128)}, u32[]{:S(2)}) copy-start(s32[4,1]{1,0:T(4,128)} %constant.94) | copy-start | bytes 52
  39.5 12.2 %copy-start.22 = (s32[8]{0:T(128)S(1)}, s32[8]{0:T(128)}, u32[]{:S(2)}) copy-start(s32[8]{0:T(128)} %constant.84.clone) | copy-start | bytes 100
  45.5 10.0 %copy-start = (bf16[512,3072]{1,0:T(8,128)(2,1)}, bf16[512,3072]{1,0:T(8,128)(2,1)S(1)}, u32[]{:S(2)}) copy-start(bf16[512,3072]{1,0:T(8,128)(2,1)S(1)} %constant_dynamic-update-slice_fusion.2.weight_a.refs_6_) | copy-start | bytes 9437188
  45.5 12.0 %collective-permute-start.4 = (bf16[512,3072]{1,0:T(8,128)(2,1)S(1)}, bf16[512,3072]{1,0:T(8,128)(2,1)}, u32[]{:S(2)}, u32[]{:S(2)}) collective-permute-start(bf16[512,3072]{1,0:T(8,128)(2,1)S(1)} %constant_dynamic-update-slice_fusion.2.weight_a.refs_6_), channel_id=1, source_target_pairs={{0,4},{4,0},{8,12},{12,8},{16,20},{20,16},{24,28},{28,24},{1,5},{5... | collective-permute-start | bytes 9437192 | tf_op jit(solution)/shard_map/ppermute | solution.py:936
  50.7 17.3 %copy-start.6 = (bf16[16,1024]{1,0:T(8,128)(2,1)}, bf16[16,1024]{1,0:T(8,128)(2,1)S(1)}, u32[]{:S(2)}) copy-start(bf16[16,1024]{1,0:T(8,128)(2,1)S(1)} %fusion.1.refs_5_) | copy-start | bytes 98308
  86.6 31.7 %collective-permute-start.6 = (bf16[512,1024]{1,0:T(8,128)(2,1)}, bf16[512,1024]{1,0:T(8,128)(2,1)S(1)}, u32[]{:S(2)}, u32[]{:S(2)}) collective-permute-start(bf16[512,1024]{1,0:T(8,128)(2,1)} %get-tuple-element.64.x), channel_id=1, source_target_pairs={{0,1},{1,2},{2,3},{3,0},{4,5},{5,6},{6,7},{7,4},{8,9},{9,10},{10,1... | collective-permute-start | bytes 3145736 | tf_op jit(solution)/shard_map/ppermute | solution.py:1084
  88.6 27.2 %copy-start.18 = (bf16[512,1024]{1,0:T(8,128)(2,1)S(1)}, bf16[512,1024]{1,0:T(8,128)(2,1)}, u32[]{:S(2)}) copy-start(bf16[512,1024]{1,0:T(8,128)(2,1)} %get-tuple-element.64.x) | copy-start | bytes 3145732
  115.8 30.5 %collective-permute-start.5 = (bf16[512,1024]{1,0:T(8,128)(2,1)S(1)}, bf16[512,1024]{1,0:T(8,128)(2,1)S(1)}, u32[]{:S(2)}, u32[]{:S(2)}) collective-permute-start(bf16[512,1024]{1,0:T(8,128)(2,1)S(1)} %copy-done.18), channel_id=1, source_target_pairs={{0,3},{1,0},{2,1},{3,2},{4,7},{5,4},{6,5},{7,6},{8,11},{9,8},{10,9... | collective-permute-start | bytes 3145736 | tf_op jit(solution)/shard_map/ppermute | solution.py:1108
  118.3 1.0 copy-start.17
  146.1 29.6 %collective-permute-start.7 = (bf16[512,1024]{1,0:T(8,128)(2,1)}, bf16[512,1024]{1,0:T(8,128)(2,1)S(1)}, u32[]{:S(2)}, u32[]{:S(2)}) collective-permute-start(bf16[512,1024]{1,0:T(8,128)(2,1)} %copy-done.17), channel_id=1, source_target_pairs={{0,1},{1,2},{2,3},{3,0},{4,5},{5,6},{6,7},{7,4},{8,9},{9,10},{10,1... | collective-permute-start | bytes 3145736 | tf_op jit(solution)/shard_map/ppermute | solution.py:1111
  146.3 1.0 copy-start.20
  174.1 50.5 %collective-permute-start.8 = (bf16[1040,1024]{1,0:T(8,128)(2,1)}, bf16[1040,1024]{1,0:T(8,128)(2,1)}, u32[]{:S(2)}, u32[]{:S(2)}) collective-permute-start(bf16[1040,1024]{1,0:T(8,128)(2,1)} %get-tuple-element.74), channel_id=1, source_target_pairs={{0,1},{1,2},{2,3},{3,0},{4,5},{5,6},{6,7},{7,4},{8,9},{9,10},{10,1... | collective-permute-start | bytes 6389768 | tf_op jit(solution)/shard_map/ppermute | solution.py:1120
  175.7 1.0 copy-start.19
  203.5 33.0 %all-to-all-start.1 = ((bf16[8,4,288,128]{3,2,1,0:T(8,128)(2,1)}), bf16[8,4,288,128]{3,2,1,0:T(8,128)(2,1)S(1)}, u32[]{:S(2)}, u32[]{:S(2)}) async-start(bf16[8,4,288,128]{3,2,1,0:T(8,128)(2,1)} %get-tuple-element.75), calls=%async_computation.1 | async-start | bytes 4718592 | tf_op jit(solution)/shard_map/all_to_all | solution.py:1115
  227.5 26.9 %collective-permute-start.9 = (bf16[528,1024]{1,0:T(8,128)(2,1)}, bf16[528,1024]{1,0:T(8,128)(2,1)}, u32[]{:S(2)}, u32[]{:S(2)}) collective-permute-start(bf16[528,1024]{1,0:T(8,128)(2,1)} %add_convert_fusion.1), channel_id=1, source_target_pairs={{0,1},{1,2},{2,3},{3,0},{4,5},{5,6},{6,7},{7,4},{8,9},{9,10},{10,1... | collective-permute-start | bytes 3244040 | tf_op jit(solution)/shard_map/ppermute | solution.py:1126
  236.4 1.4 copy-start.2
  236.4 18.0 %copy-start.4 = (bf16[1040,1024]{1,0:T(8,128)(2,1)S(1)}, bf16[1040,1024]{1,0:T(8,128)(2,1)}, u32[]{:S(2)}) copy-start(bf16[1040,1024]{1,0:T(8,128)(2,1)} %get-tuple-element.68) | copy-start | bytes 6389764
  256.1 25.8 %collective-permute-start.10 = (bf16[528,1024]{1,0:T(8,128)(2,1)S(1)}, bf16[528,1024]{1,0:T(8,128)(2,1)S(1)}, u32[]{:S(2)}, u32[]{:S(2)}) collective-permute-start(bf16[528,1024]{1,0:T(8,128)(2,1)S(1)} %add_convert_fusion), channel_id=1, source_target_pairs={{0,1},{1,2},{2,3},{3,0},{4,5},{5,6},{6,7},{7,4},{8,9},{9,10},{10,1... | collective-permute-start | bytes 3244040 | tf_op jit(solution)/shard_map/ppermute | solution.py:1126
  281.9 1.0 copy-start.1
  281.9 30.3 %collective-permute-start.11 = (bf16[512,1024]{1,0:T(8,128)(2,1)S(1)}, bf16[512,1024]{1,0:T(8,128)(2,1)S(1)}, u32[]{:S(2)}, u32[]{:S(2)}) collective-permute-start(bf16[512,1024]{1,0:T(8,128)(2,1)S(1)} %add_convert_fusion.4), channel_id=1, source_target_pairs={{0,1},{1,2},{2,3},{3,0},{4,5},{5,6},{6,7},{7,4},{8,9},{9,10},{10,1... | collective-permute-start | bytes 3145736 | tf_op jit(solution)/shard_map/ppermute | solution.py:1130
  313.6 33.1 %collective-permute-start.12 = (bf16[512,1024]{1,0:T(8,128)(2,1)}, bf16[512,1024]{1,0:T(8,128)(2,1)S(1)}, u32[]{:S(2)}, u32[]{:S(2)}) collective-permute-start(bf16[512,1024]{1,0:T(8,128)(2,1)} %add_convert_fusion.3), channel_id=1, source_target_pairs={{0,1},{1,2},{2,3},{3,0},{4,5},{5,6},{6,7},{7,4},{8,9},{9,10},{10,1... | collective-permute-start | bytes 3145736 | tf_op jit(solution)/shard_map/ppermute | solution.py:1149
  318.0 25.9 %all-to-all-start.2 = ((bf16[32,16,256]{2,1,0:T(8,128)(2,1)}), bf16[32,16,256]{2,1,0:T(8,128)(2,1)S(1)}, u32[]{:S(2)}, u32[]{:S(2)}) async-start(bf16[32,16,256]{2,1,0:T(8,128)(2,1)} %get-tuple-element.95), calls=%async_computation.2 | async-start | bytes 524288 | tf_op jit(solution)/shard_map/all_to_all | solution.py:1153
  323.9 22.8 %copy-start.3 = (f32[512,1024]{1,0:T(8,128)S(1)}, f32[512,1024]{1,0:T(8,128)}, u32[]{:S(2)}) copy-start(f32[512,1024]{1,0:T(8,128)} %get-tuple-element.60.refs_2_) | copy-start | bytes 6291460
  344.0 0.7 copy-start.5
Sparse Core Ops, SparseCore 0:
  15.6 83.2 all-gather.1

commit v5 on v4

--- a/solution.py
+++ b/solution.py
@@ -409,7 +409,8 @@
     *rest,
 ):
     (
-        sums_out,
+        out,
+        grad_normed,
         gates_out,
         packed,
         gates,
@@ -426,7 +427,7 @@
         down_acc,
         out_acc,
         grad_acc,
-    ) = rest[-17:]
+    ) = rest[-18:]
     expert = pl.program_id(0)
     last = pl.num_programs(0) - 1
     rows = x.shape[0]
@@ -439,10 +440,14 @@
     @pl.when(expert == 0)
     def _():
         logits = nt(x[...], router[...])
+        experts = gates_out.shape[0]
         lane = lanes_of(logits.shape)
-        chosen = lane == routes[:, 0:1]
+        name = lane + scalars[4]
+        name = jnp.where(name >= experts, name - experts, name)
+        name = jnp.where(lane < experts, name, -1)
+        chosen = name == routes[:, 0:1]
         for k in range(1, TOP):
-            chosen = chosen | (lane == routes[:, k : k + 1])
+            chosen = chosen | (name == routes[:, k : k + 1])
         top = jnp.max(jnp.where(chosen, logits, -1e30), -1, keepdims=True)
         shifted = jnp.where(chosen, jnp.exp(jnp.where(chosen, logits - top, 0.0)), 0.0)
         weights = shifted / jnp.sum(shifted, -1, keepdims=True)
@@ -518,14 +523,13 @@
 
     @pl.when(expert == last)
     def _():
-        sums_out[:rows, :] = (grad_acc[...] + nn(back_in[...], a_in_all)).astype(bf16)
+        out[...] = (out_acc[...] + nn(gated_low[...], b_down_all)).astype(bf16)
+        grad_normed[:rows, :] = (grad_acc[...] + nn(back_in[...], a_in_all)).astype(bf16)
         experts = gates_out.shape[0]
         sums = gate_sums[...].T[:experts, :]
         sums = jnp.concatenate([sums[: experts // 2], sums[experts // 2 :]], 1)
         high = sums.astype(bf16).astype(f32)
-        edge = rows + experts
-        sums_out[rows:edge, :] = jnp.concatenate([high, sums - high], 0).astype(bf16)
-        sums_out[edge:, :] = (out_acc[...] + nn(gated_low[...], b_down_all)).astype(bf16)
+        grad_normed[rows:, :] = jnp.concatenate([high, sums - high], 0).astype(bf16)
         wide = tn(back_in[...], x[...]).astype(bf16)
         tall = tn(gated_low[...], cot[...]).astype(bf16)
         for at in range(BLOCKS):
@@ -541,14 +545,13 @@
 
 
 def run_experts(
-    scalars, x, cot, routes, router, w_in, w_down, a_in, b_in, a_down, b_down, experts, slots, packed
+    scalars, x, cot, routes, router, w_in, w_down, a_in, b_in, a_down, b_down, experts, packed
 ):
     rows = x.shape[0]
     local = w_in.shape[0]
     ranks_in = local * 2 * R
     ranks_down = local * R
-    height = local * 9 * R // 2
-    kept = [] if packed is None else [packed]
+    height = packed.shape[2]
     full = lambda shape: pl.BlockSpec(shape, lambda e, s: (0,) * len(shape))
     return pl.pallas_call(
         expert_kernel,
@@ -557,7 +560,7 @@
             grid=(local,),
             in_specs=[
                 full((rows, MODEL_WIDTH)),
-                pl.BlockSpec((rows, MODEL_WIDTH), lambda e, s: (s[4], 0)),
+                pl.BlockSpec((rows, MODEL_WIDTH), lambda e, s: (s[5], 0)),
                 pl.BlockSpec((rows, TOP), lambda e, s: (s[0], 0)),
                 full((128, MODEL_WIDTH)),
                 pl.BlockSpec((1, MODEL_WIDTH, 2 * H), lambda e, s: (e, 0, 0)),
@@ -567,9 +570,10 @@
                 pl.BlockSpec((local, 1, R, H), lambda e, s: (0, s[1], 0, 0)),
                 pl.BlockSpec((local, 1, R, MODEL_WIDTH), lambda e, s: (0, s[1], 0, 0)),
             ]
-            + [pl.BlockSpec(memory_space=pl.ANY)] * len(kept),
+            + [pl.BlockSpec(memory_space=pl.ANY)],
             out_specs=[
-                full((2 * rows + experts, MODEL_WIDTH)),
+                full((rows, MODEL_WIDTH)),
+                full((rows + experts, MODEL_WIDTH)),
                 full((experts, rows)),
                 pl.BlockSpec((BLOCKS, 1, height, BLOCK), lambda e, s: (0, s[3], 0, 0)),
             ],
@@ -591,11 +595,12 @@
             ],
         ),
         out_shape=[
-            jax.ShapeDtypeStruct((2 * rows + experts, MODEL_WIDTH), bf16),
+            jax.ShapeDtypeStruct((rows, MODEL_WIDTH), bf16),
+            jax.ShapeDtypeStruct((rows + experts, MODEL_WIDTH), bf16),
             jax.ShapeDtypeStruct((experts, rows), f32),
-            jax.ShapeDtypeStruct((BLOCKS, slots, height, BLOCK), bf16),
+            jax.ShapeDtypeStruct(packed.shape, bf16),
         ],
-        input_output_aliases={11: 2} if kept else {},
+        input_output_aliases={11: 3},
         compiler_params=params_of(1),
         name="experts",
         cost_estimate=pl.CostEstimate(
@@ -603,7 +608,38 @@
             transcendentals=local * rows * H,
             bytes_accessed=20 << 20,
         ),
-    )(scalars, x, cot, routes, router, w_in, w_down, a_in, b_in, a_down, b_down, *kept)
+    )(scalars, x, cot, routes, router, w_in, w_down, a_in, b_in, a_down, b_down, packed)
+
+
+def room_for(shape):
+    return pl.pallas_call(
+        lambda ref: None,
+        out_specs=pl.BlockSpec(memory_space=pl.ANY),
+        out_shape=jax.ShapeDtypeStruct(shape, bf16),
+        name="room",
+    )()
+
+
+def pack_kernel(left, right, both, done):
+    middle = left.shape[1]
+    one = pltpu.make_async_copy(left, both.at[:, :middle], done.at[0])
+    two = pltpu.make_async_copy(right, both.at[:, middle:], done.at[1])
+    one.start()
+    two.start()
+    one.wait()
+    two.wait()
+
+
+def pack(left, right):
+    anywhere = pl.BlockSpec(memory_space=pl.ANY)
+    return pl.pallas_call(
+        pack_kernel,
+        in_specs=[anywhere, anywhere],
+        out_specs=anywhere,
+        out_shape=jax.ShapeDtypeStruct((left.shape[0], left.shape[1] + right.shape[1]), left.dtype),
+        scratch_shapes=[pltpu.SemaphoreType.DMA((2,))],
+        name="pack",
+    )(left, right)
 
 
 def open_back_kernel(count, order, cot, mid, gain, gates, router, weight_a, weight_b, low_map, up_map, low, att, *rest):
@@ -1021,16 +1057,6 @@
     adapters = jnp.concatenate([low_turned, up_turned, attention_output_upmap], 1)[mine]
     adapters = lax.all_to_all(adapters, "dp", 0, 0, tiled=True)
     order = order_of(row)
-    both = jnp.concatenate([query_key_value_weight, w_out], 1)
-    if owners == BLOCKS:
-        pair = both_neighbours(both)
-        near = jnp.concatenate([both, *pair, *across(pair)], 0)
-        near, adapters = tied(near, adapters)
-        weights = near, swap(near, 1)
-    else:
-        whole = lax.all_gather(both, "dp", axis=0, tiled=True)
-        weights = whole, whole
-
     low_map = adapters[:, : 4 * R].transpose(1, 0, 2).reshape(4 * R, MODEL_WIDTH)
     up = (
         adapters[:, 4 * R : 6 * R]
@@ -1046,24 +1072,11 @@
     ).reshape(4 * R, QKV)
     up_out_map = jnp.concatenate([jnp.zeros((3 * R, MODEL_WIDTH), bf16), up_out], 0)
 
-    cos, sin = rope_tables(rows)
-
-    cots = lax.all_gather(cotangent, "expert", axis=0, tiled=True)
-
-    qkv, low, normed_in = project(order, hidden, attn_gain, weights, low_map, up_map, cos, sin)
-    attended, lse = attend(length, qkv)
-    mid, normed_mid, low_out = close_mixer(
-        order, attended, hidden, ffn_gain, weights, low_map, up_out_map
-    )
-
     first = place * local
-    routes_here = (routes - first + experts) % experts
     router = jnp.roll(w_router.T, -first, axis=0)
     router_wide = jnp.concatenate(
         [router, jnp.zeros((128 - experts, MODEL_WIDTH), router.dtype)], 0
     )
-    a_in = expert_gate_up_lowmap.transpose(0, 1, 3, 2)
-    a_down = expert_down_lowmap.transpose(0, 1, 3, 2)
 
     offsets = [0, 1] + [groups - 1] * (groups > 2) + list(range(2, groups - 1))
     offset = jnp.array(offsets, jnp.int32)
@@ -1076,20 +1089,47 @@
             lax.dynamic_slice(tags, (row, 0), (1, groups))[0],
             offset * local,
             slot,
+            jnp.full((groups,), first, jnp.int32),
             jnp.where(slot == 0, 0, source),
         ],
         1,
     )
 
+    both = pack(query_key_value_weight, w_out)
+    if owners == BLOCKS:
+        pair = both_neighbours(both)
+        pair, order, router, router_wide, table, tags, attn_gain, ffn_gain, length = tied(
+            pair, order, router, router_wide, table, tags, attn_gain, ffn_gain, length
+        )
+        near = jnp.concatenate([both, *pair, *across(pair)], 0)
+        near, low_map, up_map, up_out_map = tied(near, low_map, up_map, up_out_map)
+        weights = near, swap(near, 1)
+    else:
+        whole = lax.all_gather(both, "dp", axis=0, tiled=True)
+        weights = whole, whole
+
+    cos, sin = rope_tables(rows)
+
+    cots = lax.all_gather(cotangent, "expert", axis=0, tiled=True)
+
+    qkv, low, normed_in = project(order, hidden, attn_gain, weights, low_map, up_map, cos, sin)
+    attended, lse = attend(length, qkv)
+    mid, normed_mid, low_out = close_mixer(
+        order, attended, hidden, ffn_gain, weights, low_map, up_out_map
+    )
+
+    a_in = expert_gate_up_lowmap.transpose(0, 1, 3, 2)
+    a_down = expert_down_lowmap.transpose(0, 1, 3, 2)
+
     xs = {0: normed_mid, 1: lax.ppermute(normed_mid, "expert", forward)}
-    packed = None
+    packed = room_for((BLOCKS, groups, local * 9 * R // 2, BLOCK))
     ran = {}
     for at, offset in enumerate(offsets):
-        ran[offset], gate_part, packed = run_experts(
+        *ran[offset], gate_part, packed = run_experts(
             table[at],
             xs[offset],
             cotangent if at == 0 else cots,
-            routes_here,
+            routes,
             router_wide,
             w_gate_up,
             w_down,
@@ -1098,7 +1138,6 @@
             a_down,
             expert_down_upmap,
             experts,
-            groups,
             packed,
         )
         if at == 0:
@@ -1110,22 +1149,22 @@
             value, packed = tied(xs[at], packed)
             xs[at + 1] = lax.ppermute(value, "expert", forward)
         if at == 2:
-            first_sums, packed = tied(ran[1], packed)
-
-    pieces = lax.all_to_all(to_owners(packed, owners, local), "dp", 0, 0, tiled=True)
-    pieces = pieces.reshape(devices, pieces.shape[2], width)
-    g_a_in, g_b_in, g_a_down, g_b_down = sum_experts(tags.reshape(devices), pieces, local)
-
-    edge = rows + experts
-    both_far = lax.ppermute(first_sums if groups > 2 else ran[1], "expert", forward)
-    grad_far, out_far = both_far, both_far[edge:]
+            ran[1][1], ran[1][0], packed = tied(ran[1][1], ran[1][0], packed)
+
+    grad_far = lax.ppermute(ran[1][1], "expert", forward)
+    out_far = lax.ppermute(ran[1][0], "expert", forward)
     for offset in range(2, groups):
-        grad_part = joined(ran[offset][:edge], grad_far[:edge])
+        grad_part = joined(ran[offset][1], grad_far)
+        if offset == 2:
+            packed, out_far = tied(packed, out_far)
         if offset == groups - 1:
+            pieces = lax.all_to_all(to_owners(packed, owners, local), "dp", 0, 0, tiled=True)
+            pieces = pieces.reshape(devices, pieces.shape[2], width)
+            g_a_in, g_b_in, g_a_down, g_b_down = sum_experts(tags.reshape(devices), pieces, local)
             grad_part, g_a_down = tied(grad_part, g_a_down)
         grad_far = lax.ppermute(grad_part, "expert", forward)
     if groups > 2:
-        out_part = joined(ran[2][edge:], out_far)
+        out_part = joined(ran[2][0], out_far)
         out_part, grad_far = tied(out_part, grad_far)
         out_far = lax.ppermute(out_part, "expert", forward)
 
@@ -1141,12 +1180,12 @@
         up_out_map,
         low_out,
         attended,
-        [ran[0], grad_far],
+        [ran[0][1], grad_far],
     )
     grad_query, grad_key, grad_value = attend_back(length, qkv, grad_attended, lse, cos, sin)
     out_far, grad_query = tied(out_far, grad_query)
     for offset in range(3, groups):
-        out_far = lax.ppermute(joined(ran[offset][edge:], out_far), "expert", forward)
+        out_far = lax.ppermute(joined(ran[offset][0], out_far), "expert", forward)
     packed, back_low = adapters_back(
         grad_query, grad_key, grad_value, low, normed_in, up_map, grad_low_out, grad_up_out, devices
     )
@@ -1156,7 +1195,7 @@
     grad_hidden = input_back(
         order, grad_query, grad_key, grad_value, back_low, weights, low_map, hidden, attn_gain, grad_mid
     )
-    out = (mid + ran[0][edge:].astype(f32) + out_far.astype(f32)).astype(bf16)
+    out = (mid + ran[0][0].astype(f32) + out_far.astype(f32)).astype(bf16)
     return (
         out,
         grad_hidden,

time: 363 us -> 389 us (1.072)
  Pallas kernels: 185 us -> 210 us
  waiting for transfers between devices: 88.5 us -> 96 us
  other arithmetic: 17 us -> 12.9 us
    pallas_call x0 -> x2, Pallas kernels: none -> 24.9 us  [the longest x1 24.9 us: pack(): pl.pallas_call(pack_kernel, in_specs=[anywhere, anywhere], out_specs=anyw...]
    ppermute x2, waiting for transfers between devices: 36.8 us -> 49.8 us  [on_device(): grad_far = lax.ppermute(grad_part, 'expert', forward)]
    all_to_all x1, waiting for transfers between devices: 0.01 us -> 9.38 us  [on_device(): adapters = lax.all_to_all(adapters, 'dp', 0, 0, tiled=True)]
    all_to_all x1, waiting for transfers between devices: 8.16 us -> 0.01 us  [on_device(): lax.all_to_all(to_owners(packed, owners, local), 'dp', 0, 0, tiled=True)]
    ppermute x5, waiting for transfers between devices: 14.7 us -> 10.2 us  [swap(): return lax.ppermute(value, 'dp', [(at, at ^ bit) for at in range(BLOCKS)])]
    ppermute x2 -> x3, waiting for transfers between devices: 17.5 us -> 15.2 us  [the longest x1 15.2 us: on_device(): grad_far = lax.ppermute(ran[1][1], 'expert', forward)]
    unnamed x51 -> x60, local copies, waits for them, and re-layouts: 10.4 us -> 10.3 us
  transfers between devices with their start and end apart: 17 -> 18, of which waited for: 8 -> 8; matrix products, arithmetic and copies ran while one was open for 7% -> 7% of each run, Pallas kernels for 52% -> 47%
where the time goes in v5:
time: 389 us; the launch traced here: 383 us
  Pallas kernels  210 us (54%)
  waiting for transfers between devices  96 us (25%)
  starting transfers between devices  27.8 us (7%)
  local copies, waits for them, and re-layouts  21.4 us (6%)
  between operations  15 us (4%)
  other arithmetic  12.9 us (3%)
    pallas_call x4, Pallas kernels, run_experts(): pl.pallas_call(expert_kernel, grid_spec=pltpu.PrefetchScalarGridSpec(num_...  108 us
    ppermute x2, waiting for transfers between devices, on_device(): grad_far = lax.ppermute(grad_part, 'expert', forward)  49.8 us
    pallas_call x1, Pallas kernels, pack(): pl.pallas_call(pack_kernel, in_specs=[anywhere, anywhere], out_specs=anyw...  24.9 us
    pallas_call x1, Pallas kernels, attend_back(): pl.pallas_call(attend_back_kernel, grid_spec=pltpu.PrefetchScalarGridSpec...  19.7 us
    ppermute x1, waiting for transfers between devices, on_device(): grad_far = lax.ppermute(ran[1][1], 'expert', forward)  15.2 us
    pallas_call x1, Pallas kernels, attend(): pl.pallas_call(attend_kernel, grid_spec=pltpu.PrefetchScalarGridSpec(num_...  12.6 us
    all_to_all x1, waiting for transfers between devices, on_device(): packed = lax.all_to_all(packed, ('dp', 'expert'), 0, 0, tiled=True)  11.3 us
    pallas_call x1, Pallas kernels, project(): pl.pallas_call(project_kernel, grid_spec=pltpu.PrefetchScalarGridSpec(num...  10.4 us
  transfers between devices with their start and end apart: 18, of which 8 were waited for; matrix products, arithmetic and copies ran while one was open for 7% of the time, Pallas kernels for 47%

profile of v5, /device:TPU:0, one launch (start us, length us, event | category | flops | bytes accessed | tf_op | source)
XLA Modules:
  0.0 383.2 jit_solution(13454301265764517632)
XLA Ops:
  7.3 24.9 %pack.1 = bf16[128,3072]{1,0:T(8,128)(2,1)} custom-call(bf16[128,2048]{1,0:T(8,128)(2,1)} %left.1, bf16[128,1024]{1,0:T(8,128)(2,1)} %right.1), custom_call_target="tpu_custom_call" | custom-call | tf_op jit(solution)/shard_map/pack/pallas_call | solution.py:635
  32.3 3.1 collective-permute-start.1
  35.3 1.5 collective-permute-start
  37.3 1.3 gather_fusion.1
  38.6 3.4 all-to-all-start
  42.1 1.3 constant_dynamic-update-slice_fusion.4
  47.4 9.4 %all-to-all-done = bf16[8,112,128]{2,1,0:T(8,128)(2,1)S(1)} async-done(((bf16[8,112,128]{2,1,0:T(8,128)(2,1)}), bf16[8,112,128]{2,1,0:T(8,128)(2,1)S(1)}, u32[]{:S(2)}, u32[]{:S(2)}) %all-to-all-start) | async-done | bytes 229408 | tf_op jit(solution)/shard_map/all_to_all | solution.py:1058
  57.5 1.4 concatenate.20.up_map.refs_9_
  60.4 1.0 slice.28
  61.4 1.0 slice.27
  62.4 1.8 collective-permute-start.2
  64.2 1.2 collective-permute-start.3
  65.3 1.2 constant_dynamic-update-slice_fusion.3
  66.5 1.2 constant_dynamic-update-slice_fusion.2
  67.7 5.4 %collective-permute-done.2 = bf16[64,3072]{1,0:T(8,128)(2,1)S(1)} collective-permute-done((bf16[64,3072]{1,0:T(8,128)(2,1)S(1)}, bf16[64,3072]{1,0:T(8,128)(2,1)S(1)}, u32[]{:S(2)}, u32[]{:S(2)}) %collective-permute-start.2) | collective-permute-done | bytes 393248 | tf_op jit(solution)/shard_map/ppermute | solution.py:972
  73.1 1.4 collective-permute-done.3
  74.7 1.7 copy.64.routes
  77.0 3.5 collective-permute-done.4.weight_b.refs_7_
  80.4 10.4 %project.1 = (bf16[512,2048]{1,0:T(8,128)(2,1)}, bf16[512,64]{1,0:T(8,128)(2,1)}, bf16[512,1024]{1,0:T(8,128)(2,1)}) custom-call(s32[8]{0:T(128)} %broadcast_xor_fusion.order.refs_0_, bf16[512,1024]{1,0:T(8,128)(2,1)} %hid.5, bf16[1,1024]{1,0:T(2,128)(2,1)} %reshape.89.gain, bf16[512,3072]{1,0:T(8,128)(2,1)} %copy-done, ...), custom_call_target="tpu_custom_call" | custom-call | flops 2147483648 | bytes 8388608 | tf_op jit(solution)/shard_map/project/pallas_call | solution.py:141
  90.8 12.6 %attend.1 = (bf16[512,1024]{1,0:T(8,128)(2,1)}, f32[8,2,512]{2,1,0:T(2,128)}) custom-call(s32[1]{0:T(128)} %dynamic_slice.15.scalars, bf16[512,2048]{1,0:T(8,128)(2,1)} %get-tuple-element.83.query.key.value, bf16[512,2048]{1,0:T(8,128)(2,1)} %get-tuple-element.83.query.key.value, bf16[512,2048]{1,0:T(8,128)(2,1)} %get-tuple-element.83.query.key.value), custom_call_target="tpu_custom_call" | custom-call | flops 2147483648 | bytes 4194304 | tf_op jit(solution)/shard_map/attend/pallas_call | solution.py:223
  103.4 6.0 %close_mixer.1 = (f32[512,1024]{1,0:T(8,128)}, bf16[512,1024]{1,0:T(8,128)(2,1)}, bf16[512,64]{1,0:T(8,128)(2,1)}) custom-call(s32[8]{0:T(128)} %broadcast_xor_fusion.order.refs_0_, bf16[512,1024]{1,0:T(8,128)(2,1)} %get-tuple-element.84.att.refs_11_, bf16[512,1024]{1,0:T(8,128)(2,1)} %hid.5, bf16[1,1024]{1,0:T(2,128)(2,1)} %reshape.90.gain.refs_3_, ...), custom_call_target="tpu_custom_call" | custom-call | flops 1073741824 | bytes 8388608 | tf_op jit(solution)/shard_map/close_mixer/pallas_call | solution.py:356
  109.4 2.1 collective-permute-start.6
  111.5 27.5 %experts.4 = (bf16[512,1024]{1,0:T(8,128)(2,1)}, bf16[528,1024]{1,0:T(8,128)(2,1)}, f32[16,512]{1,0:T(8,128)}, bf16[8,4,288,128]{3,2,1,0:T(8,128)(2,1)}) custom-call(s32[6]{0:T(128)} %get-tuple-element.146.scalars, bf16[512,1024]{1,0:T(8,128)(2,1)} %get-tuple-element.93.x, bf16[512,1024]{1,0:T(8,128)(2,1)} %refs_1_.1, ...), custom_call_target="tpu_custom_call", output_to_operand_aliasing={{3}: (11, {})} | custom-call | flops 19327352832 | bytes 20971520 | tf_op jit(solution)/shard_map/experts/pallas_call | solution.py:556
  139.0 2.5 collective-permute-start.5
  142.5 26.8 %experts.5 = (bf16[512,1024]{1,0:T(8,128)(2,1)}, bf16[528,1024]{1,0:T(8,128)(2,1)}, f32[16,512]{1,0:T(8,128)}, bf16[8,4,288,128]{3,2,1,0:T(8,128)(2,1)}) custom-call(s32[6]{0:T(128)} %get-tuple-element.145.scalars, bf16[512,1024]{1,0:T(8,128)(2,1)} %copy-done.21, ...), custom_call_target="tpu_custom_call", output_to_operand_aliasing={{3}: (11, {})} | custom-call | flops 19327352832 | bytes 20971520 | tf_op jit(solution)/shard_map/experts/pallas_call | solution.py:556
  169.5 26.9 %experts.6 = (bf16[512,1024]{1,0:T(8,128)(2,1)}, bf16[528,1024]{1,0:T(8,128)(2,1)}, f32[16,512]{1,0:T(8,128)}, bf16[8,4,288,128]{3,2,1,0:T(8,128)(2,1)}) custom-call(s32[6]{0:T(128)} %get-tuple-element.143.scalars, bf16[512,1024]{1,0:T(8,128)(2,1)} %collective-permute-done.5.x, ...), custom_call_target="tpu_custom_call", output_to_operand_aliasing={{3}: (11, {})} | custom-call | flops 19327352832 | bytes 20971520 | tf_op jit(solution)/shard_map/experts/pallas_call | solution.py:556
  196.4 1.4 collective-permute-start.8
  197.8 1.8 collective-permute-start.9
  199.6 1.0 copy-done.24
  200.6 26.8 %experts.7 = (bf16[512,1024]{1,0:T(8,128)(2,1)}, bf16[528,1024]{1,0:T(8,128)(2,1)}, f32[16,512]{1,0:T(8,128)}, bf16[8,4,288,128]{3,2,1,0:T(8,128)(2,1)}) custom-call(s32[6]{0:T(128)} %get-tuple-element.144.scalars, bf16[512,1024]{1,0:T(8,128)(2,1)} %copy-done.24, ...), custom_call_target="tpu_custom_call", output_to_operand_aliasing={{3}: (11, {})} | custom-call | flops 19327352832 | bytes 20971520 | tf_op jit(solution)/shard_map/experts/pallas_call | solution.py:556
  227.4 3.6 all-to-all-start.1
  231.1 15.2 %collective-permute-done.9 = bf16[528,1024]{1,0:T(8,128)(2,1)} collective-permute-done((bf16[528,1024]{1,0:T(8,128)(2,1)}, bf16[528,1024]{1,0:T(8,128)(2,1)}, u32[]{:S(2)}, u32[]{:S(2)}) %collective-permute-start.9) | collective-permute-done | bytes 1081376 | tf_op jit(solution)/shard_map/ppermute | solution.py:1154
  246.3 3.0 add_convert_fusion.1
  250.0 25.9 %collective-permute-done.10 = bf16[528,1024]{1,0:T(8,128)(2,1)} collective-permute-done((bf16[528,1024]{1,0:T(8,128)(2,1)}, bf16[528,1024]{1,0:T(8,128)(2,1)}, u32[]{:S(2)}, u32[]{:S(2)}) %collective-permute-start.10) | collective-permute-done | bytes 1081376 | tf_op jit(solution)/shard_map/ppermute | solution.py:1165
  276.0 2.7 add_convert_fusion
  278.6 1.4 copy-done.2
  280.0 3.6 sum_experts.1
  283.7 1.6 add_convert_fusion.4
  285.3 23.9 %collective-permute-done.11.refs_13_.refs_16_.refs_17_ = bf16[528,1024]{1,0:T(8,128)(2,1)S(1)} collective-permute-done((bf16[528,1024]{1,0:T(8,128)(2,1)S(1)}, bf16[528,1024]{1,0:T(8,128)(2,1)S(1)}, u32[]{:S(2)}, u32[]{:S(2)}) %collective-permute-start.11) | collective-permute-done | bytes 1081376 | tf_op jit(solution)/shard_map/ppermute | solution.py:1165
  310.2 9.5 %open_back.1 = (f32[512,1024]{1,0:T(8,128)}, bf16[512,1024]{1,0:T(8,128)(2,1)}, f32[64,1024]{1,0:T(8,128)}, f32[64,1024]{1,0:T(8,128)}) custom-call(s32[8]{0:T(128)} %broadcast_xor_fusion.order.refs_0_, bf16[512,1024]{1,0:T(8,128)(2,1)} %refs_1_.1, f32[512,1024]{1,0:T(8,128)} %get-tuple-element.87.refs_2_, bf16[1,1024]{1,0:T(2,128)(2,1)} %reshape.90.gain.refs_3_, ...), custom_call_target="tpu_custom_call" | custom-call | flops 1073741824 | bytes 14680064 | tf_op jit(solution)/shard_map/open_back/pallas_call | solution.py:709
  319.7 19.7 %attend_back.1 = (bf16[512,1024]{1,0:T(8,128)(2,1)}, bf16[512,512]{1,0:T(8,128)(2,1)}, bf16[512,512]{1,0:T(8,128)(2,1)}) custom-call(s32[1]{0:T(128)} %dynamic_slice.15.scalars, bf16[512,2048]{1,0:T(8,128)(2,1)} %get-tuple-element.83.query.key.value, bf16[512,2048]{1,0:T(8,128)(2,1)} %get-tuple-element.83.query.key.value, ...), custom_call_target="tpu_custom_call" | custom-call | flops 5368709120 | bytes 8388608 | tf_op jit(solution)/shard_map/attend_back/pallas_call | solution.py:303
  339.5 1.4 add_convert_fusion.3
  340.8 4.5 %adapters_back.1 = (bf16[512,64]{1,0:T(8,128)(2,1)}, bf16[32,16,256]{2,1,0:T(8,128)(2,1)}) custom-call(bf16[512,1024]{1,0:T(8,128)(2,1)} %get-tuple-element.124.grad_query, bf16[512,512]{1,0:T(8,128)(2,1)} %get-tuple-element.125.grad_key, bf16[512,512]{1,0:T(8,128)(2,1)} %get-tuple-element.126.grad_value, bf16[512,64]{1,0:T(8,128)(2,1)} %get-tuple-element.127.low, ...), custom_call_target="tpu_custom_call" | custom-call | flops 1610612736 | bytes 4194304 | tf_op jit(solution)/shard_map/adapters_back/pallas_call | solution.py:809
  345.3 5.0 %all-to-all-start.2 = ((bf16[32,16,256]{2,1,0:T(8,128)(2,1)}), bf16[32,16,256]{2,1,0:T(8,128)(2,1)S(1)}, u32[]{:S(2)}, u32[]{:S(2)}) async-start(bf16[32,16,256]{2,1,0:T(8,128)(2,1)} %get-tuple-element.133), calls=%async_computation.2 | async-start | bytes 524288 | tf_op jit(solution)/shard_map/all_to_all | solution.py:1192
  350.4 8.7 %input_back.1 = bf16[512,1024]{1,0:T(8,128)(2,1)} custom-call(s32[8]{0:T(128)} %broadcast_xor_fusion.order.refs_0_, bf16[512,1024]{1,0:T(8,128)(2,1)} %get-tuple-element.124.grad_query, bf16[512,512]{1,0:T(8,128)(2,1)} %get-tuple-element.125.grad_key, bf16[512,512]{1,0:T(8,128)(2,1)} %get-tuple-element.126.grad_value, ...), custom_call_target="tpu_custom_call" | custom-call | flops 2147483648 | bytes 12582912 | tf_op jit(solution)/shard_map/input_back/pallas_call | solution.py:854
  359.1 11.3 %all-to-all-done.2.pieces = bf16[32,16,256]{2,1,0:T(8,128)(2,1)S(1)} async-done(((bf16[32,16,256]{2,1,0:T(8,128)(2,1)}), bf16[32,16,256]{2,1,0:T(8,128)(2,1)S(1)}, u32[]{:S(2)}, u32[]{:S(2)}) %all-to-all-start.2) | async-done | bytes 262176 | tf_op jit(solution)/shard_map/all_to_all | solution.py:1192
  371.1 2.0 sum_mixer.1
  373.2 2.7 add_convert_fusion.2
  (107 shorter events, 11.2 us)
Async XLA Ops:
  7.2 29.7 %copy-start.20 = (s32[4]{0:T(128)S(1)}, s32[4]{0:T(128)}, u32[]{:S(2)}) copy-start(s32[4]{0:T(128)} %constant.82) | copy-start | bytes 52
  7.2 29.7 %copy-start.16 = (s32[32]{0:T(128)S(1)}, s32[32]{0:T(128)}, u32[]{:S(2)}) copy-start(s32[32]{0:T(128)} %ids.1) | copy-start | bytes 388
  7.2 29.8 %copy-start.13 = (bf16[8,16,256]{2,1,0:T(8,128)(2,1)S(1)}, bf16[8,16,256]{2,1,0:T(8,128)(2,1)}, u32[]{:S(2)}) copy-start(bf16[8,16,256]{2,1,0:T(8,128)(2,1)} %param.36) | copy-start | bytes 196612
  7.2 29.8 %copy-start.11 = (bf16[4,8,128,16]{2,3,1,0:T(8,128)(2,1)S(1)}, bf16[4,8,128,16]{2,3,1,0:T(8,128)(2,1)}, u32[]{:S(2)}) copy-start(bf16[4,8,128,16]{2,3,1,0:T(8,128)(2,1)} %param.35) | copy-start | bytes 393220
  7.2 30.1 %copy-start.14 = (bf16[8,16,128]{2,1,0:T(8,128)(2,1)S(1)}, bf16[8,16,128]{2,1,0:T(8,128)(2,1)}, u32[]{:S(2)}) copy-start(bf16[8,16,128]{2,1,0:T(8,128)(2,1)} %param.37) | copy-start | bytes 98308
  7.2 134.2 %all-gather.2.cloned.1.call-start = ((), (), s32[]{:S(2)}) async-start(), calls=%async_computation.3 | async-start | bytes 5242880 | tf_op jit(solution)/shard_map/all_gather | solution.py:1113
  32.2 11.3 %copy-start.17 = (bf16[1024]{0:T(1024)(128)(2,1)S(1)}, bf16[1024]{0:T(1024)(128)(2,1)}, u32[]{:S(2)}) copy-start(bf16[1024]{0:T(1024)(128)(2,1)} %param.28) | copy-start | bytes 6148
  32.2 11.9 %copy-start.18 = (bf16[1024]{0:T(1024)(128)(2,1)S(1)}, bf16[1024]{0:T(1024)(128)(2,1)}, u32[]{:S(2)}) copy-start(bf16[1024]{0:T(1024)(128)(2,1)} %param.29) | copy-start | bytes 6148
  32.3 12.6 %copy-start.25 = (s32[32]{0:T(128)S(1)}, s32[32]{0:T(128)}, u32[]{:S(2)}) copy-start(s32[32]{0:T(128)} %param.25) | copy-start | bytes 388
  32.3 13.8 %copy-start.15 = (bf16[1024,16]{0,1:T(8,128)(2,1)S(1)}, bf16[1024,16]{0,1:T(8,128)(2,1)}, u32[]{:S(2)}) copy-start(bf16[1024,16]{0,1:T(8,128)(2,1)} %param.32) | copy-start | bytes 98308
  32.3 28.1 %collective-permute-start.1 = (bf16[128,3072]{1,0:T(8,128)(2,1)}, bf16[128,3072]{1,0:T(8,128)(2,1)}, u32[]{:S(2)}, u32[]{:S(2)}) collective-permute-start(bf16[128,3072]{1,0:T(8,128)(2,1)} %pack.1), channel_id=1, source_target_pairs={{0,16},{4,20},{8,24},{12,28},{16,0},{20,4},{24,8},{28,12},{1,17},{... | collective-permute-start | bytes 2359304 | tf_op jit(solution)/shard_map/ppermute | solution.py:972
  35.3 25.0 %collective-permute-start = (bf16[128,3072]{1,0:T(8,128)(2,1)}, bf16[128,3072]{1,0:T(8,128)(2,1)}, u32[]{:S(2)}, u32[]{:S(2)}) collective-permute-start(bf16[128,3072]{1,0:T(8,128)(2,1)} %pack.1), channel_id=1, source_target_pairs={{0,8},{4,12},{8,0},{12,4},{16,24},{20,28},{24,16},{28,20},{1,9},{5... | collective-permute-start | bytes 2359304 | tf_op jit(solution)/shard_map/ppermute | solution.py:972
  36.9 10.0 %copy-start.19 = (s32[4,1]{1,0:T(4,128)S(1)}, s32[4,1]{1,0:T(4,128)}, u32[]{:S(2)}) copy-start(s32[4,1]{1,0:T(4,128)} %constant.84) | copy-start | bytes 52
  36.9 10.0 %copy-start.26 = (s32[8]{0:T(128)S(1)}, s32[8]{0:T(128)}, u32[]{:S(2)}) copy-start(s32[8]{0:T(128)} %constant.74.clone) | copy-start | bytes 100
  38.6 18.2 %all-to-all-start = ((bf16[8,112,128]{2,1,0:T(8,128)(2,1)}), bf16[8,112,128]{2,1,0:T(8,128)(2,1)S(1)}, u32[]{:S(2)}, u32[]{:S(2)}) async-start(bf16[8,112,128]{2,1,0:T(8,128)(2,1)} %gather_fusion.1), calls=%async_computation | async-start | bytes 458752 | tf_op jit(solution)/shard_map/all_to_all | solution.py:1058
  46.1 20.5 %copy-start.10 = (bf16[16,1024]{1,0:T(8,128)(2,1)}, bf16[16,1024]{1,0:T(8,128)(2,1)S(1)}, u32[]{:S(2)}) copy-start(bf16[16,1024]{1,0:T(8,128)(2,1)S(1)} %fusion.refs_5_) | copy-start | bytes 98308
  62.4 10.7 %collective-permute-start.2 = (bf16[64,3072]{1,0:T(8,128)(2,1)S(1)}, bf16[64,3072]{1,0:T(8,128)(2,1)S(1)}, u32[]{:S(2)}, u32[]{:S(2)}) collective-permute-start(bf16[64,3072]{1,0:T(8,128)(2,1)S(1)} %slice.27), channel_id=1, source_target_pairs={{0,8},{4,12},{8,0},{12,4},{16,24},{20,28},{24,16},{28,20},{1,9},{5... | collective-permute-start | bytes 1179656 | tf_op jit(solution)/shard_map/ppermute | solution.py:972
  64.2 10.3 %collective-permute-start.3 = (bf16[64,3072]{1,0:T(8,128)(2,1)S(1)}, bf16[64,3072]{1,0:T(8,128)(2,1)S(1)}, u32[]{:S(2)}, u32[]{:S(2)}) collective-permute-start(bf16[64,3072]{1,0:T(8,128)(2,1)S(1)} %slice.28), channel_id=1, source_target_pairs={{0,16},{4,20},{8,24},{12,28},{16,0},{20,4},{24,8},{28,12},{1,17},{... | collective-permute-start | bytes 1179656 | tf_op jit(solution)/shard_map/ppermute | solution.py:972
  67.7 6.9 %copy-start.12 = (s32[2048,8]{0,1:T(8,128)S(1)}, s32[2048,8]{0,1:T(8,128)}, u32[]{:S(2)}) copy-start(s32[2048,8]{0,1:T(8,128)} %param.27) | copy-start | bytes 196612
  74.6 5.9 %copy-start = (bf16[512,3072]{1,0:T(8,128)(2,1)}, bf16[512,3072]{1,0:T(8,128)(2,1)S(1)}, u32[]{:S(2)}) copy-start(bf16[512,3072]{1,0:T(8,128)(2,1)S(1)} %constant_dynamic-update-slice_fusion.weight_a.refs_6_) | copy-start | bytes 9437188
  74.6 5.9 %collective-permute-start.4 = (bf16[512,3072]{1,0:T(8,128)(2,1)S(1)}, bf16[512,3072]{1,0:T(8,128)(2,1)}, u32[]{:S(2)}, u32[]{:S(2)}) collective-permute-start(bf16[512,3072]{1,0:T(8,128)(2,1)S(1)} %constant_dynamic-update-slice_fusion.weight_a.refs_6_), channel_id=1, source_target_pairs={{0,4},{4,0},{8,12},{12,8},{16,20},{20,16},{24,28},{28,24},{1,5},{5... | collective-permute-start | bytes 9437192 | tf_op jit(solution)/shard_map/ppermute | solution.py:972
  109.4 32.0 %collective-permute-start.6 = (bf16[512,1024]{1,0:T(8,128)(2,1)}, bf16[512,1024]{1,0:T(8,128)(2,1)S(1)}, u32[]{:S(2)}, u32[]{:S(2)}) collective-permute-start(bf16[512,1024]{1,0:T(8,128)(2,1)} %get-tuple-element.93.x), channel_id=1, source_target_pairs={{0,1},{1,2},{2,3},{3,0},{4,5},{5,6},{6,7},{7,4},{8,9},{9,10},{10,1... | collective-permute-start | bytes 3145736 | tf_op jit(solution)/shard_map/ppermute | solution.py:1124
  111.5 27.5 %copy-start.23 = (bf16[512,1024]{1,0:T(8,128)(2,1)S(1)}, bf16[512,1024]{1,0:T(8,128)(2,1)}, u32[]{:S(2)}) copy-start(bf16[512,1024]{1,0:T(8,128)(2,1)} %get-tuple-element.93.x) | copy-start | bytes 3145732
  139.0 30.5 %collective-permute-start.5 = (bf16[512,1024]{1,0:T(8,128)(2,1)S(1)}, bf16[512,1024]{1,0:T(8,128)(2,1)}, u32[]{:S(2)}, u32[]{:S(2)}) collective-permute-start(bf16[512,1024]{1,0:T(8,128)(2,1)S(1)} %copy-done.23), channel_id=1, source_target_pairs={{0,3},{1,0},{2,1},{3,2},{4,7},{5,4},{6,5},{7,6},{8,11},{9,8},{10,9... | collective-permute-start | bytes 3145736 | tf_op jit(solution)/shard_map/ppermute | solution.py:1147
  141.5 1.0 copy-start.21
  169.3 30.3 %collective-permute-start.7 = (bf16[512,1024]{1,0:T(8,128)(2,1)}, bf16[512,1024]{1,0:T(8,128)(2,1)S(1)}, u32[]{:S(2)}, u32[]{:S(2)}) collective-permute-start(bf16[512,1024]{1,0:T(8,128)(2,1)} %copy-done.21), channel_id=1, source_target_pairs={{0,1},{1,2},{2,3},{3,0},{4,5},{5,6},{6,7},{7,4},{8,9},{9,10},{10,1... | collective-permute-start | bytes 3145736 | tf_op jit(solution)/shard_map/ppermute | solution.py:1150
  169.5 26.9 %copy-start.22 = (bf16[512,1024]{1,0:T(8,128)(2,1)S(1)}, bf16[512,1024]{1,0:T(8,128)(2,1)}, u32[]{:S(2)}) copy-start(bf16[512,1024]{1,0:T(8,128)(2,1)} %get-tuple-element.105) | copy-start | bytes 3145732
  196.4 31.0 %collective-permute-start.8 = (bf16[512,1024]{1,0:T(8,128)(2,1)S(1)}, bf16[512,1024]{1,0:T(8,128)(2,1)}, u32[]{:S(2)}, u32[]{:S(2)}) collective-permute-start(bf16[512,1024]{1,0:T(8,128)(2,1)S(1)} %copy-done.22), channel_id=1, source_target_pairs={{0,1},{1,2},{2,3},{3,0},{4,5},{5,6},{6,7},{7,4},{8,9},{9,10},{10,1... | collective-permute-start | bytes 3145736 | tf_op jit(solution)/shard_map/ppermute | solution.py:1155
  197.8 48.5 %collective-permute-start.9 = (bf16[528,1024]{1,0:T(8,128)(2,1)}, bf16[528,1024]{1,0:T(8,128)(2,1)}, u32[]{:S(2)}, u32[]{:S(2)}) collective-permute-start(bf16[528,1024]{1,0:T(8,128)(2,1)} %get-tuple-element.109), channel_id=1, source_target_pairs={{0,1},{1,2},{2,3},{3,0},{4,5},{5,6},{6,7},{7,4},{8,9},{9,10},{10,1... | collective-permute-start | bytes 3244040 | tf_op jit(solution)/shard_map/ppermute | solution.py:1154
  199.6 1.0 copy-start.24
  227.4 51.2 %all-to-all-start.1 = ((bf16[8,4,288,128]{3,2,1,0:T(8,128)(2,1)}), bf16[8,4,288,128]{3,2,1,0:T(8,128)(2,1)S(1)}, u32[]{:S(2)}, u32[]{:S(2)}) async-start(bf16[8,4,288,128]{3,2,1,0:T(8,128)(2,1)} %get-tuple-element.111), calls=%async_computation.1 | async-start | bytes 4718592 | tf_op jit(solution)/shard_map/all_to_all | solution.py:1161
  231.1 44.9 %copy-start.4 = (bf16[528,1024]{1,0:T(8,128)(2,1)S(1)}, bf16[528,1024]{1,0:T(8,128)(2,1)}, u32[]{:S(2)}) copy-start(bf16[528,1024]{1,0:T(8,128)(2,1)} %get-tuple-element.107) | copy-start | bytes 3244036
  249.3 26.7 %collective-permute-start.10 = (bf16[528,1024]{1,0:T(8,128)(2,1)}, bf16[528,1024]{1,0:T(8,128)(2,1)}, u32[]{:S(2)}, u32[]{:S(2)}) collective-permute-start(bf16[528,1024]{1,0:T(8,128)(2,1)} %add_convert_fusion.1), channel_id=1, source_target_pairs={{0,1},{1,2},{2,3},{3,0},{4,5},{5,6},{6,7},{7,4},{8,9},{9,10},{10,1... | collective-permute-start | bytes 3244040 | tf_op jit(solution)/shard_map/ppermute | solution.py:1165
  278.6 5.0 %copy-start.5 = (bf16[528,1024]{1,0:T(8,128)(2,1)S(1)}, bf16[528,1024]{1,0:T(8,128)(2,1)}, u32[]{:S(2)}) copy-start(bf16[528,1024]{1,0:T(8,128)(2,1)} %add_convert_fusion) | copy-start | bytes 3244036
  278.6 1.4 copy-start.2
  278.6 5.0 %copy-start.8 = (bf16[512,1024]{1,0:T(8,128)(2,1)S(1)}, bf16[512,1024]{1,0:T(8,128)(2,1)}, u32[]{:S(2)}) copy-start(bf16[512,1024]{1,0:T(8,128)(2,1)} %get-tuple-element.103) | copy-start | bytes 3145732
  283.6 25.5 %collective-permute-start.11 = (bf16[528,1024]{1,0:T(8,128)(2,1)S(1)}, bf16[528,1024]{1,0:T(8,128)(2,1)S(1)}, u32[]{:S(2)}, u32[]{:S(2)}) collective-permute-start(bf16[528,1024]{1,0:T(8,128)(2,1)S(1)} %copy-done.5), channel_id=1, source_target_pairs={{0,1},{1,2},{2,3},{3,0},{4,5},{5,6},{6,7},{7,4},{8,9},{9,10},{10,1... | collective-permute-start | bytes 3244040 | tf_op jit(solution)/shard_map/ppermute | solution.py:1165
  309.2 1.0 copy-start.1
  309.2 30.3 %collective-permute-start.12 = (bf16[512,1024]{1,0:T(8,128)(2,1)S(1)}, bf16[512,1024]{1,0:T(8,128)(2,1)S(1)}, u32[]{:S(2)}, u32[]{:S(2)}) collective-permute-start(bf16[512,1024]{1,0:T(8,128)(2,1)S(1)} %add_convert_fusion.4), channel_id=1, source_target_pairs={{0,1},{1,2},{2,3},{3,0},{4,5},{5,6},{6,7},{7,4},{8,9},{9,10},{10,1... | collective-permute-start | bytes 3145736 | tf_op jit(solution)/shard_map/ppermute | solution.py:1169
  319.7 19.7 %copy-start.7 = (bf16[512,1024]{1,0:T(8,128)(2,1)S(1)}, bf16[512,1024]{1,0:T(8,128)(2,1)}, u32[]{:S(2)}) copy-start(bf16[512,1024]{1,0:T(8,128)(2,1)} %get-tuple-element.97) | copy-start | bytes 3145732
  340.8 32.3 %collective-permute-start.13 = (bf16[512,1024]{1,0:T(8,128)(2,1)}, bf16[512,1024]{1,0:T(8,128)(2,1)}, u32[]{:S(2)}, u32[]{:S(2)}) collective-permute-start(bf16[512,1024]{1,0:T(8,128)(2,1)} %add_convert_fusion.3), channel_id=1, source_target_pairs={{0,1},{1,2},{2,3},{3,0},{4,5},{5,6},{6,7},{7,4},{8,9},{9,10},{10,1... | collective-permute-start | bytes 3145736 | tf_op jit(solution)/shard_map/ppermute | solution.py:1188
  345.3 25.1 %all-to-all-start.2 = ((bf16[32,16,256]{2,1,0:T(8,128)(2,1)}), bf16[32,16,256]{2,1,0:T(8,128)(2,1)S(1)}, u32[]{:S(2)}, u32[]{:S(2)}) async-start(bf16[32,16,256]{2,1,0:T(8,128)(2,1)} %get-tuple-element.133), calls=%async_computation.2 | async-start | bytes 524288 | tf_op jit(solution)/shard_map/all_to_all | solution.py:1192
  350.3 22.8 %copy-start.3 = (f32[512,1024]{1,0:T(8,128)S(1)}, f32[512,1024]{1,0:T(8,128)}, u32[]{:S(2)}) copy-start(f32[512,1024]{1,0:T(8,128)} %get-tuple-element.87.refs_2_) | copy-start | bytes 6291460
  350.3 22.8 %copy-start.6 = (bf16[512,1024]{1,0:T(8,128)(2,1)S(1)}, bf16[512,1024]{1,0:T(8,128)(2,1)}, u32[]{:S(2)}) copy-start(bf16[512,1024]{1,0:T(8,128)(2,1)} %get-tuple-element.91) | copy-start | bytes 3145732
  370.4 0.7 copy-start.9
Sparse Core Ops, SparseCore 0:
  37.0 81.7 all-gather.1

commit v6 on v4

--- a/solution.py
+++ b/solution.py
@@ -439,10 +439,14 @@
     @pl.when(expert == 0)
     def _():
         logits = nt(x[...], router[...])
+        experts = gates_out.shape[0]
         lane = lanes_of(logits.shape)
-        chosen = lane == routes[:, 0:1]
+        name = lane + scalars[4]
+        name = jnp.where(name >= experts, name - experts, name)
+        name = jnp.where(lane < experts, name, -1)
+        chosen = name == routes[:, 0:1]
         for k in range(1, TOP):
-            chosen = chosen | (lane == routes[:, k : k + 1])
+            chosen = chosen | (name == routes[:, k : k + 1])
         top = jnp.max(jnp.where(chosen, logits, -1e30), -1, keepdims=True)
         shifted = jnp.where(chosen, jnp.exp(jnp.where(chosen, logits - top, 0.0)), 0.0)
         weights = shifted / jnp.sum(shifted, -1, keepdims=True)
@@ -557,7 +561,7 @@
             grid=(local,),
             in_specs=[
                 full((rows, MODEL_WIDTH)),
-                pl.BlockSpec((rows, MODEL_WIDTH), lambda e, s: (s[4], 0)),
+                pl.BlockSpec((rows, MODEL_WIDTH), lambda e, s: (s[5], 0)),
                 pl.BlockSpec((rows, TOP), lambda e, s: (s[0], 0)),
                 full((128, MODEL_WIDTH)),
                 pl.BlockSpec((1, MODEL_WIDTH, 2 * H), lambda e, s: (e, 0, 0)),
@@ -604,6 +608,19 @@
             bytes_accessed=20 << 20,
         ),
     )(scalars, x, cot, routes, router, w_in, w_down, a_in, b_in, a_down, b_down, *kept)
+
+
+def pack_kernel(left, right, both):
+    both[:, : left.shape[1]] = left[...]
+    both[:, left.shape[1] :] = right[...]
+
+
+def pack(left, right):
+    return pl.pallas_call(
+        pack_kernel,
+        out_shape=jax.ShapeDtypeStruct((left.shape[0], left.shape[1] + right.shape[1]), left.dtype),
+        name="pack",
+    )(left, right)
 
 
 def open_back_kernel(count, order, cot, mid, gain, gates, router, weight_a, weight_b, low_map, up_map, low, att, *rest):
@@ -1021,49 +1038,11 @@
     adapters = jnp.concatenate([low_turned, up_turned, attention_output_upmap], 1)[mine]
     adapters = lax.all_to_all(adapters, "dp", 0, 0, tiled=True)
     order = order_of(row)
-    both = jnp.concatenate([query_key_value_weight, w_out], 1)
-    if owners == BLOCKS:
-        pair = both_neighbours(both)
-        near = jnp.concatenate([both, *pair, *across(pair)], 0)
-        near, adapters = tied(near, adapters)
-        weights = near, swap(near, 1)
-    else:
-        whole = lax.all_gather(both, "dp", axis=0, tiled=True)
-        weights = whole, whole
-
-    low_map = adapters[:, : 4 * R].transpose(1, 0, 2).reshape(4 * R, MODEL_WIDTH)
-    up = (
-        adapters[:, 4 * R : 6 * R]
-        .reshape(owners, 2, R, width)
-        .transpose(2, 0, 1, 3)
-        .reshape(R, QKV)
-    )
-    up_out = adapters[:, 6 * R :].transpose(1, 0, 2).reshape(R, MODEL_WIDTH)
-    column = jnp.arange(QKV, dtype=jnp.int32)
-    part = jnp.where(column < QD, 0, jnp.where(column < QD + KD, 1, 2))
-    up_map = jnp.where(
-        part[None, None, :] == jnp.arange(4, dtype=jnp.int32)[:, None, None], up[None], 0
-    ).reshape(4 * R, QKV)
-    up_out_map = jnp.concatenate([jnp.zeros((3 * R, MODEL_WIDTH), bf16), up_out], 0)
-
-    cos, sin = rope_tables(rows)
-
-    cots = lax.all_gather(cotangent, "expert", axis=0, tiled=True)
-
-    qkv, low, normed_in = project(order, hidden, attn_gain, weights, low_map, up_map, cos, sin)
-    attended, lse = attend(length, qkv)
-    mid, normed_mid, low_out = close_mixer(
-        order, attended, hidden, ffn_gain, weights, low_map, up_out_map
-    )
-
     first = place * local
-    routes_here = (routes - first + experts) % experts
     router = jnp.roll(w_router.T, -first, axis=0)
     router_wide = jnp.concatenate(
         [router, jnp.zeros((128 - experts, MODEL_WIDTH), router.dtype)], 0
     )
-    a_in = expert_gate_up_lowmap.transpose(0, 1, 3, 2)
-    a_down = expert_down_lowmap.transpose(0, 1, 3, 2)
 
     offsets = [0, 1] + [groups - 1] * (groups > 2) + list(range(2, groups - 1))
     offset = jnp.array(offsets, jnp.int32)
@@ -1076,10 +1055,52 @@
             lax.dynamic_slice(tags, (row, 0), (1, groups))[0],
             offset * local,
             slot,
+            jnp.full((groups,), first, jnp.int32),
             jnp.where(slot == 0, 0, source),
         ],
         1,
     )
+
+    both = pack(query_key_value_weight, w_out)
+    if owners == BLOCKS:
+        pair = both_neighbours(both)
+        pair, order, router, router_wide, table, tags, attn_gain, ffn_gain, length = tied(
+            pair, order, router, router_wide, table, tags, attn_gain, ffn_gain, length
+        )
+        near = jnp.concatenate([both, *pair, *across(pair)], 0)
+        near, adapters = tied(near, adapters)
+        weights = near, swap(near, 1)
+    else:
+        whole = lax.all_gather(both, "dp", axis=0, tiled=True)
+        weights = whole, whole
+
+    low_map = adapters[:, : 4 * R].transpose(1, 0, 2).reshape(4 * R, MODEL_WIDTH)
+    up = (
+        adapters[:, 4 * R : 6 * R]
+        .reshape(owners, 2, R, width)
+        .transpose(2, 0, 1, 3)
+        .reshape(R, QKV)
+    )
+    up_out = adapters[:, 6 * R :].transpose(1, 0, 2).reshape(R, MODEL_WIDTH)
+    column = jnp.arange(QKV, dtype=jnp.int32)
+    part = jnp.where(column < QD, 0, jnp.where(column < QD + KD, 1, 2))
+    up_map = jnp.where(
+        part[None, None, :] == jnp.arange(4, dtype=jnp.int32)[:, None, None], up[None], 0
+    ).reshape(4 * R, QKV)
+    up_out_map = jnp.concatenate([jnp.zeros((3 * R, MODEL_WIDTH), bf16), up_out], 0)
+
+    cos, sin = rope_tables(rows)
+
+    cots = lax.all_gather(cotangent, "expert", axis=0, tiled=True)
+
+    qkv, low, normed_in = project(order, hidden, attn_gain, weights, low_map, up_map, cos, sin)
+    attended, lse = attend(length, qkv)
+    mid, normed_mid, low_out = close_mixer(
+        order, attended, hidden, ffn_gain, weights, low_map, up_out_map
+    )
+
+    a_in = expert_gate_up_lowmap.transpose(0, 1, 3, 2)
+    a_down = expert_down_lowmap.transpose(0, 1, 3, 2)
 
     xs = {0: normed_mid, 1: lax.ppermute(normed_mid, "expert", forward)}
     packed = None
@@ -1089,7 +1110,7 @@
             table[at],
             xs[offset],
             cotangent if at == 0 else cots,
-            routes_here,
+            routes,
             router_wide,
             w_gate_up,
             w_down,

time: 363 us -> 358 us (0.986)
  other arithmetic: 17 us -> 11 us
  waiting for transfers between devices: 88.5 us -> 94.5 us
  local copies, waits for them, and re-layouts: 24 us -> 20.1 us
    ppermute x1, waiting for transfers between devices: 0.01 us -> 5.3 us  [on_device(): xs = {0: normed_mid, 1: lax.ppermute(normed_mid, 'expert', forward)}]
    unnamed x51 -> x50, local copies, waits for them, and re-layouts: 10.4 us -> 10.3 us
  transfers between devices with their start and end apart: 17 -> 17, of which waited for: 8 -> 11; matrix products, arithmetic and copies ran while one was open for 7% -> 6% of each run, Pallas kernels for 52% -> 52%
where the time goes in v6:
time: 358 us; the launch traced here: 352 us
  Pallas kernels  187 us (52%)
  waiting for transfers between devices  94.5 us (26%)
  starting transfers between devices  24.9 us (7%)
  local copies, waits for them, and re-layouts  20.1 us (6%)
  between operations  15 us (4%)
  other arithmetic  11 us (3%)
    pallas_call x4, Pallas kernels, run_experts(): pl.pallas_call(expert_kernel, grid_spec=pltpu.PrefetchScalarGridSpec(num_...  108 us
    ppermute x2, waiting for transfers between devices, on_device(): grad_far = lax.ppermute(grad_part, 'expert', forward)  37.2 us
    pallas_call x1, Pallas kernels, attend_back(): pl.pallas_call(attend_back_kernel, grid_spec=pltpu.PrefetchScalarGridSpec...  19.7 us
    ppermute x1, waiting for transfers between devices, on_device(): lax.ppermute(first_sums if groups > 2 else ran[1], 'expert', forward)  18.5 us
    ppermute x5, waiting for transfers between devices, swap(): return lax.ppermute(value, 'dp', [(at, at ^ bit) for at in range(BLOCKS)])  15 us
    pallas_call x1, Pallas kernels, attend(): pl.pallas_call(attend_kernel, grid_spec=pltpu.PrefetchScalarGridSpec(num_...  12.7 us
    all_to_all x1, waiting for transfers between devices, on_device(): packed = lax.all_to_all(packed, ('dp', 'expert'), 0, 0, tiled=True)  11.2 us
    pallas_call x1, Pallas kernels, project(): pl.pallas_call(project_kernel, grid_spec=pltpu.PrefetchScalarGridSpec(num...  10.4 us
  transfers between devices with their start and end apart: 17, of which 11 were waited for; matrix products, arithmetic and copies ran while one was open for 6% of the time, Pallas kernels for 52%

profile of v6, /device:TPU:0, one launch (start us, length us, event | category | flops | bytes accessed | tf_op | source)
XLA Modules:
  0.0 352.2 jit_solution(6748233342803071429)
XLA Ops:
  7.3 2.1 pack.1
  9.4 3.0 collective-permute-start.1
  12.4 1.5 collective-permute-start
  14.4 1.3 gather_fusion.1
  15.6 3.4 all-to-all-start
  23.3 1.2 constant_dynamic-update-slice_fusion.4
  24.6 6.3 %collective-permute-done.1 = bf16[128,3072]{1,0:T(8,128)(2,1)} collective-permute-done((bf16[128,3072]{1,0:T(8,128)(2,1)}, bf16[128,3072]{1,0:T(8,128)(2,1)}, u32[]{:S(2)}, u32[]{:S(2)}) %collective-permute-start.1) | collective-permute-done | bytes 786464 | tf_op jit(solution)/shard_map/ppermute | solution.py:953
  30.9 2.1 collective-permute-done
  33.0 1.0 slice.49
  34.0 1.0 slice.48
  35.0 1.6 collective-permute-start.2
  37.1 1.2 constant_dynamic-update-slice_fusion.3
  38.3 1.2 constant_dynamic-update-slice_fusion.2
  39.5 4.1 %collective-permute-done.2 = bf16[64,3072]{1,0:T(8,128)(2,1)S(1)} collective-permute-done((bf16[64,3072]{1,0:T(8,128)(2,1)S(1)}, bf16[64,3072]{1,0:T(8,128)(2,1)S(1)}, u32[]{:S(2)}, u32[]{:S(2)}) %collective-permute-start.2) | collective-permute-done | bytes 393248 | tf_op jit(solution)/shard_map/ppermute | solution.py:953
  43.6 1.2 collective-permute-done.3
  44.9 1.7 copy.63.routes
  49.4 1.3 collective-permute-done.4.weight_b.refs_7_
  50.7 10.4 %project.1 = (bf16[512,2048]{1,0:T(8,128)(2,1)}, bf16[512,64]{1,0:T(8,128)(2,1)}, bf16[512,1024]{1,0:T(8,128)(2,1)}) custom-call(s32[8]{0:T(128)} %broadcast_xor_fusion.order.refs_0_, bf16[512,1024]{1,0:T(8,128)(2,1)} %hid.5, bf16[1,1024]{1,0:T(2,128)(2,1)} %reshape.89.gain, bf16[512,3072]{1,0:T(8,128)(2,1)} %copy-done, ...), custom_call_target="tpu_custom_call" | custom-call | flops 2147483648 | bytes 8388608 | tf_op jit(solution)/shard_map/project/pallas_call | solution.py:141
  61.1 12.7 %attend.1 = (bf16[512,1024]{1,0:T(8,128)(2,1)}, f32[8,2,512]{2,1,0:T(2,128)}) custom-call(s32[1]{0:T(128)} %dynamic_slice.15.scalars, bf16[512,2048]{1,0:T(8,128)(2,1)} %get-tuple-element.73.query.key.value, bf16[512,2048]{1,0:T(8,128)(2,1)} %get-tuple-element.73.query.key.value, bf16[512,2048]{1,0:T(8,128)(2,1)} %get-tuple-element.73.query.key.value), custom_call_target="tpu_custom_call" | custom-call | flops 2147483648 | bytes 4194304 | tf_op jit(solution)/shard_map/attend/pallas_call | solution.py:223
  73.8 6.0 %close_mixer.1 = (f32[512,1024]{1,0:T(8,128)}, bf16[512,1024]{1,0:T(8,128)(2,1)}, bf16[512,64]{1,0:T(8,128)(2,1)}) custom-call(s32[8]{0:T(128)} %broadcast_xor_fusion.order.refs_0_, bf16[512,1024]{1,0:T(8,128)(2,1)} %get-tuple-element.74.att.refs_11_, bf16[512,1024]{1,0:T(8,128)(2,1)} %hid.5, bf16[1,1024]{1,0:T(2,128)(2,1)} %reshape.90.gain.refs_3_, ...), custom_call_target="tpu_custom_call" | custom-call | flops 1073741824 | bytes 8388608 | tf_op jit(solution)/shard_map/close_mixer/pallas_call | solution.py:356
  79.8 2.1 collective-permute-start.6
  81.9 27.2 %experts.4 = (bf16[1040,1024]{1,0:T(8,128)(2,1)}, f32[16,512]{1,0:T(8,128)}, bf16[8,4,288,128]{3,2,1,0:T(8,128)(2,1)}) custom-call(s32[6]{0:T(128)} %get-tuple-element.128.scalars, bf16[512,1024]{1,0:T(8,128)(2,1)} %get-tuple-element.82.x, bf16[512,1024]{1,0:T(8,128)(2,1)} %refs_1_.1, s32[2048,8]{1,0:T(8,128)} %copy.63.routes, ...), custom_call_target="tpu_custom_call" | custom-call | flops 19327352832 | bytes 20971520 | tf_op jit(solution)/shard_map/experts/pallas_call | solution.py:557
  109.1 2.4 collective-permute-start.5
  111.5 5.3 %collective-permute-done.6.x = bf16[512,1024]{1,0:T(8,128)(2,1)S(1)} collective-permute-done((bf16[512,1024]{1,0:T(8,128)(2,1)}, bf16[512,1024]{1,0:T(8,128)(2,1)S(1)}, u32[]{:S(2)}, u32[]{:S(2)}) %collective-permute-start.6) | collective-permute-done | bytes 1048608 | tf_op jit(solution)/shard_map/ppermute | solution.py:1105
  116.8 1.0 copy-done.17
  117.8 26.8 %experts.5 = (bf16[1040,1024]{1,0:T(8,128)(2,1)}, f32[16,512]{1,0:T(8,128)}, bf16[8,4,288,128]{3,2,1,0:T(8,128)(2,1)}) custom-call(s32[6]{0:T(128)} %get-tuple-element.126.scalars, bf16[512,1024]{1,0:T(8,128)(2,1)} %copy-done.17, bf16[2048,1024]{1,0:T(8,128)(2,1)} %all-gather.2.cloned.1.call-done.cot, ...), custom_call_target="tpu_custom_call", output_to_operand_aliasing={{2}: (11, {})} | custom-call | flops 19327352832 | bytes 20971520 | tf_op jit(solution)/shard_map/experts/pallas_call | solution.py:557
  144.8 26.8 %experts.6 = (bf16[1040,1024]{1,0:T(8,128)(2,1)}, f32[16,512]{1,0:T(8,128)}, bf16[8,4,288,128]{3,2,1,0:T(8,128)(2,1)}) custom-call(s32[6]{0:T(128)} %get-tuple-element.127.scalars, bf16[512,1024]{1,0:T(8,128)(2,1)} %collective-permute-done.5.x, bf16[2048,1024]{1,0:T(8,128)(2,1)} %all-gather.2.cloned.1.call-done.cot, ...), custom_call_target="tpu_custom_call", output_to_operand_aliasing={{2}: (11, {})} | custom-call | flops 19327352832 | bytes 20971520 | tf_op jit(solution)/shard_map/experts/pallas_call | solution.py:557
  171.9 1.0 copy-done.19
  172.9 26.8 %experts.7 = (bf16[1040,1024]{1,0:T(8,128)(2,1)}, f32[16,512]{1,0:T(8,128)}, bf16[8,4,288,128]{3,2,1,0:T(8,128)(2,1)}) custom-call(s32[6]{0:T(128)} %get-tuple-element.125.scalars, bf16[512,1024]{1,0:T(8,128)(2,1)} %copy-done.19, bf16[2048,1024]{1,0:T(8,128)(2,1)} %all-gather.2.cloned.1.call-done.cot, ...), custom_call_target="tpu_custom_call", output_to_operand_aliasing={{2}: (11, {})} | custom-call | flops 19327352832 | bytes 20971520 | tf_op jit(solution)/shard_map/experts/pallas_call | solution.py:557
  199.7 3.7 %all-to-all-start.1 = ((bf16[8,4,288,128]{3,2,1,0:T(8,128)(2,1)}), bf16[8,4,288,128]{3,2,1,0:T(8,128)(2,1)S(1)}, u32[]{:S(2)}, u32[]{:S(2)}) async-start(bf16[8,4,288,128]{3,2,1,0:T(8,128)(2,1)} %get-tuple-element.94), calls=%async_computation.1 | async-start | bytes 4718592 | tf_op jit(solution)/shard_map/all_to_all | solution.py:1136
  203.4 18.5 %collective-permute-done.8 = bf16[1040,1024]{1,0:T(8,128)(2,1)} collective-permute-done((bf16[1040,1024]{1,0:T(8,128)(2,1)}, bf16[1040,1024]{1,0:T(8,128)(2,1)}, u32[]{:S(2)}, u32[]{:S(2)}) %collective-permute-start.8) | collective-permute-done | bytes 2129952 | tf_op jit(solution)/shard_map/ppermute | solution.py:1141
  221.9 3.0 add_convert_fusion.1
  225.6 7.2 %all-to-all-done.1 = bf16[8,4,288,128]{3,2,1,0:T(8,128)(2,1)S(1)} async-done(((bf16[8,4,288,128]{3,2,1,0:T(8,128)(2,1)}), bf16[8,4,288,128]{3,2,1,0:T(8,128)(2,1)S(1)}, u32[]{:S(2)}, u32[]{:S(2)}) %all-to-all-start.1) | async-done | bytes 2359328 | tf_op jit(solution)/shard_map/all_to_all | solution.py:1136
  232.8 1.4 copy-done.2
  234.2 3.6 %sum_experts.1 = (f32[4,8,32,128]{3,2,1,0:T(8,128)}, f32[4,8,2,16,64]{4,3,2,1,0:T(8,128)}, f32[4,8,16,64]{3,2,1,0:T(8,128)}, f32[4,8,16,128]{3,2,1,0:T(8,128)}) custom-call(s32[32]{0:T(128)} %reshape.97.ids, bf16[32,288,128]{2,1,0:T(8,128)(2,1)} %bitcast.41), custom_call_target="tpu_custom_call" | custom-call | tf_op jit(solution)/shard_map/sum_experts/pallas_call | solution.py:890
  237.8 13.7 %collective-permute-done.9 = bf16[528,1024]{1,0:T(8,128)(2,1)S(1)} collective-permute-done((bf16[528,1024]{1,0:T(8,128)(2,1)}, bf16[528,1024]{1,0:T(8,128)(2,1)S(1)}, u32[]{:S(2)}, u32[]{:S(2)}) %collective-permute-start.9) | collective-permute-done | bytes 1081376 | tf_op jit(solution)/shard_map/ppermute | solution.py:1147
  252.0 1.9 add_convert_fusion.4
  253.9 23.6 %collective-permute-done.10.refs_13_.refs_16_.refs_17_ = bf16[528,1024]{1,0:T(8,128)(2,1)S(1)} collective-permute-done((bf16[528,1024]{1,0:T(8,128)(2,1)S(1)}, bf16[528,1024]{1,0:T(8,128)(2,1)S(1)}, u32[]{:S(2)}, u32[]{:S(2)}) %collective-permute-start.10) | collective-permute-done | bytes 1081376 | tf_op jit(solution)/shard_map/ppermute | solution.py:1147
  277.8 0.8 copy-done.1
  278.6 9.6 %open_back.1 = (f32[512,1024]{1,0:T(8,128)}, bf16[512,1024]{1,0:T(8,128)(2,1)}, f32[64,1024]{1,0:T(8,128)}, f32[64,1024]{1,0:T(8,128)}) custom-call(s32[8]{0:T(128)} %broadcast_xor_fusion.order.refs_0_, bf16[512,1024]{1,0:T(8,128)(2,1)} %refs_1_.1, f32[512,1024]{1,0:T(8,128)} %get-tuple-element.76.refs_2_, bf16[1,1024]{1,0:T(2,128)(2,1)} %reshape.90.gain.refs_3_, ...), custom_call_target="tpu_custom_call" | custom-call | flops 1073741824 | bytes 14680064 | tf_op jit(solution)/shard_map/open_back/pallas_call | solution.py:690
  288.1 19.7 %attend_back.1 = (bf16[512,1024]{1,0:T(8,128)(2,1)}, bf16[512,512]{1,0:T(8,128)(2,1)}, bf16[512,512]{1,0:T(8,128)(2,1)}) custom-call(s32[1]{0:T(128)} %dynamic_slice.15.scalars, bf16[512,2048]{1,0:T(8,128)(2,1)} %get-tuple-element.73.query.key.value, bf16[512,2048]{1,0:T(8,128)(2,1)} %get-tuple-element.73.query.key.value, ...), custom_call_target="tpu_custom_call" | custom-call | flops 5368709120 | bytes 8388608 | tf_op jit(solution)/shard_map/attend_back/pallas_call | solution.py:303
  307.9 1.4 add_convert_fusion.3
  309.2 4.5 %adapters_back.1 = (bf16[512,64]{1,0:T(8,128)(2,1)}, bf16[32,16,256]{2,1,0:T(8,128)(2,1)}) custom-call(bf16[512,1024]{1,0:T(8,128)(2,1)} %get-tuple-element.106.grad_query, bf16[512,512]{1,0:T(8,128)(2,1)} %get-tuple-element.107.grad_key, bf16[512,512]{1,0:T(8,128)(2,1)} %get-tuple-element.108.grad_value, bf16[512,64]{1,0:T(8,128)(2,1)} %get-tuple-element.109.low, ...), custom_call_target="tpu_custom_call" | custom-call | flops 1610612736 | bytes 4194304 | tf_op jit(solution)/shard_map/adapters_back/pallas_call | solution.py:790
  313.7 5.8 %all-to-all-start.2 = ((bf16[32,16,256]{2,1,0:T(8,128)(2,1)}), bf16[32,16,256]{2,1,0:T(8,128)(2,1)S(1)}, u32[]{:S(2)}, u32[]{:S(2)}) async-start(bf16[32,16,256]{2,1,0:T(8,128)(2,1)} %get-tuple-element.115), calls=%async_computation.2 | async-start | bytes 524288 | tf_op jit(solution)/shard_map/all_to_all | solution.py:1174
  319.6 8.6 %input_back.1 = bf16[512,1024]{1,0:T(8,128)(2,1)} custom-call(s32[8]{0:T(128)} %broadcast_xor_fusion.order.refs_0_, bf16[512,1024]{1,0:T(8,128)(2,1)} %get-tuple-element.106.grad_query, bf16[512,512]{1,0:T(8,128)(2,1)} %get-tuple-element.107.grad_key, bf16[512,512]{1,0:T(8,128)(2,1)} %get-tuple-element.108.grad_value, ...), custom_call_target="tpu_custom_call" | custom-call | flops 2147483648 | bytes 12582912 | tf_op jit(solution)/shard_map/input_back/pallas_call | solution.py:835
  328.2 11.2 %all-to-all-done.2.pieces = bf16[32,16,256]{2,1,0:T(8,128)(2,1)S(1)} async-done(((bf16[32,16,256]{2,1,0:T(8,128)(2,1)}), bf16[32,16,256]{2,1,0:T(8,128)(2,1)S(1)}, u32[]{:S(2)}, u32[]{:S(2)}) %all-to-all-start.2) | async-done | bytes 262176 | tf_op jit(solution)/shard_map/all_to_all | solution.py:1174
  340.1 2.0 sum_mixer.1
  342.2 2.7 add_convert_fusion.2
  (94 shorter events, 10.7 us)
Async XLA Ops:
  7.2 6.8 %copy-start.16 = (s32[4]{0:T(128)S(1)}, s32[4]{0:T(128)}, u32[]{:S(2)}) copy-start(s32[4]{0:T(128)} %constant.82) | copy-start | bytes 52
  7.2 6.8 %copy-start.12 = (s32[32]{0:T(128)S(1)}, s32[32]{0:T(128)}, u32[]{:S(2)}) copy-start(s32[32]{0:T(128)} %ids.1) | copy-start | bytes 388
  7.2 6.9 %copy-start.9 = (bf16[8,16,256]{2,1,0:T(8,128)(2,1)S(1)}, bf16[8,16,256]{2,1,0:T(8,128)(2,1)}, u32[]{:S(2)}) copy-start(bf16[8,16,256]{2,1,0:T(8,128)(2,1)} %param.36) | copy-start | bytes 196612
  7.2 6.9 %copy-start.7 = (bf16[4,8,128,16]{2,3,1,0:T(8,128)(2,1)S(1)}, bf16[4,8,128,16]{2,3,1,0:T(8,128)(2,1)}, u32[]{:S(2)}) copy-start(bf16[4,8,128,16]{2,3,1,0:T(8,128)(2,1)} %param.35) | copy-start | bytes 393220
  7.2 7.1 %copy-start.10 = (bf16[8,16,128]{2,1,0:T(8,128)(2,1)S(1)}, bf16[8,16,128]{2,1,0:T(8,128)(2,1)}, u32[]{:S(2)}) copy-start(bf16[8,16,128]{2,1,0:T(8,128)(2,1)} %param.37) | copy-start | bytes 98308
  7.2 12.1 %copy-start.13 = (bf16[1024]{0:T(1024)(128)(2,1)S(1)}, bf16[1024]{0:T(1024)(128)(2,1)}, u32[]{:S(2)}) copy-start(bf16[1024]{0:T(1024)(128)(2,1)} %param.28) | copy-start | bytes 6148
  7.2 12.7 %copy-start.14 = (bf16[1024]{0:T(1024)(128)(2,1)S(1)}, bf16[1024]{0:T(1024)(128)(2,1)}, u32[]{:S(2)}) copy-start(bf16[1024]{0:T(1024)(128)(2,1)} %param.29) | copy-start | bytes 6148
  7.3 13.3 %copy-start.20 = (s32[32]{0:T(128)S(1)}, s32[32]{0:T(128)}, u32[]{:S(2)}) copy-start(s32[32]{0:T(128)} %param.25) | copy-start | bytes 388
  7.3 14.5 %copy-start.11 = (bf16[1024,16]{0,1:T(8,128)(2,1)S(1)}, bf16[1024,16]{0,1:T(8,128)(2,1)}, u32[]{:S(2)}) copy-start(bf16[1024,16]{0,1:T(8,128)(2,1)} %param.32) | copy-start | bytes 98308
  7.3 109.6 %all-gather.2.cloned.1.call-start = ((), (), s32[]{:S(2)}) async-start(), calls=%async_computation.3 | async-start | bytes 5242880 | tf_op jit(solution)/shard_map/all_gather | solution.py:1094
  9.4 13.2 %copy-start.15 = (s32[4,1]{1,0:T(4,128)S(1)}, s32[4,1]{1,0:T(4,128)}, u32[]{:S(2)}) copy-start(s32[4,1]{1,0:T(4,128)} %constant.84) | copy-start | bytes 52
  9.4 13.3 %copy-start.21 = (s32[8]{0:T(128)S(1)}, s32[8]{0:T(128)}, u32[]{:S(2)}) copy-start(s32[8]{0:T(128)} %constant.74.clone) | copy-start | bytes 100
  9.4 21.5 %collective-permute-start.1 = (bf16[128,3072]{1,0:T(8,128)(2,1)}, bf16[128,3072]{1,0:T(8,128)(2,1)}, u32[]{:S(2)}, u32[]{:S(2)}) collective-permute-start(bf16[128,3072]{1,0:T(8,128)(2,1)} %pack.1), channel_id=1, source_target_pairs={{0,16},{4,20},{8,24},{12,28},{16,0},{20,4},{24,8},{28,12},{1,17},{... | collective-permute-start | bytes 2359304 | tf_op jit(solution)/shard_map/ppermute | solution.py:953
  12.4 20.5 %collective-permute-start = (bf16[128,3072]{1,0:T(8,128)(2,1)}, bf16[128,3072]{1,0:T(8,128)(2,1)}, u32[]{:S(2)}, u32[]{:S(2)}) collective-permute-start(bf16[128,3072]{1,0:T(8,128)(2,1)} %pack.1), channel_id=1, source_target_pairs={{0,8},{4,12},{8,0},{12,4},{16,24},{20,28},{24,16},{28,20},{1,9},{5... | collective-permute-start | bytes 2359304 | tf_op jit(solution)/shard_map/ppermute | solution.py:953
  15.6 29.2 %all-to-all-start = ((bf16[8,112,128]{2,1,0:T(8,128)(2,1)}), bf16[8,112,128]{2,1,0:T(8,128)(2,1)S(1)}, u32[]{:S(2)}, u32[]{:S(2)}) async-start(bf16[8,112,128]{2,1,0:T(8,128)(2,1)} %gather_fusion.1), calls=%async_computation | async-start | bytes 458752 | tf_op jit(solution)/shard_map/all_to_all | solution.py:1039
  21.8 16.5 %copy-start.6 = (bf16[16,1024]{1,0:T(8,128)(2,1)}, bf16[16,1024]{1,0:T(8,128)(2,1)S(1)}, u32[]{:S(2)}) copy-start(bf16[16,1024]{1,0:T(8,128)(2,1)S(1)} %fusion.refs_5_) | copy-start | bytes 98308
  35.0 9.9 %copy-start.8 = (s32[2048,8]{0,1:T(8,128)S(1)}, s32[2048,8]{0,1:T(8,128)}, u32[]{:S(2)}) copy-start(s32[2048,8]{0,1:T(8,128)} %param.27) | copy-start | bytes 196612
  35.0 8.5 %collective-permute-start.2 = (bf16[64,3072]{1,0:T(8,128)(2,1)S(1)}, bf16[64,3072]{1,0:T(8,128)(2,1)S(1)}, u32[]{:S(2)}, u32[]{:S(2)}) collective-permute-start(bf16[64,3072]{1,0:T(8,128)(2,1)S(1)} %slice.48), channel_id=1, source_target_pairs={{0,8},{4,12},{8,0},{12,4},{16,24},{20,28},{24,16},{28,20},{1,9},{5... | collective-permute-start | bytes 1179656 | tf_op jit(solution)/shard_map/ppermute | solution.py:953
  36.6 8.2 %collective-permute-start.3 = (bf16[64,3072]{1,0:T(8,128)(2,1)S(1)}, bf16[64,3072]{1,0:T(8,128)(2,1)S(1)}, u32[]{:S(2)}, u32[]{:S(2)}) collective-permute-start(bf16[64,3072]{1,0:T(8,128)(2,1)S(1)} %slice.49), channel_id=1, source_target_pairs={{0,16},{4,20},{8,24},{12,28},{16,0},{20,4},{24,8},{28,12},{1,17},{... | collective-permute-start | bytes 1179656 | tf_op jit(solution)/shard_map/ppermute | solution.py:953
  44.8 5.9 %copy-start = (bf16[512,3072]{1,0:T(8,128)(2,1)}, bf16[512,3072]{1,0:T(8,128)(2,1)S(1)}, u32[]{:S(2)}) copy-start(bf16[512,3072]{1,0:T(8,128)(2,1)S(1)} %constant_dynamic-update-slice_fusion.weight_a.refs_6_) | copy-start | bytes 9437188
  44.9 5.9 %collective-permute-start.4 = (bf16[512,3072]{1,0:T(8,128)(2,1)S(1)}, bf16[512,3072]{1,0:T(8,128)(2,1)}, u32[]{:S(2)}, u32[]{:S(2)}) collective-permute-start(bf16[512,3072]{1,0:T(8,128)(2,1)S(1)} %constant_dynamic-update-slice_fusion.weight_a.refs_6_), channel_id=1, source_target_pairs={{0,4},{4,0},{8,12},{12,8},{16,20},{20,16},{24,28},{28,24},{1,5},{5... | collective-permute-start | bytes 9437192 | tf_op jit(solution)/shard_map/ppermute | solution.py:953
  79.8 37.0 %collective-permute-start.6 = (bf16[512,1024]{1,0:T(8,128)(2,1)}, bf16[512,1024]{1,0:T(8,128)(2,1)S(1)}, u32[]{:S(2)}, u32[]{:S(2)}) collective-permute-start(bf16[512,1024]{1,0:T(8,128)(2,1)} %get-tuple-element.82.x), channel_id=1, source_target_pairs={{0,1},{1,2},{2,3},{3,0},{4,5},{5,6},{6,7},{7,4},{8,9},{9,10},{10,1... | collective-permute-start | bytes 3145736 | tf_op jit(solution)/shard_map/ppermute | solution.py:1105
  81.9 27.2 %copy-start.18 = (bf16[512,1024]{1,0:T(8,128)(2,1)S(1)}, bf16[512,1024]{1,0:T(8,128)(2,1)}, u32[]{:S(2)}) copy-start(bf16[512,1024]{1,0:T(8,128)(2,1)} %get-tuple-element.82.x) | copy-start | bytes 3145732
  109.1 35.7 %collective-permute-start.5 = (bf16[512,1024]{1,0:T(8,128)(2,1)S(1)}, bf16[512,1024]{1,0:T(8,128)(2,1)}, u32[]{:S(2)}, u32[]{:S(2)}) collective-permute-start(bf16[512,1024]{1,0:T(8,128)(2,1)S(1)} %copy-done.18), channel_id=1, source_target_pairs={{0,3},{1,0},{2,1},{3,2},{4,7},{5,4},{6,5},{7,6},{8,11},{9,8},{10,9... | collective-permute-start | bytes 3145736 | tf_op jit(solution)/shard_map/ppermute | solution.py:1129
  116.8 1.0 copy-start.17
  144.6 27.2 %collective-permute-start.7 = (bf16[512,1024]{1,0:T(8,128)(2,1)}, bf16[512,1024]{1,0:T(8,128)(2,1)S(1)}, u32[]{:S(2)}, u32[]{:S(2)}) collective-permute-start(bf16[512,1024]{1,0:T(8,128)(2,1)} %copy-done.17), channel_id=1, source_target_pairs={{0,1},{1,2},{2,3},{3,0},{4,5},{5,6},{6,7},{7,4},{8,9},{9,10},{10,1... | collective-permute-start | bytes 3145736 | tf_op jit(solution)/shard_map/ppermute | solution.py:1132
  171.6 50.3 %collective-permute-start.8 = (bf16[1040,1024]{1,0:T(8,128)(2,1)}, bf16[1040,1024]{1,0:T(8,128)(2,1)}, u32[]{:S(2)}, u32[]{:S(2)}) collective-permute-start(bf16[1040,1024]{1,0:T(8,128)(2,1)} %get-tuple-element.92), channel_id=1, source_target_pairs={{0,1},{1,2},{2,3},{3,0},{4,5},{5,6},{6,7},{7,4},{8,9},{9,10},{10,1... | collective-permute-start | bytes 6389768 | tf_op jit(solution)/shard_map/ppermute | solution.py:1141
  171.9 1.0 copy-start.19
  199.7 33.1 %all-to-all-start.1 = ((bf16[8,4,288,128]{3,2,1,0:T(8,128)(2,1)}), bf16[8,4,288,128]{3,2,1,0:T(8,128)(2,1)S(1)}, u32[]{:S(2)}, u32[]{:S(2)}) async-start(bf16[8,4,288,128]{3,2,1,0:T(8,128)(2,1)} %get-tuple-element.94), calls=%async_computation.1 | async-start | bytes 4718592 | tf_op jit(solution)/shard_map/all_to_all | solution.py:1136
  224.9 26.6 %collective-permute-start.9 = (bf16[528,1024]{1,0:T(8,128)(2,1)}, bf16[528,1024]{1,0:T(8,128)(2,1)S(1)}, u32[]{:S(2)}, u32[]{:S(2)}) collective-permute-start(bf16[528,1024]{1,0:T(8,128)(2,1)} %add_convert_fusion.1), channel_id=1, source_target_pairs={{0,1},{1,2},{2,3},{3,0},{4,5},{5,6},{6,7},{7,4},{8,9},{9,10},{10,1... | collective-permute-start | bytes 3244040 | tf_op jit(solution)/shard_map/ppermute | solution.py:1147
  232.8 1.4 copy-start.2
  232.8 18.7 %copy-start.4 = (bf16[1040,1024]{1,0:T(8,128)(2,1)S(1)}, bf16[1040,1024]{1,0:T(8,128)(2,1)}, u32[]{:S(2)}) copy-start(bf16[1040,1024]{1,0:T(8,128)(2,1)} %get-tuple-element.86) | copy-start | bytes 6389764
  251.9 25.6 %collective-permute-start.10 = (bf16[528,1024]{1,0:T(8,128)(2,1)S(1)}, bf16[528,1024]{1,0:T(8,128)(2,1)S(1)}, u32[]{:S(2)}, u32[]{:S(2)}) collective-permute-start(bf16[528,1024]{1,0:T(8,128)(2,1)S(1)} %add_convert_fusion), channel_id=1, source_target_pairs={{0,1},{1,2},{2,3},{3,0},{4,5},{5,6},{6,7},{7,4},{8,9},{9,10},{10,1... | collective-permute-start | bytes 3244040 | tf_op jit(solution)/shard_map/ppermute | solution.py:1147
  277.5 1.0 copy-start.1
  277.5 30.3 %collective-permute-start.11 = (bf16[512,1024]{1,0:T(8,128)(2,1)S(1)}, bf16[512,1024]{1,0:T(8,128)(2,1)S(1)}, u32[]{:S(2)}, u32[]{:S(2)}) collective-permute-start(bf16[512,1024]{1,0:T(8,128)(2,1)S(1)} %add_convert_fusion.4), channel_id=1, source_target_pairs={{0,1},{1,2},{2,3},{3,0},{4,5},{5,6},{6,7},{7,4},{8,9},{9,10},{10,1... | collective-permute-start | bytes 3145736 | tf_op jit(solution)/shard_map/ppermute | solution.py:1151
  309.2 32.9 %collective-permute-start.12 = (bf16[512,1024]{1,0:T(8,128)(2,1)}, bf16[512,1024]{1,0:T(8,128)(2,1)S(1)}, u32[]{:S(2)}, u32[]{:S(2)}) collective-permute-start(bf16[512,1024]{1,0:T(8,128)(2,1)} %add_convert_fusion.3), channel_id=1, source_target_pairs={{0,1},{1,2},{2,3},{3,0},{4,5},{5,6},{6,7},{7,4},{8,9},{9,10},{10,1... | collective-permute-start | bytes 3145736 | tf_op jit(solution)/shard_map/ppermute | solution.py:1170
  313.7 25.7 %all-to-all-start.2 = ((bf16[32,16,256]{2,1,0:T(8,128)(2,1)}), bf16[32,16,256]{2,1,0:T(8,128)(2,1)S(1)}, u32[]{:S(2)}, u32[]{:S(2)}) async-start(bf16[32,16,256]{2,1,0:T(8,128)(2,1)} %get-tuple-element.115), calls=%async_computation.2 | async-start | bytes 524288 | tf_op jit(solution)/shard_map/all_to_all | solution.py:1174
  319.5 22.6 %copy-start.3 = (f32[512,1024]{1,0:T(8,128)S(1)}, f32[512,1024]{1,0:T(8,128)}, u32[]{:S(2)}) copy-start(f32[512,1024]{1,0:T(8,128)} %get-tuple-element.76.refs_2_) | copy-start | bytes 6291460
  339.4 0.7 copy-start.5
Sparse Core Ops, SparseCore 0:
  14.1 88.4 all-gather.1

commit v7 on v6

--- a/solution.py
+++ b/solution.py
@@ -561,7 +561,7 @@
             grid=(local,),
             in_specs=[
                 full((rows, MODEL_WIDTH)),
-                pl.BlockSpec((rows, MODEL_WIDTH), lambda e, s: (s[5], 0)),
+                full((rows, MODEL_WIDTH)),
                 pl.BlockSpec((rows, TOP), lambda e, s: (s[0], 0)),
                 full((128, MODEL_WIDTH)),
                 pl.BlockSpec((1, MODEL_WIDTH, 2 * H), lambda e, s: (e, 0, 0)),
@@ -1056,23 +1056,25 @@
             offset * local,
             slot,
             jnp.full((groups,), first, jnp.int32),
-            jnp.where(slot == 0, 0, source),
         ],
         1,
     )
 
     both = pack(query_key_value_weight, w_out)
+    cots = {0: cotangent, 1: lax.ppermute(cotangent, "expert", forward)}
     if owners == BLOCKS:
         pair = both_neighbours(both)
         pair, order, router, router_wide, table, tags, attn_gain, ffn_gain, length = tied(
             pair, order, router, router_wide, table, tags, attn_gain, ffn_gain, length
         )
         near = jnp.concatenate([both, *pair, *across(pair)], 0)
-        near, adapters = tied(near, adapters)
+        near, adapters, cots[1], cotangent = tied(near, adapters, cots[1], cotangent)
         weights = near, swap(near, 1)
     else:
         whole = lax.all_gather(both, "dp", axis=0, tiled=True)
         weights = whole, whole
+    if groups > 2:
+        cots[groups - 1] = lax.ppermute(cotangent, "expert", backward)
 
     low_map = adapters[:, : 4 * R].transpose(1, 0, 2).reshape(4 * R, MODEL_WIDTH)
     up = (
@@ -1091,9 +1093,12 @@
 
     cos, sin = rope_tables(rows)
 
-    cots = lax.all_gather(cotangent, "expert", axis=0, tiled=True)
 
     qkv, low, normed_in = project(order, hidden, attn_gain, weights, low_map, up_map, cos, sin)
+    if groups > 3:
+        cots[1], low = tied(cots[1], low)
+    for at in range(2, groups - 1):
+        cots[at] = lax.ppermute(cots[at - 1], "expert", forward)
     attended, lse = attend(length, qkv)
     mid, normed_mid, low_out = close_mixer(
         order, attended, hidden, ffn_gain, weights, low_map, up_out_map
@@ -1109,7 +1114,7 @@
         ran[offset], gate_part, packed = run_experts(
             table[at],
             xs[offset],
-            cotangent if at == 0 else cots,
+            cots[offset],
             routes,
             router_wide,
             w_gate_up,

time: 358 us -> 352 us (0.983)
  between operations: 15 us -> 1.46 us
  starting transfers between devices: 24.9 us -> 32.2 us
  waiting for transfers between devices: 94.5 us -> 89.9 us
    ppermute x5, waiting for transfers between devices: 15 us -> 9.32 us  [swap(): return lax.ppermute(value, 'dp', [(at, at ^ bit) for at in range(BLOCKS)])]
    ppermute x0 -> x3, waiting for transfers between devices: none -> 4.82 us  [the longest x1 4.81 us: on_device(): cots = {0: cotangent, 1: lax.ppermute(cotangent, 'expert', forward)}]
    ppermute x2, waiting for transfers between devices: 37.2 us -> 33.1 us  [on_device(): grad_far = lax.ppermute(grad_part, 'expert', forward)]
    ppermute x0 -> x3, starting transfers between devices: none -> 3.65 us  [the longest x1 1.74 us: on_device(): cots[groups - 1] = lax.ppermute(cotangent, 'expert', backward)]
    unnamed x50 -> x48, local copies, waits for them, and re-layouts: 10.3 us -> 12.4 us
  transfers between devices with their start and end apart: 17 -> 19, of which waited for: 11 -> 11; matrix products, arithmetic and copies ran while one was open for 6% -> 7% of each run, Pallas kernels for 52% -> 53%
where the time goes in v7:
time: 352 us; the launch traced here: 346 us
  Pallas kernels  187 us (53%)
  waiting for transfers between devices  89.9 us (26%)
  starting transfers between devices  32.2 us (9%)
  local copies, waits for them, and re-layouts  23.6 us (7%)
  other arithmetic  11.7 us (3%)
    pallas_call x4, Pallas kernels, run_experts(): pl.pallas_call(expert_kernel, grid_spec=pltpu.PrefetchScalarGridSpec(num_...  108 us
    ppermute x2, waiting for transfers between devices, on_device(): grad_far = lax.ppermute(grad_part, 'expert', forward)  33.1 us
    pallas_call x1, Pallas kernels, attend_back(): pl.pallas_call(attend_back_kernel, grid_spec=pltpu.PrefetchScalarGridSpec...  19.6 us
    ppermute x1, waiting for transfers between devices, on_device(): lax.ppermute(first_sums if groups > 2 else ran[1], 'expert', forward)  15.9 us
    pallas_call x1, Pallas kernels, attend(): pl.pallas_call(attend_kernel, grid_spec=pltpu.PrefetchScalarGridSpec(num_...  12.6 us
    unnamed x48, local copies, waits for them, and re-layouts  12.4 us
    all_to_all x1, waiting for transfers between devices, on_device(): packed = lax.all_to_all(packed, ('dp', 'expert'), 0, 0, tiled=True)  10.5 us
    pallas_call x1, Pallas kernels, project(): pl.pallas_call(project_kernel, grid_spec=pltpu.PrefetchScalarGridSpec(num...  10.4 us
  transfers between devices with their start and end apart: 19, of which 11 were waited for; matrix products, arithmetic and copies ran while one was open for 7% of the time, Pallas kernels for 53%

profile of v7, /device:TPU:0, one launch (start us, length us, event | category | flops | bytes accessed | tf_op | source)
XLA Modules:
  0.0 345.7 jit_solution(12518997181718749610)
XLA Ops:
  0.7 2.1 pack.1
  2.8 3.0 collective-permute-start.1
  5.8 1.5 collective-permute-start
  10.7 1.3 gather_fusion.1
  12.0 3.4 all-to-all-start
  15.4 1.6 collective-permute-start.4
  21.1 1.2 constant_dynamic-update-slice_fusion.4
  22.3 2.0 collective-permute-done.1
  24.3 2.1 collective-permute-done
  28.4 1.6 collective-permute-start.2
  30.5 1.2 constant_dynamic-update-slice_fusion.3
  31.7 1.2 constant_dynamic-update-slice_fusion.2
  32.8 4.1 %collective-permute-done.2 = bf16[64,3072]{1,0:T(8,128)(2,1)S(1)} collective-permute-done((bf16[64,3072]{1,0:T(8,128)(2,1)S(1)}, bf16[64,3072]{1,0:T(8,128)(2,1)S(1)}, u32[]{:S(2)}, u32[]{:S(2)}) %collective-permute-start.2) | collective-permute-done | bytes 393248 | tf_op jit(solution)/shard_map/ppermute | solution.py:953
  37.0 1.2 collective-permute-done.3
  38.2 4.8 %collective-permute-done.4.cot = bf16[512,1024]{1,0:T(8,128)(2,1)} collective-permute-done((bf16[512,1024]{1,0:T(8,128)(2,1)}, bf16[512,1024]{1,0:T(8,128)(2,1)}, u32[]{:S(2)}, u32[]{:S(2)}) %collective-permute-start.4) | collective-permute-done | bytes 1048608 | tf_op jit(solution)/shard_map/ppermute | solution.py:1064
  43.0 1.4 copy.60.routes
  45.8 1.7 collective-permute-start.7
  49.0 10.4 %project.1 = (bf16[512,2048]{1,0:T(8,128)(2,1)}, bf16[512,64]{1,0:T(8,128)(2,1)}, bf16[512,1024]{1,0:T(8,128)(2,1)}) custom-call(s32[8]{0:T(128)} %broadcast_xor_fusion.order.refs_0_, bf16[512,1024]{1,0:T(8,128)(2,1)} %hid.5, bf16[1,1024]{1,0:T(2,128)(2,1)} %reshape.89.gain, bf16[512,3072]{1,0:T(8,128)(2,1)} %copy-done, ...), custom_call_target="tpu_custom_call" | custom-call | flops 2147483648 | bytes 8388608 | tf_op jit(solution)/shard_map/project/pallas_call | solution.py:141
  59.7 12.6 %attend.1 = (bf16[512,1024]{1,0:T(8,128)(2,1)}, f32[8,2,512]{2,1,0:T(2,128)}) custom-call(s32[1]{0:T(128)} %dynamic_slice.15.scalars, bf16[512,2048]{1,0:T(8,128)(2,1)} %get-tuple-element.77.query.key.value, bf16[512,2048]{1,0:T(8,128)(2,1)} %get-tuple-element.77.query.key.value, bf16[512,2048]{1,0:T(8,128)(2,1)} %get-tuple-element.77.query.key.value), custom_call_target="tpu_custom_call" | custom-call | flops 2147483648 | bytes 4194304 | tf_op jit(solution)/shard_map/attend/pallas_call | solution.py:223
  72.3 6.0 %close_mixer.1 = (f32[512,1024]{1,0:T(8,128)}, bf16[512,1024]{1,0:T(8,128)(2,1)}, bf16[512,64]{1,0:T(8,128)(2,1)}) custom-call(s32[8]{0:T(128)} %broadcast_xor_fusion.order.refs_0_, bf16[512,1024]{1,0:T(8,128)(2,1)} %get-tuple-element.78.att.refs_11_, bf16[512,1024]{1,0:T(8,128)(2,1)} %hid.5, bf16[1,1024]{1,0:T(2,128)(2,1)} %reshape.90.gain.refs_3_, ...), custom_call_target="tpu_custom_call" | custom-call | flops 1073741824 | bytes 8388608 | tf_op jit(solution)/shard_map/close_mixer/pallas_call | solution.py:356
  78.3 1.3 collective-permute-start.8
  79.6 27.6 %experts.4 = (bf16[1040,1024]{1,0:T(8,128)(2,1)}, f32[16,512]{1,0:T(8,128)}, bf16[8,4,288,128]{3,2,1,0:T(8,128)(2,1)}) custom-call(s32[5]{0:T(128)} %get-tuple-element.136.scalars, bf16[512,1024]{1,0:T(8,128)(2,1)} %get-tuple-element.86.x, bf16[512,1024]{1,0:T(8,128)(2,1)} %refs_1_, s32[2048,8]{1,0:T(8,128)} %copy.60.routes, ...), custom_call_target="tpu_custom_call" | custom-call | flops 19327352832 | bytes 20971520 | tf_op jit(solution)/shard_map/experts/pallas_call | solution.py:557
  107.3 3.2 collective-permute-start.6
  110.5 6.7 %collective-permute-done.8.x = bf16[512,1024]{1,0:T(8,128)(2,1)S(1)} collective-permute-done((bf16[512,1024]{1,0:T(8,128)(2,1)}, bf16[512,1024]{1,0:T(8,128)(2,1)S(1)}, u32[]{:S(2)}, u32[]{:S(2)}) %collective-permute-start.8) | collective-permute-done | bytes 1048608 | tf_op jit(solution)/shard_map/ppermute | solution.py:1110
  118.2 26.8 %experts.5 = (bf16[1040,1024]{1,0:T(8,128)(2,1)}, f32[16,512]{1,0:T(8,128)}, bf16[8,4,288,128]{3,2,1,0:T(8,128)(2,1)}) custom-call(s32[5]{0:T(128)} %get-tuple-element.134.scalars, bf16[512,1024]{1,0:T(8,128)(2,1)} %copy-done.15, bf16[512,1024]{1,0:T(8,128)(2,1)} %collective-permute-done.4.cot, ...), custom_call_target="tpu_custom_call", output_to_operand_aliasing={{2}: (11, {})} | custom-call | flops 19327352832 | bytes 20971520 | tf_op jit(solution)/shard_map/experts/pallas_call | solution.py:557
  145.1 1.7 collective-permute-start.9
  148.1 26.8 %experts.6 = (bf16[1040,1024]{1,0:T(8,128)(2,1)}, f32[16,512]{1,0:T(8,128)}, bf16[8,4,288,128]{3,2,1,0:T(8,128)(2,1)}) custom-call(s32[5]{0:T(128)} %get-tuple-element.135.scalars, bf16[512,1024]{1,0:T(8,128)(2,1)} %copy-done.18, bf16[512,1024]{1,0:T(8,128)(2,1)} %copy-done.14, s32[2048,8]{1,0:T(8,128)} %copy.60.routes, ...), custom_call_target="tpu_custom_call", output_to_operand_aliasing={{2}: (11, {})} | custom-call | flops 19327352832 | bytes 20971520 | tf_op jit(solution)/shard_map/experts/pallas_call | solution.py:557
  174.9 1.6 collective-permute-start.11
  176.5 1.0 copy-done.13
  177.9 26.7 %experts.7 = (bf16[1040,1024]{1,0:T(8,128)(2,1)}, f32[16,512]{1,0:T(8,128)}, bf16[8,4,288,128]{3,2,1,0:T(8,128)(2,1)}) custom-call(s32[5]{0:T(128)} %get-tuple-element.133.scalars, bf16[512,1024]{1,0:T(8,128)(2,1)} %copy-done.16, bf16[512,1024]{1,0:T(8,128)(2,1)} %copy-done.13, s32[2048,8]{1,0:T(8,128)} %copy.60.routes, ...), custom_call_target="tpu_custom_call", output_to_operand_aliasing={{2}: (11, {})} | custom-call | flops 19327352832 | bytes 20971520 | tf_op jit(solution)/shard_map/experts/pallas_call | solution.py:557
  204.6 3.8 %all-to-all-start.1 = ((bf16[8,4,288,128]{3,2,1,0:T(8,128)(2,1)}), bf16[8,4,288,128]{3,2,1,0:T(8,128)(2,1)S(1)}, u32[]{:S(2)}, u32[]{:S(2)}) async-start(bf16[8,4,288,128]{3,2,1,0:T(8,128)(2,1)} %get-tuple-element.102), calls=%async_computation.1 | async-start | bytes 4718592 | tf_op jit(solution)/shard_map/all_to_all | solution.py:1141
  208.4 15.9 %collective-permute-done.11 = bf16[1040,1024]{1,0:T(8,128)(2,1)} collective-permute-done((bf16[1040,1024]{1,0:T(8,128)(2,1)}, bf16[1040,1024]{1,0:T(8,128)(2,1)}, u32[]{:S(2)}, u32[]{:S(2)}) %collective-permute-start.11) | collective-permute-done | bytes 2129952 | tf_op jit(solution)/shard_map/ppermute | solution.py:1146
  224.4 3.0 add_convert_fusion.1
  228.4 9.5 %all-to-all-done.1 = bf16[8,4,288,128]{3,2,1,0:T(8,128)(2,1)S(1)} async-done(((bf16[8,4,288,128]{3,2,1,0:T(8,128)(2,1)}), bf16[8,4,288,128]{3,2,1,0:T(8,128)(2,1)S(1)}, u32[]{:S(2)}, u32[]{:S(2)}) %all-to-all-start.1) | async-done | bytes 2359328 | tf_op jit(solution)/shard_map/all_to_all | solution.py:1141
  237.9 1.5 copy-done.2
  239.3 3.6 %sum_experts.1 = (f32[4,8,32,128]{3,2,1,0:T(8,128)}, f32[4,8,2,16,64]{4,3,2,1,0:T(8,128)}, f32[4,8,16,64]{3,2,1,0:T(8,128)}, f32[4,8,16,128]{3,2,1,0:T(8,128)}) custom-call(s32[32]{0:T(128)} %reshape.97.ids, bf16[32,288,128]{2,1,0:T(8,128)(2,1)} %bitcast.39), custom_call_target="tpu_custom_call" | custom-call | tf_op jit(solution)/shard_map/sum_experts/pallas_call | solution.py:890
  242.9 10.3 %collective-permute-done.12 = bf16[528,1024]{1,0:T(8,128)(2,1)S(1)} collective-permute-done((bf16[528,1024]{1,0:T(8,128)(2,1)}, bf16[528,1024]{1,0:T(8,128)(2,1)S(1)}, u32[]{:S(2)}, u32[]{:S(2)}) %collective-permute-start.12) | collective-permute-done | bytes 1081376 | tf_op jit(solution)/shard_map/ppermute | solution.py:1152
  253.7 1.9 add_convert_fusion.4
  255.6 22.8 %collective-permute-done.13.refs_13_.refs_16_.refs_17_ = bf16[528,1024]{1,0:T(8,128)(2,1)S(1)} collective-permute-done((bf16[528,1024]{1,0:T(8,128)(2,1)S(1)}, bf16[528,1024]{1,0:T(8,128)(2,1)S(1)}, u32[]{:S(2)}, u32[]{:S(2)}) %collective-permute-start.13) | collective-permute-done | bytes 1081376 | tf_op jit(solution)/shard_map/ppermute | solution.py:1152
  279.4 9.6 %open_back.1 = (f32[512,1024]{1,0:T(8,128)}, bf16[512,1024]{1,0:T(8,128)(2,1)}, f32[64,1024]{1,0:T(8,128)}, f32[64,1024]{1,0:T(8,128)}) custom-call(s32[8]{0:T(128)} %broadcast_xor_fusion.order.refs_0_, bf16[512,1024]{1,0:T(8,128)(2,1)} %refs_1_, f32[512,1024]{1,0:T(8,128)} %get-tuple-element.80.refs_2_, bf16[1,1024]{1,0:T(2,128)(2,1)} %reshape.90.gain.refs_3_, ...), custom_call_target="tpu_custom_call" | custom-call | flops 1073741824 | bytes 14680064 | tf_op jit(solution)/shard_map/open_back/pallas_call | solution.py:690
  289.0 19.6 %attend_back.1 = (bf16[512,1024]{1,0:T(8,128)(2,1)}, bf16[512,512]{1,0:T(8,128)(2,1)}, bf16[512,512]{1,0:T(8,128)(2,1)}) custom-call(s32[1]{0:T(128)} %dynamic_slice.15.scalars, bf16[512,2048]{1,0:T(8,128)(2,1)} %get-tuple-element.77.query.key.value, bf16[512,2048]{1,0:T(8,128)(2,1)} %get-tuple-element.77.query.key.value, ...), custom_call_target="tpu_custom_call" | custom-call | flops 5368709120 | bytes 8388608 | tf_op jit(solution)/shard_map/attend_back/pallas_call | solution.py:303
  308.7 1.4 add_convert_fusion.3
  310.1 4.5 %adapters_back.1 = (bf16[512,64]{1,0:T(8,128)(2,1)}, bf16[32,16,256]{2,1,0:T(8,128)(2,1)}) custom-call(bf16[512,1024]{1,0:T(8,128)(2,1)} %get-tuple-element.114.grad_query, bf16[512,512]{1,0:T(8,128)(2,1)} %get-tuple-element.115.grad_key, bf16[512,512]{1,0:T(8,128)(2,1)} %get-tuple-element.116.grad_value, bf16[512,64]{1,0:T(8,128)(2,1)} %get-tuple-element.117.low, ...), custom_call_target="tpu_custom_call" | custom-call | flops 1610612736 | bytes 4194304 | tf_op jit(solution)/shard_map/adapters_back/pallas_call | solution.py:790
  314.5 6.1 %all-to-all-start.2 = ((bf16[32,16,256]{2,1,0:T(8,128)(2,1)}), bf16[32,16,256]{2,1,0:T(8,128)(2,1)S(1)}, u32[]{:S(2)}, u32[]{:S(2)}) async-start(bf16[32,16,256]{2,1,0:T(8,128)(2,1)} %get-tuple-element.123), calls=%async_computation.2 | async-start | bytes 524288 | tf_op jit(solution)/shard_map/all_to_all | solution.py:1179
  320.7 8.6 %input_back.1 = bf16[512,1024]{1,0:T(8,128)(2,1)} custom-call(s32[8]{0:T(128)} %broadcast_xor_fusion.order.refs_0_, bf16[512,1024]{1,0:T(8,128)(2,1)} %get-tuple-element.114.grad_query, bf16[512,512]{1,0:T(8,128)(2,1)} %get-tuple-element.115.grad_key, bf16[512,512]{1,0:T(8,128)(2,1)} %get-tuple-element.116.grad_value, ...), custom_call_target="tpu_custom_call" | custom-call | flops 2147483648 | bytes 12582912 | tf_op jit(solution)/shard_map/input_back/pallas_call | solution.py:835
  329.3 10.5 %all-to-all-done.2.pieces = bf16[32,16,256]{2,1,0:T(8,128)(2,1)S(1)} async-done(((bf16[32,16,256]{2,1,0:T(8,128)(2,1)}), bf16[32,16,256]{2,1,0:T(8,128)(2,1)S(1)}, u32[]{:S(2)}, u32[]{:S(2)}) %all-to-all-start.2) | async-done | bytes 262176 | tf_op jit(solution)/shard_map/all_to_all | solution.py:1179
  340.5 2.0 sum_mixer.1
  342.5 2.7 add_convert_fusion.2
  (93 shorter events, 19.0 us)
Async XLA Ops:
  0.6 19.8 %copy-start.12 = (s32[4,1]{1,0:T(4,128)S(1)}, s32[4,1]{1,0:T(4,128)}, u32[]{:S(2)}) copy-start(s32[4,1]{1,0:T(4,128)} %constant.84) | copy-start | bytes 52
  0.7 19.9 %copy-start.20 = (s32[8]{0:T(128)S(1)}, s32[8]{0:T(128)}, u32[]{:S(2)}) copy-start(s32[8]{0:T(128)} %constant.74.clone) | copy-start | bytes 100
  0.7 10.0 %copy-start.8 = (bf16[8,16,128]{2,1,0:T(8,128)(2,1)S(1)}, bf16[8,16,128]{2,1,0:T(8,128)(2,1)}, u32[]{:S(2)}) copy-start(bf16[8,16,128]{2,1,0:T(8,128)(2,1)} %param.37) | copy-start | bytes 98308
  0.7 16.5 %copy-start.10 = (bf16[1024]{0:T(1024)(128)(2,1)S(1)}, bf16[1024]{0:T(1024)(128)(2,1)}, u32[]{:S(2)}) copy-start(bf16[1024]{0:T(1024)(128)(2,1)} %param.28) | copy-start | bytes 6148
  0.7 17.1 %copy-start.11 = (bf16[1024]{0:T(1024)(128)(2,1)S(1)}, bf16[1024]{0:T(1024)(128)(2,1)}, u32[]{:S(2)}) copy-start(bf16[1024]{0:T(1024)(128)(2,1)} %param.29) | copy-start | bytes 6148
  0.7 17.7 %copy-start.19 = (s32[32]{0:T(128)S(1)}, s32[32]{0:T(128)}, u32[]{:S(2)}) copy-start(s32[32]{0:T(128)} %param.25) | copy-start | bytes 388
  0.7 18.8 %copy-start.9 = (bf16[1024,16]{0,1:T(8,128)(2,1)S(1)}, bf16[1024,16]{0,1:T(8,128)(2,1)}, u32[]{:S(2)}) copy-start(bf16[1024,16]{0,1:T(8,128)(2,1)} %param.32) | copy-start | bytes 98308
  2.8 21.5 %collective-permute-start.1 = (bf16[128,3072]{1,0:T(8,128)(2,1)}, bf16[128,3072]{1,0:T(8,128)(2,1)}, u32[]{:S(2)}, u32[]{:S(2)}) collective-permute-start(bf16[128,3072]{1,0:T(8,128)(2,1)} %pack.1), channel_id=1, source_target_pairs={{0,16},{4,20},{8,24},{12,28},{16,0},{20,4},{24,8},{28,12},{1,17},{... | collective-permute-start | bytes 2359304 | tf_op jit(solution)/shard_map/ppermute | solution.py:953
  5.8 20.5 %collective-permute-start = (bf16[128,3072]{1,0:T(8,128)(2,1)}, bf16[128,3072]{1,0:T(8,128)(2,1)}, u32[]{:S(2)}, u32[]{:S(2)}) collective-permute-start(bf16[128,3072]{1,0:T(8,128)(2,1)} %pack.1), channel_id=1, source_target_pairs={{0,8},{4,12},{8,0},{12,4},{16,24},{20,28},{24,16},{28,20},{1,9},{5... | collective-permute-start | bytes 2359304 | tf_op jit(solution)/shard_map/ppermute | solution.py:953
  12.0 26.2 %all-to-all-start = ((bf16[8,112,128]{2,1,0:T(8,128)(2,1)}), bf16[8,112,128]{2,1,0:T(8,128)(2,1)S(1)}, u32[]{:S(2)}, u32[]{:S(2)}) async-start(bf16[8,112,128]{2,1,0:T(8,128)(2,1)} %gather_fusion.1), calls=%async_computation | async-start | bytes 458752 | tf_op jit(solution)/shard_map/all_to_all | solution.py:1039
  15.4 27.6 %collective-permute-start.4 = (bf16[512,1024]{1,0:T(8,128)(2,1)}, bf16[512,1024]{1,0:T(8,128)(2,1)}, u32[]{:S(2)}, u32[]{:S(2)}) collective-permute-start(bf16[512,1024]{1,0:T(8,128)(2,1)} %refs_1_), channel_id=1, source_target_pairs={{0,1},{1,2},{2,3},{3,0},{4,5},{5,6},{6,7},{7,4},{8,9},{9,10},{10,1... | collective-permute-start | bytes 3145736 | tf_op jit(solution)/shard_map/ppermute | solution.py:1064
  19.6 12.0 %copy-start.6 = (bf16[16,1024]{1,0:T(8,128)(2,1)}, bf16[16,1024]{1,0:T(8,128)(2,1)S(1)}, u32[]{:S(2)}) copy-start(bf16[16,1024]{1,0:T(8,128)(2,1)S(1)} %fusion.refs_5_) | copy-start | bytes 98308
  28.4 14.7 %copy-start.7 = (s32[2048,8]{0,1:T(8,128)S(1)}, s32[2048,8]{0,1:T(8,128)}, u32[]{:S(2)}) copy-start(s32[2048,8]{0,1:T(8,128)} %param.27) | copy-start | bytes 196612
  28.4 8.6 %collective-permute-start.2 = (bf16[64,3072]{1,0:T(8,128)(2,1)S(1)}, bf16[64,3072]{1,0:T(8,128)(2,1)S(1)}, u32[]{:S(2)}, u32[]{:S(2)}) collective-permute-start(bf16[64,3072]{1,0:T(8,128)(2,1)S(1)} %slice.48), channel_id=1, source_target_pairs={{0,8},{4,12},{8,0},{12,4},{16,24},{20,28},{24,16},{28,20},{1,9},{5... | collective-permute-start | bytes 1179656 | tf_op jit(solution)/shard_map/ppermute | solution.py:953
  30.0 8.2 %collective-permute-start.3 = (bf16[64,3072]{1,0:T(8,128)(2,1)S(1)}, bf16[64,3072]{1,0:T(8,128)(2,1)S(1)}, u32[]{:S(2)}, u32[]{:S(2)}) collective-permute-start(bf16[64,3072]{1,0:T(8,128)(2,1)S(1)} %slice.49), channel_id=1, source_target_pairs={{0,16},{4,20},{8,24},{12,28},{16,0},{20,4},{24,8},{28,12},{1,17},{... | collective-permute-start | bytes 1179656 | tf_op jit(solution)/shard_map/ppermute | solution.py:953
  38.2 10.8 %copy-start = (bf16[512,3072]{1,0:T(8,128)(2,1)}, bf16[512,3072]{1,0:T(8,128)(2,1)S(1)}, u32[]{:S(2)}) copy-start(bf16[512,3072]{1,0:T(8,128)(2,1)S(1)} %constant_dynamic-update-slice_fusion.weight_a.refs_6_) | copy-start | bytes 9437188
  43.0 6.0 %collective-permute-start.5 = (bf16[512,3072]{1,0:T(8,128)(2,1)S(1)}, bf16[512,3072]{1,0:T(8,128)(2,1)}, u32[]{:S(2)}, u32[]{:S(2)}) collective-permute-start(bf16[512,3072]{1,0:T(8,128)(2,1)S(1)} %constant_dynamic-update-slice_fusion.weight_a.refs_6_), channel_id=1, source_target_pairs={{0,4},{4,0},{8,12},{12,8},{16,20},{20,16},{24,28},{28,24},{1,5},{5... | collective-permute-start | bytes 9437192 | tf_op jit(solution)/shard_map/ppermute | solution.py:953
  45.8 101.0 %collective-permute-start.7 = (bf16[512,1024]{1,0:T(8,128)(2,1)}, bf16[512,1024]{1,0:T(8,128)(2,1)S(1)}, u32[]{:S(2)}, u32[]{:S(2)}) collective-permute-start(bf16[512,1024]{1,0:T(8,128)(2,1)} %refs_1_), channel_id=1, source_target_pairs={{0,3},{1,0},{2,1},{3,2},{4,7},{5,4},{6,5},{7,6},{8,11},{9,8},{10,9... | collective-permute-start | bytes 3145736 | tf_op jit(solution)/shard_map/ppermute | solution.py:1077
  59.4 117.1 %collective-permute-start.10 = (bf16[512,1024]{1,0:T(8,128)(2,1)}, bf16[512,1024]{1,0:T(8,128)(2,1)S(1)}, u32[]{:S(2)}, u32[]{:S(2)}) collective-permute-start(bf16[512,1024]{1,0:T(8,128)(2,1)} %collective-permute-done.4.cot), channel_id=1, source_target_pairs={{0,1},{1,2},{2,3},{3,0},{4,5},{5,6},{6,7},{7,4},{8,9},{9,10},{10,1... | collective-permute-start | bytes 3145736 | tf_op jit(solution)/shard_map/ppermute | solution.py:1101
  78.3 39.0 %collective-permute-start.8 = (bf16[512,1024]{1,0:T(8,128)(2,1)}, bf16[512,1024]{1,0:T(8,128)(2,1)S(1)}, u32[]{:S(2)}, u32[]{:S(2)}) collective-permute-start(bf16[512,1024]{1,0:T(8,128)(2,1)} %get-tuple-element.86.x), channel_id=1, source_target_pairs={{0,1},{1,2},{2,3},{3,0},{4,5},{5,6},{6,7},{7,4},{8,9},{9,10},{10,1... | collective-permute-start | bytes 3145736 | tf_op jit(solution)/shard_map/ppermute | solution.py:1110
  79.6 27.6 %copy-start.17 = (bf16[512,1024]{1,0:T(8,128)(2,1)S(1)}, bf16[512,1024]{1,0:T(8,128)(2,1)}, u32[]{:S(2)}) copy-start(bf16[512,1024]{1,0:T(8,128)(2,1)} %get-tuple-element.86.x) | copy-start | bytes 3145732
  107.3 39.5 %collective-permute-start.6 = (bf16[512,1024]{1,0:T(8,128)(2,1)S(1)}, bf16[512,1024]{1,0:T(8,128)(2,1)S(1)}, u32[]{:S(2)}, u32[]{:S(2)}) collective-permute-start(bf16[512,1024]{1,0:T(8,128)(2,1)S(1)} %copy-done.17), channel_id=1, source_target_pairs={{0,3},{1,0},{2,1},{3,2},{4,7},{5,4},{6,5},{7,6},{8,11},{9,8},{10,9... | collective-permute-start | bytes 3145736 | tf_op jit(solution)/shard_map/ppermute | solution.py:1134
  117.3 1.0 copy-start.15
  145.1 31.4 %collective-permute-start.9 = (bf16[512,1024]{1,0:T(8,128)(2,1)}, bf16[512,1024]{1,0:T(8,128)(2,1)S(1)}, u32[]{:S(2)}, u32[]{:S(2)}) collective-permute-start(bf16[512,1024]{1,0:T(8,128)(2,1)} %copy-done.15), channel_id=1, source_target_pairs={{0,1},{1,2},{2,3},{3,0},{4,5},{5,6},{6,7},{7,4},{8,9},{9,10},{10,1... | collective-permute-start | bytes 3145736 | tf_op jit(solution)/shard_map/ppermute | solution.py:1137
  146.8 1.0 copy-start.14
  146.8 1.3 copy-start.18
  174.9 49.5 %collective-permute-start.11 = (bf16[1040,1024]{1,0:T(8,128)(2,1)}, bf16[1040,1024]{1,0:T(8,128)(2,1)}, u32[]{:S(2)}, u32[]{:S(2)}) collective-permute-start(bf16[1040,1024]{1,0:T(8,128)(2,1)} %get-tuple-element.100), channel_id=1, source_target_pairs={{0,1},{1,2},{2,3},{3,0},{4,5},{5,6},{6,7},{7,4},{8,9},{9,10},{10,1... | collective-permute-start | bytes 6389768 | tf_op jit(solution)/shard_map/ppermute | solution.py:1146
  176.5 1.1 copy-start.13
  176.5 1.4 copy-start.16
  204.6 33.2 %all-to-all-start.1 = ((bf16[8,4,288,128]{3,2,1,0:T(8,128)(2,1)}), bf16[8,4,288,128]{3,2,1,0:T(8,128)(2,1)S(1)}, u32[]{:S(2)}, u32[]{:S(2)}) async-start(bf16[8,4,288,128]{3,2,1,0:T(8,128)(2,1)} %get-tuple-element.102), calls=%async_computation.1 | async-start | bytes 4718592 | tf_op jit(solution)/shard_map/all_to_all | solution.py:1141
  227.3 25.8 %collective-permute-start.12 = (bf16[528,1024]{1,0:T(8,128)(2,1)}, bf16[528,1024]{1,0:T(8,128)(2,1)S(1)}, u32[]{:S(2)}, u32[]{:S(2)}) collective-permute-start(bf16[528,1024]{1,0:T(8,128)(2,1)} %add_convert_fusion.1), channel_id=1, source_target_pairs={{0,1},{1,2},{2,3},{3,0},{4,5},{5,6},{6,7},{7,4},{8,9},{9,10},{10,1... | collective-permute-start | bytes 3244040 | tf_op jit(solution)/shard_map/ppermute | solution.py:1152
  237.8 1.5 copy-start.2
  237.8 15.3 %copy-start.4 = (bf16[1040,1024]{1,0:T(8,128)(2,1)S(1)}, bf16[1040,1024]{1,0:T(8,128)(2,1)}, u32[]{:S(2)}) copy-start(bf16[1040,1024]{1,0:T(8,128)(2,1)} %get-tuple-element.94) | copy-start | bytes 6389764
  253.6 24.8 %collective-permute-start.13 = (bf16[528,1024]{1,0:T(8,128)(2,1)S(1)}, bf16[528,1024]{1,0:T(8,128)(2,1)S(1)}, u32[]{:S(2)}, u32[]{:S(2)}) collective-permute-start(bf16[528,1024]{1,0:T(8,128)(2,1)S(1)} %add_convert_fusion), channel_id=1, source_target_pairs={{0,1},{1,2},{2,3},{3,0},{4,5},{5,6},{6,7},{7,4},{8,9},{9,10},{10,1... | collective-permute-start | bytes 3244040 | tf_op jit(solution)/shard_map/ppermute | solution.py:1152
  278.4 1.0 copy-start.1
  278.4 30.2 %collective-permute-start.14 = (bf16[512,1024]{1,0:T(8,128)(2,1)S(1)}, bf16[512,1024]{1,0:T(8,128)(2,1)S(1)}, u32[]{:S(2)}, u32[]{:S(2)}) collective-permute-start(bf16[512,1024]{1,0:T(8,128)(2,1)S(1)} %add_convert_fusion.4), channel_id=1, source_target_pairs={{0,1},{1,2},{2,3},{3,0},{4,5},{5,6},{6,7},{7,4},{8,9},{9,10},{10,1... | collective-permute-start | bytes 3145736 | tf_op jit(solution)/shard_map/ppermute | solution.py:1156
  310.1 32.4 %collective-permute-start.15 = (bf16[512,1024]{1,0:T(8,128)(2,1)}, bf16[512,1024]{1,0:T(8,128)(2,1)S(1)}, u32[]{:S(2)}, u32[]{:S(2)}) collective-permute-start(bf16[512,1024]{1,0:T(8,128)(2,1)} %add_convert_fusion.3), channel_id=1, source_target_pairs={{0,1},{1,2},{2,3},{3,0},{4,5},{5,6},{6,7},{7,4},{8,9},{9,10},{10,1... | collective-permute-start | bytes 3145736 | tf_op jit(solution)/shard_map/ppermute | solution.py:1175
  314.5 25.2 %all-to-all-start.2 = ((bf16[32,16,256]{2,1,0:T(8,128)(2,1)}), bf16[32,16,256]{2,1,0:T(8,128)(2,1)S(1)}, u32[]{:S(2)}, u32[]{:S(2)}) async-start(bf16[32,16,256]{2,1,0:T(8,128)(2,1)} %get-tuple-element.123), calls=%async_computation.2 | async-start | bytes 524288 | tf_op jit(solution)/shard_map/all_to_all | solution.py:1179
  320.7 21.8 %copy-start.3 = (f32[512,1024]{1,0:T(8,128)S(1)}, f32[512,1024]{1,0:T(8,128)}, u32[]{:S(2)}) copy-start(f32[512,1024]{1,0:T(8,128)} %get-tuple-element.80.refs_2_) | copy-start | bytes 6291460
  339.8 0.7 copy-start.5

commit v8 on v7

--- a/solution.py
+++ b/solution.py
@@ -173,6 +173,7 @@
 
 
 ROWB = 128
+BACKB = 256
 
 
 def length_column(length, count):
@@ -180,13 +181,13 @@
     return jnp.where(key < length, 0.0, -1e30)
 
 
-def causal_block():
-    key = lax.broadcasted_iota(jnp.int32, (ROWB, 2 * ROWB), 0)
-    return jnp.where(key <= lanes_of((ROWB, 2 * ROWB)) % ROWB, 0.0, -1e30)
+def causal_block(block):
+    key = lax.broadcasted_iota(jnp.int32, (block, 2 * block), 0)
+    return jnp.where(key <= lanes_of((block, 2 * block)) % block, 0.0, -1e30)
 
 
 def masked_scores(queries, keys, start, bias, causal):
-    count = start + ROWB
+    count = start + causal.shape[0]
     scores = nt(keys[:count], (queries.astype(f32) * 0.125).astype(bf16))
     near = scores[start:] + (bias[start:count] + causal)
     if start == 0:
@@ -200,7 +201,7 @@
     values = both_halves(value[...], half)
     rows = query.shape[0]
     bias = length_column(scalars[0], rows)
-    causal = causal_block()
+    causal = causal_block(ROWB)
     for start in range(0, rows, ROWB):
         count = start + ROWB
         stacked = stacked_heads(query[start:count, :])
@@ -255,9 +256,9 @@
     values = both_halves(value[...], half)
     rows = query.shape[0]
     bias = length_column(scalars[0], rows)
-    causal = causal_block()
-    for start in reversed(range(0, rows, ROWB)):
-        count = start + ROWB
+    causal = causal_block(BACKB)
+    for start in reversed(range(0, rows, BACKB)):
+        count = start + BACKB
         stacked = stacked_heads(query[start:count, :])
         grads = stacked_heads(grad[start:count, :])
         scores = masked_scores(stacked, keys, start, bias, causal)
@@ -267,8 +268,8 @@
         delta = jnp.sum(prob * grad_prob, 0, keepdims=True)
         grad_score = (prob * (grad_prob - delta)).astype(bf16)
         mixed = tn(grad_score, keys[:count])
-        lane = lanes_of((ROWB, 128))
-        turned = 0.125 * jnp.where(lane < HS, mixed[:ROWB], mixed[ROWB:])
+        lane = lanes_of((BACKB, 128))
+        turned = 0.125 * jnp.where(lane < HS, mixed[:BACKB], mixed[BACKB:])
         turned = turned * cos[start:count, :] - rope_swap(turned) * sin[start:count, :]
         grad_query[start:count, :] = turned.astype(bf16)
         key_part = nn(grad_score, stacked)
@@ -1177,12 +1178,13 @@
         grad_query, grad_key, grad_value, low, normed_in, up_map, grad_low_out, grad_up_out, devices
     )
     packed = lax.all_to_all(packed, ("dp", "expert"), 0, 0, tiled=True)
-    m_a, m_b, m_o = sum_mixer(adapter_ids, packed)
 
     grad_hidden = input_back(
         order, grad_query, grad_key, grad_value, back_low, weights, low_map, hidden, attn_gain, grad_mid
     )
     out = (mid + ran[0][edge:].astype(f32) + out_far.astype(f32)).astype(bf16)
+    out, packed = tied(out, packed)
+    m_a, m_b, m_o = sum_mixer(adapter_ids, packed)
     return (
         out,
         grad_hidden,

time: 352 us -> 346 us (0.983)
    all_to_all x1, waiting for transfers between devices: 10.5 us -> 1.39 us  [on_device(): packed = lax.all_to_all(packed, ('dp', 'expert'), 0, 0, tiled=True)]
    ppermute x1, waiting for transfers between devices: 0.01 us -> 6.08 us  [on_device(): lax.ppermute(joined(ran[offset][edge:], out_far), 'expert', forward)]
  transfers between devices with their start and end apart: 19 -> 19, of which waited for: 11 -> 12; matrix products, arithmetic and copies ran while one was open for 7% -> 8% of each run, Pallas kernels for 53% -> 53%
where the time goes in v8:
time: 346 us; the launch traced here: 340 us
  Pallas kernels  185 us (53%)
  waiting for transfers between devices  86.8 us (25%)
  starting transfers between devices  32.2 us (9%)
  local copies, waits for them, and re-layouts  23.6 us (7%)
  other arithmetic  10.7 us (3%)
    pallas_call x4, Pallas kernels, run_experts(): pl.pallas_call(expert_kernel, grid_spec=pltpu.PrefetchScalarGridSpec(num_...  108 us
    ppermute x2, waiting for transfers between devices, on_device(): grad_far = lax.ppermute(grad_part, 'expert', forward)  33.1 us
    pallas_call x1, Pallas kernels, attend_back(): pl.pallas_call(attend_back_kernel, grid_spec=pltpu.PrefetchScalarGridSpec...  18.1 us
    ppermute x1, waiting for transfers between devices, on_device(): lax.ppermute(first_sums if groups > 2 else ran[1], 'expert', forward)  15.9 us
    pallas_call x1, Pallas kernels, attend(): pl.pallas_call(attend_kernel, grid_spec=pltpu.PrefetchScalarGridSpec(num_...  12.6 us
    unnamed x48, local copies, waits for them, and re-layouts  12.4 us
    pallas_call x1, Pallas kernels, project(): pl.pallas_call(project_kernel, grid_spec=pltpu.PrefetchScalarGridSpec(num...  10.4 us
    pallas_call x1, Pallas kernels, open_back(): pl.pallas_call(body, grid_spec=pltpu.PrefetchScalarGridSpec(num_scalar_pr...  9.6 us
  transfers between devices with their start and end apart: 19, of which 12 were waited for; matrix products, arithmetic and copies ran while one was open for 8% of the time, Pallas kernels for 53%

profile of v8, /device:TPU:0, one launch (start us, length us, event | category | flops | bytes accessed | tf_op | source)
XLA Modules:
  0.0 340.2 jit_solution(5205759712448903867)
XLA Ops:
  0.7 2.1 pack.1
  2.8 3.0 collective-permute-start.1
  5.8 1.5 collective-permute-start
  10.7 1.3 gather_fusion.1
  12.0 3.4 %all-to-all-start = ((bf16[8,112,128]{2,1,0:T(8,128)(2,1)}), bf16[8,112,128]{2,1,0:T(8,128)(2,1)S(1)}, u32[]{:S(2)}, u32[]{:S(2)}) async-start(bf16[8,112,128]{2,1,0:T(8,128)(2,1)} %gather_fusion.1), calls=%async_computation | async-start | bytes 458752 | tf_op jit(solution)/shard_map/all_to_all | solution.py:1040
  15.4 1.6 collective-permute-start.4
  21.1 1.2 constant_dynamic-update-slice_fusion.4
  22.3 2.0 collective-permute-done.1
  24.3 2.1 collective-permute-done
  28.4 1.6 collective-permute-start.2
  30.5 1.2 constant_dynamic-update-slice_fusion.3
  31.7 1.2 constant_dynamic-update-slice_fusion.2
  32.8 4.1 %collective-permute-done.2 = bf16[64,3072]{1,0:T(8,128)(2,1)S(1)} collective-permute-done((bf16[64,3072]{1,0:T(8,128)(2,1)S(1)}, bf16[64,3072]{1,0:T(8,128)(2,1)S(1)}, u32[]{:S(2)}, u32[]{:S(2)}) %collective-permute-start.2) | collective-permute-done | bytes 393248 | tf_op jit(solution)/shard_map/ppermute | solution.py:954
  37.0 1.2 collective-permute-done.3
  38.2 4.8 %collective-permute-done.4.cot = bf16[512,1024]{1,0:T(8,128)(2,1)} collective-permute-done((bf16[512,1024]{1,0:T(8,128)(2,1)}, bf16[512,1024]{1,0:T(8,128)(2,1)}, u32[]{:S(2)}, u32[]{:S(2)}) %collective-permute-start.4) | collective-permute-done | bytes 1048608 | tf_op jit(solution)/shard_map/ppermute | solution.py:1065
  43.0 1.4 copy.60.routes
  45.8 1.7 collective-permute-start.7
  49.0 10.4 %project.1 = (bf16[512,2048]{1,0:T(8,128)(2,1)}, bf16[512,64]{1,0:T(8,128)(2,1)}, bf16[512,1024]{1,0:T(8,128)(2,1)}) custom-call(s32[8]{0:T(128)} %broadcast_xor_fusion.order.refs_0_, bf16[512,1024]{1,0:T(8,128)(2,1)} %hid.5, bf16[1,1024]{1,0:T(2,128)(2,1)} %reshape.89.gain, bf16[512,3072]{1,0:T(8,128)(2,1)} %copy-done, ...), custom_call_target="tpu_custom_call" | custom-call | flops 2147483648 | bytes 8388608 | tf_op jit(solution)/shard_map/project/pallas_call | solution.py:141
  59.7 12.6 %attend.1 = (bf16[512,1024]{1,0:T(8,128)(2,1)}, f32[8,2,512]{2,1,0:T(2,128)}) custom-call(s32[1]{0:T(128)} %dynamic_slice.15.scalars, bf16[512,2048]{1,0:T(8,128)(2,1)} %get-tuple-element.79.query.key.value, bf16[512,2048]{1,0:T(8,128)(2,1)} %get-tuple-element.79.query.key.value, bf16[512,2048]{1,0:T(8,128)(2,1)} %get-tuple-element.79.query.key.value), custom_call_target="tpu_custom_call" | custom-call | flops 2147483648 | bytes 4194304 | tf_op jit(solution)/shard_map/attend/pallas_call | solution.py:224
  72.3 6.0 %close_mixer.1 = (f32[512,1024]{1,0:T(8,128)}, bf16[512,1024]{1,0:T(8,128)(2,1)}, bf16[512,64]{1,0:T(8,128)(2,1)}) custom-call(s32[8]{0:T(128)} %broadcast_xor_fusion.order.refs_0_, bf16[512,1024]{1,0:T(8,128)(2,1)} %get-tuple-element.80.att.refs_11_, bf16[512,1024]{1,0:T(8,128)(2,1)} %hid.5, bf16[1,1024]{1,0:T(2,128)(2,1)} %reshape.90.gain.refs_3_, ...), custom_call_target="tpu_custom_call" | custom-call | flops 1073741824 | bytes 8388608 | tf_op jit(solution)/shard_map/close_mixer/pallas_call | solution.py:357
  78.3 1.3 collective-permute-start.8
  79.6 27.6 %experts.4 = (bf16[1040,1024]{1,0:T(8,128)(2,1)}, f32[16,512]{1,0:T(8,128)}, bf16[8,4,288,128]{3,2,1,0:T(8,128)(2,1)}) custom-call(s32[5]{0:T(128)} %get-tuple-element.140.scalars, bf16[512,1024]{1,0:T(8,128)(2,1)} %get-tuple-element.88.x, bf16[512,1024]{1,0:T(8,128)(2,1)} %refs_1_, s32[2048,8]{1,0:T(8,128)} %copy.60.routes, ...), custom_call_target="tpu_custom_call" | custom-call | flops 19327352832 | bytes 20971520 | tf_op jit(solution)/shard_map/experts/pallas_call | solution.py:558
  107.3 3.2 collective-permute-start.6
  110.5 6.7 %collective-permute-done.8.x = bf16[512,1024]{1,0:T(8,128)(2,1)S(1)} collective-permute-done((bf16[512,1024]{1,0:T(8,128)(2,1)}, bf16[512,1024]{1,0:T(8,128)(2,1)S(1)}, u32[]{:S(2)}, u32[]{:S(2)}) %collective-permute-start.8) | collective-permute-done | bytes 1048608 | tf_op jit(solution)/shard_map/ppermute | solution.py:1111
  118.2 26.8 %experts.5 = (bf16[1040,1024]{1,0:T(8,128)(2,1)}, f32[16,512]{1,0:T(8,128)}, bf16[8,4,288,128]{3,2,1,0:T(8,128)(2,1)}) custom-call(s32[5]{0:T(128)} %get-tuple-element.138.scalars, bf16[512,1024]{1,0:T(8,128)(2,1)} %copy-done.15, bf16[512,1024]{1,0:T(8,128)(2,1)} %collective-permute-done.4.cot, ...), custom_call_target="tpu_custom_call", output_to_operand_aliasing={{2}: (11, {})} | custom-call | flops 19327352832 | bytes 20971520 | tf_op jit(solution)/shard_map/experts/pallas_call | solution.py:558
  145.1 1.7 collective-permute-start.9
  148.1 26.8 %experts.6 = (bf16[1040,1024]{1,0:T(8,128)(2,1)}, f32[16,512]{1,0:T(8,128)}, bf16[8,4,288,128]{3,2,1,0:T(8,128)(2,1)}) custom-call(s32[5]{0:T(128)} %get-tuple-element.139.scalars, bf16[512,1024]{1,0:T(8,128)(2,1)} %copy-done.18, bf16[512,1024]{1,0:T(8,128)(2,1)} %copy-done.14, s32[2048,8]{1,0:T(8,128)} %copy.60.routes, ...), custom_call_target="tpu_custom_call", output_to_operand_aliasing={{2}: (11, {})} | custom-call | flops 19327352832 | bytes 20971520 | tf_op jit(solution)/shard_map/experts/pallas_call | solution.py:558
  174.9 1.6 collective-permute-start.11
  176.5 1.0 copy-done.13
  177.8 26.7 %experts.7 = (bf16[1040,1024]{1,0:T(8,128)(2,1)}, f32[16,512]{1,0:T(8,128)}, bf16[8,4,288,128]{3,2,1,0:T(8,128)(2,1)}) custom-call(s32[5]{0:T(128)} %get-tuple-element.137.scalars, bf16[512,1024]{1,0:T(8,128)(2,1)} %copy-done.16, bf16[512,1024]{1,0:T(8,128)(2,1)} %copy-done.13, s32[2048,8]{1,0:T(8,128)} %copy.60.routes, ...), custom_call_target="tpu_custom_call", output_to_operand_aliasing={{2}: (11, {})} | custom-call | flops 19327352832 | bytes 20971520 | tf_op jit(solution)/shard_map/experts/pallas_call | solution.py:558
  204.6 3.8 %all-to-all-start.1 = ((bf16[8,4,288,128]{3,2,1,0:T(8,128)(2,1)}), bf16[8,4,288,128]{3,2,1,0:T(8,128)(2,1)S(1)}, u32[]{:S(2)}, u32[]{:S(2)}) async-start(bf16[8,4,288,128]{3,2,1,0:T(8,128)(2,1)} %get-tuple-element.104), calls=%async_computation.1 | async-start | bytes 4718592 | tf_op jit(solution)/shard_map/all_to_all | solution.py:1142
  208.4 15.9 %collective-permute-done.11 = bf16[1040,1024]{1,0:T(8,128)(2,1)} collective-permute-done((bf16[1040,1024]{1,0:T(8,128)(2,1)}, bf16[1040,1024]{1,0:T(8,128)(2,1)}, u32[]{:S(2)}, u32[]{:S(2)}) %collective-permute-start.11) | collective-permute-done | bytes 2129952 | tf_op jit(solution)/shard_map/ppermute | solution.py:1147
  224.3 3.0 add_convert_fusion.1
  228.4 9.4 %all-to-all-done.1 = bf16[8,4,288,128]{3,2,1,0:T(8,128)(2,1)S(1)} async-done(((bf16[8,4,288,128]{3,2,1,0:T(8,128)(2,1)}), bf16[8,4,288,128]{3,2,1,0:T(8,128)(2,1)S(1)}, u32[]{:S(2)}, u32[]{:S(2)}) %all-to-all-start.1) | async-done | bytes 2359328 | tf_op jit(solution)/shard_map/all_to_all | solution.py:1142
  237.9 1.5 copy-done.2
  239.3 3.6 %sum_experts.1 = (f32[4,8,32,128]{3,2,1,0:T(8,128)}, f32[4,8,2,16,64]{4,3,2,1,0:T(8,128)}, f32[4,8,16,64]{3,2,1,0:T(8,128)}, f32[4,8,16,128]{3,2,1,0:T(8,128)}) custom-call(s32[32]{0:T(128)} %reshape.97.ids, bf16[32,288,128]{2,1,0:T(8,128)(2,1)} %bitcast.39), custom_call_target="tpu_custom_call" | custom-call | tf_op jit(solution)/shard_map/sum_experts/pallas_call | solution.py:891
  242.9 10.3 %collective-permute-done.12 = bf16[528,1024]{1,0:T(8,128)(2,1)S(1)} collective-permute-done((bf16[528,1024]{1,0:T(8,128)(2,1)}, bf16[528,1024]{1,0:T(8,128)(2,1)S(1)}, u32[]{:S(2)}, u32[]{:S(2)}) %collective-permute-start.12) | collective-permute-done | bytes 1081376 | tf_op jit(solution)/shard_map/ppermute | solution.py:1153
  253.6 1.9 add_convert_fusion.4
  255.6 22.8 %collective-permute-done.13.refs_13_.refs_16_.refs_17_ = bf16[528,1024]{1,0:T(8,128)(2,1)S(1)} collective-permute-done((bf16[528,1024]{1,0:T(8,128)(2,1)S(1)}, bf16[528,1024]{1,0:T(8,128)(2,1)S(1)}, u32[]{:S(2)}, u32[]{:S(2)}) %collective-permute-start.13) | collective-permute-done | bytes 1081376 | tf_op jit(solution)/shard_map/ppermute | solution.py:1153
  279.4 9.6 %open_back.1 = (f32[512,1024]{1,0:T(8,128)}, bf16[512,1024]{1,0:T(8,128)(2,1)}, f32[64,1024]{1,0:T(8,128)}, f32[64,1024]{1,0:T(8,128)}) custom-call(s32[8]{0:T(128)} %broadcast_xor_fusion.order.refs_0_, bf16[512,1024]{1,0:T(8,128)(2,1)} %refs_1_, f32[512,1024]{1,0:T(8,128)} %get-tuple-element.82.refs_2_, bf16[1,1024]{1,0:T(2,128)(2,1)} %reshape.90.gain.refs_3_, ...), custom_call_target="tpu_custom_call" | custom-call | flops 1073741824 | bytes 14680064 | tf_op jit(solution)/shard_map/open_back/pallas_call | solution.py:691
  289.0 18.1 %attend_back.1 = (bf16[512,1024]{1,0:T(8,128)(2,1)}, bf16[512,512]{1,0:T(8,128)(2,1)}, bf16[512,512]{1,0:T(8,128)(2,1)}) custom-call(s32[1]{0:T(128)} %dynamic_slice.15.scalars, bf16[512,2048]{1,0:T(8,128)(2,1)} %get-tuple-element.79.query.key.value, bf16[512,2048]{1,0:T(8,128)(2,1)} %get-tuple-element.79.query.key.value, ...), custom_call_target="tpu_custom_call" | custom-call | flops 5368709120 | bytes 8388608 | tf_op jit(solution)/shard_map/attend_back/pallas_call | solution.py:304
  307.5 4.5 %adapters_back.1 = (bf16[512,64]{1,0:T(8,128)(2,1)}, bf16[32,16,256]{2,1,0:T(8,128)(2,1)}) custom-call(bf16[512,1024]{1,0:T(8,128)(2,1)} %get-tuple-element.116.grad_query, bf16[512,512]{1,0:T(8,128)(2,1)} %get-tuple-element.117.grad_key, bf16[512,512]{1,0:T(8,128)(2,1)} %get-tuple-element.118.grad_value, bf16[512,64]{1,0:T(8,128)(2,1)} %get-tuple-element.119.low, ...), custom_call_target="tpu_custom_call" | custom-call | flops 1610612736 | bytes 4194304 | tf_op jit(solution)/shard_map/adapters_back/pallas_call | solution.py:791
  312.0 6.1 %all-to-all-start.2 = ((bf16[32,16,256]{2,1,0:T(8,128)(2,1)}), bf16[32,16,256]{2,1,0:T(8,128)(2,1)S(1)}, u32[]{:S(2)}, u32[]{:S(2)}) async-start(bf16[32,16,256]{2,1,0:T(8,128)(2,1)} %get-tuple-element.123), calls=%async_computation.2 | async-start | bytes 524288 | tf_op jit(solution)/shard_map/all_to_all | solution.py:1180
  318.2 8.6 %input_back.1 = bf16[512,1024]{1,0:T(8,128)(2,1)} custom-call(s32[8]{0:T(128)} %broadcast_xor_fusion.order.refs_0_, bf16[512,1024]{1,0:T(8,128)(2,1)} %get-tuple-element.116.grad_query, bf16[512,512]{1,0:T(8,128)(2,1)} %get-tuple-element.117.grad_key, bf16[512,512]{1,0:T(8,128)(2,1)} %get-tuple-element.118.grad_value, ...), custom_call_target="tpu_custom_call" | custom-call | flops 2147483648 | bytes 12582912 | tf_op jit(solution)/shard_map/input_back/pallas_call | solution.py:836
  326.8 6.1 %collective-permute-done.15 = bf16[512,1024]{1,0:T(8,128)(2,1)S(1)} collective-permute-done((bf16[512,1024]{1,0:T(8,128)(2,1)S(1)}, bf16[512,1024]{1,0:T(8,128)(2,1)S(1)}, u32[]{:S(2)}, u32[]{:S(2)}) %collective-permute-start.15) | collective-permute-done | bytes 1048608 | tf_op jit(solution)/shard_map/ppermute | solution.py:1176
  332.9 2.7 add_convert_fusion.2
  335.6 1.4 all-to-all-done.2.pieces
  337.7 2.0 sum_mixer.1
  (93 shorter events, 19.5 us)
Async XLA Ops:
  0.6 19.8 %copy-start.12 = (s32[4,1]{1,0:T(4,128)S(1)}, s32[4,1]{1,0:T(4,128)}, u32[]{:S(2)}) copy-start(s32[4,1]{1,0:T(4,128)} %constant.84) | copy-start | bytes 52
  0.7 19.9 %copy-start.20 = (s32[8]{0:T(128)S(1)}, s32[8]{0:T(128)}, u32[]{:S(2)}) copy-start(s32[8]{0:T(128)} %constant.74.clone) | copy-start | bytes 100
  0.7 10.0 %copy-start.8 = (bf16[8,16,128]{2,1,0:T(8,128)(2,1)S(1)}, bf16[8,16,128]{2,1,0:T(8,128)(2,1)}, u32[]{:S(2)}) copy-start(bf16[8,16,128]{2,1,0:T(8,128)(2,1)} %param.37) | copy-start | bytes 98308
  0.7 16.5 %copy-start.10 = (bf16[1024]{0:T(1024)(128)(2,1)S(1)}, bf16[1024]{0:T(1024)(128)(2,1)}, u32[]{:S(2)}) copy-start(bf16[1024]{0:T(1024)(128)(2,1)} %param.28) | copy-start | bytes 6148
  0.7 17.1 %copy-start.11 = (bf16[1024]{0:T(1024)(128)(2,1)S(1)}, bf16[1024]{0:T(1024)(128)(2,1)}, u32[]{:S(2)}) copy-start(bf16[1024]{0:T(1024)(128)(2,1)} %param.29) | copy-start | bytes 6148
  0.7 17.7 %copy-start.19 = (s32[32]{0:T(128)S(1)}, s32[32]{0:T(128)}, u32[]{:S(2)}) copy-start(s32[32]{0:T(128)} %param.25) | copy-start | bytes 388
  0.7 18.8 %copy-start.9 = (bf16[1024,16]{0,1:T(8,128)(2,1)S(1)}, bf16[1024,16]{0,1:T(8,128)(2,1)}, u32[]{:S(2)}) copy-start(bf16[1024,16]{0,1:T(8,128)(2,1)} %param.32) | copy-start | bytes 98308
  2.8 21.5 %collective-permute-start.1 = (bf16[128,3072]{1,0:T(8,128)(2,1)}, bf16[128,3072]{1,0:T(8,128)(2,1)}, u32[]{:S(2)}, u32[]{:S(2)}) collective-permute-start(bf16[128,3072]{1,0:T(8,128)(2,1)} %pack.1), channel_id=1, source_target_pairs={{0,16},{4,20},{8,24},{12,28},{16,0},{20,4},{24,8},{28,12},{1,17},{... | collective-permute-start | bytes 2359304 | tf_op jit(solution)/shard_map/ppermute | solution.py:954
  5.8 20.5 %collective-permute-start = (bf16[128,3072]{1,0:T(8,128)(2,1)}, bf16[128,3072]{1,0:T(8,128)(2,1)}, u32[]{:S(2)}, u32[]{:S(2)}) collective-permute-start(bf16[128,3072]{1,0:T(8,128)(2,1)} %pack.1), channel_id=1, source_target_pairs={{0,8},{4,12},{8,0},{12,4},{16,24},{20,28},{24,16},{28,20},{1,9},{5... | collective-permute-start | bytes 2359304 | tf_op jit(solution)/shard_map/ppermute | solution.py:954
  12.0 26.2 %all-to-all-start = ((bf16[8,112,128]{2,1,0:T(8,128)(2,1)}), bf16[8,112,128]{2,1,0:T(8,128)(2,1)S(1)}, u32[]{:S(2)}, u32[]{:S(2)}) async-start(bf16[8,112,128]{2,1,0:T(8,128)(2,1)} %gather_fusion.1), calls=%async_computation | async-start | bytes 458752 | tf_op jit(solution)/shard_map/all_to_all | solution.py:1040
  15.4 27.6 %collective-permute-start.4 = (bf16[512,1024]{1,0:T(8,128)(2,1)}, bf16[512,1024]{1,0:T(8,128)(2,1)}, u32[]{:S(2)}, u32[]{:S(2)}) collective-permute-start(bf16[512,1024]{1,0:T(8,128)(2,1)} %refs_1_), channel_id=1, source_target_pairs={{0,1},{1,2},{2,3},{3,0},{4,5},{5,6},{6,7},{7,4},{8,9},{9,10},{10,1... | collective-permute-start | bytes 3145736 | tf_op jit(solution)/shard_map/ppermute | solution.py:1065
  19.6 12.0 %copy-start.6 = (bf16[16,1024]{1,0:T(8,128)(2,1)}, bf16[16,1024]{1,0:T(8,128)(2,1)S(1)}, u32[]{:S(2)}) copy-start(bf16[16,1024]{1,0:T(8,128)(2,1)S(1)} %fusion.refs_5_) | copy-start | bytes 98308
  28.4 14.7 %copy-start.7 = (s32[2048,8]{0,1:T(8,128)S(1)}, s32[2048,8]{0,1:T(8,128)}, u32[]{:S(2)}) copy-start(s32[2048,8]{0,1:T(8,128)} %param.27) | copy-start | bytes 196612
  28.4 8.6 %collective-permute-start.2 = (bf16[64,3072]{1,0:T(8,128)(2,1)S(1)}, bf16[64,3072]{1,0:T(8,128)(2,1)S(1)}, u32[]{:S(2)}, u32[]{:S(2)}) collective-permute-start(bf16[64,3072]{1,0:T(8,128)(2,1)S(1)} %slice.48), channel_id=1, source_target_pairs={{0,8},{4,12},{8,0},{12,4},{16,24},{20,28},{24,16},{28,20},{1,9},{5... | collective-permute-start | bytes 1179656 | tf_op jit(solution)/shard_map/ppermute | solution.py:954
  30.0 8.2 %collective-permute-start.3 = (bf16[64,3072]{1,0:T(8,128)(2,1)S(1)}, bf16[64,3072]{1,0:T(8,128)(2,1)S(1)}, u32[]{:S(2)}, u32[]{:S(2)}) collective-permute-start(bf16[64,3072]{1,0:T(8,128)(2,1)S(1)} %slice.49), channel_id=1, source_target_pairs={{0,16},{4,20},{8,24},{12,28},{16,0},{20,4},{24,8},{28,12},{1,17},{... | collective-permute-start | bytes 1179656 | tf_op jit(solution)/shard_map/ppermute | solution.py:954
  38.2 10.8 %copy-start = (bf16[512,3072]{1,0:T(8,128)(2,1)}, bf16[512,3072]{1,0:T(8,128)(2,1)S(1)}, u32[]{:S(2)}) copy-start(bf16[512,3072]{1,0:T(8,128)(2,1)S(1)} %constant_dynamic-update-slice_fusion.weight_a.refs_6_) | copy-start | bytes 9437188
  43.0 6.0 %collective-permute-start.5 = (bf16[512,3072]{1,0:T(8,128)(2,1)S(1)}, bf16[512,3072]{1,0:T(8,128)(2,1)}, u32[]{:S(2)}, u32[]{:S(2)}) collective-permute-start(bf16[512,3072]{1,0:T(8,128)(2,1)S(1)} %constant_dynamic-update-slice_fusion.weight_a.refs_6_), channel_id=1, source_target_pairs={{0,4},{4,0},{8,12},{12,8},{16,20},{20,16},{24,28},{28,24},{1,5},{5... | collective-permute-start | bytes 9437192 | tf_op jit(solution)/shard_map/ppermute | solution.py:954
  45.8 101.0 %collective-permute-start.7 = (bf16[512,1024]{1,0:T(8,128)(2,1)}, bf16[512,1024]{1,0:T(8,128)(2,1)S(1)}, u32[]{:S(2)}, u32[]{:S(2)}) collective-permute-start(bf16[512,1024]{1,0:T(8,128)(2,1)} %refs_1_), channel_id=1, source_target_pairs={{0,3},{1,0},{2,1},{3,2},{4,7},{5,4},{6,5},{7,6},{8,11},{9,8},{10,9... | collective-permute-start | bytes 3145736 | tf_op jit(solution)/shard_map/ppermute | solution.py:1078
  59.4 117.1 %collective-permute-start.10 = (bf16[512,1024]{1,0:T(8,128)(2,1)}, bf16[512,1024]{1,0:T(8,128)(2,1)S(1)}, u32[]{:S(2)}, u32[]{:S(2)}) collective-permute-start(bf16[512,1024]{1,0:T(8,128)(2,1)} %collective-permute-done.4.cot), channel_id=1, source_target_pairs={{0,1},{1,2},{2,3},{3,0},{4,5},{5,6},{6,7},{7,4},{8,9},{9,10},{10,1... | collective-permute-start | bytes 3145736 | tf_op jit(solution)/shard_map/ppermute | solution.py:1102
  78.3 39.0 %collective-permute-start.8 = (bf16[512,1024]{1,0:T(8,128)(2,1)}, bf16[512,1024]{1,0:T(8,128)(2,1)S(1)}, u32[]{:S(2)}, u32[]{:S(2)}) collective-permute-start(bf16[512,1024]{1,0:T(8,128)(2,1)} %get-tuple-element.88.x), channel_id=1, source_target_pairs={{0,1},{1,2},{2,3},{3,0},{4,5},{5,6},{6,7},{7,4},{8,9},{9,10},{10,1... | collective-permute-start | bytes 3145736 | tf_op jit(solution)/shard_map/ppermute | solution.py:1111
  79.6 27.6 %copy-start.17 = (bf16[512,1024]{1,0:T(8,128)(2,1)S(1)}, bf16[512,1024]{1,0:T(8,128)(2,1)}, u32[]{:S(2)}) copy-start(bf16[512,1024]{1,0:T(8,128)(2,1)} %get-tuple-element.88.x) | copy-start | bytes 3145732
  107.3 39.5 %collective-permute-start.6 = (bf16[512,1024]{1,0:T(8,128)(2,1)S(1)}, bf16[512,1024]{1,0:T(8,128)(2,1)S(1)}, u32[]{:S(2)}, u32[]{:S(2)}) collective-permute-start(bf16[512,1024]{1,0:T(8,128)(2,1)S(1)} %copy-done.17), channel_id=1, source_target_pairs={{0,3},{1,0},{2,1},{3,2},{4,7},{5,4},{6,5},{7,6},{8,11},{9,8},{10,9... | collective-permute-start | bytes 3145736 | tf_op jit(solution)/shard_map/ppermute | solution.py:1135
  117.3 1.0 copy-start.15
  145.1 31.4 %collective-permute-start.9 = (bf16[512,1024]{1,0:T(8,128)(2,1)}, bf16[512,1024]{1,0:T(8,128)(2,1)S(1)}, u32[]{:S(2)}, u32[]{:S(2)}) collective-permute-start(bf16[512,1024]{1,0:T(8,128)(2,1)} %copy-done.15), channel_id=1, source_target_pairs={{0,1},{1,2},{2,3},{3,0},{4,5},{5,6},{6,7},{7,4},{8,9},{9,10},{10,1... | collective-permute-start | bytes 3145736 | tf_op jit(solution)/shard_map/ppermute | solution.py:1138
  146.8 1.0 copy-start.14
  146.8 1.3 copy-start.18
  174.9 49.5 %collective-permute-start.11 = (bf16[1040,1024]{1,0:T(8,128)(2,1)}, bf16[1040,1024]{1,0:T(8,128)(2,1)}, u32[]{:S(2)}, u32[]{:S(2)}) collective-permute-start(bf16[1040,1024]{1,0:T(8,128)(2,1)} %get-tuple-element.102), channel_id=1, source_target_pairs={{0,1},{1,2},{2,3},{3,0},{4,5},{5,6},{6,7},{7,4},{8,9},{9,10},{10,1... | collective-permute-start | bytes 6389768 | tf_op jit(solution)/shard_map/ppermute | solution.py:1147
  176.5 1.1 copy-start.13
  176.5 1.4 copy-start.16
  204.6 33.3 %all-to-all-start.1 = ((bf16[8,4,288,128]{3,2,1,0:T(8,128)(2,1)}), bf16[8,4,288,128]{3,2,1,0:T(8,128)(2,1)S(1)}, u32[]{:S(2)}, u32[]{:S(2)}) async-start(bf16[8,4,288,128]{3,2,1,0:T(8,128)(2,1)} %get-tuple-element.104), calls=%async_computation.1 | async-start | bytes 4718592 | tf_op jit(solution)/shard_map/all_to_all | solution.py:1142
  227.3 25.8 %collective-permute-start.12 = (bf16[528,1024]{1,0:T(8,128)(2,1)}, bf16[528,1024]{1,0:T(8,128)(2,1)S(1)}, u32[]{:S(2)}, u32[]{:S(2)}) collective-permute-start(bf16[528,1024]{1,0:T(8,128)(2,1)} %add_convert_fusion.1), channel_id=1, source_target_pairs={{0,1},{1,2},{2,3},{3,0},{4,5},{5,6},{6,7},{7,4},{8,9},{9,10},{10,1... | collective-permute-start | bytes 3244040 | tf_op jit(solution)/shard_map/ppermute | solution.py:1153
  237.8 1.5 copy-start.2
  237.8 15.3 %copy-start.4 = (bf16[1040,1024]{1,0:T(8,128)(2,1)S(1)}, bf16[1040,1024]{1,0:T(8,128)(2,1)}, u32[]{:S(2)}) copy-start(bf16[1040,1024]{1,0:T(8,128)(2,1)} %get-tuple-element.96) | copy-start | bytes 6389764
  253.6 24.8 %collective-permute-start.13 = (bf16[528,1024]{1,0:T(8,128)(2,1)S(1)}, bf16[528,1024]{1,0:T(8,128)(2,1)S(1)}, u32[]{:S(2)}, u32[]{:S(2)}) collective-permute-start(bf16[528,1024]{1,0:T(8,128)(2,1)S(1)} %add_convert_fusion), channel_id=1, source_target_pairs={{0,1},{1,2},{2,3},{3,0},{4,5},{5,6},{6,7},{7,4},{8,9},{9,10},{10,1... | collective-permute-start | bytes 3244040 | tf_op jit(solution)/shard_map/ppermute | solution.py:1153
  278.4 1.0 copy-start.1
  278.4 28.7 %collective-permute-start.14 = (bf16[512,1024]{1,0:T(8,128)(2,1)S(1)}, bf16[512,1024]{1,0:T(8,128)(2,1)S(1)}, u32[]{:S(2)}, u32[]{:S(2)}) collective-permute-start(bf16[512,1024]{1,0:T(8,128)(2,1)S(1)} %add_convert_fusion.4), channel_id=1, source_target_pairs={{0,1},{1,2},{2,3},{3,0},{4,5},{5,6},{6,7},{7,4},{8,9},{9,10},{10,1... | collective-permute-start | bytes 3145736 | tf_op jit(solution)/shard_map/ppermute | solution.py:1157
  307.5 25.4 %collective-permute-start.15 = (bf16[512,1024]{1,0:T(8,128)(2,1)S(1)}, bf16[512,1024]{1,0:T(8,128)(2,1)S(1)}, u32[]{:S(2)}, u32[]{:S(2)}) collective-permute-start(bf16[512,1024]{1,0:T(8,128)(2,1)S(1)} %add_convert_fusion.3), channel_id=1, source_target_pairs={{0,1},{1,2},{2,3},{3,0},{4,5},{5,6},{6,7},{7,4},{8,9},{9,10},{10,1... | collective-permute-start | bytes 3145736 | tf_op jit(solution)/shard_map/ppermute | solution.py:1176
  312.0 25.0 %all-to-all-start.2 = ((bf16[32,16,256]{2,1,0:T(8,128)(2,1)}), bf16[32,16,256]{2,1,0:T(8,128)(2,1)S(1)}, u32[]{:S(2)}, u32[]{:S(2)}) async-start(bf16[32,16,256]{2,1,0:T(8,128)(2,1)} %get-tuple-element.123), calls=%async_computation.2 | async-start | bytes 524288 | tf_op jit(solution)/shard_map/all_to_all | solution.py:1180
  318.2 14.7 %copy-start.3 = (f32[512,1024]{1,0:T(8,128)S(1)}, f32[512,1024]{1,0:T(8,128)}, u32[]{:S(2)}) copy-start(f32[512,1024]{1,0:T(8,128)} %get-tuple-element.82.refs_2_) | copy-start | bytes 6291460
  337.0 0.7 copy-start.5

commit v9 on v8

--- a/solution.py
+++ b/solution.py
@@ -992,6 +992,24 @@
     return (left.astype(f32) + right.astype(f32)).astype(bf16)
 
 
+def maps_of(adapters, owners, width):
+    low_map = adapters[:, : 4 * R].transpose(1, 0, 2).reshape(4 * R, MODEL_WIDTH)
+    up = (
+        adapters[:, 4 * R : 6 * R]
+        .reshape(owners, 2, R, width)
+        .transpose(2, 0, 1, 3)
+        .reshape(R, QKV)
+    )
+    up_out = adapters[:, 6 * R :].transpose(1, 0, 2).reshape(R, MODEL_WIDTH)
+    column = jnp.arange(QKV, dtype=jnp.int32)
+    part = jnp.where(column < QD, 0, jnp.where(column < QD + KD, 1, 2))
+    up_map = jnp.where(
+        part[None, None, :] == jnp.arange(4, dtype=jnp.int32)[:, None, None], up[None], 0
+    ).reshape(4 * R, QKV)
+    up_out_map = jnp.concatenate([jnp.zeros((3 * R, MODEL_WIDTH), bf16), up_out], 0)
+    return low_map, up_map, up_out_map
+
+
 def on_device(
     hidden,
     cotangent,
@@ -1061,36 +1079,27 @@
         1,
     )
 
+    steps = [table[at] for at in range(groups)]
     both = pack(query_key_value_weight, w_out)
     cots = {0: cotangent, 1: lax.ppermute(cotangent, "expert", forward)}
     if owners == BLOCKS:
         pair = both_neighbours(both)
-        pair, order, router, router_wide, table, tags, attn_gain, ffn_gain, length = tied(
-            pair, order, router, router_wide, table, tags, attn_gain, ffn_gain, length
+        pair, order, router, router_wide, steps, tags, attn_gain, ffn_gain, length = tied(
+            pair, order, router, router_wide, steps, tags, attn_gain, ffn_gain, length
         )
-        near = jnp.concatenate([both, *pair, *across(pair)], 0)
-        near, adapters, cots[1], cotangent = tied(near, adapters, cots[1], cotangent)
+        sides, adapters = tied(across(pair), adapters)
+        low_map, up_map, up_out_map = maps_of(adapters, owners, width)
+        near = jnp.concatenate([both, *pair, *sides], 0)
+        near, low_map, up_map, up_out_map, cots[1], cotangent = tied(
+            near, low_map, up_map, up_out_map, cots[1], cotangent
+        )
         weights = near, swap(near, 1)
     else:
+        low_map, up_map, up_out_map = maps_of(adapters, owners, width)
         whole = lax.all_gather(both, "dp", axis=0, tiled=True)
         weights = whole, whole
     if groups > 2:
         cots[groups - 1] = lax.ppermute(cotangent, "expert", backward)
-
-    low_map = adapters[:, : 4 * R].transpose(1, 0, 2).reshape(4 * R, MODEL_WIDTH)
-    up = (
-        adapters[:, 4 * R : 6 * R]
-        .reshape(owners, 2, R, width)
-        .transpose(2, 0, 1, 3)
-        .reshape(R, QKV)
-    )
-    up_out = adapters[:, 6 * R :].transpose(1, 0, 2).reshape(R, MODEL_WIDTH)
-    column = jnp.arange(QKV, dtype=jnp.int32)
-    part = jnp.where(column < QD, 0, jnp.where(column < QD + KD, 1, 2))
-    up_map = jnp.where(
-        part[None, None, :] == jnp.arange(4, dtype=jnp.int32)[:, None, None], up[None], 0
-    ).reshape(4 * R, QKV)
-    up_out_map = jnp.concatenate([jnp.zeros((3 * R, MODEL_WIDTH), bf16), up_out], 0)
 
     cos, sin = rope_tables(rows)
 
@@ -1113,7 +1122,7 @@
     ran = {}
     for at, offset in enumerate(offsets):
         ran[offset], gate_part, packed = run_experts(
-            table[at],
+            steps[at],
             xs[offset],
             cots[offset],
             routes,

time: 346 us -> 348 us (level)
  local copies, waits for them, and re-layouts: 23.6 us -> 29.4 us
  waiting for transfers between devices: 86.8 us -> 81.5 us
    ppermute x1, waiting for transfers between devices: 4.81 us -> 0.01 us  [on_device(): cots = {0: cotangent, 1: lax.ppermute(cotangent, 'expert', forward)}]
    unnamed x48 -> x46, local copies, waits for them, and re-layouts: 12.4 us -> 15.7 us
  transfers between devices with their start and end apart: 19 -> 19, of which waited for: 12 -> 11; matrix products, arithmetic and copies ran while one was open for 8% -> 9% of each run, Pallas kernels for 53% -> 53%
where the time goes in v9:
time: 348 us; the launch traced here: 342 us
  Pallas kernels  185 us (53%)
  waiting for transfers between devices  81.5 us (23%)
  starting transfers between devices  33.3 us (10%)
  local copies, waits for them, and re-layouts  29.4 us (8%)
  other arithmetic  10.7 us (3%)
    pallas_call x4, Pallas kernels, run_experts(): pl.pallas_call(expert_kernel, grid_spec=pltpu.PrefetchScalarGridSpec(num_...  108 us
    ppermute x2, waiting for transfers between devices, on_device(): grad_far = lax.ppermute(grad_part, 'expert', forward)  32.1 us
    pallas_call x1, Pallas kernels, attend_back(): pl.pallas_call(attend_back_kernel, grid_spec=pltpu.PrefetchScalarGridSpec...  18.1 us
    unnamed x46, local copies, waits for them, and re-layouts  15.7 us
    ppermute x1, waiting for transfers between devices, on_device(): lax.ppermute(first_sums if groups > 2 else ran[1], 'expert', forward)  15.2 us
    pallas_call x1, Pallas kernels, attend(): pl.pallas_call(attend_kernel, grid_spec=pltpu.PrefetchScalarGridSpec(num_...  12.7 us
    pallas_call x1, Pallas kernels, project(): pl.pallas_call(project_kernel, grid_spec=pltpu.PrefetchScalarGridSpec(num...  10.4 us
    all_to_all x1, waiting for transfers between devices, on_device(): lax.all_to_all(to_owners(packed, owners, local), 'dp', 0, 0, tiled=True)  9.91 us
  transfers between devices with their start and end apart: 19, of which 11 were waited for; matrix products, arithmetic and copies ran while one was open for 9% of the time, Pallas kernels for 53%

profile of v9, /device:TPU:0, one launch (start us, length us, event | category | flops | bytes accessed | tf_op | source)
XLA Modules:
  0.0 341.8 jit_solution(17218278891801025515)
XLA Ops:
  0.7 2.1 pack.1
  2.8 3.0 collective-permute-start.1
  5.8 1.5 collective-permute-start
  10.7 1.3 gather_fusion.1
  12.0 3.4 all-to-all-start
  15.4 1.6 collective-permute-start.4
  21.8 1.2 constant_dynamic-update-slice_fusion.4
  23.0 1.3 collective-permute-done.1
  24.3 2.1 collective-permute-done
  26.3 1.8 slice.53
  28.1 1.8 slice.52
  29.9 1.5 collective-permute-start.2
  31.9 1.2 constant_dynamic-update-slice_fusion.3
  33.1 1.2 constant_dynamic-update-slice_fusion.2
  34.3 4.4 %collective-permute-done.2 = bf16[64,3072]{1,0:T(8,128)(2,1)} collective-permute-done((bf16[64,3072]{1,0:T(8,128)(2,1)}, bf16[64,3072]{1,0:T(8,128)(2,1)}, u32[]{:S(2)}, u32[]{:S(2)}) %collective-permute-start.2) | collective-permute-done | bytes 393248 | tf_op jit(solution)/shard_map/ppermute | solution.py:954
  38.7 1.2 collective-permute-done.3
  44.2 2.3 copy.60.routes
  46.5 3.6 %collective-permute-start.7 = (bf16[512,1024]{1,0:T(8,128)(2,1)}, bf16[512,1024]{1,0:T(8,128)(2,1)S(1)}, u32[]{:S(2)}, u32[]{:S(2)}) collective-permute-start(bf16[512,1024]{1,0:T(8,128)(2,1)} %refs_1_), channel_id=1, source_target_pairs={{0,3},{1,0},{2,1},{3,2},{4,7},{5,4},{6,5},{7,6},{8,11},{9,8},{10,9... | collective-permute-start | bytes 3145736 | tf_op jit(solution)/shard_map/ppermute | solution.py:1102
  50.2 10.4 %project.1 = (bf16[512,2048]{1,0:T(8,128)(2,1)}, bf16[512,64]{1,0:T(8,128)(2,1)}, bf16[512,1024]{1,0:T(8,128)(2,1)}) custom-call(s32[8]{0:T(128)} %broadcast_xor_fusion.order.refs_0_, bf16[512,1024]{1,0:T(8,128)(2,1)} %hid.5, bf16[1,1024]{1,0:T(2,128)(2,1)} %reshape.89.gain, bf16[512,3072]{1,0:T(8,128)(2,1)} %copy-done, ...), custom_call_target="tpu_custom_call" | custom-call | flops 2147483648 | bytes 8388608 | tf_op jit(solution)/shard_map/project/pallas_call | solution.py:141
  60.5 1.5 collective-permute-start.10
  62.0 12.7 %attend.1 = (bf16[512,1024]{1,0:T(8,128)(2,1)}, f32[8,2,512]{2,1,0:T(2,128)}) custom-call(s32[1]{0:T(128)} %dynamic_slice.15.scalars, bf16[512,2048]{1,0:T(8,128)(2,1)} %get-tuple-element.91.query.key.value, bf16[512,2048]{1,0:T(8,128)(2,1)} %get-tuple-element.91.query.key.value, bf16[512,2048]{1,0:T(8,128)(2,1)} %get-tuple-element.91.query.key.value), custom_call_target="tpu_custom_call" | custom-call | flops 2147483648 | bytes 4194304 | tf_op jit(solution)/shard_map/attend/pallas_call | solution.py:224
  74.7 5.9 %close_mixer.1 = (f32[512,1024]{1,0:T(8,128)}, bf16[512,1024]{1,0:T(8,128)(2,1)}, bf16[512,64]{1,0:T(8,128)(2,1)}) custom-call(s32[8]{0:T(128)} %broadcast_xor_fusion.order.refs_0_, bf16[512,1024]{1,0:T(8,128)(2,1)} %get-tuple-element.92.att.refs_11_, bf16[512,1024]{1,0:T(8,128)(2,1)} %hid.5, bf16[1,1024]{1,0:T(2,128)(2,1)} %reshape.90.gain.refs_3_, ...), custom_call_target="tpu_custom_call" | custom-call | flops 1073741824 | bytes 8388608 | tf_op jit(solution)/shard_map/close_mixer/pallas_call | solution.py:357
  80.6 2.1 collective-permute-start.8
  82.7 27.7 %experts.4 = (bf16[1040,1024]{1,0:T(8,128)(2,1)}, f32[16,512]{1,0:T(8,128)}, bf16[8,4,288,128]{3,2,1,0:T(8,128)(2,1)}) custom-call(s32[5]{0:T(128)} %get-tuple-element.96.scalars, bf16[512,1024]{1,0:T(8,128)(2,1)} %get-tuple-element.102.x, bf16[512,1024]{1,0:T(8,128)(2,1)} %refs_1_, s32[2048,8]{1,0:T(8,128)} %copy.60.routes, ...), custom_call_target="tpu_custom_call" | custom-call | flops 19327352832 | bytes 20971520 | tf_op jit(solution)/shard_map/experts/pallas_call | solution.py:558
  110.4 2.5 collective-permute-start.6
  112.8 7.0 %collective-permute-done.8.x = bf16[512,1024]{1,0:T(8,128)(2,1)S(1)} collective-permute-done((bf16[512,1024]{1,0:T(8,128)(2,1)}, bf16[512,1024]{1,0:T(8,128)(2,1)S(1)}, u32[]{:S(2)}, u32[]{:S(2)}) %collective-permute-start.8) | collective-permute-done | bytes 1048608 | tf_op jit(solution)/shard_map/ppermute | solution.py:1120
  120.8 26.8 %experts.5 = (bf16[1040,1024]{1,0:T(8,128)(2,1)}, f32[16,512]{1,0:T(8,128)}, bf16[8,4,288,128]{3,2,1,0:T(8,128)(2,1)}) custom-call(s32[5]{0:T(128)} %get-tuple-element.104.scalars, bf16[512,1024]{1,0:T(8,128)(2,1)} %copy-done.14, bf16[512,1024]{1,0:T(8,128)(2,1)} %collective-permute-done.4.cot, ...), custom_call_target="tpu_custom_call", output_to_operand_aliasing={{2}: (11, {})} | custom-call | flops 19327352832 | bytes 20971520 | tf_op jit(solution)/shard_map/experts/pallas_call | solution.py:558
  147.5 1.8 collective-permute-start.9
  151.3 26.8 %experts.6 = (bf16[1040,1024]{1,0:T(8,128)(2,1)}, f32[16,512]{1,0:T(8,128)}, bf16[8,4,288,128]{3,2,1,0:T(8,128)(2,1)}) custom-call(s32[5]{0:T(128)} %get-tuple-element.100.scalars, bf16[512,1024]{1,0:T(8,128)(2,1)} %copy-done.17, bf16[512,1024]{1,0:T(8,128)(2,1)} %copy-done.13, s32[2048,8]{1,0:T(8,128)} %copy.60.routes, ...), custom_call_target="tpu_custom_call", output_to_operand_aliasing={{2}: (11, {})} | custom-call | flops 19327352832 | bytes 20971520 | tf_op jit(solution)/shard_map/experts/pallas_call | solution.py:558
  178.0 1.6 collective-permute-start.11
  181.7 26.8 %experts.7 = (bf16[1040,1024]{1,0:T(8,128)(2,1)}, f32[16,512]{1,0:T(8,128)}, bf16[8,4,288,128]{3,2,1,0:T(8,128)(2,1)}) custom-call(s32[5]{0:T(128)} %get-tuple-element.112.scalars, bf16[512,1024]{1,0:T(8,128)(2,1)} %copy-done.15, bf16[512,1024]{1,0:T(8,128)(2,1)} %copy-done.12, s32[2048,8]{1,0:T(8,128)} %copy.60.routes, ...), custom_call_target="tpu_custom_call", output_to_operand_aliasing={{2}: (11, {})} | custom-call | flops 19327352832 | bytes 20971520 | tf_op jit(solution)/shard_map/experts/pallas_call | solution.py:558
  208.5 3.6 %all-to-all-start.1 = ((bf16[8,4,288,128]{3,2,1,0:T(8,128)(2,1)}), bf16[8,4,288,128]{3,2,1,0:T(8,128)(2,1)S(1)}, u32[]{:S(2)}, u32[]{:S(2)}) async-start(bf16[8,4,288,128]{3,2,1,0:T(8,128)(2,1)} %get-tuple-element.120), calls=%async_computation.1 | async-start | bytes 4718592 | tf_op jit(solution)/shard_map/all_to_all | solution.py:1151
  212.1 15.2 %collective-permute-done.11 = bf16[1040,1024]{1,0:T(8,128)(2,1)} collective-permute-done((bf16[1040,1024]{1,0:T(8,128)(2,1)}, bf16[1040,1024]{1,0:T(8,128)(2,1)}, u32[]{:S(2)}, u32[]{:S(2)}) %collective-permute-start.11) | collective-permute-done | bytes 2129952 | tf_op jit(solution)/shard_map/ppermute | solution.py:1156
  227.3 3.0 add_convert_fusion.1
  231.6 9.9 %all-to-all-done.1 = bf16[8,4,288,128]{3,2,1,0:T(8,128)(2,1)S(1)} async-done(((bf16[8,4,288,128]{3,2,1,0:T(8,128)(2,1)}), bf16[8,4,288,128]{3,2,1,0:T(8,128)(2,1)S(1)}, u32[]{:S(2)}, u32[]{:S(2)}) %all-to-all-start.1) | async-done | bytes 2359328 | tf_op jit(solution)/shard_map/all_to_all | solution.py:1151
  241.5 1.5 copy-done.2
  242.9 3.6 %sum_experts.1 = (f32[4,8,32,128]{3,2,1,0:T(8,128)}, f32[4,8,2,16,64]{4,3,2,1,0:T(8,128)}, f32[4,8,16,64]{3,2,1,0:T(8,128)}, f32[4,8,16,128]{3,2,1,0:T(8,128)}) custom-call(s32[32]{0:T(128)} %reshape.97.ids, bf16[32,288,128]{2,1,0:T(8,128)(2,1)} %bitcast.39), custom_call_target="tpu_custom_call" | custom-call | tf_op jit(solution)/shard_map/sum_experts/pallas_call | solution.py:891
  246.5 9.4 %collective-permute-done.12 = bf16[528,1024]{1,0:T(8,128)(2,1)S(1)} collective-permute-done((bf16[528,1024]{1,0:T(8,128)(2,1)}, bf16[528,1024]{1,0:T(8,128)(2,1)S(1)}, u32[]{:S(2)}, u32[]{:S(2)}) %collective-permute-start.12) | collective-permute-done | bytes 1081376 | tf_op jit(solution)/shard_map/ppermute | solution.py:1162
  256.4 1.9 add_convert_fusion.4
  258.4 22.6 %collective-permute-done.13.refs_13_.refs_16_.refs_17_ = bf16[528,1024]{1,0:T(8,128)(2,1)S(1)} collective-permute-done((bf16[528,1024]{1,0:T(8,128)(2,1)S(1)}, bf16[528,1024]{1,0:T(8,128)(2,1)S(1)}, u32[]{:S(2)}, u32[]{:S(2)}) %collective-permute-start.13) | collective-permute-done | bytes 1081376 | tf_op jit(solution)/shard_map/ppermute | solution.py:1162
  282.0 9.5 %open_back.1 = (f32[512,1024]{1,0:T(8,128)}, bf16[512,1024]{1,0:T(8,128)(2,1)}, f32[64,1024]{1,0:T(8,128)}, f32[64,1024]{1,0:T(8,128)}) custom-call(s32[8]{0:T(128)} %broadcast_xor_fusion.order.refs_0_, bf16[512,1024]{1,0:T(8,128)(2,1)} %refs_1_, f32[512,1024]{1,0:T(8,128)} %get-tuple-element.95.refs_2_, bf16[1,1024]{1,0:T(2,128)(2,1)} %reshape.90.gain.refs_3_, ...), custom_call_target="tpu_custom_call" | custom-call | flops 1073741824 | bytes 14680064 | tf_op jit(solution)/shard_map/open_back/pallas_call | solution.py:691
  291.5 18.1 %attend_back.1 = (bf16[512,1024]{1,0:T(8,128)(2,1)}, bf16[512,512]{1,0:T(8,128)(2,1)}, bf16[512,512]{1,0:T(8,128)(2,1)}) custom-call(s32[1]{0:T(128)} %dynamic_slice.15.scalars, bf16[512,2048]{1,0:T(8,128)(2,1)} %get-tuple-element.91.query.key.value, bf16[512,2048]{1,0:T(8,128)(2,1)} %get-tuple-element.91.query.key.value, ...), custom_call_target="tpu_custom_call" | custom-call | flops 5368709120 | bytes 8388608 | tf_op jit(solution)/shard_map/attend_back/pallas_call | solution.py:304
  310.1 4.5 %adapters_back.1 = (bf16[512,64]{1,0:T(8,128)(2,1)}, bf16[32,16,256]{2,1,0:T(8,128)(2,1)}) custom-call(bf16[512,1024]{1,0:T(8,128)(2,1)} %get-tuple-element.132.grad_query, bf16[512,512]{1,0:T(8,128)(2,1)} %get-tuple-element.133.grad_key, bf16[512,512]{1,0:T(8,128)(2,1)} %get-tuple-element.134.grad_value, bf16[512,64]{1,0:T(8,128)(2,1)} %get-tuple-element.135.low, ...), custom_call_target="tpu_custom_call" | custom-call | flops 1610612736 | bytes 4194304 | tf_op jit(solution)/shard_map/adapters_back/pallas_call | solution.py:791
  314.6 4.3 %all-to-all-start.2 = ((bf16[32,16,256]{2,1,0:T(8,128)(2,1)}), bf16[32,16,256]{2,1,0:T(8,128)(2,1)S(1)}, u32[]{:S(2)}, u32[]{:S(2)}) async-start(bf16[32,16,256]{2,1,0:T(8,128)(2,1)} %get-tuple-element.139), calls=%async_computation.2 | async-start | bytes 524288 | tf_op jit(solution)/shard_map/all_to_all | solution.py:1189
  318.9 8.6 %input_back.1 = bf16[512,1024]{1,0:T(8,128)(2,1)} custom-call(s32[8]{0:T(128)} %broadcast_xor_fusion.order.refs_0_, bf16[512,1024]{1,0:T(8,128)(2,1)} %get-tuple-element.132.grad_query, bf16[512,512]{1,0:T(8,128)(2,1)} %get-tuple-element.133.grad_key, bf16[512,512]{1,0:T(8,128)(2,1)} %get-tuple-element.134.grad_value, ...), custom_call_target="tpu_custom_call" | custom-call | flops 2147483648 | bytes 12582912 | tf_op jit(solution)/shard_map/input_back/pallas_call | solution.py:836
  327.5 7.7 %collective-permute-done.15 = bf16[512,1024]{1,0:T(8,128)(2,1)S(1)} collective-permute-done((bf16[512,1024]{1,0:T(8,128)(2,1)S(1)}, bf16[512,1024]{1,0:T(8,128)(2,1)S(1)}, u32[]{:S(2)}, u32[]{:S(2)}) %collective-permute-start.15) | collective-permute-done | bytes 1048608 | tf_op jit(solution)/shard_map/ppermute | solution.py:1185
  335.3 2.7 add_convert_fusion.2
  339.2 2.0 sum_mixer.1
  (91 shorter events, 22.4 us)
Async XLA Ops:
  0.6 16.5 %copy-start.19 = (s32[8]{0:T(128)S(1)}, s32[8]{0:T(128)}, u32[]{:S(2)}) copy-start(s32[8]{0:T(128)} %constant.74.clone) | copy-start | bytes 100
  0.7 18.9 %copy-start.11 = (s32[4,1]{1,0:T(4,128)S(1)}, s32[4,1]{1,0:T(4,128)}, u32[]{:S(2)}) copy-start(s32[4,1]{1,0:T(4,128)} %constant.84) | copy-start | bytes 52
  0.7 10.0 %copy-start.7 = (bf16[8,16,128]{2,1,0:T(8,128)(2,1)S(1)}, bf16[8,16,128]{2,1,0:T(8,128)(2,1)}, u32[]{:S(2)}) copy-start(bf16[8,16,128]{2,1,0:T(8,128)(2,1)} %param.37) | copy-start | bytes 98308
  0.7 17.1 %copy-start.9 = (bf16[1024]{0:T(1024)(128)(2,1)S(1)}, bf16[1024]{0:T(1024)(128)(2,1)}, u32[]{:S(2)}) copy-start(bf16[1024]{0:T(1024)(128)(2,1)} %param.28) | copy-start | bytes 6148
  0.7 17.7 %copy-start.10 = (bf16[1024]{0:T(1024)(128)(2,1)S(1)}, bf16[1024]{0:T(1024)(128)(2,1)}, u32[]{:S(2)}) copy-start(bf16[1024]{0:T(1024)(128)(2,1)} %param.29) | copy-start | bytes 6148
  0.7 19.6 %copy-start.18 = (s32[32]{0:T(128)S(1)}, s32[32]{0:T(128)}, u32[]{:S(2)}) copy-start(s32[32]{0:T(128)} %param.25) | copy-start | bytes 388
  0.7 20.3 %copy-start.8 = (bf16[1024,16]{0,1:T(8,128)(2,1)S(1)}, bf16[1024,16]{0,1:T(8,128)(2,1)}, u32[]{:S(2)}) copy-start(bf16[1024,16]{0,1:T(8,128)(2,1)} %param.32) | copy-start | bytes 98308
  2.8 21.5 %collective-permute-start.1 = (bf16[128,3072]{1,0:T(8,128)(2,1)}, bf16[128,3072]{1,0:T(8,128)(2,1)}, u32[]{:S(2)}, u32[]{:S(2)}) collective-permute-start(bf16[128,3072]{1,0:T(8,128)(2,1)} %pack.1), channel_id=1, source_target_pairs={{0,16},{4,20},{8,24},{12,28},{16,0},{20,4},{24,8},{28,12},{1,17},{... | collective-permute-start | bytes 2359304 | tf_op jit(solution)/shard_map/ppermute | solution.py:954
  5.8 20.5 %collective-permute-start = (bf16[128,3072]{1,0:T(8,128)(2,1)}, bf16[128,3072]{1,0:T(8,128)(2,1)}, u32[]{:S(2)}, u32[]{:S(2)}) collective-permute-start(bf16[128,3072]{1,0:T(8,128)(2,1)} %pack.1), channel_id=1, source_target_pairs={{0,8},{4,12},{8,0},{12,4},{16,24},{20,28},{24,16},{28,20},{1,9},{5... | collective-permute-start | bytes 2359304 | tf_op jit(solution)/shard_map/ppermute | solution.py:954
  12.0 22.3 %all-to-all-start = ((bf16[8,112,128]{2,1,0:T(8,128)(2,1)}), bf16[8,112,128]{2,1,0:T(8,128)(2,1)S(1)}, u32[]{:S(2)}, u32[]{:S(2)}) async-start(bf16[8,112,128]{2,1,0:T(8,128)(2,1)} %gather_fusion.1), calls=%async_computation | async-start | bytes 458752 | tf_op jit(solution)/shard_map/all_to_all | solution.py:1058
  15.4 28.8 %collective-permute-start.4 = (bf16[512,1024]{1,0:T(8,128)(2,1)}, bf16[512,1024]{1,0:T(8,128)(2,1)}, u32[]{:S(2)}, u32[]{:S(2)}) collective-permute-start(bf16[512,1024]{1,0:T(8,128)(2,1)} %refs_1_), channel_id=1, source_target_pairs={{0,1},{1,2},{2,3},{3,0},{4,5},{5,6},{6,7},{7,4},{8,9},{9,10},{10,1... | collective-permute-start | bytes 3145736 | tf_op jit(solution)/shard_map/ppermute | solution.py:1084
  21.0 12.0 %copy-start.6 = (bf16[16,1024]{1,0:T(8,128)(2,1)}, bf16[16,1024]{1,0:T(8,128)(2,1)S(1)}, u32[]{:S(2)}) copy-start(bf16[16,1024]{1,0:T(8,128)(2,1)S(1)} %fusion.refs_5_) | copy-start | bytes 98308
  29.9 8.8 %collective-permute-start.2 = (bf16[64,3072]{1,0:T(8,128)(2,1)}, bf16[64,3072]{1,0:T(8,128)(2,1)}, u32[]{:S(2)}, u32[]{:S(2)}) collective-permute-start(bf16[64,3072]{1,0:T(8,128)(2,1)} %slice.52), channel_id=1, source_target_pairs={{0,8},{4,12},{8,0},{12,4},{16,24},{20,28},{24,16},{28,20},{1,9},{5... | collective-permute-start | bytes 1179656 | tf_op jit(solution)/shard_map/ppermute | solution.py:954
  31.4 8.5 %collective-permute-start.3 = (bf16[64,3072]{1,0:T(8,128)(2,1)}, bf16[64,3072]{1,0:T(8,128)(2,1)}, u32[]{:S(2)}, u32[]{:S(2)}) collective-permute-start(bf16[64,3072]{1,0:T(8,128)(2,1)} %slice.53), channel_id=1, source_target_pairs={{0,16},{4,20},{8,24},{12,28},{16,0},{20,4},{24,8},{28,12},{1,17},{... | collective-permute-start | bytes 1179656 | tf_op jit(solution)/shard_map/ppermute | solution.py:954
  43.4 6.7 %copy-start = (bf16[512,3072]{1,0:T(8,128)(2,1)}, bf16[512,3072]{1,0:T(8,128)(2,1)S(1)}, u32[]{:S(2)}) copy-start(bf16[512,3072]{1,0:T(8,128)(2,1)S(1)} %constant_dynamic-update-slice_fusion.weight_a.refs_6_) | copy-start | bytes 9437188
  44.2 5.9 %collective-permute-start.5 = (bf16[512,3072]{1,0:T(8,128)(2,1)S(1)}, bf16[512,3072]{1,0:T(8,128)(2,1)}, u32[]{:S(2)}, u32[]{:S(2)}) collective-permute-start(bf16[512,3072]{1,0:T(8,128)(2,1)S(1)} %constant_dynamic-update-slice_fusion.weight_a.refs_6_), channel_id=1, source_target_pairs={{0,4},{4,0},{8,12},{12,8},{16,20},{20,16},{24,28},{28,24},{1,5},{5... | collective-permute-start | bytes 9437192 | tf_op jit(solution)/shard_map/ppermute | solution.py:954
  46.5 102.8 %collective-permute-start.7 = (bf16[512,1024]{1,0:T(8,128)(2,1)}, bf16[512,1024]{1,0:T(8,128)(2,1)S(1)}, u32[]{:S(2)}, u32[]{:S(2)}) collective-permute-start(bf16[512,1024]{1,0:T(8,128)(2,1)} %refs_1_), channel_id=1, source_target_pairs={{0,3},{1,0},{2,1},{3,2},{4,7},{5,4},{6,5},{7,6},{8,11},{9,8},{10,9... | collective-permute-start | bytes 3145736 | tf_op jit(solution)/shard_map/ppermute | solution.py:1102
  60.5 119.1 %collective-permute-start.10 = (bf16[512,1024]{1,0:T(8,128)(2,1)}, bf16[512,1024]{1,0:T(8,128)(2,1)S(1)}, u32[]{:S(2)}, u32[]{:S(2)}) collective-permute-start(bf16[512,1024]{1,0:T(8,128)(2,1)} %collective-permute-done.4.cot), channel_id=1, source_target_pairs={{0,1},{1,2},{2,3},{3,0},{4,5},{5,6},{6,7},{7,4},{8,9},{9,10},{10,1... | collective-permute-start | bytes 3145736 | tf_op jit(solution)/shard_map/ppermute | solution.py:1111
  80.6 39.2 %collective-permute-start.8 = (bf16[512,1024]{1,0:T(8,128)(2,1)}, bf16[512,1024]{1,0:T(8,128)(2,1)S(1)}, u32[]{:S(2)}, u32[]{:S(2)}) collective-permute-start(bf16[512,1024]{1,0:T(8,128)(2,1)} %get-tuple-element.102.x), channel_id=1, source_target_pairs={{0,1},{1,2},{2,3},{3,0},{4,5},{5,6},{6,7},{7,4},{8,9},{9,10},{10,1... | collective-permute-start | bytes 3145736 | tf_op jit(solution)/shard_map/ppermute | solution.py:1120
  82.7 27.7 %copy-start.16 = (bf16[512,1024]{1,0:T(8,128)(2,1)S(1)}, bf16[512,1024]{1,0:T(8,128)(2,1)}, u32[]{:S(2)}) copy-start(bf16[512,1024]{1,0:T(8,128)(2,1)} %get-tuple-element.102.x) | copy-start | bytes 3145732
  110.4 39.0 %collective-permute-start.6 = (bf16[512,1024]{1,0:T(8,128)(2,1)S(1)}, bf16[512,1024]{1,0:T(8,128)(2,1)S(1)}, u32[]{:S(2)}, u32[]{:S(2)}) collective-permute-start(bf16[512,1024]{1,0:T(8,128)(2,1)S(1)} %copy-done.16), channel_id=1, source_target_pairs={{0,3},{1,0},{2,1},{3,2},{4,7},{5,4},{6,5},{7,6},{8,11},{9,8},{10,9... | collective-permute-start | bytes 3145736 | tf_op jit(solution)/shard_map/ppermute | solution.py:1144
  119.8 1.0 copy-start.14
  147.5 32.1 %collective-permute-start.9 = (bf16[512,1024]{1,0:T(8,128)(2,1)}, bf16[512,1024]{1,0:T(8,128)(2,1)S(1)}, u32[]{:S(2)}, u32[]{:S(2)}) collective-permute-start(bf16[512,1024]{1,0:T(8,128)(2,1)} %copy-done.14), channel_id=1, source_target_pairs={{0,1},{1,2},{2,3},{3,0},{4,5},{5,6},{6,7},{7,4},{8,9},{9,10},{10,1... | collective-permute-start | bytes 3145736 | tf_op jit(solution)/shard_map/ppermute | solution.py:1147
  149.3 1.0 copy-start.13
  150.3 1.0 copy-start.17
  178.0 49.3 %collective-permute-start.11 = (bf16[1040,1024]{1,0:T(8,128)(2,1)}, bf16[1040,1024]{1,0:T(8,128)(2,1)}, u32[]{:S(2)}, u32[]{:S(2)}) collective-permute-start(bf16[1040,1024]{1,0:T(8,128)(2,1)} %get-tuple-element.118), channel_id=1, source_target_pairs={{0,1},{1,2},{2,3},{3,0},{4,5},{5,6},{6,7},{7,4},{8,9},{9,10},{10,1... | collective-permute-start | bytes 6389768 | tf_op jit(solution)/shard_map/ppermute | solution.py:1156
  179.7 1.1 copy-start.12
  180.7 1.0 copy-start.15
  208.5 33.0 %all-to-all-start.1 = ((bf16[8,4,288,128]{3,2,1,0:T(8,128)(2,1)}), bf16[8,4,288,128]{3,2,1,0:T(8,128)(2,1)S(1)}, u32[]{:S(2)}, u32[]{:S(2)}) async-start(bf16[8,4,288,128]{3,2,1,0:T(8,128)(2,1)} %get-tuple-element.120), calls=%async_computation.1 | async-start | bytes 4718592 | tf_op jit(solution)/shard_map/all_to_all | solution.py:1151
  230.3 25.6 %collective-permute-start.12 = (bf16[528,1024]{1,0:T(8,128)(2,1)}, bf16[528,1024]{1,0:T(8,128)(2,1)S(1)}, u32[]{:S(2)}, u32[]{:S(2)}) collective-permute-start(bf16[528,1024]{1,0:T(8,128)(2,1)} %add_convert_fusion.1), channel_id=1, source_target_pairs={{0,1},{1,2},{2,3},{3,0},{4,5},{5,6},{6,7},{7,4},{8,9},{9,10},{10,1... | collective-permute-start | bytes 3244040 | tf_op jit(solution)/shard_map/ppermute | solution.py:1162
  241.5 1.5 copy-start.2
  241.5 14.5 %copy-start.4 = (bf16[1040,1024]{1,0:T(8,128)(2,1)S(1)}, bf16[1040,1024]{1,0:T(8,128)(2,1)}, u32[]{:S(2)}) copy-start(bf16[1040,1024]{1,0:T(8,128)(2,1)} %get-tuple-element.111) | copy-start | bytes 6389764
  256.4 24.6 %collective-permute-start.13 = (bf16[528,1024]{1,0:T(8,128)(2,1)S(1)}, bf16[528,1024]{1,0:T(8,128)(2,1)S(1)}, u32[]{:S(2)}, u32[]{:S(2)}) collective-permute-start(bf16[528,1024]{1,0:T(8,128)(2,1)S(1)} %add_convert_fusion), channel_id=1, source_target_pairs={{0,1},{1,2},{2,3},{3,0},{4,5},{5,6},{6,7},{7,4},{8,9},{9,10},{10,1... | collective-permute-start | bytes 3244040 | tf_op jit(solution)/shard_map/ppermute | solution.py:1162
  281.0 1.0 copy-start.1
  281.0 28.7 %collective-permute-start.14 = (bf16[512,1024]{1,0:T(8,128)(2,1)S(1)}, bf16[512,1024]{1,0:T(8,128)(2,1)S(1)}, u32[]{:S(2)}, u32[]{:S(2)}) collective-permute-start(bf16[512,1024]{1,0:T(8,128)(2,1)S(1)} %add_convert_fusion.4), channel_id=1, source_target_pairs={{0,1},{1,2},{2,3},{3,0},{4,5},{5,6},{6,7},{7,4},{8,9},{9,10},{10,1... | collective-permute-start | bytes 3145736 | tf_op jit(solution)/shard_map/ppermute | solution.py:1166
  310.1 25.2 %collective-permute-start.15 = (bf16[512,1024]{1,0:T(8,128)(2,1)S(1)}, bf16[512,1024]{1,0:T(8,128)(2,1)S(1)}, u32[]{:S(2)}, u32[]{:S(2)}) collective-permute-start(bf16[512,1024]{1,0:T(8,128)(2,1)S(1)} %add_convert_fusion.3), channel_id=1, source_target_pairs={{0,1},{1,2},{2,3},{3,0},{4,5},{5,6},{6,7},{7,4},{8,9},{9,10},{10,1... | collective-permute-start | bytes 3145736 | tf_op jit(solution)/shard_map/ppermute | solution.py:1185
  314.6 23.9 %all-to-all-start.2 = ((bf16[32,16,256]{2,1,0:T(8,128)(2,1)}), bf16[32,16,256]{2,1,0:T(8,128)(2,1)S(1)}, u32[]{:S(2)}, u32[]{:S(2)}) async-start(bf16[32,16,256]{2,1,0:T(8,128)(2,1)} %get-tuple-element.139), calls=%async_computation.2 | async-start | bytes 524288 | tf_op jit(solution)/shard_map/all_to_all | solution.py:1189
  318.9 16.4 %copy-start.3 = (f32[512,1024]{1,0:T(8,128)S(1)}, f32[512,1024]{1,0:T(8,128)}, u32[]{:S(2)}) copy-start(f32[512,1024]{1,0:T(8,128)} %get-tuple-element.95.refs_2_) | copy-start | bytes 6291460
  338.5 0.7 copy-start.5

commit v10 on v8

--- a/solution.py
+++ b/solution.py
@@ -1061,12 +1061,13 @@
         1,
     )
 
+    steps = [table[at] for at in range(groups)]
     both = pack(query_key_value_weight, w_out)
     cots = {0: cotangent, 1: lax.ppermute(cotangent, "expert", forward)}
     if owners == BLOCKS:
         pair = both_neighbours(both)
-        pair, order, router, router_wide, table, tags, attn_gain, ffn_gain, length = tied(
-            pair, order, router, router_wide, table, tags, attn_gain, ffn_gain, length
+        pair, order, router, router_wide, steps, tags, attn_gain, ffn_gain, length = tied(
+            pair, order, router, router_wide, steps, tags, attn_gain, ffn_gain, length
         )
         near = jnp.concatenate([both, *pair, *across(pair)], 0)
         near, adapters, cots[1], cotangent = tied(near, adapters, cots[1], cotangent)
@@ -1113,7 +1114,7 @@
     ran = {}
     for at, offset in enumerate(offsets):
         ran[offset], gate_part, packed = run_experts(
-            table[at],
+            steps[at],
             xs[offset],
             cots[offset],
             routes,

time: 346 us -> 346 us (level)
  transfers between devices with their start and end apart: 19 -> 19, of which waited for: 12 -> 13; matrix products, arithmetic and copies ran while one was open for 8% -> 8% of each run, Pallas kernels for 53% -> 53%
where the time goes in v10:
time: 346 us; the launch traced here: 340 us
  Pallas kernels  185 us (53%)
  waiting for transfers between devices  85.9 us (25%)
  starting transfers between devices  32 us (9%)
  local copies, waits for them, and re-layouts  24.9 us (7%)
  other arithmetic  10.7 us (3%)
    pallas_call x4, Pallas kernels, run_experts(): pl.pallas_call(expert_kernel, grid_spec=pltpu.PrefetchScalarGridSpec(num_...  108 us
    ppermute x2, waiting for transfers between devices, on_device(): grad_far = lax.ppermute(grad_part, 'expert', forward)  32.5 us
    pallas_call x1, Pallas kernels, attend_back(): pl.pallas_call(attend_back_kernel, grid_spec=pltpu.PrefetchScalarGridSpec...  18.1 us
    ppermute x1, waiting for transfers between devices, on_device(): lax.ppermute(first_sums if groups > 2 else ran[1], 'expert', forward)  15.3 us
    unnamed x48, local copies, waits for them, and re-layouts  13.7 us
    pallas_call x1, Pallas kernels, attend(): pl.pallas_call(attend_kernel, grid_spec=pltpu.PrefetchScalarGridSpec(num_...  12.6 us
    pallas_call x1, Pallas kernels, project(): pl.pallas_call(project_kernel, grid_spec=pltpu.PrefetchScalarGridSpec(num...  10.4 us
    all_to_all x1, waiting for transfers between devices, on_device(): lax.all_to_all(to_owners(packed, owners, local), 'dp', 0, 0, tiled=True)  10.1 us
  transfers between devices with their start and end apart: 19, of which 13 were waited for; matrix products, arithmetic and copies ran while one was open for 8% of the time, Pallas kernels for 53%

profile of v10, /device:TPU:0, one launch (start us, length us, event | category | flops | bytes accessed | tf_op | source)
XLA Modules:
  0.0 340.4 jit_solution(11315826267898691302)
XLA Ops:
  0.7 2.1 pack.1
  2.8 3.0 collective-permute-start.1
  5.8 1.5 collective-permute-start
  10.7 1.3 gather_fusion.1
  12.0 3.4 all-to-all-start
  15.4 1.6 collective-permute-start.4
  21.7 1.2 constant_dynamic-update-slice_fusion.4
  22.9 1.4 collective-permute-done.1
  24.3 2.1 collective-permute-done
  28.4 1.6 collective-permute-start.2
  30.5 1.2 constant_dynamic-update-slice_fusion.3
  31.7 1.2 constant_dynamic-update-slice_fusion.2
  32.8 4.1 %collective-permute-done.2 = bf16[64,3072]{1,0:T(8,128)(2,1)S(1)} collective-permute-done((bf16[64,3072]{1,0:T(8,128)(2,1)S(1)}, bf16[64,3072]{1,0:T(8,128)(2,1)S(1)}, u32[]{:S(2)}, u32[]{:S(2)}) %collective-permute-start.2) | collective-permute-done | bytes 393248 | tf_op jit(solution)/shard_map/ppermute | solution.py:954
  37.0 1.2 collective-permute-done.3
  38.2 4.8 %collective-permute-done.4.cot = bf16[512,1024]{1,0:T(8,128)(2,1)} collective-permute-done((bf16[512,1024]{1,0:T(8,128)(2,1)}, bf16[512,1024]{1,0:T(8,128)(2,1)}, u32[]{:S(2)}, u32[]{:S(2)}) %collective-permute-start.4) | collective-permute-done | bytes 1048608 | tf_op jit(solution)/shard_map/ppermute | solution.py:1066
  43.0 1.4 copy.60.routes
  45.2 1.7 collective-permute-start.7
  48.8 10.4 %project.1 = (bf16[512,2048]{1,0:T(8,128)(2,1)}, bf16[512,64]{1,0:T(8,128)(2,1)}, bf16[512,1024]{1,0:T(8,128)(2,1)}) custom-call(s32[8]{0:T(128)} %broadcast_xor_fusion.order.refs_0_, bf16[512,1024]{1,0:T(8,128)(2,1)} %hid.5, bf16[1,1024]{1,0:T(2,128)(2,1)} %reshape.89.gain, bf16[512,3072]{1,0:T(8,128)(2,1)} %copy-done, ...), custom_call_target="tpu_custom_call" | custom-call | flops 2147483648 | bytes 8388608 | tf_op jit(solution)/shard_map/project/pallas_call | solution.py:141
  59.2 12.6 %attend.1 = (bf16[512,1024]{1,0:T(8,128)(2,1)}, f32[8,2,512]{2,1,0:T(2,128)}) custom-call(s32[1]{0:T(128)} %dynamic_slice.15.scalars, bf16[512,2048]{1,0:T(8,128)(2,1)} %get-tuple-element.82.query.key.value, bf16[512,2048]{1,0:T(8,128)(2,1)} %get-tuple-element.82.query.key.value, bf16[512,2048]{1,0:T(8,128)(2,1)} %get-tuple-element.82.query.key.value), custom_call_target="tpu_custom_call" | custom-call | flops 2147483648 | bytes 4194304 | tf_op jit(solution)/shard_map/attend/pallas_call | solution.py:224
  71.8 6.0 %close_mixer.1 = (f32[512,1024]{1,0:T(8,128)}, bf16[512,1024]{1,0:T(8,128)(2,1)}, bf16[512,64]{1,0:T(8,128)(2,1)}) custom-call(s32[8]{0:T(128)} %broadcast_xor_fusion.order.refs_0_, bf16[512,1024]{1,0:T(8,128)(2,1)} %get-tuple-element.83.att.refs_11_, bf16[512,1024]{1,0:T(8,128)(2,1)} %hid.5, bf16[1,1024]{1,0:T(2,128)(2,1)} %reshape.90.gain.refs_3_, ...), custom_call_target="tpu_custom_call" | custom-call | flops 1073741824 | bytes 8388608 | tf_op jit(solution)/shard_map/close_mixer/pallas_call | solution.py:357
  77.8 1.8 collective-permute-start.8
  79.6 27.6 %experts.4 = (bf16[1040,1024]{1,0:T(8,128)(2,1)}, f32[16,512]{1,0:T(8,128)}, bf16[8,4,288,128]{3,2,1,0:T(8,128)(2,1)}) custom-call(s32[5]{0:T(128)} %get-tuple-element.86.scalars, bf16[512,1024]{1,0:T(8,128)(2,1)} %get-tuple-element.92.x, bf16[512,1024]{1,0:T(8,128)(2,1)} %refs_1_, s32[2048,8]{1,0:T(8,128)} %copy.60.routes, ...), custom_call_target="tpu_custom_call" | custom-call | flops 19327352832 | bytes 20971520 | tf_op jit(solution)/shard_map/experts/pallas_call | solution.py:558
  107.3 2.8 collective-permute-start.6
  110.1 6.6 %collective-permute-done.8.x = bf16[512,1024]{1,0:T(8,128)(2,1)S(1)} collective-permute-done((bf16[512,1024]{1,0:T(8,128)(2,1)}, bf16[512,1024]{1,0:T(8,128)(2,1)S(1)}, u32[]{:S(2)}, u32[]{:S(2)}) %collective-permute-start.8) | collective-permute-done | bytes 1048608 | tf_op jit(solution)/shard_map/ppermute | solution.py:1112
  117.6 26.8 %experts.5 = (bf16[1040,1024]{1,0:T(8,128)(2,1)}, f32[16,512]{1,0:T(8,128)}, bf16[8,4,288,128]{3,2,1,0:T(8,128)(2,1)}) custom-call(s32[5]{0:T(128)} %get-tuple-element.94.scalars, bf16[512,1024]{1,0:T(8,128)(2,1)} %copy-done.15, bf16[512,1024]{1,0:T(8,128)(2,1)} %collective-permute-done.4.cot, ...), custom_call_target="tpu_custom_call", output_to_operand_aliasing={{2}: (11, {})} | custom-call | flops 19327352832 | bytes 20971520 | tf_op jit(solution)/shard_map/experts/pallas_call | solution.py:558
  144.4 1.8 collective-permute-start.9
  148.2 26.8 %experts.6 = (bf16[1040,1024]{1,0:T(8,128)(2,1)}, f32[16,512]{1,0:T(8,128)}, bf16[8,4,288,128]{3,2,1,0:T(8,128)(2,1)}) custom-call(s32[5]{0:T(128)} %get-tuple-element.90.scalars, bf16[512,1024]{1,0:T(8,128)(2,1)} %copy-done.18, bf16[512,1024]{1,0:T(8,128)(2,1)} %copy-done.14, s32[2048,8]{1,0:T(8,128)} %copy.60.routes, ...), custom_call_target="tpu_custom_call", output_to_operand_aliasing={{2}: (11, {})} | custom-call | flops 19327352832 | bytes 20971520 | tf_op jit(solution)/shard_map/experts/pallas_call | solution.py:558
  174.9 1.6 collective-permute-start.11
  176.5 1.0 copy-done.13
  178.6 26.7 %experts.7 = (bf16[1040,1024]{1,0:T(8,128)(2,1)}, f32[16,512]{1,0:T(8,128)}, bf16[8,4,288,128]{3,2,1,0:T(8,128)(2,1)}) custom-call(s32[5]{0:T(128)} %get-tuple-element.102.scalars, bf16[512,1024]{1,0:T(8,128)(2,1)} %copy-done.16, bf16[512,1024]{1,0:T(8,128)(2,1)} %copy-done.13, s32[2048,8]{1,0:T(8,128)} %copy.60.routes, ...), custom_call_target="tpu_custom_call", output_to_operand_aliasing={{2}: (11, {})} | custom-call | flops 19327352832 | bytes 20971520 | tf_op jit(solution)/shard_map/experts/pallas_call | solution.py:558
  205.3 3.8 %all-to-all-start.1 = ((bf16[8,4,288,128]{3,2,1,0:T(8,128)(2,1)}), bf16[8,4,288,128]{3,2,1,0:T(8,128)(2,1)S(1)}, u32[]{:S(2)}, u32[]{:S(2)}) async-start(bf16[8,4,288,128]{3,2,1,0:T(8,128)(2,1)} %get-tuple-element.110), calls=%async_computation.1 | async-start | bytes 4718592 | tf_op jit(solution)/shard_map/all_to_all | solution.py:1143
  209.2 15.3 %collective-permute-done.11 = bf16[1040,1024]{1,0:T(8,128)(2,1)} collective-permute-done((bf16[1040,1024]{1,0:T(8,128)(2,1)}, bf16[1040,1024]{1,0:T(8,128)(2,1)}, u32[]{:S(2)}, u32[]{:S(2)}) %collective-permute-start.11) | collective-permute-done | bytes 2129952 | tf_op jit(solution)/shard_map/ppermute | solution.py:1148
  224.4 3.0 add_convert_fusion.1
  228.4 10.1 %all-to-all-done.1 = bf16[8,4,288,128]{3,2,1,0:T(8,128)(2,1)S(1)} async-done(((bf16[8,4,288,128]{3,2,1,0:T(8,128)(2,1)}), bf16[8,4,288,128]{3,2,1,0:T(8,128)(2,1)S(1)}, u32[]{:S(2)}, u32[]{:S(2)}) %all-to-all-start.1) | async-done | bytes 2359328 | tf_op jit(solution)/shard_map/all_to_all | solution.py:1143
  238.6 1.5 copy-done.2
  240.0 3.6 %sum_experts.1 = (f32[4,8,32,128]{3,2,1,0:T(8,128)}, f32[4,8,2,16,64]{4,3,2,1,0:T(8,128)}, f32[4,8,16,64]{3,2,1,0:T(8,128)}, f32[4,8,16,128]{3,2,1,0:T(8,128)}) custom-call(s32[32]{0:T(128)} %reshape.97.ids, bf16[32,288,128]{2,1,0:T(8,128)(2,1)} %bitcast.39), custom_call_target="tpu_custom_call" | custom-call | tf_op jit(solution)/shard_map/sum_experts/pallas_call | solution.py:891
  243.6 9.6 %collective-permute-done.12 = bf16[528,1024]{1,0:T(8,128)(2,1)S(1)} collective-permute-done((bf16[528,1024]{1,0:T(8,128)(2,1)}, bf16[528,1024]{1,0:T(8,128)(2,1)S(1)}, u32[]{:S(2)}, u32[]{:S(2)}) %collective-permute-start.12) | collective-permute-done | bytes 1081376 | tf_op jit(solution)/shard_map/ppermute | solution.py:1154
  253.7 1.9 add_convert_fusion.4
  255.7 22.8 %collective-permute-done.13.refs_13_.refs_16_.refs_17_ = bf16[528,1024]{1,0:T(8,128)(2,1)S(1)} collective-permute-done((bf16[528,1024]{1,0:T(8,128)(2,1)S(1)}, bf16[528,1024]{1,0:T(8,128)(2,1)S(1)}, u32[]{:S(2)}, u32[]{:S(2)}) %collective-permute-start.13) | collective-permute-done | bytes 1081376 | tf_op jit(solution)/shard_map/ppermute | solution.py:1154
  279.5 9.6 %open_back.1 = (f32[512,1024]{1,0:T(8,128)}, bf16[512,1024]{1,0:T(8,128)(2,1)}, f32[64,1024]{1,0:T(8,128)}, f32[64,1024]{1,0:T(8,128)}) custom-call(s32[8]{0:T(128)} %broadcast_xor_fusion.order.refs_0_, bf16[512,1024]{1,0:T(8,128)(2,1)} %refs_1_, f32[512,1024]{1,0:T(8,128)} %get-tuple-element.85.refs_2_, bf16[1,1024]{1,0:T(2,128)(2,1)} %reshape.90.gain.refs_3_, ...), custom_call_target="tpu_custom_call" | custom-call | flops 1073741824 | bytes 14680064 | tf_op jit(solution)/shard_map/open_back/pallas_call | solution.py:691
  289.1 18.1 %attend_back.1 = (bf16[512,1024]{1,0:T(8,128)(2,1)}, bf16[512,512]{1,0:T(8,128)(2,1)}, bf16[512,512]{1,0:T(8,128)(2,1)}) custom-call(s32[1]{0:T(128)} %dynamic_slice.15.scalars, bf16[512,2048]{1,0:T(8,128)(2,1)} %get-tuple-element.82.query.key.value, bf16[512,2048]{1,0:T(8,128)(2,1)} %get-tuple-element.82.query.key.value, ...), custom_call_target="tpu_custom_call" | custom-call | flops 5368709120 | bytes 8388608 | tf_op jit(solution)/shard_map/attend_back/pallas_call | solution.py:304
  307.7 4.5 %adapters_back.1 = (bf16[512,64]{1,0:T(8,128)(2,1)}, bf16[32,16,256]{2,1,0:T(8,128)(2,1)}) custom-call(bf16[512,1024]{1,0:T(8,128)(2,1)} %get-tuple-element.122.grad_query, bf16[512,512]{1,0:T(8,128)(2,1)} %get-tuple-element.123.grad_key, bf16[512,512]{1,0:T(8,128)(2,1)} %get-tuple-element.124.grad_value, bf16[512,64]{1,0:T(8,128)(2,1)} %get-tuple-element.125.low, ...), custom_call_target="tpu_custom_call" | custom-call | flops 1610612736 | bytes 4194304 | tf_op jit(solution)/shard_map/adapters_back/pallas_call | solution.py:791
  312.1 6.1 %all-to-all-start.2 = ((bf16[32,16,256]{2,1,0:T(8,128)(2,1)}), bf16[32,16,256]{2,1,0:T(8,128)(2,1)S(1)}, u32[]{:S(2)}, u32[]{:S(2)}) async-start(bf16[32,16,256]{2,1,0:T(8,128)(2,1)} %get-tuple-element.129), calls=%async_computation.2 | async-start | bytes 524288 | tf_op jit(solution)/shard_map/all_to_all | solution.py:1181
  318.3 8.6 %input_back.1 = bf16[512,1024]{1,0:T(8,128)(2,1)} custom-call(s32[8]{0:T(128)} %broadcast_xor_fusion.order.refs_0_, bf16[512,1024]{1,0:T(8,128)(2,1)} %get-tuple-element.122.grad_query, bf16[512,512]{1,0:T(8,128)(2,1)} %get-tuple-element.123.grad_key, bf16[512,512]{1,0:T(8,128)(2,1)} %get-tuple-element.124.grad_value, ...), custom_call_target="tpu_custom_call" | custom-call | flops 2147483648 | bytes 12582912 | tf_op jit(solution)/shard_map/input_back/pallas_call | solution.py:836
  326.9 6.1 %collective-permute-done.15 = bf16[512,1024]{1,0:T(8,128)(2,1)S(1)} collective-permute-done((bf16[512,1024]{1,0:T(8,128)(2,1)S(1)}, bf16[512,1024]{1,0:T(8,128)(2,1)S(1)}, u32[]{:S(2)}, u32[]{:S(2)}) %collective-permute-start.15) | collective-permute-done | bytes 1048608 | tf_op jit(solution)/shard_map/ppermute | solution.py:1177
  333.0 2.7 add_convert_fusion.2
  335.7 1.4 all-to-all-done.2.pieces
  337.8 2.0 sum_mixer.1
  (93 shorter events, 20.9 us)
Async XLA Ops:
  0.6 19.8 %copy-start.12 = (s32[4,1]{1,0:T(4,128)S(1)}, s32[4,1]{1,0:T(4,128)}, u32[]{:S(2)}) copy-start(s32[4,1]{1,0:T(4,128)} %constant.84) | copy-start | bytes 52
  0.7 19.9 %copy-start.20 = (s32[8]{0:T(128)S(1)}, s32[8]{0:T(128)}, u32[]{:S(2)}) copy-start(s32[8]{0:T(128)} %constant.74.clone) | copy-start | bytes 100
  0.7 10.0 %copy-start.8 = (bf16[8,16,128]{2,1,0:T(8,128)(2,1)S(1)}, bf16[8,16,128]{2,1,0:T(8,128)(2,1)}, u32[]{:S(2)}) copy-start(bf16[8,16,128]{2,1,0:T(8,128)(2,1)} %param.37) | copy-start | bytes 98308
  0.7 16.5 %copy-start.10 = (bf16[1024]{0:T(1024)(128)(2,1)S(1)}, bf16[1024]{0:T(1024)(128)(2,1)}, u32[]{:S(2)}) copy-start(bf16[1024]{0:T(1024)(128)(2,1)} %param.28) | copy-start | bytes 6148
  0.7 17.1 %copy-start.11 = (bf16[1024]{0:T(1024)(128)(2,1)S(1)}, bf16[1024]{0:T(1024)(128)(2,1)}, u32[]{:S(2)}) copy-start(bf16[1024]{0:T(1024)(128)(2,1)} %param.29) | copy-start | bytes 6148
  0.7 17.7 %copy-start.19 = (s32[32]{0:T(128)S(1)}, s32[32]{0:T(128)}, u32[]{:S(2)}) copy-start(s32[32]{0:T(128)} %param.25) | copy-start | bytes 388
  0.7 18.9 %copy-start.9 = (bf16[1024,16]{0,1:T(8,128)(2,1)S(1)}, bf16[1024,16]{0,1:T(8,128)(2,1)}, u32[]{:S(2)}) copy-start(bf16[1024,16]{0,1:T(8,128)(2,1)} %param.32) | copy-start | bytes 98308
  2.8 21.5 %collective-permute-start.1 = (bf16[128,3072]{1,0:T(8,128)(2,1)}, bf16[128,3072]{1,0:T(8,128)(2,1)}, u32[]{:S(2)}, u32[]{:S(2)}) collective-permute-start(bf16[128,3072]{1,0:T(8,128)(2,1)} %pack.1), channel_id=1, source_target_pairs={{0,16},{4,20},{8,24},{12,28},{16,0},{20,4},{24,8},{28,12},{1,17},{... | collective-permute-start | bytes 2359304 | tf_op jit(solution)/shard_map/ppermute | solution.py:954
  5.8 20.5 %collective-permute-start = (bf16[128,3072]{1,0:T(8,128)(2,1)}, bf16[128,3072]{1,0:T(8,128)(2,1)}, u32[]{:S(2)}, u32[]{:S(2)}) collective-permute-start(bf16[128,3072]{1,0:T(8,128)(2,1)} %pack.1), channel_id=1, source_target_pairs={{0,8},{4,12},{8,0},{12,4},{16,24},{20,28},{24,16},{28,20},{1,9},{5... | collective-permute-start | bytes 2359304 | tf_op jit(solution)/shard_map/ppermute | solution.py:954
  12.0 26.2 %all-to-all-start = ((bf16[8,112,128]{2,1,0:T(8,128)(2,1)}), bf16[8,112,128]{2,1,0:T(8,128)(2,1)S(1)}, u32[]{:S(2)}, u32[]{:S(2)}) async-start(bf16[8,112,128]{2,1,0:T(8,128)(2,1)} %gather_fusion.1), calls=%async_computation | async-start | bytes 458752 | tf_op jit(solution)/shard_map/all_to_all | solution.py:1040
  15.4 27.6 %collective-permute-start.4 = (bf16[512,1024]{1,0:T(8,128)(2,1)}, bf16[512,1024]{1,0:T(8,128)(2,1)}, u32[]{:S(2)}, u32[]{:S(2)}) collective-permute-start(bf16[512,1024]{1,0:T(8,128)(2,1)} %refs_1_), channel_id=1, source_target_pairs={{0,1},{1,2},{2,3},{3,0},{4,5},{5,6},{6,7},{7,4},{8,9},{9,10},{10,1... | collective-permute-start | bytes 3145736 | tf_op jit(solution)/shard_map/ppermute | solution.py:1066
  19.7 12.0 %copy-start.6 = (bf16[16,1024]{1,0:T(8,128)(2,1)}, bf16[16,1024]{1,0:T(8,128)(2,1)S(1)}, u32[]{:S(2)}) copy-start(bf16[16,1024]{1,0:T(8,128)(2,1)S(1)} %fusion.refs_5_) | copy-start | bytes 98308
  28.4 14.7 %copy-start.7 = (s32[2048,8]{0,1:T(8,128)S(1)}, s32[2048,8]{0,1:T(8,128)}, u32[]{:S(2)}) copy-start(s32[2048,8]{0,1:T(8,128)} %param.27) | copy-start | bytes 196612
  28.4 8.6 %collective-permute-start.2 = (bf16[64,3072]{1,0:T(8,128)(2,1)S(1)}, bf16[64,3072]{1,0:T(8,128)(2,1)S(1)}, u32[]{:S(2)}, u32[]{:S(2)}) collective-permute-start(bf16[64,3072]{1,0:T(8,128)(2,1)S(1)} %slice.52), channel_id=1, source_target_pairs={{0,8},{4,12},{8,0},{12,4},{16,24},{20,28},{24,16},{28,20},{1,9},{5... | collective-permute-start | bytes 1179656 | tf_op jit(solution)/shard_map/ppermute | solution.py:954
  30.0 8.2 %collective-permute-start.3 = (bf16[64,3072]{1,0:T(8,128)(2,1)S(1)}, bf16[64,3072]{1,0:T(8,128)(2,1)S(1)}, u32[]{:S(2)}, u32[]{:S(2)}) collective-permute-start(bf16[64,3072]{1,0:T(8,128)(2,1)S(1)} %slice.53), channel_id=1, source_target_pairs={{0,16},{4,20},{8,24},{12,28},{16,0},{20,4},{24,8},{28,12},{1,17},{... | collective-permute-start | bytes 1179656 | tf_op jit(solution)/shard_map/ppermute | solution.py:954
  38.2 10.6 %copy-start = (bf16[512,3072]{1,0:T(8,128)(2,1)}, bf16[512,3072]{1,0:T(8,128)(2,1)S(1)}, u32[]{:S(2)}) copy-start(bf16[512,3072]{1,0:T(8,128)(2,1)S(1)} %constant_dynamic-update-slice_fusion.weight_a.refs_6_) | copy-start | bytes 9437188
  43.0 5.8 %collective-permute-start.5 = (bf16[512,3072]{1,0:T(8,128)(2,1)S(1)}, bf16[512,3072]{1,0:T(8,128)(2,1)}, u32[]{:S(2)}, u32[]{:S(2)}) collective-permute-start(bf16[512,3072]{1,0:T(8,128)(2,1)S(1)} %constant_dynamic-update-slice_fusion.weight_a.refs_6_), channel_id=1, source_target_pairs={{0,4},{4,0},{8,12},{12,8},{16,20},{20,16},{24,28},{28,24},{1,5},{5... | collective-permute-start | bytes 9437192 | tf_op jit(solution)/shard_map/ppermute | solution.py:954
  45.2 101.0 %collective-permute-start.7 = (bf16[512,1024]{1,0:T(8,128)(2,1)}, bf16[512,1024]{1,0:T(8,128)(2,1)S(1)}, u32[]{:S(2)}, u32[]{:S(2)}) collective-permute-start(bf16[512,1024]{1,0:T(8,128)(2,1)} %refs_1_), channel_id=1, source_target_pairs={{0,3},{1,0},{2,1},{3,2},{4,7},{5,4},{6,5},{7,6},{8,11},{9,8},{10,9... | collective-permute-start | bytes 3145736 | tf_op jit(solution)/shard_map/ppermute | solution.py:1079
  59.2 117.3 %collective-permute-start.10 = (bf16[512,1024]{1,0:T(8,128)(2,1)}, bf16[512,1024]{1,0:T(8,128)(2,1)S(1)}, u32[]{:S(2)}, u32[]{:S(2)}) collective-permute-start(bf16[512,1024]{1,0:T(8,128)(2,1)} %collective-permute-done.4.cot), channel_id=1, source_target_pairs={{0,1},{1,2},{2,3},{3,0},{4,5},{5,6},{6,7},{7,4},{8,9},{9,10},{10,1... | collective-permute-start | bytes 3145736 | tf_op jit(solution)/shard_map/ppermute | solution.py:1103
  77.8 38.8 %collective-permute-start.8 = (bf16[512,1024]{1,0:T(8,128)(2,1)}, bf16[512,1024]{1,0:T(8,128)(2,1)S(1)}, u32[]{:S(2)}, u32[]{:S(2)}) collective-permute-start(bf16[512,1024]{1,0:T(8,128)(2,1)} %get-tuple-element.92.x), channel_id=1, source_target_pairs={{0,1},{1,2},{2,3},{3,0},{4,5},{5,6},{6,7},{7,4},{8,9},{9,10},{10,1... | collective-permute-start | bytes 3145736 | tf_op jit(solution)/shard_map/ppermute | solution.py:1112
  79.6 27.6 %copy-start.17 = (bf16[512,1024]{1,0:T(8,128)(2,1)S(1)}, bf16[512,1024]{1,0:T(8,128)(2,1)}, u32[]{:S(2)}) copy-start(bf16[512,1024]{1,0:T(8,128)(2,1)} %get-tuple-element.92.x) | copy-start | bytes 3145732
  107.3 38.9 %collective-permute-start.6 = (bf16[512,1024]{1,0:T(8,128)(2,1)S(1)}, bf16[512,1024]{1,0:T(8,128)(2,1)S(1)}, u32[]{:S(2)}, u32[]{:S(2)}) collective-permute-start(bf16[512,1024]{1,0:T(8,128)(2,1)S(1)} %copy-done.17), channel_id=1, source_target_pairs={{0,3},{1,0},{2,1},{3,2},{4,7},{5,4},{6,5},{7,6},{8,11},{9,8},{10,9... | collective-permute-start | bytes 3145736 | tf_op jit(solution)/shard_map/ppermute | solution.py:1136
  116.6 1.0 copy-start.15
  144.4 32.1 %collective-permute-start.9 = (bf16[512,1024]{1,0:T(8,128)(2,1)}, bf16[512,1024]{1,0:T(8,128)(2,1)S(1)}, u32[]{:S(2)}, u32[]{:S(2)}) collective-permute-start(bf16[512,1024]{1,0:T(8,128)(2,1)} %copy-done.15), channel_id=1, source_target_pairs={{0,1},{1,2},{2,3},{3,0},{4,5},{5,6},{6,7},{7,4},{8,9},{9,10},{10,1... | collective-permute-start | bytes 3145736 | tf_op jit(solution)/shard_map/ppermute | solution.py:1139
  146.2 1.0 copy-start.14
  147.2 1.0 copy-start.18
  174.9 49.5 %collective-permute-start.11 = (bf16[1040,1024]{1,0:T(8,128)(2,1)}, bf16[1040,1024]{1,0:T(8,128)(2,1)}, u32[]{:S(2)}, u32[]{:S(2)}) collective-permute-start(bf16[1040,1024]{1,0:T(8,128)(2,1)} %get-tuple-element.108), channel_id=1, source_target_pairs={{0,1},{1,2},{2,3},{3,0},{4,5},{5,6},{6,7},{7,4},{8,9},{9,10},{10,1... | collective-permute-start | bytes 6389768 | tf_op jit(solution)/shard_map/ppermute | solution.py:1148
  176.5 1.1 copy-start.13
  177.6 1.0 copy-start.16
  205.3 33.3 %all-to-all-start.1 = ((bf16[8,4,288,128]{3,2,1,0:T(8,128)(2,1)}), bf16[8,4,288,128]{3,2,1,0:T(8,128)(2,1)S(1)}, u32[]{:S(2)}, u32[]{:S(2)}) async-start(bf16[8,4,288,128]{3,2,1,0:T(8,128)(2,1)} %get-tuple-element.110), calls=%async_computation.1 | async-start | bytes 4718592 | tf_op jit(solution)/shard_map/all_to_all | solution.py:1143
  227.4 25.8 %collective-permute-start.12 = (bf16[528,1024]{1,0:T(8,128)(2,1)}, bf16[528,1024]{1,0:T(8,128)(2,1)S(1)}, u32[]{:S(2)}, u32[]{:S(2)}) collective-permute-start(bf16[528,1024]{1,0:T(8,128)(2,1)} %add_convert_fusion.1), channel_id=1, source_target_pairs={{0,1},{1,2},{2,3},{3,0},{4,5},{5,6},{6,7},{7,4},{8,9},{9,10},{10,1... | collective-permute-start | bytes 3244040 | tf_op jit(solution)/shard_map/ppermute | solution.py:1154
  238.6 1.5 copy-start.2
  238.6 14.7 %copy-start.4 = (bf16[1040,1024]{1,0:T(8,128)(2,1)S(1)}, bf16[1040,1024]{1,0:T(8,128)(2,1)}, u32[]{:S(2)}) copy-start(bf16[1040,1024]{1,0:T(8,128)(2,1)} %get-tuple-element.101) | copy-start | bytes 6389764
  253.7 24.8 %collective-permute-start.13 = (bf16[528,1024]{1,0:T(8,128)(2,1)S(1)}, bf16[528,1024]{1,0:T(8,128)(2,1)S(1)}, u32[]{:S(2)}, u32[]{:S(2)}) collective-permute-start(bf16[528,1024]{1,0:T(8,128)(2,1)S(1)} %add_convert_fusion), channel_id=1, source_target_pairs={{0,1},{1,2},{2,3},{3,0},{4,5},{5,6},{6,7},{7,4},{8,9},{9,10},{10,1... | collective-permute-start | bytes 3244040 | tf_op jit(solution)/shard_map/ppermute | solution.py:1154
  278.5 1.0 copy-start.1
  278.5 28.7 %collective-permute-start.14 = (bf16[512,1024]{1,0:T(8,128)(2,1)S(1)}, bf16[512,1024]{1,0:T(8,128)(2,1)S(1)}, u32[]{:S(2)}, u32[]{:S(2)}) collective-permute-start(bf16[512,1024]{1,0:T(8,128)(2,1)S(1)} %add_convert_fusion.4), channel_id=1, source_target_pairs={{0,1},{1,2},{2,3},{3,0},{4,5},{5,6},{6,7},{7,4},{8,9},{9,10},{10,1... | collective-permute-start | bytes 3145736 | tf_op jit(solution)/shard_map/ppermute | solution.py:1158
  307.6 25.4 %collective-permute-start.15 = (bf16[512,1024]{1,0:T(8,128)(2,1)S(1)}, bf16[512,1024]{1,0:T(8,128)(2,1)S(1)}, u32[]{:S(2)}, u32[]{:S(2)}) collective-permute-start(bf16[512,1024]{1,0:T(8,128)(2,1)S(1)} %add_convert_fusion.3), channel_id=1, source_target_pairs={{0,1},{1,2},{2,3},{3,0},{4,5},{5,6},{6,7},{7,4},{8,9},{9,10},{10,1... | collective-permute-start | bytes 3145736 | tf_op jit(solution)/shard_map/ppermute | solution.py:1177
  312.1 25.0 %all-to-all-start.2 = ((bf16[32,16,256]{2,1,0:T(8,128)(2,1)}), bf16[32,16,256]{2,1,0:T(8,128)(2,1)S(1)}, u32[]{:S(2)}, u32[]{:S(2)}) async-start(bf16[32,16,256]{2,1,0:T(8,128)(2,1)} %get-tuple-element.129), calls=%async_computation.2 | async-start | bytes 524288 | tf_op jit(solution)/shard_map/all_to_all | solution.py:1181
  318.3 14.8 %copy-start.3 = (f32[512,1024]{1,0:T(8,128)S(1)}, f32[512,1024]{1,0:T(8,128)}, u32[]{:S(2)}) copy-start(f32[512,1024]{1,0:T(8,128)} %get-tuple-element.85.refs_2_) | copy-start | bytes 6291460
  337.1 0.7 copy-start.5
